TPU v7x, 32 devices: a whole 2x2x4 slice. The times are simulated.
32 devices in a mesh: dp: 8 (over z, y), ctx: 4 (over x, core).
Axes of the slice: x: 2, y: 2, z: 4, core: 2. Of those that a mesh axis runs over, the one named last changes fastest.
Arguments:
- tokens: bfloat16 [8, 2048, 1024], P('dp', 'ctx'), may hold values from -6 to 6
- time_feat: bfloat16 [8, 1024], P('dp'), may hold values from -6 to 6
- cotangent: bfloat16 [8, 2048, 1024], P('dp', 'ctx'), may hold values from -6 to 6
- segment_ids: int32 [8, 2048], P('dp'), may hold values from 0 to 7, never falling along the last dimension, each value on 1 to 1024 neighbouring positions
- time_weight: bfloat16 [1024, 1024], P(('dp', 'ctx')), may hold values from -0.1875 to 0.1875
- time_bias: bfloat16 [1024], P(('dp', 'ctx')), may hold values from -3 to 3
- query_weight: bfloat16 [1024, 1024], P(('dp', 'ctx')), may hold values from -0.1875 to 0.1875
- query_bias: bfloat16 [1024], P(('dp', 'ctx')), may hold values from -3 to 3
- key_weight: bfloat16 [1024, 1024], P(('dp', 'ctx')), may hold values from -0.1875 to 0.1875
- value_weight: bfloat16 [1024, 1024], P(('dp', 'ctx')), may hold values from -0.1875 to 0.1875
- value_bias: bfloat16 [1024], P(('dp', 'ctx')), may hold values from -3 to 3
- output_weight: bfloat16 [1024, 1024], P(('dp', 'ctx')), may hold values from -3 to 3
- output_bias: bfloat16 [1024], P(('dp', 'ctx')), may hold values from -3 to 3
- mixing_gain: bfloat16 [1024], P(('dp', 'ctx')), may hold values from 0.5 to 1.5
- mixing_bias: bfloat16 [1024], P(('dp', 'ctx')), may hold values from -3 to 3
- up_weight: bfloat16 [1024, 4096], P(('dp', 'ctx')), may hold values from -0.1875 to 0.1875
- up_bias: bfloat16 [4096], P(('dp', 'ctx')), may hold values from -3 to 3
- down_weight: bfloat16 [4096, 1024], P(('dp', 'ctx')), may hold values from -0.09375 to 0.09375
- down_bias: bfloat16 [1024], P(('dp', 'ctx')), may hold values from -3 to 3
- final_gain: bfloat16 [1024], P(('dp', 'ctx')), may hold values from 0.5 to 1.5
- final_bias: bfloat16 [1024], P(('dp', 'ctx')), may hold values from -3 to 3
Outputs:
- layer_out: bfloat16 [8, 2048, 1024], P('dp', 'ctx')
- tokens_grad: bfloat16 [8, 2048, 1024], P('dp', 'ctx')
- time_weight_grad: float32 [1024, 1024], P(('dp', 'ctx'))
- time_bias_grad: float32 [1024], P(('dp', 'ctx'))
- query_weight_grad: float32 [1024, 1024], P(('dp', 'ctx'))
- query_bias_grad: float32 [1024], P(('dp', 'ctx'))
- key_weight_grad: float32 [1024, 1024], P(('dp', 'ctx'))
- value_weight_grad: float32 [1024, 1024], P(('dp', 'ctx'))
- value_bias_grad: float32 [1024], P(('dp', 'ctx'))
- output_weight_grad: float32 [1024, 1024], P(('dp', 'ctx'))
- output_bias_grad: float32 [1024], P(('dp', 'ctx'))
- mixing_gain_grad: float32 [1024], P(('dp', 'ctx'))
- mixing_bias_grad: float32 [1024], P(('dp', 'ctx'))
- up_weight_grad: float32 [1024, 4096], P(('dp', 'ctx'))
- up_bias_grad: float32 [4096], P(('dp', 'ctx'))
- down_weight_grad: float32 [4096, 1024], P(('dp', 'ctx'))
- down_bias_grad: float32 [1024], P(('dp', 'ctx'))
- final_gain_grad: float32 [1024], P(('dp', 'ctx'))
- final_bias_grad: float32 [1024], P(('dp', 'ctx'))
Inputs may be any that keep to these rules, and one draw needn't show every extreme that they name: `segment_ids`: in each row the document numbers never fall, every number appears, each document holds 1 to 1024 tokens and some document of every row holds exactly 1024.
All inputs are finite; a program needn't handle non-finite values.
Results may differ from a plain program's by a relative error of at most 0.018.
Values may be sent and summed in bfloat16 or wider, within the bound.
No kernel may reach another device: no remote copies, remote signals or barrier semaphores. Data moves between devices by JAX's collectives and lax.ppermute only.
A program may use at most 192 MiB of HBM per device.

v0:
```python
from functools import partial

import jax
import jax.numpy as jnp
from jax import lax
from jax.sharding import PartitionSpec as P

HEAD_DIM = 64


highest = lax.Precision.HIGHEST
norm_epsilon = 1e-05
masked_score = -1e30


def matmul_plain(left, right):
    return jnp.dot(left, right, preferred_element_type=jnp.float32)


def matmul_lead(left, right):
    return lax.dot_general(
        left, right, (((0,), (0,)), ((), ())), preferred_element_type=jnp.float32
    )


def matmul_tail(left, right):
    return lax.dot_general(
        left, right, (((1,), (1,)), ((), ())), preferred_element_type=jnp.float32
    )


def normalize(values, gain, shift):
    average = jnp.mean(values, axis=-1, keepdims=True)
    centered = values - average
    variance = jnp.mean(centered * centered, axis=-1, keepdims=True)
    inverse = lax.rsqrt(variance + norm_epsilon)
    normed = centered * inverse
    return (normed * gain.astype(jnp.float32) + shift.astype(jnp.float32), normed, inverse)


def normalize_back(upstream, normed, inverse, gain):
    scaled = upstream * gain.astype(jnp.float32)
    plain_mean = jnp.mean(scaled, axis=-1, keepdims=True)
    cross_mean = jnp.mean(scaled * normed, axis=-1, keepdims=True)
    result = inverse * (scaled - plain_mean - normed * cross_mean)
    return (result, jnp.sum(upstream * normed, axis=0), jnp.sum(upstream, axis=0))


def head_scores(query_head, key_head, same_doc):
    scores = matmul_tail(query_head, key_head) * HEAD_DIM ** (-0.5)
    return jnp.where(same_doc, scores, masked_score)


def head_slice(matrix, head_index):
    return lax.dynamic_slice_in_dim(matrix, head_index * HEAD_DIM, HEAD_DIM, 1)


def merge_heads(stacked):
    return stacked.transpose(1, 0, 2).reshape(stacked.shape[1], stacked.shape[0] * stacked.shape[2])


def row_forward(row_item):
    query_row, key_row, value_row, same_doc = row_item

    def one_head(head_index):
        query_head = head_slice(query_row, head_index)
        key_head = head_slice(key_row, head_index)
        value_head = head_slice(value_row, head_index)
        scores = head_scores(query_head, key_head, same_doc)
        row_peak = jnp.max(scores, axis=1, keepdims=True)
        unscaled = jnp.exp(scores - row_peak)
        row_total = jnp.sum(unscaled, axis=1, keepdims=True)
        attn_probs = (unscaled / row_total).astype(jnp.bfloat16)
        return (matmul_plain(attn_probs, value_head), row_peak + jnp.log(row_total))

    mixture, logsum = lax.map(one_head, jnp.arange(query_row.shape[1] // HEAD_DIM))
    return (merge_heads(mixture), logsum)


def row_backward(with_keys, row_item):
    query_row, key_row, value_row, grad_row, logsum_row, same_doc = row_item
    scale = HEAD_DIM ** (-0.5)

    def one_head(head_index):
        query_head = head_slice(query_row, head_index)
        key_head = head_slice(key_row, head_index)
        value_head = head_slice(value_row, head_index)
        grad_head = head_slice(grad_row, head_index)
        scores = head_scores(query_head, key_head, same_doc)
        attn_probs = jnp.exp(scores - logsum_row[head_index])
        grad_probs = matmul_tail(grad_head, value_head)
        row_delta = jnp.sum(attn_probs * grad_probs, axis=1, keepdims=True)
        grad_scores = (attn_probs * (grad_probs - row_delta)).astype(jnp.bfloat16)
        grad_query_head = matmul_plain(grad_scores, key_head) * scale
        grad_key_head = matmul_lead(grad_scores, query_head) * scale
        grad_value_head = matmul_lead(attn_probs.astype(jnp.bfloat16), grad_head)
        return (grad_query_head, grad_key_head, grad_value_head)

    heads_out = lax.map(one_head, jnp.arange(query_row.shape[1] // HEAD_DIM))
    return (merge_heads(heads_out[0]), merge_heads(heads_out[1]), merge_heads(heads_out[2]))


def shards(
    tokens,
    time_feat,
    cotangent,
    segment_ids,
    time_weight,
    time_bias,
    query_weight,
    query_bias,
    key_weight,
    value_weight,
    value_bias,
    output_weight,
    output_bias,
    mixing_gain,
    mixing_bias,
    up_weight,
    up_bias,
    down_weight,
    down_bias,
    final_gain,
    final_bias,
):
    attention_shards = (
        time_weight,
        query_weight,
        key_weight,
        value_weight,
        output_weight,
        time_bias,
        query_bias,
        value_bias,
        output_bias,
        mixing_gain,
        mixing_bias,
    )
    feed_shards = (up_weight, down_weight, up_bias, down_bias, final_gain, final_bias)
    (
        time_full,
        query_full,
        key_full,
        value_full,
        output_full,
        time_shift_full,
        query_shift,
        value_shift,
        output_shift,
        gain_one,
        bias_one,
    ) = (
        lax.all_gather(attention_shards[0], ("dp", "ctx"), axis=0, tiled=True),
        lax.all_gather(attention_shards[1], ("dp", "ctx"), axis=0, tiled=True),
        lax.all_gather(attention_shards[2], ("dp", "ctx"), axis=0, tiled=True),
        lax.all_gather(attention_shards[3], ("dp", "ctx"), axis=0, tiled=True),
        lax.all_gather(attention_shards[4], ("dp", "ctx"), axis=0, tiled=True),
        lax.all_gather(attention_shards[5], ("dp", "ctx"), axis=0, tiled=True),
        lax.all_gather(attention_shards[6], ("dp", "ctx"), axis=0, tiled=True),
        lax.all_gather(attention_shards[7], ("dp", "ctx"), axis=0, tiled=True),
        lax.all_gather(attention_shards[8], ("dp", "ctx"), axis=0, tiled=True),
        lax.all_gather(attention_shards[9], ("dp", "ctx"), axis=0, tiled=True),
        lax.all_gather(attention_shards[10], ("dp", "ctx"), axis=0, tiled=True),
    )
    row_count, piece_len, model_width = tokens.shape
    token_count = row_count * piece_len
    offset = lax.axis_index("ctx") * piece_len
    local_ids = lax.dynamic_slice_in_dim(segment_ids, offset, piece_len, 1)
    same_rows = local_ids[:, :, None] == segment_ids[:, None, :]
    time_shift = matmul_plain(time_feat, time_full) + time_shift_full.astype(jnp.float32)
    residual_in = (tokens.astype(jnp.float32) + time_shift[:, None, :]).reshape(
        token_count, model_width
    )
    start_low = residual_in.astype(jnp.bfloat16)
    queries = (matmul_plain(start_low, query_full) + query_shift.astype(jnp.float32)).astype(
        jnp.bfloat16
    )
    keys_local = matmul_plain(start_low, key_full).astype(jnp.bfloat16)
    values_local = (matmul_plain(start_low, value_full) + value_shift.astype(jnp.float32)).astype(
        jnp.bfloat16
    )
    key_pieces = keys_local.reshape(row_count, piece_len, model_width)
    value_pieces = values_local.reshape(row_count, piece_len, model_width)
    key_rows, value_rows = (
        lax.all_gather(key_pieces, "ctx", axis=1, tiled=True),
        lax.all_gather(value_pieces, "ctx", axis=1, tiled=True),
    )
    query_pieces = queries.reshape(row_count, piece_len, model_width)
    mixture, logsum = lax.map(row_forward, (query_pieces, key_rows, value_rows, same_rows))
    attended = mixture.reshape(token_count, model_width).astype(jnp.bfloat16)
    branch = matmul_plain(attended, output_full) + output_shift.astype(jnp.float32)
    hidden_one, normed_one, inverse_one = normalize(residual_in + branch, gain_one, bias_one)
    hidden_low = hidden_one.astype(jnp.bfloat16)
    up_full, down_full, up_shift, down_shift, gain_two, bias_two = (
        lax.all_gather(feed_shards[0], ("dp", "ctx"), axis=0, tiled=True),
        lax.all_gather(feed_shards[1], ("dp", "ctx"), axis=0, tiled=True),
        lax.all_gather(feed_shards[2], ("dp", "ctx"), axis=0, tiled=True),
        lax.all_gather(feed_shards[3], ("dp", "ctx"), axis=0, tiled=True),
        lax.all_gather(feed_shards[4], ("dp", "ctx"), axis=0, tiled=True),
        lax.all_gather(feed_shards[5], ("dp", "ctx"), axis=0, tiled=True),
    )
    pre_gelu = matmul_plain(hidden_low, up_full) + up_shift.astype(jnp.float32)
    activated = jax.nn.gelu(pre_gelu, approximate=False).astype(jnp.bfloat16)
    feed_out = matmul_plain(activated, down_full) + down_shift.astype(jnp.float32)
    result, normed_two, inverse_two = normalize(hidden_one + feed_out, gain_two, bias_two)
    layer_out = result.astype(jnp.bfloat16).reshape(row_count, piece_len, model_width)
    up_full, down_full, up_shift, down_shift, gain_two, bias_two = (
        lax.all_gather(feed_shards[0], ("dp", "ctx"), axis=0, tiled=True),
        lax.all_gather(feed_shards[1], ("dp", "ctx"), axis=0, tiled=True),
        lax.all_gather(feed_shards[2], ("dp", "ctx"), axis=0, tiled=True),
        lax.all_gather(feed_shards[3], ("dp", "ctx"), axis=0, tiled=True),
        lax.all_gather(feed_shards[4], ("dp", "ctx"), axis=0, tiled=True),
        lax.all_gather(feed_shards[5], ("dp", "ctx"), axis=0, tiled=True),
    )
    upstream = cotangent.astype(jnp.float32).reshape(token_count, model_width)
    grad_two, gain_two_grad, bias_two_grad = normalize_back(
        upstream, normed_two, inverse_two, gain_two
    )
    grad_feed = grad_two.astype(jnp.bfloat16)
    down_grad = matmul_lead(activated, grad_feed)
    down_shift_grad = jnp.sum(grad_feed.astype(jnp.float32), axis=0)
    unused_value, gelu_pull = jax.vjp(partial(jax.nn.gelu, approximate=False), pre_gelu)
    grad_inner = gelu_pull(matmul_tail(grad_feed, down_full))[0].astype(jnp.bfloat16)
    up_grad = matmul_lead(hidden_low, grad_inner)
    up_shift_grad = jnp.sum(grad_inner.astype(jnp.float32), axis=0)
    grad_hidden = grad_two + matmul_tail(grad_inner, up_full)
    (
        up_weight_grad,
        down_weight_grad,
        up_bias_grad,
        down_bias_grad,
        final_gain_grad,
        final_bias_grad,
    ) = (
        lax.psum_scatter(up_grad, ("dp", "ctx"), scatter_dimension=0, tiled=True),
        lax.psum_scatter(down_grad, ("dp", "ctx"), scatter_dimension=0, tiled=True),
        lax.psum_scatter(up_shift_grad, ("dp", "ctx"), scatter_dimension=0, tiled=True),
        lax.psum_scatter(down_shift_grad, ("dp", "ctx"), scatter_dimension=0, tiled=True),
        lax.psum_scatter(gain_two_grad, ("dp", "ctx"), scatter_dimension=0, tiled=True),
        lax.psum_scatter(bias_two_grad, ("dp", "ctx"), scatter_dimension=0, tiled=True),
    )
    (
        time_full,
        query_full,
        key_full,
        value_full,
        output_full,
        time_shift_full,
        query_shift,
        value_shift,
        output_shift,
        gain_one,
        bias_one,
    ) = (
        lax.all_gather(attention_shards[0], ("dp", "ctx"), axis=0, tiled=True),
        lax.all_gather(attention_shards[1], ("dp", "ctx"), axis=0, tiled=True),
        lax.all_gather(attention_shards[2], ("dp", "ctx"), axis=0, tiled=True),
        lax.all_gather(attention_shards[3], ("dp", "ctx"), axis=0, tiled=True),
        lax.all_gather(attention_shards[4], ("dp", "ctx"), axis=0, tiled=True),
        lax.all_gather(attention_shards[5], ("dp", "ctx"), axis=0, tiled=True),
        lax.all_gather(attention_shards[6], ("dp", "ctx"), axis=0, tiled=True),
        lax.all_gather(attention_shards[7], ("dp", "ctx"), axis=0, tiled=True),
        lax.all_gather(attention_shards[8], ("dp", "ctx"), axis=0, tiled=True),
        lax.all_gather(attention_shards[9], ("dp", "ctx"), axis=0, tiled=True),
        lax.all_gather(attention_shards[10], ("dp", "ctx"), axis=0, tiled=True),
    )
    grad_one, gain_one_grad, bias_one_grad = normalize_back(
        grad_hidden, normed_one, inverse_one, gain_one
    )
    grad_branch = grad_one.astype(jnp.bfloat16)
    output_grad = matmul_lead(attended, grad_branch)
    output_shift_grad = jnp.sum(grad_branch.astype(jnp.float32), axis=0)
    grad_attended = matmul_tail(grad_branch, output_full).astype(jnp.bfloat16)
    grad_pieces = grad_attended.reshape(row_count, piece_len, model_width)
    grad_query_rows, grad_key_parts, grad_value_parts = lax.map(
        partial(row_backward, True),
        (query_pieces, key_rows, value_rows, grad_pieces, logsum, same_rows),
    )
    grad_key_sum, grad_value_sum = (
        lax.psum_scatter(
            grad_key_parts.astype(jnp.bfloat16), "ctx", scatter_dimension=1, tiled=True
        ).astype(jnp.float32),
        lax.psum_scatter(
            grad_value_parts.astype(jnp.bfloat16), "ctx", scatter_dimension=1, tiled=True
        ).astype(jnp.float32),
    )
    grad_query = grad_query_rows.reshape(token_count, model_width).astype(jnp.bfloat16)
    grad_key = grad_key_sum.reshape(token_count, model_width).astype(jnp.bfloat16)
    grad_value = grad_value_sum.reshape(token_count, model_width).astype(jnp.bfloat16)
    query_grad = matmul_lead(start_low, grad_query)
    query_shift_grad = jnp.sum(grad_query.astype(jnp.float32), axis=0)
    key_grad = matmul_lead(start_low, grad_key)
    value_grad = matmul_lead(start_low, grad_value)
    value_shift_grad = jnp.sum(grad_value.astype(jnp.float32), axis=0)
    grad_start = (
        grad_one
        + matmul_tail(grad_query, query_full)
        + matmul_tail(grad_key, key_full)
        + matmul_tail(grad_value, value_full)
    )
    tokens_grad = grad_start.astype(jnp.bfloat16).reshape(row_count, piece_len, model_width)
    time_shift_grad = jnp.sum(grad_start, axis=0)
    row_sums = jnp.sum(grad_start.reshape(row_count, piece_len, model_width), axis=1)
    time_grad = lax.dot_general(
        time_feat.astype(jnp.float32),
        row_sums,
        (((0,), (0,)), ((), ())),
        precision=highest,
        preferred_element_type=jnp.float32,
    )
    (
        time_weight_grad,
        query_weight_grad,
        key_weight_grad,
        value_weight_grad,
        output_weight_grad,
        time_bias_grad,
        query_bias_grad,
        value_bias_grad,
        output_bias_grad,
        mixing_gain_grad,
        mixing_bias_grad,
    ) = (
        lax.psum_scatter(time_grad, ("dp", "ctx"), scatter_dimension=0, tiled=True),
        lax.psum_scatter(query_grad, ("dp", "ctx"), scatter_dimension=0, tiled=True),
        lax.psum_scatter(key_grad, ("dp", "ctx"), scatter_dimension=0, tiled=True),
        lax.psum_scatter(value_grad, ("dp", "ctx"), scatter_dimension=0, tiled=True),
        lax.psum_scatter(output_grad, ("dp", "ctx"), scatter_dimension=0, tiled=True),
        lax.psum_scatter(time_shift_grad, ("dp", "ctx"), scatter_dimension=0, tiled=True),
        lax.psum_scatter(query_shift_grad, ("dp", "ctx"), scatter_dimension=0, tiled=True),
        lax.psum_scatter(value_shift_grad, ("dp", "ctx"), scatter_dimension=0, tiled=True),
        lax.psum_scatter(output_shift_grad, ("dp", "ctx"), scatter_dimension=0, tiled=True),
        lax.psum_scatter(gain_one_grad, ("dp", "ctx"), scatter_dimension=0, tiled=True),
        lax.psum_scatter(bias_one_grad, ("dp", "ctx"), scatter_dimension=0, tiled=True),
    )
    return (
        layer_out,
        tokens_grad,
        time_weight_grad,
        time_bias_grad,
        query_weight_grad,
        query_bias_grad,
        key_weight_grad,
        value_weight_grad,
        value_bias_grad,
        output_weight_grad,
        output_bias_grad,
        mixing_gain_grad,
        mixing_bias_grad,
        up_weight_grad,
        up_bias_grad,
        down_weight_grad,
        down_bias_grad,
        final_gain_grad,
        final_bias_grad,
    )


def solution(mesh):
    placed = (
        P("dp", "ctx", None),
        P("dp", None),
        P("dp", "ctx", None),
        P("dp", None),
        P(("dp", "ctx"), None),
        P(("dp", "ctx")),
        P(("dp", "ctx"), None),
        P(("dp", "ctx")),
        P(("dp", "ctx"), None),
        P(("dp", "ctx"), None),
        P(("dp", "ctx")),
        P(("dp", "ctx"), None),
        P(("dp", "ctx")),
        P(("dp", "ctx")),
        P(("dp", "ctx")),
        P(("dp", "ctx"), None),
        P(("dp", "ctx")),
        P(("dp", "ctx"), None),
        P(("dp", "ctx")),
        P(("dp", "ctx")),
        P(("dp", "ctx")),
    )
    return jax.shard_map(
        shards,
        mesh=mesh,
        in_specs=placed,
        out_specs=(
            P("dp", "ctx", None),
            P("dp", "ctx", None),
            P(("dp", "ctx"), None),
            P(("dp", "ctx")),
            P(("dp", "ctx"), None),
            P(("dp", "ctx")),
            P(("dp", "ctx"), None),
            P(("dp", "ctx"), None),
            P(("dp", "ctx")),
            P(("dp", "ctx"), None),
            P(("dp", "ctx")),
            P(("dp", "ctx")),
            P(("dp", "ctx")),
            P(("dp", "ctx"), None),
            P(("dp", "ctx")),
            P(("dp", "ctx"), None),
            P(("dp", "ctx")),
            P(("dp", "ctx")),
            P(("dp", "ctx")),
        ),
        check_vma=False,
    )
```

profile of v0, /device:TPU:0, one launch (start us, length us, event | category | flops | bytes accessed | tf_op | source)
XLA Modules:
  0.0 2039.5 jit_solution(10440876434843074150)
XLA Ops:
  17.6 42.5 %all-reduce.20 = (bf16[1024]{0:T(1024)(128)(2,1)S(1)}, bf16[1024]{0:T(1024)(128)(2,1)S(1)}, bf16[1024]{0:T(1024)(128)(2,1)S(1)}, bf16[1024]{0:T(1024)(128)(2,1)S...) all-reduce(bf16[1024]{0:T(1024)(128)(2,1)S(1)} %dynamic-update-slic, ...), channel_id=1, replica_groups=mesh['dp'=8,'ctx'=4] {'dp','ctx'}, use_global_device_ids=true, to_apply=%add.1 | all-reduce | flops 9216 | bytes 36864
  72.2 55.9 %all-gather.19.cloned.1.call-done = bf16[1024,1024]{1,0:T(8,128)(2,1)} async-done(((bf16[32,1024]{1,0:T(8,128)(2,1)}), bf16[1024,1024]{1,0:T(8,128)(2,1)}) %all-gather.19.cloned.1.call-update) | async-done | bytes 2097168 | tf_op jit(solution)/shard_map/all_gather | solution.py:156
  132.3 53.7 %all-gather.17.cloned.1.call-done = bf16[1024,1024]{1,0:T(8,128)(2,1)} async-done(((bf16[32,1024]{1,0:T(8,128)(2,1)}), bf16[1024,1024]{1,0:T(8,128)(2,1)}) %all-gather.17.cloned.1.call-update) | async-done | bytes 2097168 | tf_op jit(solution)/shard_map/all_gather | solution.py:155
  192.2 39.4 %all-gather.2 = bf16[32,1,128]{2,1,0:T(2,128)(2,1)S(1)} all-gather(bf16[1,1,128]{2,1,0:T(2,128)(2,1)S(1)} %bitcast.148), channel_id=1, replica_groups=mesh['dp'=8,'ctx'=4] {'dp','ctx'}, dimensions={0}, use_global_device_ids=true | all-gather | bytes 8448 | tf_op jit(solution)/shard_map/all_gather | solution.py:197
  231.7 12.1 all-gather.15.cloned.1.call-done
  246.6 32.5 %all-gather.29.cloned.1.call-done = bf16[2048,1024]{1,0:T(8,128)(2,1)} async-done(((bf16[512,1024]{1,0:T(8,128)(2,1)}), bf16[2048,1024]{1,0:T(8,128)(2,1)}) %all-gather.29.cloned.1.call-update) | async-done | bytes 4194320 | tf_op jit(solution)/shard_map/all_gather | solution.py:186
  279.1 36.5 %all-gather.27.cloned.1.call-done = bf16[2048,1024]{1,0:T(8,128)(2,1)} async-done(((bf16[512,1024]{1,0:T(8,128)(2,1)}), bf16[2048,1024]{1,0:T(8,128)(2,1)}) %all-gather.27.cloned.1.call-update) | async-done | bytes 4194320 | tf_op jit(solution)/shard_map/all_gather | solution.py:185
  315.7 100.0 %while.48 = (s32[]{:T(128)}, bf16[16,512,64]{1,2,0:T(8,128)(2,1)S(1)}, f32[16,512,1]{1,2,0:T(1,128)S(1)}, s32[16]{0:T(128)S(1)}, bf16[512,1024]{1,0:T(8,128)(2,1...) while((s32[]{:T(128)}, ...), condition=%wide.region_3.4_spmd.clone, body=%wide.region_0.3_spmd.clone.sunk | while | flops 277872128 | bytes 13926079 | solution.py:76
  420.3 33.4 %all-gather.23.cloned.1.call-done = bf16[1024,4096]{1,0:T(8,128)(2,1)} async-done(((bf16[32,4096]{1,0:T(8,128)(2,1)}), bf16[1024,4096]{1,0:T(8,128)(2,1)}) %all-gather.23.cloned.1.call-update) | async-done | bytes 8388624 | tf_op jit(solution)/shard_map/all_gather | solution.py:195
  453.7 27.5 %multiply_convert_fusion.1 = (bf16[512,4096]{1,0:T(8,128)(2,1)}, f32[512,4096]{1,0:T(8,128)}, f32[512,4096]{1,0:T(8,128)}) fusion(f32[4096]{0:T(1024)S(1)} %bitcast.146, bf16[1024,4096]{1,0:T(8,128)(2,1)} %all-gather.23.cloned.1.call-done, f32[512,1024]{1,0:T(8,128)S(1)} %get-tuple-element.309, f32[1024]{0:T(1024)S(1)} %convert_element_type.187, ...), kind=kOutput, calls=%fused_computation.46 | convolution fusion | flops 4436000768 | bytes 31485952 | tf_op jit(solution)/shard_map/dot_general | solution.py:17
  481.1 51.1 %all-gather.25.cloned.1.call-done = bf16[4096,1024]{1,0:T(8,128)(2,1)} async-done(((bf16[128,1024]{1,0:T(8,128)(2,1)}), bf16[4096,1024]{1,0:T(8,128)(2,1)}) %all-gather.25.cloned.1.call-update) | async-done | bytes 8388624 | tf_op jit(solution)/shard_map/all_gather | solution.py:196
  544.1 14.2 convert_reduce_fusion
  572.8 288.2 %while.49 = (s32[]{:T(128)}, bf16[16,512,64]{1,2,0:T(8,128)(2,1)S(1)}, bf16[16,2048,64]{1,2,0:T(8,128)(2,1)}, bf16[16,2048,64]{1,2,0:T(8,128)(2,1)}, s32[16]{0:T...) while((s32[]{:T(128)}, ...), condition=%wide.region_14.15_spmd.clone, body=%wide.region_12.14_spmd.clone.sunk | while | flops 681737728 | bytes 51535652 | solution.py:99
  876.5 27.7 %reduce-scatter.10.cloned.1.call-done = bf16[1,512,1024]{1,2,0:T(8,128)(2,1)} async-done(((bf16[1,2048,1024]{1,2,0:T(8,128)(2,1)}), bf16[1,512,1024]{1,2,0:T(8,128)(2,1)}) %reduce-scatter.10.cloned.1.call-update) | async-done | bytes 1048592 | tf_op jit(solution)/shard_map/reduce_scatter | solution.py:280
  908.8 42.4 %reduce-scatter.12.cloned.1.call-done = bf16[1,512,1024]{1,2,0:T(8,128)(2,1)} async-done(((bf16[1,2048,1024]{1,2,0:T(8,128)(2,1)}), bf16[1,512,1024]{1,2,0:T(8,128)(2,1)}) %reduce-scatter.12.cloned.1.call-update) | async-done | bytes 1048592 | tf_op jit(solution)/shard_map/reduce_scatter | solution.py:283
  968.8 10.5 fusion.73
  993.3 41.1 %all-reduce.19 = (f32[1024]{0:T(1024)S(1)}, f32[1024]{0:T(1024)S(1)}, f32[1024]{0:T(1024)S(1)}, f32[1024]{0:T(1024)S(1)}, f32[1024]{0:T(1024)S(1)}, /*index=5*/f...) all-reduce(f32[1024]{0:T(1024)S(1)} %get-tuple-element.306, ...), channel_id=7, replica_groups=mesh['dp'=8,'ctx'=4] {'dp','ctx'}, use_global_device_ids=true, to_apply=%region_19.20.clone | all-reduce | flops 13312 | bytes 106496
  1040.2 56.7 %reduce-scatter.16.cloned.1.call-done = f32[32,1024]{1,0:T(8,128)} async-done(((f32[1024,1024]{1,0:T(8,128)}), f32[32,1024]{1,0:T(8,128)}) %reduce-scatter.16.cloned.1.call-update) | async-done | bytes 131088 | tf_op jit(solution)/shard_map/reduce_scatter | solution.py:325
  1096.9 141.8 %reduce-scatter.22.cloned.1.call-done = f32[32,1024]{1,0:T(8,128)} async-done(((f32[1024,1024]{1,0:T(8,128)}), f32[32,1024]{1,0:T(8,128)}) %reduce-scatter.22.cloned.1.call-update) | async-done | bytes 131088 | tf_op jit(solution)/shard_map/reduce_scatter | solution.py:328
  1238.6 141.6 %reduce-scatter.14.cloned.1.call-done = f32[32,1024]{1,0:T(8,128)} async-done(((f32[1024,1024]{1,0:T(8,128)}), f32[32,1024]{1,0:T(8,128)}) %reduce-scatter.14.cloned.1.call-update) | async-done | bytes 131088 | tf_op jit(solution)/shard_map/reduce_scatter | solution.py:324
  1380.2 141.6 %reduce-scatter.18.cloned.1.call-done = f32[32,1024]{1,0:T(8,128)} async-done(((f32[1024,1024]{1,0:T(8,128)}), f32[32,1024]{1,0:T(8,128)}) %reduce-scatter.18.cloned.1.call-update) | async-done | bytes 131088 | tf_op jit(solution)/shard_map/reduce_scatter | solution.py:326
  1521.8 141.6 %reduce-scatter.20.cloned.1.call-done = f32[32,1024]{1,0:T(8,128)} async-done(((f32[1024,1024]{1,0:T(8,128)}), f32[32,1024]{1,0:T(8,128)}) %reduce-scatter.20.cloned.1.call-update) | async-done | bytes 131088 | tf_op jit(solution)/shard_map/reduce_scatter | solution.py:327
  1663.4 181.5 %reduce-scatter.24.cloned.1.call-done = f32[32,4096]{1,0:T(8,128)} async-done(((f32[1024,4096]{1,0:T(8,128)}), f32[32,4096]{1,0:T(8,128)}) %reduce-scatter.24.cloned.1.call-update) | async-done | bytes 524304 | tf_op jit(solution)/shard_map/reduce_scatter | solution.py:235
  1844.9 187.4 %reduce-scatter.26.cloned.1.call-done = f32[128,1024]{1,0:T(8,128)} async-done(((f32[4096,1024]{1,0:T(8,128)}), f32[128,1024]{1,0:T(8,128)}) %reduce-scatter.26.cloned.1.call-update) | async-done | bytes 524304 | tf_op jit(solution)/shard_map/reduce_scatter | solution.py:236
  (421 shorter events, 457.9 us)
Async XLA Ops:
  7.2 63.0 %all-gather.13.cloned.1.call-start = ((), (), s32[]{:S(2)}) async-start(), calls=%async_computation.9 | async-start | bytes 2162688 | tf_op jit(solution)/shard_map/all_gather | solution.py:153
  7.9 120.1 %all-gather.19.cloned.1.call-start = ((), (), s32[]{:S(2)}) async-start(), calls=%async_computation.12 | async-start | bytes 2162688 | tf_op jit(solution)/shard_map/all_gather | solution.py:156
  8.7 177.3 %all-gather.17.cloned.1.call-start = ((), (), s32[]{:S(2)}) async-start(), calls=%async_computation.11 | async-start | bytes 2162688 | tf_op jit(solution)/shard_map/all_gather | solution.py:155
  9.4 234.4 %all-gather.15.cloned.1.call-start = ((), (), s32[]{:S(2)}) async-start(), calls=%async_computation.10 | async-start | bytes 2162688 | tf_op jit(solution)/shard_map/all_gather | solution.py:154
  10.0 269.1 %all-gather.29.cloned.1.call-start = ((), (), s32[]{:S(2)}) async-start(), calls=%async_computation.26 | async-start | bytes 5242880 | tf_op jit(solution)/shard_map/all_gather | solution.py:186
  72.2 344.5 %copy-start.18 = (f32[1024]{0:T(1024)}, f32[1024]{0:T(1024)S(1)}, u32[]{:S(2)}) copy-start(f32[1024]{0:T(1024)S(1)} %convert_add_fusion.1) | copy-start | bytes 12292
  72.2 113.8 %copy-start.15 = (bf16[1,512,1024]{2,1,0:T(8,128)(2,1)S(1)}, bf16[1,512,1024]{2,1,0:T(8,128)(2,1)}, u32[]{:S(2)}) copy-start(bf16[1,512,1024]{2,1,0:T(8,128)(2,1)} %param.25) | copy-start | bytes 3145732
  132.2 60.0 %copy-start.21 = (bf16[128]{0:T(256)(128)(2,1)S(1)}, bf16[128]{0:T(256)(128)(2,1)}, u32[]{:S(2)}) copy-start(bf16[128]{0:T(256)(128)(2,1)} %param.41) | copy-start | bytes 772
  132.2 99.5 %copy-start.17 = (s32[1,2048]{1,0:T(1,128)S(1)}, s32[1,2048]{1,0:T(1,128)}, u32[]{:S(2)}) copy-start(s32[1,2048]{1,0:T(1,128)} %param.28) | copy-start | bytes 24580
  132.2 183.4 %all-gather.27.cloned.1.call-start = ((), (), s32[]{:S(2)}) async-start(), calls=%async_computation.25 | async-start | bytes 5242880 | tf_op jit(solution)/shard_map/all_gather | solution.py:185
  189.8 225.9 %all-gather.21.cloned.1.call-start = ((), (), s32[]{:S(2)}) async-start(), calls=%async_computation.13 | async-start | bytes 2162688 | tf_op jit(solution)/shard_map/all_gather | solution.py:157
  190.6 263.1 %all-gather.23.cloned.1.call-start = ((), (), s32[]{:S(2)}) async-start(), calls=%async_computation.14 | async-start | bytes 8650752 | tf_op jit(solution)/shard_map/all_gather | solution.py:195
  191.3 340.9 %all-gather.25.cloned.1.call-start = ((), (), s32[]{:S(2)}) async-start(), calls=%async_computation.15 | async-start | bytes 8650752 | tf_op jit(solution)/shard_map/all_gather | solution.py:196
  192.1 712.1 %reduce-scatter.10.cloned.1.call-start = ((), (), s32[]{:S(2)}) async-start(), calls=%async_computation.16 | async-start | bytes 5242880 | tf_op jit(solution)/shard_map/reduce_scatter | solution.py:280
  419.9 138.4 %copy-start.1 = (f32[512,1024]{1,0:T(8,128)}, f32[512,1024]{1,0:T(8,128)S(1)}, u32[]{:S(2)}) copy-start(f32[512,1024]{1,0:T(8,128)S(1)} %get-tuple-element.309) | copy-start | bytes 6291460
  544.1 14.2 copy-start.12
  861.0 90.2 %reduce-scatter.12.cloned.1.call-start = ((), (), s32[]{:S(2)}) async-start(), calls=%async_computation.17 | async-start | bytes 5242880 | tf_op jit(solution)/shard_map/reduce_scatter | solution.py:283
  861.7 235.1 %reduce-scatter.16.cloned.1.call-start = ((), (), s32[]{:S(2)}) async-start(), calls=%async_computation.19 | async-start | bytes 4325376 | tf_op jit(solution)/shard_map/reduce_scatter | solution.py:325
  866.5 372.1 %reduce-scatter.22.cloned.1.call-start = ((), (), s32[]{:S(2)}) async-start(), calls=%async_computation.22 | async-start | bytes 4325376 | tf_op jit(solution)/shard_map/reduce_scatter | solution.py:328
  871.1 509.2 %reduce-scatter.14.cloned.1.call-start = ((), (), s32[]{:S(2)}) async-start(), calls=%async_computation.18 | async-start | bytes 4325376 | tf_op jit(solution)/shard_map/reduce_scatter | solution.py:324
  959.0 562.8 %reduce-scatter.18.cloned.1.call-start = ((), (), s32[]{:S(2)}) async-start(), calls=%async_computation.20 | async-start | bytes 4325376 | tf_op jit(solution)/shard_map/reduce_scatter | solution.py:326
  962.7 700.7 %reduce-scatter.20.cloned.1.call-start = ((), (), s32[]{:S(2)}) async-start(), calls=%async_computation.21 | async-start | bytes 4325376 | tf_op jit(solution)/shard_map/reduce_scatter | solution.py:327
  967.2 877.7 %reduce-scatter.24.cloned.1.call-start = ((), (), s32[]{:S(2)}) async-start(), calls=%async_computation.23 | async-start | bytes 17301504 | tf_op jit(solution)/shard_map/reduce_scatter | solution.py:235
  979.3 1053.0 %reduce-scatter.26.cloned.1.call-start = ((), (), s32[]{:S(2)}) async-start(), calls=%async_computation.24 | async-start | bytes 17301504 | tf_op jit(solution)/shard_map/reduce_scatter | solution.py:236
  (33 other events, 109.6 us)
Sparse Core Ops, SparseCore 0:
  10.8 59.2 all-gather.12
  73.0 54.9 all-gather.18
  130.9 55.0 all-gather.16
  188.7 55.0 all-gather.14
  245.8 33.2 all-gather.28
  281.1 34.4 all-gather.26
  318.4 56.3 all-gather.20
  377.7 75.9 all-gather.22
  456.5 75.6 all-gather.24
  861.1 43.0 reduce-scatter.9
  906.7 44.3 reduce-scatter.11
  953.9 142.9 reduce-scatter.15
  1099.7 138.8 reduce-scatter.21
  1241.3 138.8 reduce-scatter.13
  1382.9 138.8 reduce-scatter.17
  1524.5 138.8 reduce-scatter.19
  1666.1 178.7 reduce-scatter.23
  1847.6 184.5 reduce-scatter.25
where the time goes:
time: 2050 us; the launch traced here: 2040 us
  waiting for transfers between devices  1350 us (66%)
  matrix products  425 us (21%)
  blocking collectives  123 us (6%)
  loops' own time  53.9 us (3%)
  local copies, waits for them, and re-layouts  41.9 us (2%)
  other arithmetic  27.1 us (1%)
    dot_general x54, matrix products, matmul_tail(): lax.dot_general(left, right, (((1,), (1,)), ((), ())), preferred_element_...  199 us
    reduce_scatter x1, waiting for transfers between devices, shards(): lax.psum_scatter(down_grad, ('dp', 'ctx'), scatter_dimension=0, tiled=True)  187 us
    reduce_scatter x1, waiting for transfers between devices, shards(): lax.psum_scatter(up_grad, ('dp', 'ctx'), scatter_dimension=0, tiled=True)  182 us
    reduce_scatter x1, waiting for transfers between devices, shards(): lax.psum_scatter(output_grad, ('dp', 'ctx'), scatter_dimension=0, tiled=T...  142 us
    reduce_scatter x1, waiting for transfers between devices, shards(): lax.psum_scatter(time_grad, ('dp', 'ctx'), scatter_dimension=0, tiled=True)  142 us
    reduce_scatter x1, waiting for transfers between devices, shards(): lax.psum_scatter(value_grad, ('dp', 'ctx'), scatter_dimension=0, tiled=True)  142 us
    reduce_scatter x1, waiting for transfers between devices, shards(): lax.psum_scatter(key_grad, ('dp', 'ctx'), scatter_dimension=0, tiled=True)  142 us
    dot_general x39, matrix products, matmul_plain(): return jnp.dot(left, right, preferred_element_type=jnp.float32)  120 us
  transfers between devices with their start and end apart: 18, of which 17 were waited for; matrix products, arithmetic and copies ran while one was open for 10% of the time, Pallas kernels for 0%

commit v1 on v0

v1 whole, which is shorter than its diff:
```python
import functools

import jax
import jax.numpy as jnp
from jax import lax
from jax.experimental import pallas as pl
from jax.experimental.pallas import tpu as pltpu
from jax.sharding import PartitionSpec as P

HEAD_DIM = 64
BLOCK = 256
MASKED = -1e30
EPSILON = 1e-05
SCALE = HEAD_DIM**-0.5
SCALE_LOG2 = SCALE * 1.4426950408889634
BOTH = ("dp", "ctx")
f32, bf16 = jnp.float32, jnp.bfloat16


def nn(left, right):
    return jnp.dot(left, right, preferred_element_type=f32)


def tn(left, right):
    return lax.dot_general(left, right, (((0,), (0,)), ((), ())), preferred_element_type=f32)


def nt(left, right):
    return lax.dot_general(left, right, (((1,), (1,)), ((), ())), preferred_element_type=f32)


def head_only(pair, which):
    lane = lax.broadcasted_iota(jnp.int32, pair.shape, 1)
    keep = (lane < HEAD_DIM) if which == 0 else (lane >= HEAD_DIM)
    return jnp.where(keep, pair, jnp.zeros_like(pair))


def place(block, me, per_chunk):
    return lax.bitwise_xor(block // per_chunk, me) * per_chunk + lax.rem(block, per_chunk)


def forward_kernel(
    per_chunk, pairs, info, q_ref, k_ref, v_ref, idc_ref, idr_ref, o_ref, lse_ref, o_acc, m_acc, l_acc
):
    i = pl.program_id(0)
    me = info[2, 0]
    m_acc[...] = jnp.full_like(m_acc, MASKED)
    l_acc[...] = jnp.zeros_like(l_acc)
    o_acc[...] = jnp.zeros_like(o_acc)
    ids_q = idr_ref[pl.ds(i, 1)][0]

    def step(j, carry):
        at = pl.multiple_of(place(j, me, per_chunk) * BLOCK, BLOCK)
        same = idc_ref[pl.ds(pl.multiple_of(j * BLOCK, BLOCK), BLOCK), :] == ids_q
        for p in range(pairs):
            cols = slice(p * 128, (p + 1) * 128)
            k_pair, v_pair, q_pair = k_ref[pl.ds(at, BLOCK), cols], v_ref[pl.ds(at, BLOCK), cols], q_ref[:, cols]
            for w in range(2):
                h = 2 * p + w
                t = jnp.where(same, nt(k_pair, head_only(q_pair, w)) * SCALE_LOG2, MASKED)
                m_old = m_acc[h]
                m_new = jnp.maximum(m_old, jnp.max(t, axis=0, keepdims=True))
                alpha = jnp.exp2(m_old - m_new)
                e = jnp.exp2(t - m_new)
                l_acc[h] = l_acc[h] * alpha + jnp.sum(e, axis=0, keepdims=True)
                m_acc[h] = m_new
                rows = slice(h * HEAD_DIM, (h + 1) * HEAD_DIM)
                o_acc[rows] = o_acc[rows] * alpha + tn(v_pair, e.astype(bf16))[w * HEAD_DIM : (w + 1) * HEAD_DIM]
        return carry

    lax.fori_loop(info[0, i], info[1, i], step, 0)
    for p in range(pairs):
        parts = []
        for w in range(2):
            h = 2 * p + w
            parts.append(o_acc[h * HEAD_DIM : (h + 1) * HEAD_DIM] / l_acc[h])
            lse_ref[0, h : h + 1, :] = m_acc[h] + jnp.log2(l_acc[h])
        o_ref[:, p * 128 : (p + 1) * 128] = jnp.concatenate(parts, axis=0).T.astype(bf16)


def attention_forward(info, qkv, ids_col, ids_row, per_chunk):
    rows, width = qkv.shape[0], qkv.shape[1] // 3
    blocks, heads = rows // BLOCK, width // HEAD_DIM
    return pl.pallas_call(
        functools.partial(forward_kernel, per_chunk, heads // 2),
        grid_spec=pltpu.PrefetchScalarGridSpec(
            num_scalar_prefetch=1,
            grid=(blocks,),
            in_specs=[
                pl.BlockSpec((BLOCK, width), lambda i, info: (place(i, info[2, 0], per_chunk), 0)),
                pl.BlockSpec((rows, width), lambda i, info: (0, 1)),
                pl.BlockSpec((rows, width), lambda i, info: (0, 2)),
                pl.BlockSpec((rows, 1), lambda i, info: (0, 0)),
                pl.BlockSpec((blocks, 1, BLOCK), lambda i, info: (0, 0, 0)),
            ],
            out_specs=[
                pl.BlockSpec((BLOCK, width), lambda i, info: (place(i, info[2, 0], per_chunk), 0)),
                pl.BlockSpec((1, heads, BLOCK), lambda i, info: (i, 0, 0)),
            ],
            scratch_shapes=[
                pltpu.VMEM((width, BLOCK), f32),
                pltpu.VMEM((heads, 1, BLOCK), f32),
                pltpu.VMEM((heads, 1, BLOCK), f32),
            ],
        ),
        out_shape=[
            jax.ShapeDtypeStruct((rows, width), bf16),
            jax.ShapeDtypeStruct((blocks, heads, BLOCK), f32),
        ],
        name="attention_forward",
    )(info, qkv, qkv, qkv, ids_col, ids_row)


def backward_kernel(
    per_chunk, pairs, info, q_ref, k_ref, v_ref, do_ref, o_ref, lse_ref, idc_ref, idr_ref,
    out_ref, delta_ref, dq_acc, dk_acc, dv_acc,
):
    j = pl.program_id(0)
    blocks = pl.num_programs(0)
    me = info[2, 0]
    width = 128 * pairs

    @pl.when(j == 0)
    def _():
        dq_acc[...] = jnp.zeros_like(dq_acc)

        def fill(i, carry):
            at = pl.multiple_of(place(i, me, per_chunk) * BLOCK, BLOCK)
            for p in range(pairs):
                cols = slice(p * 128, (p + 1) * 128)
                prod = (do_ref[pl.ds(at, BLOCK), cols].astype(f32) * o_ref[pl.ds(at, BLOCK), cols].astype(f32)).T
                for w in range(2):
                    h = 2 * p + w
                    delta_ref[i, h : h + 1, :] = jnp.sum(
                        prod[w * HEAD_DIM : (w + 1) * HEAD_DIM], axis=0, keepdims=True
                    )
            return carry

        lax.fori_loop(0, blocks, fill, 0)

    dk_acc[...] = jnp.zeros_like(dk_acc)
    dv_acc[...] = jnp.zeros_like(dv_acc)
    ids_k = idc_ref[pl.ds(pl.multiple_of(j * BLOCK, BLOCK), BLOCK), :]

    def step(i, carry):
        at = pl.multiple_of(place(i, me, per_chunk) * BLOCK, BLOCK)
        same = ids_k == idr_ref[pl.ds(i, 1)][0]
        for p in range(pairs):
            cols = slice(p * 128, (p + 1) * 128)
            k_pair, v_pair = k_ref[:, cols], v_ref[:, cols]
            q_pair, do_pair = q_ref[pl.ds(at, BLOCK), cols], do_ref[pl.ds(at, BLOCK), cols]
            for w in range(2):
                h = 2 * p + w
                q_one, do_one = head_only(q_pair, w), head_only(do_pair, w)
                t = nt(k_pair, q_one) * SCALE_LOG2 - lse_ref[i, h : h + 1, :]
                e = jnp.exp2(jnp.where(same, t, MASKED))
                ds = (e * (nt(v_pair, do_one) - delta_ref[i, h : h + 1, :])).astype(bf16)
                dv_acc[:, cols] += nn(e.astype(bf16), do_one)
                dk_acc[:, cols] += nn(ds, q_one)
                dq_acc[pl.ds(at, BLOCK), cols] += tn(ds, head_only(k_pair, w))
        return carry

    lax.fori_loop(info[0, j], info[1, j], step, 0)
    mine = pl.multiple_of(place(j, me, per_chunk) * BLOCK, BLOCK)
    out_ref[pl.ds(mine, BLOCK), width : 2 * width] = (dk_acc[...] * SCALE).astype(bf16)
    out_ref[pl.ds(mine, BLOCK), 2 * width : 3 * width] = dv_acc[...].astype(bf16)

    @pl.when(j == blocks - 1)
    def _():
        out_ref[:, 0:width] = (dq_acc[...] * SCALE).astype(bf16)


def attention_backward(info, qkv, do, o, lse, ids_col, ids_row, per_chunk):
    rows, width = o.shape
    blocks, heads = rows // BLOCK, width // HEAD_DIM
    return pl.pallas_call(
        functools.partial(backward_kernel, per_chunk, heads // 2),
        grid_spec=pltpu.PrefetchScalarGridSpec(
            num_scalar_prefetch=1,
            grid=(blocks,),
            in_specs=[
                pl.BlockSpec((rows, width), lambda i, info: (0, 0)),
                pl.BlockSpec((BLOCK, width), lambda i, info: (place(i, info[2, 0], per_chunk), 1)),
                pl.BlockSpec((BLOCK, width), lambda i, info: (place(i, info[2, 0], per_chunk), 2)),
                pl.BlockSpec((rows, width), lambda i, info: (0, 0)),
                pl.BlockSpec((rows, width), lambda i, info: (0, 0)),
                pl.BlockSpec((blocks, heads, BLOCK), lambda i, info: (0, 0, 0)),
                pl.BlockSpec((rows, 1), lambda i, info: (0, 0)),
                pl.BlockSpec((blocks, 1, BLOCK), lambda i, info: (0, 0, 0)),
            ],
            out_specs=pl.BlockSpec((rows, 3 * width), lambda i, info: (0, 0)),
            scratch_shapes=[
                pltpu.VMEM((blocks, heads, BLOCK), f32),
                pltpu.VMEM((rows, width), f32),
                pltpu.VMEM((BLOCK, width), f32),
                pltpu.VMEM((BLOCK, width), f32),
            ],
        ),
        out_shape=jax.ShapeDtypeStruct((rows, 3 * width), bf16),
        name="attention_backward",
    )(info, qkv, qkv, qkv, do, o, lse, ids_col, ids_row)


def spans(ids, me):
    blocks = ids.shape[0] // BLOCK
    per_block = ids.reshape(blocks, BLOCK)
    low = jnp.sum(ids[None, :] < per_block[:, :1], axis=1) // BLOCK
    high = (jnp.sum(ids[None, :] <= per_block[:, -1:], axis=1) + BLOCK - 1) // BLOCK
    return jnp.stack([low, high, jnp.full((blocks,), me)]).astype(jnp.int32)


def swap(value, axis, mask):
    size = lax.axis_size(axis)
    return lax.ppermute(value, axis, [(i, i ^ mask) for i in range(size)])


def bits(size):
    return [1 << b for b in range(size.bit_length() - 1)]


def gather_relative(value, axis):
    held = {0: value}
    for bit in reversed(bits(lax.axis_size(axis))):
        held.update({k | bit: swap(v, axis, bit) for k, v in list(held.items())})
    return [held[k] for k in range(len(held))]


def trade(pieces, axis):
    return [pieces[0]] + [swap(pieces[k], axis, k) for k in range(1, len(pieces))]


def to_absolute(pieces, me):
    stacked = jnp.stack(pieces)
    return [lax.dynamic_index_in_dim(stacked, lax.bitwise_xor(me, c), 0, False) for c in range(len(pieces))]


def halve(value, axis, dtype):
    me, size = lax.axis_index(axis), lax.axis_size(axis)
    count = size
    for bit in bits(size):
        value = value.reshape((count // 2, 2) + value.shape[1:])
        mine = lax.rem(me // bit, 2)
        give = lax.dynamic_index_in_dim(value, 1 - mine, 1, False).astype(dtype)
        keep = lax.dynamic_index_in_dim(value, mine, 1, False)
        value = keep + swap(give, axis, bit).astype(f32)
        count //= 2
    return value[0]


def normalize(values, gain, shift):
    average = jnp.mean(values, axis=-1, keepdims=True)
    centered = values - average
    inverse = lax.rsqrt(jnp.mean(centered * centered, axis=-1, keepdims=True) + EPSILON)
    normed = centered * inverse
    return normed * gain + shift, normed, inverse


def normalize_back(upstream, normed, inverse, gain):
    scaled = upstream * gain
    plain = jnp.mean(scaled, axis=-1, keepdims=True)
    cross = jnp.mean(scaled * normed, axis=-1, keepdims=True)
    result = inverse * (scaled - plain - normed * cross)
    return result, jnp.sum(upstream * normed, axis=0), jnp.sum(upstream, axis=0)


def shards(
    tokens, time_feat, cotangent, segment_ids, time_weight, time_bias, query_weight, query_bias, key_weight,
    value_weight, value_bias, output_weight, output_bias, mixing_gain, mixing_bias, up_weight, up_bias,
    down_weight, down_bias, final_gain, final_bias,
):
    me_dp, me = lax.axis_index("dp"), lax.axis_index("ctx")
    dp, ctx = lax.axis_size("dp"), lax.axis_size("ctx")
    devices = dp * ctx
    piece, width = tokens.shape[1], tokens.shape[2]
    hidden = up_weight.shape[1]
    own, ratio = width // devices, hidden // width
    cols = width // ctx
    per_chunk = piece // BLOCK
    tokens, cotangent, ids = tokens[0], cotangent[0], segment_ids[0]

    vectors = [
        time_bias, query_bias, value_bias, output_bias, mixing_gain, mixing_bias, down_bias, final_gain, final_bias
    ]
    small = jnp.concatenate([jnp.stack(vectors), up_bias.reshape(ratio, own)]).T
    small = jnp.pad(small, ((0, 0), (0, 128 - small.shape[1])))
    first = lax.all_gather(
        jnp.concatenate([query_weight, key_weight, value_weight, time_weight, small], axis=1), BOTH, axis=0, tiled=True
    )
    second = lax.all_gather(jnp.concatenate([up_weight, output_weight], axis=1), BOTH, axis=0, tiled=True)
    down_full = lax.all_gather(down_weight, BOTH, axis=0, tiled=True)
    up_full, output_full = second[:, :hidden], second[:, hidden:]

    token_chunks = gather_relative(tokens, "ctx")
    time_feats = jnp.concatenate(gather_relative(time_feat, "dp"))

    table = first[:, 4 * width :].astype(f32).T
    time_shift_bias, query_shift, value_shift, output_shift, gain_one, bias_one, down_shift, gain_two, bias_two = [
        table[n] for n in range(len(vectors))
    ]
    up_shift = table[len(vectors) : len(vectors) + ratio].reshape(ratio, devices, own).transpose(1, 0, 2).reshape(hidden)
    time_shift = nn(time_feat, first[:, 3 * width : 4 * width]) + time_shift_bias

    def my_cols(n):
        return lax.dynamic_slice_in_dim(first, n * width + me * cols, cols, 1)

    qkv_weight = jnp.concatenate([my_cols(n) for n in range(3)], axis=1)
    qkv_shift = jnp.concatenate(
        [
            lax.dynamic_slice_in_dim(query_shift, me * cols, cols),
            jnp.zeros((cols,), f32),
            lax.dynamic_slice_in_dim(value_shift, me * cols, cols),
        ]
    )
    start_row = (jnp.concatenate(token_chunks).astype(f32) + time_shift).astype(bf16)
    residual_in = tokens.astype(f32) + time_shift
    qkv = (nn(start_row, qkv_weight) + qkv_shift).astype(bf16)

    info = spans(ids, me)
    ids_col, ids_row = ids.reshape(-1, 1), ids.reshape(-1, 1, BLOCK)
    mixed, logsum = attention_forward(info, qkv, ids_col, ids_row, per_chunk)
    returned = trade([mixed[k * piece : (k + 1) * piece] for k in range(ctx)], "ctx")
    attended = jnp.concatenate(to_absolute(returned, me), axis=1)

    branch = nn(attended, output_full) + output_shift
    hidden_one, normed_one, inverse_one = normalize(residual_in + branch, gain_one, bias_one)
    hidden_low = hidden_one.astype(bf16)
    pre_gelu = nn(hidden_low, up_full) + up_shift
    share = 0.5 * (1.0 + lax.erf(pre_gelu * 0.5**0.5))
    activated = (pre_gelu * share).astype(bf16)
    slope = (share + pre_gelu * jnp.exp(-0.5 * pre_gelu * pre_gelu) * 0.3989422804014327).astype(bf16)
    activated, slope = lax.optimization_barrier((activated, slope))
    feed_out = nn(activated, down_full) + down_shift
    result, normed_two, inverse_two = normalize(hidden_one + feed_out, gain_two, bias_two)
    layer_out = result.astype(bf16)

    upstream = cotangent.astype(f32)
    grad_two, gain_two_grad, bias_two_grad = normalize_back(upstream, normed_two, inverse_two, gain_two)
    grad_feed = grad_two.astype(bf16)
    down_grad = tn(activated, grad_feed).astype(bf16)
    down_shift_grad = jnp.sum(grad_feed.astype(f32), axis=0)
    grad_inner = (nt(grad_feed, down_full) * slope.astype(f32)).astype(bf16)
    up_grad = tn(hidden_low, grad_inner).astype(bf16)
    up_shift_grad = jnp.sum(grad_inner.astype(f32), axis=0)
    grad_hidden = grad_two + nt(grad_inner, up_full)
    grad_one, gain_one_grad, bias_one_grad = normalize_back(grad_hidden, normed_one, inverse_one, gain_one)
    grad_branch = grad_one.astype(bf16)
    output_grad = tn(attended, grad_branch).astype(bf16)
    output_shift_grad = jnp.sum(grad_branch.astype(f32), axis=0)
    down_blocks = down_grad.reshape(devices, ratio, own, width)
    packed = jnp.concatenate(
        [up_grad] + [down_blocks[:, n].reshape(width, width) for n in range(ratio)] + [output_grad], axis=1
    )
    packed = lax.psum_scatter(packed, BOTH, scatter_dimension=0, tiled=True).astype(f32)
    up_weight_grad = packed[:, :hidden]
    down_weight_grad = jnp.concatenate(
        [packed[:, hidden + n * width : hidden + (n + 1) * width] for n in range(ratio)], axis=0
    )
    output_weight_grad = packed[:, 2 * hidden :]

    grad_attended = nt(grad_branch, output_full).astype(bf16)
    pieces = [lax.dynamic_slice_in_dim(grad_attended, lax.bitwise_xor(me, k) * cols, cols, 1) for k in range(ctx)]
    grad_mixed = jnp.concatenate(trade(pieces, "ctx"))
    grad_qkv = attention_backward(info, qkv, grad_mixed, mixed, logsum, ids_col, ids_row, per_chunk)

    partial = {}
    for k in reversed(range(ctx)):
        partial[k] = nt(grad_qkv[k * piece : (k + 1) * piece], qkv_weight)
    for bit in bits(ctx):
        for k in [k for k in partial if k & bit]:
            partial[k ^ bit] = partial[k ^ bit] + swap(partial.pop(k).astype(bf16), "ctx", bit).astype(f32)
    tokens_grad = (grad_one + partial[0]).astype(bf16)

    qkv_grad = tn(start_row, grad_qkv)
    qkv_sum = jnp.sum(grad_qkv.astype(f32), axis=0)
    row_sum = jnp.sum(grad_one, axis=0, keepdims=True) + lax.dot_general(
        qkv_sum[None],
        qkv_weight.astype(f32),
        (((1,), (1,)), ((), ())),
        precision=lax.Precision.HIGHEST,
        preferred_element_type=f32,
    )
    for bit in bits(ctx):
        row_sum = row_sum + swap(row_sum, "ctx", bit)
    row_sums = jnp.concatenate(gather_relative(row_sum, "dp"))
    mine = (me_dp * ctx + me) * own
    time_weight_grad = lax.dot_general(
        lax.dynamic_slice_in_dim(time_feats, mine, own, 1).astype(f32),
        row_sums,
        (((0,), (0,)), ((), ())),
        precision=lax.Precision.HIGHEST,
        preferred_element_type=f32,
    )
    time_bias_grad = lax.dynamic_slice_in_dim(jnp.sum(row_sums, axis=0), mine, own)

    summed = halve(qkv_grad.reshape(dp, ctx * own, 3 * cols), "dp", bf16).reshape(ctx, own, 3 * cols)
    blocks_out = to_absolute(
        trade([lax.dynamic_index_in_dim(summed, lax.bitwise_xor(me, k), 0, False) for k in range(ctx)], "ctx"), me
    )
    query_weight_grad, key_weight_grad, value_weight_grad = [
        jnp.concatenate([block[:, n * cols : (n + 1) * cols] for block in blocks_out], axis=1) for n in range(3)
    ]

    def spread(part):
        return lax.dynamic_update_slice_in_dim(jnp.zeros((width,), f32), part, me * cols, 0)

    vector_grads = jnp.stack(
        [
            spread(qkv_sum[:cols]),
            spread(qkv_sum[2 * cols :]),
            output_shift_grad,
            gain_one_grad,
            bias_one_grad,
            down_shift_grad,
            gain_two_grad,
            bias_two_grad,
        ]
    ).reshape(8, devices, own)
    vector_grads = jnp.concatenate(
        [vector_grads.transpose(1, 0, 2).reshape(devices, 8 * own), up_shift_grad.reshape(devices, ratio * own)], axis=1
    )
    vector_grads = halve(halve(vector_grads.reshape(dp, ctx, -1), "dp", f32), "ctx", f32)
    (
        query_bias_grad,
        value_bias_grad,
        output_bias_grad,
        mixing_gain_grad,
        mixing_bias_grad,
        down_bias_grad,
        final_gain_grad,
        final_bias_grad,
    ) = [vector_grads[n * own : (n + 1) * own] for n in range(8)]
    up_bias_grad = vector_grads[8 * own :]
    return (
        layer_out[None],
        tokens_grad[None],
        time_weight_grad,
        time_bias_grad,
        query_weight_grad,
        query_bias_grad,
        key_weight_grad,
        value_weight_grad,
        value_bias_grad,
        output_weight_grad,
        output_bias_grad,
        mixing_gain_grad,
        mixing_bias_grad,
        up_weight_grad,
        up_bias_grad,
        down_weight_grad,
        down_bias_grad,
        final_gain_grad,
        final_bias_grad,
    )


def solution(mesh):
    rows, split_rows, split = P("dp", "ctx", None), P(BOTH, None), P(BOTH)
    return jax.shard_map(
        shards,
        mesh=mesh,
        in_specs=(
            rows, P("dp", None), rows, P("dp", None), split_rows, split, split_rows, split, split_rows, split_rows,
            split, split_rows, split, split, split, split_rows, split, split_rows, split, split, split,
        ),
        out_specs=(
            rows, rows, split_rows, split, split_rows, split, split_rows, split_rows, split, split_rows, split, split,
            split, split_rows, split, split_rows, split, split, split,
        ),
        check_vma=False,
    )
```

time: 2050 us -> 570 us (0.28)
  waiting for transfers between devices: 1350 us -> 262 us
  matrix products: 425 us -> 90.1 us
  blocking collectives: 123 us -> 0 us
  Pallas kernels: 0 us -> 103 us
  loops' own time: 53.9 us -> 0 us
  starting transfers between devices: 0.97 us -> 40.3 us
    reduce_scatter x9 -> x1, waiting for transfers between devices: 1060 us -> 19.3 us  [shards(): lax.psum_scatter(packed, BOTH, scatter_dimension=0, tiled=True).astype(f32)]
    dot_general x131 -> x18, matrix products: 425 us -> 90.1 us  [the longest x5 30.9 us: nn(): return jnp.dot(left, right, preferred_element_type=f32)]
    all_gather x9 -> x3, waiting for transfers between devices: 285 us -> 128 us  [the longest x1 61.6 us: shards(): down_full = lax.all_gather(down_weight, BOTH, axis=0, tiled=True)]
    ppermute x0 -> x39, waiting for transfers between devices: none -> 115 us  [swap(): return lax.ppermute(value, axis, [(i, i ^ mask) for i in range(size)])]
    pallas_call x0 -> x2, Pallas kernels: none -> 103 us  [the longest x1 54.8 us: attention_backward(): pl.pallas_call(functools.partial(backward_kernel, per_chunk, heads // 2),...]
    unnamed x2 -> x0, blocking collectives: 83.6 us -> none
    another operation x2 -> x0, loops' own time: 53.9 us -> none  [the longest x1 42.5 us: row_backward(): heads_out = lax.map(one_head, jnp.arange(query_row.shape[1] // HEAD_DIM))]
    ppermute x0 -> x39, starting transfers between devices: none -> 40.2 us  [swap(): return lax.ppermute(value, axis, [(i, i ^ mask) for i in range(size)])]
  transfers between devices with their start and end apart: 18 -> 43, of which waited for: 17 -> 20; matrix products, arithmetic and copies ran while one was open for 10% -> 12% of each run, Pallas kernels for 0% -> 18%
where the time goes in v1:
time: 570 us; the launch traced here: 564 us
  waiting for transfers between devices  262 us (46%)
  Pallas kernels  103 us (18%)
  matrix products  90.1 us (16%)
  starting transfers between devices  40.3 us (7%)
  local copies, waits for them, and re-layouts  32.1 us (6%)
  other arithmetic  21 us (4%)
  between operations  15 us (3%)
    ppermute x39, waiting for transfers between devices, swap(): return lax.ppermute(value, axis, [(i, i ^ mask) for i in range(size)])  115 us
    all_gather x1, waiting for transfers between devices, shards(): down_full = lax.all_gather(down_weight, BOTH, axis=0, tiled=True)  61.6 us
    pallas_call x1, Pallas kernels, attention_backward(): pl.pallas_call(functools.partial(backward_kernel, per_chunk, heads // 2),...  54.8 us
    all_gather x1, waiting for transfers between devices, shards(): lax.all_gather(jnp.concatenate([query_weight, key_weight, value_weight, t...  51.7 us
    pallas_call x1, Pallas kernels, attention_forward(): pl.pallas_call(functools.partial(forward_kernel, per_chunk, heads // 2),...  48.4 us
    ppermute x39, starting transfers between devices, swap(): return lax.ppermute(value, axis, [(i, i ^ mask) for i in range(size)])  40.2 us
    dot_general x5, matrix products, nn(): return jnp.dot(left, right, preferred_element_type=f32)  30.9 us
    dot_general x7, matrix products, nt(): lax.dot_general(left, right, (((1,), (1,)), ((), ())), preferred_element_...  30.4 us
  transfers between devices with their start and end apart: 43, of which 20 were waited for; matrix products, arithmetic and copies ran while one was open for 12% of the time, Pallas kernels for 18%

profile of v1, /device:TPU:0, one launch (start us, length us, event | category | flops | bytes accessed | tf_op | source)
XLA Modules:
  0.0 564.2 jit_solution(6935095781928439982)
XLA Ops:
  16.4 3.0 collective-permute-start.1
  23.2 21.3 %collective-permute-done.1 = bf16[512,1024]{1,0:T(8,128)(2,1)S(1)} collective-permute-done((bf16[512,1024]{1,0:T(8,128)(2,1)S(1)}, bf16[512,1024]{1,0:T(8,128)(2,1)S(1)}, u32[]{:S(2)}, u32[]{:S(2)}) %collective-permute-start.1) | collective-permute-done | bytes 1048608 | tf_op jit(solution)/shard_map/ppermute | solution.py:214
  44.5 51.7 %all-gather.4.cloned.1.call-done = bf16[1024,4224]{1,0:T(8,128)(2,1)} async-done(((bf16[32,4224]{1,0:T(8,128)(2,1)}), bf16[1024,4224]{1,0:T(8,128)(2,1)}) %all-gather.4.cloned.1.call-update) | async-done | bytes 8650768 | tf_op jit(solution)/shard_map/all_gather | solution.py:286
  101.6 6.6 %add_convert_fusion.1.q_ref.k_ref.v_ref = bf16[2048,768]{1,0:T(8,128)(2,1)} fusion(f32[768]{0:T(1024)S(1)} %pad_maximum_fusion.12, bf16[512,1024]{1,0:T(8,128)(2,1)} %collective-permute-done.2, bf16[512,1024]{1,0:T(8,128)(2,1)S(1)} %collective-permute-done.1, bf16[512,1024]{1,0:T(8,128)(2,1)} %collective-permute-done, bf16[512,1024]{1,0:T(8,128)(2,1)S(1)} %bitcast.247, ...), kind=kOutput, calls=%fused_computation.18 | convolution fusion | flops 3250061312 | bytes 8920064 | tf_op jit(solution)/shard_map/dot_general | solution.py:21
  108.2 48.4 %attention_forward.1 = (bf16[2048,256]{1,0:T(8,128)(2,1)}, f32[8,4,256]{2,1,0:T(4,128)}) custom-call(s32[3,8]{1,0:T(4,128)} %add_add_fusion.2.info, bf16[2048,768]{1,0:T(8,128)(2,1)} %add_convert_fusion.1.q_ref.k_ref.v_ref, bf16[2048,768]{1,0:T(8,128)(2,1)} %add_convert_fusion.1.q_ref.k_ref.v_ref, bf16[2048,768]{1,0:T(8,128)(2,1)} %add_convert_fusion.1.q_ref.k_ref.v_ref, ...), custom_call_target="tpu_custom_call" | custom-call | tf_op jit(solution)/shard_map/attention_forward/pallas_call | solution.py:84
  160.1 12.1 %collective-permute-done.5 = bf16[512,256]{1,0:T(8,128)(2,1)S(1)} collective-permute-done((bf16[512,256]{1,0:T(8,128)(2,1)S(1)}, bf16[512,256]{1,0:T(8,128)(2,1)S(1)}, u32[]{:S(2)}, u32[]{:S(2)}) %collective-permute-start.5) | collective-permute-done | bytes 262176 | tf_op jit(solution)/shard_map/ppermute | solution.py:214
  172.3 8.8 %collective-permute-done.4 = bf16[512,256]{1,0:T(8,128)(2,1)S(1)} collective-permute-done((bf16[512,256]{1,0:T(8,128)(2,1)S(1)}, bf16[512,256]{1,0:T(8,128)(2,1)S(1)}, u32[]{:S(2)}, u32[]{:S(2)}) %collective-permute-start.4) | collective-permute-done | bytes 262176 | tf_op jit(solution)/shard_map/ppermute | solution.py:214
  181.3 14.4 %all-gather.6.cloned.1.call-done = bf16[1024,5120]{1,0:T(8,128)(2,1)} async-done(((bf16[32,5120]{1,0:T(8,128)(2,1)}), bf16[1024,5120]{1,0:T(8,128)(2,1)}) %all-gather.6.cloned.1.call-update) | async-done | bytes 10485776 | tf_op jit(solution)/shard_map/all_gather | solution.py:289
  195.7 3.4 fusion.86
  201.4 9.9 %fusion.4 = (bf16[512,4096]{1,0:T(8,128)(2,1)}, bf16[512,4096]{1,0:T(8,128)(2,1)}) fusion(f32[4096]{0:T(1024)S(1)} %add.331, bf16[1024,5120]{1,0:T(8,128)(2,1)S(1)} %copy-done.27, f32[512,1024]{1,0:T(8,128)S(1)} %get-tuple-element.111, f32[1024]{0:T(1024)S(1)} %bitcast.223, f32[1024]{0:T(1024)S(1)} %bitcast.217, f32[512]{0:T(512)S(1)} %add_rsqrt_fusion.1, ...), kind=kOutput, calls=%fused_computation.5 | convolution fusion | flops 4322754560 | bytes 18903040 | tf_op jit(solution)/shard_map/dot_general | solution.py:21
  211.3 61.6 %all-gather.8.cloned.1.call-done = bf16[4096,1024]{1,0:T(8,128)(2,1)} async-done(((bf16[128,1024]{1,0:T(8,128)(2,1)}), bf16[4096,1024]{1,0:T(8,128)(2,1)}) %all-gather.8.cloned.1.call-update) | async-done | bytes 8388624 | tf_op jit(solution)/shard_map/all_gather | solution.py:290
  272.9 8.4 %fusion.87 = (f32[512]{0:T(512)S(1)}, f32[512,1024]{1,0:T(8,128)S(1)}) fusion(f32[1024]{0:T(1024)S(1)} %bitcast.226, bf16[512,4096]{1,0:T(8,128)(2,1)} %get-tuple-element.24, bf16[4096,1024]{1,0:T(8,128)(2,1)} %all-gather.8.cloned.1.call-done, f32[1024]{0:T(1024)S(1)} %bitcast.224, f32[1024]{0:T(1024)S(1)} %bitcast.218, f32[512]{0:T(512)S(1)} %add_rsqrt_fusion.1, ...), kind=kOutput, calls=%fused_computation.211 | convolution fusion | flops 4298636800 | bytes 16795648 | tf_op jit(solution)/shard_map/dot_general | solution.py:21
  286.0 7.3 %convolution_convert_fusion = bf16[4096,1024]{1,0:T(8,128)(2,1)} fusion(bf16[512,4096]{1,0:T(8,128)(2,1)S(1)} %copy-done.32, f32[512,1024]{1,0:T(8,128)S(1)} %get-tuple-element.39), kind=kOutput, calls=%fused_computation.12 | convolution fusion | flops 4299685888 | bytes 14680064 | tf_op jit(solution)/shard_map/dot_general | solution.py:25
  293.3 9.7 %convert_reduce_fusion = (f32[4096]{0:T(1024)S(1)}, bf16[512,4096]{1,0:T(8,128)(2,1)}) fusion(bf16[512,4096]{1,0:T(8,128)(2,1)S(1)} %copy-done.31, bf16[4096,1024]{1,0:T(8,128)(2,1)} %all-gather.8.cloned.1.call-done, f32[512,1024]{1,0:T(8,128)S(1)} %get-tuple-element.39), kind=kOutput, calls=%fused_computation.7 | convolution fusion | flops 4305973248 | bytes 18890752 | tf_op jit(solution)/shard_map/dot_general | solution.py:29
  303.0 9.4 %convert_dynamic-update-slice_fusion = bf16[1024,9216]{1,0:T(8,128)(2,1)} fusion(bf16[512,4096]{1,0:T(8,128)(2,1)} %get-tuple-element.116, f32[512,1024]{1,0:T(8,128)S(1)} %get-tuple-element.111, f32[1024]{0:T(1024)S(1)} %bitcast.225, f32[1024]{0:T(1024)S(1)} %bitcast.219, f32[512]{0:T(512)S(1)} %add_rsqrt_fusion.1, f32[512]{0:T(512)S(1)} %broadcast_multiply_fusion.5), kind=kOutput, calls=%fused_computation.6 | convolution fusion | flops 4301783040 | bytes 14692352 | tf_op jit(solution)/shard_map/dot_general | solution.py:25
  312.4 9.1 %multiply_reduce_fusion = (f32[1024]{0:T(1024)S(1)}, f32[512]{0:T(512)S(1)}, f32[512]{0:T(512)S(1)}, f32[1024]{0:T(1024)S(1)}, f32[512,1024]{1,0:T(8,128)S(1)}) fusion(f32[512,1024]{1,0:T(8,128)S(1)} %get-tuple-element.111, f32[512]{0:T(512)S(1)} %add_rsqrt_fusion.1, f32[512]{0:T(512)S(1)} %broadcast_multiply_fusion.5, f32[1024]{0:T(1024)S(1)} %bitcast.220, ...), kind=kOutput, calls=%fused_computation.34 | convolution fusion | flops 4300207104 | bytes 18894848 | tf_op jit(solution)/shard_map/dot_general | solution.py:29
  355.9 54.8 %attention_backward.1 = bf16[2048,768]{1,0:T(8,128)(2,1)} custom-call(s32[3,8]{1,0:T(4,128)} %add_add_fusion.2.info, bf16[2048,768]{1,0:T(8,128)(2,1)} %add_convert_fusion.1.q_ref.k_ref.v_ref, bf16[2048,768]{1,0:T(8,128)(2,1)} %add_convert_fusion.1.q_ref.k_ref.v_ref, bf16[2048,768]{1,0:T(8,128)(2,1)} %add_convert_fusion.1.q_ref.k_ref.v_ref, ...), custom_call_target="tpu_custom_call" | custom-call | tf_op jit(solution)/shard_map/attention_backward/pallas_call | solution.py:176
  418.7 5.6 fusion.45
  428.0 3.5 collective-permute-start.24
  453.3 21.0 %collective-permute-done.28 = bf16[4,128,768]{2,1,0:T(8,128)(2,1)} collective-permute-done((bf16[4,128,768]{2,1,0:T(8,128)(2,1)}, bf16[4,128,768]{2,1,0:T(8,128)(2,1)}, u32[]{:S(2)}, u32[]{:S(2)}) %collective-permute-start.28) | collective-permute-done | bytes 786464 | tf_op jit(solution)/shard_map/ppermute | solution.py:214
  478.2 8.0 %collective-permute-done.29 = bf16[2,128,768]{2,1,0:T(8,128)(2,1)S(1)} collective-permute-done((bf16[2,128,768]{2,1,0:T(8,128)(2,1)S(1)}, bf16[2,128,768]{2,1,0:T(8,128)(2,1)S(1)}, u32[]{:S(2)}, u32[]{:S(2)}) %collective-permute-start.29) | collective-permute-done | bytes 393248 | tf_op jit(solution)/shard_map/ppermute | solution.py:214
  488.8 13.3 %collective-permute-done.30 = bf16[1,128,768]{2,1,0:T(8,128)(2,1)S(1)} collective-permute-done((bf16[1,128,768]{2,1,0:T(8,128)(2,1)S(1)}, bf16[1,128,768]{2,1,0:T(8,128)(2,1)S(1)}, u32[]{:S(2)}, u32[]{:S(2)}) %collective-permute-start.30) | collective-permute-done | bytes 196640 | tf_op jit(solution)/shard_map/ppermute | solution.py:214
  510.2 21.6 %collective-permute-done.11 = bf16[512,1024]{1,0:T(8,128)(2,1)S(1)} collective-permute-done((bf16[512,1024]{1,0:T(8,128)(2,1)S(1)}, bf16[512,1024]{1,0:T(8,128)(2,1)S(1)}, u32[]{:S(2)}, u32[]{:S(2)}) %collective-permute-start.11) | collective-permute-done | bytes 1048608 | tf_op jit(solution)/shard_map/ppermute | solution.py:214
  534.7 19.3 %reduce-scatter.2.cloned.1.call-done = bf16[32,9216]{1,0:T(8,128)(2,1)} async-done(((bf16[1024,9216]{1,0:T(8,128)(2,1)}), bf16[32,9216]{1,0:T(8,128)(2,1)}) %reduce-scatter.2.cloned.1.call-update) | async-done | bytes 589840 | tf_op jit(solution)/shard_map/reduce_scatter | solution.py:353
  (274 shorter events, 116.9 us)
Async XLA Ops:
  7.2 89.0 %all-gather.4.cloned.1.call-start = ((), (), s32[]{:S(2)}) async-start(), calls=%async_computation.1 | async-start | bytes 8921088 | tf_op jit(solution)/shard_map/all_gather | solution.py:286
  13.8 182.0 %all-gather.6.cloned.1.call-start = ((), (), s32[]{:S(2)}) async-start(), calls=%async_computation.2 | async-start | bytes 10813440 | tf_op jit(solution)/shard_map/all_gather | solution.py:289
  15.6 257.3 %all-gather.8.cloned.1.call-start = ((), (), s32[]{:S(2)}) async-start(), calls=%async_computation.3 | async-start | bytes 8650752 | tf_op jit(solution)/shard_map/all_gather | solution.py:290
  16.3 537.7 %reduce-scatter.2.cloned.1.call-start = ((), (), s32[]{:S(2)}) async-start(), calls=%async_computation.4 | async-start | bytes 19464192 | tf_op jit(solution)/shard_map/reduce_scatter | solution.py:353
  16.4 28.1 %collective-permute-start.1 = (bf16[512,1024]{1,0:T(8,128)(2,1)S(1)}, bf16[512,1024]{1,0:T(8,128)(2,1)S(1)}, u32[]{:S(2)}, u32[]{:S(2)}) collective-permute-start(bf16[512,1024]{1,0:T(8,128)(2,1)S(1)} %bitcast.245), channel_id=1, source_target_pairs={{0,2},{1,3},{2,0},{3,1},{4,6},{5,7},{6,4},{7,5},{8,10},{9,11},{10,... | collective-permute-start | bytes 3145736 | tf_op jit(solution)/shard_map/ppermute | solution.py:214
  19.4 82.2 %collective-permute-start = (bf16[512,1024]{1,0:T(8,128)(2,1)S(1)}, bf16[512,1024]{1,0:T(8,128)(2,1)}, u32[]{:S(2)}, u32[]{:S(2)}) collective-permute-start(bf16[512,1024]{1,0:T(8,128)(2,1)S(1)} %bitcast.246), channel_id=1, source_target_pairs={{0,1},{1,0},{2,3},{3,2},{4,5},{5,4},{6,7},{7,6},{8,9},{9,8},{10,11... | collective-permute-start | bytes 3145736 | tf_op jit(solution)/shard_map/ppermute | solution.py:214
  44.5 57.1 %collective-permute-start.2 = (bf16[512,1024]{1,0:T(8,128)(2,1)S(1)}, bf16[512,1024]{1,0:T(8,128)(2,1)}, u32[]{:S(2)}, u32[]{:S(2)}) collective-permute-start(bf16[512,1024]{1,0:T(8,128)(2,1)S(1)} %collective-permute-done.1), channel_id=1, source_target_pairs={{0,1},{1,0},{2,3},{3,2},{4,5},{5,4},{6,7},{7,6},{8,9},{9,8},{10,11... | collective-permute-start | bytes 3145736 | tf_op jit(solution)/shard_map/ppermute | solution.py:214
  157.9 14.3 %collective-permute-start.5 = (bf16[512,256]{1,0:T(8,128)(2,1)S(1)}, bf16[512,256]{1,0:T(8,128)(2,1)S(1)}, u32[]{:S(2)}, u32[]{:S(2)}) collective-permute-start(bf16[512,256]{1,0:T(8,128)(2,1)S(1)} %get-tuple-element.60), channel_id=1, source_target_pairs={{0,3},{1,2},{2,1},{3,0},{4,7},{5,6},{6,5},{7,4},{8,11},{9,10},{10,... | collective-permute-start | bytes 786440 | tf_op jit(solution)/shard_map/ppermute | solution.py:214
  159.3 21.8 %collective-permute-start.4 = (bf16[512,256]{1,0:T(8,128)(2,1)S(1)}, bf16[512,256]{1,0:T(8,128)(2,1)S(1)}, u32[]{:S(2)}, u32[]{:S(2)}) collective-permute-start(bf16[512,256]{1,0:T(8,128)(2,1)S(1)} %get-tuple-element.61), channel_id=1, source_target_pairs={{0,2},{1,3},{2,0},{3,1},{4,6},{5,7},{6,4},{7,5},{8,10},{9,11},{10,... | collective-permute-start | bytes 786440 | tf_op jit(solution)/shard_map/ppermute | solution.py:214
  159.9 21.2 %collective-permute-start.3 = (bf16[512,256]{1,0:T(8,128)(2,1)S(1)}, bf16[512,256]{1,0:T(8,128)(2,1)S(1)}, u32[]{:S(2)}, u32[]{:S(2)}) collective-permute-start(bf16[512,256]{1,0:T(8,128)(2,1)S(1)} %get-tuple-element.62), channel_id=1, source_target_pairs={{0,1},{1,0},{2,3},{3,2},{4,5},{5,4},{6,7},{7,6},{8,9},{9,8},{10,11... | collective-permute-start | bytes 786440 | tf_op jit(solution)/shard_map/ppermute | solution.py:214
  337.0 17.8 %collective-permute-start.8 = (bf16[512,256]{1,0:T(8,128)(2,1)S(1)}, bf16[512,256]{1,0:T(8,128)(2,1)S(1)}, u32[]{:S(2)}, u32[]{:S(2)}) collective-permute-start(bf16[512,256]{1,0:T(8,128)(2,1)S(1)} %get-tuple-element.52), channel_id=1, source_target_pairs={{0,3},{1,2},{2,1},{3,0},{4,7},{5,6},{6,5},{7,4},{8,11},{9,10},{10,... | collective-permute-start | bytes 786440 | tf_op jit(solution)/shard_map/ppermute | solution.py:214
  338.3 16.5 %collective-permute-start.7 = (bf16[512,256]{1,0:T(8,128)(2,1)S(1)}, bf16[512,256]{1,0:T(8,128)(2,1)S(1)}, u32[]{:S(2)}, u32[]{:S(2)}) collective-permute-start(bf16[512,256]{1,0:T(8,128)(2,1)S(1)} %get-tuple-element.53), channel_id=1, source_target_pairs={{0,2},{1,3},{2,0},{3,1},{4,6},{5,7},{6,4},{7,5},{8,10},{9,11},{10,... | collective-permute-start | bytes 786440 | tf_op jit(solution)/shard_map/ppermute | solution.py:214
  338.9 15.9 %collective-permute-start.6 = (bf16[512,256]{1,0:T(8,128)(2,1)S(1)}, bf16[512,256]{1,0:T(8,128)(2,1)S(1)}, u32[]{:S(2)}, u32[]{:S(2)}) collective-permute-start(bf16[512,256]{1,0:T(8,128)(2,1)S(1)} %get-tuple-element.54), channel_id=1, source_target_pairs={{0,1},{1,0},{2,3},{3,2},{4,5},{5,4},{6,7},{7,6},{8,9},{9,8},{10,11... | collective-permute-start | bytes 786440 | tf_op jit(solution)/shard_map/ppermute | solution.py:214
  418.6 23.3 %collective-permute-start.34 = (f32[4,4,384]{2,1,0:T(4,128)S(1)}, f32[4,4,384]{2,1,0:T(4,128)S(1)}, u32[]{:S(2)}, u32[]{:S(2)}) collective-permute-start(f32[4,4,384]{2,1,0:T(4,128)S(1)} %fusion.47), channel_id=1, source_target_pairs={{0,4},{4,0},{8,12},{12,8},{16,20},{20,16},{24,28},{28,24},{1,5},{5... | collective-permute-start | bytes 73736 | tf_op jit(solution)/shard_map/ppermute | solution.py:214
  428.0 6.1 %collective-permute-start.24 = (f32[1,1024]{1,0:T(1,128)S(1)}, f32[1,1024]{1,0:T(1,128)S(1)}, u32[]{:S(2)}, u32[]{:S(2)}) collective-permute-start(f32[1,1024]{1,0:T(1,128)S(1)} %add.358), channel_id=1, source_target_pairs={{0,16},{4,20},{8,24},{12,28},{16,0},{20,4},{24,8},{28,12},{1,17},{... | collective-permute-start | bytes 12296 | tf_op jit(solution)/shard_map/ppermute | solution.py:214
  433.5 6.4 %collective-permute-start.22 = (f32[1,1024]{1,0:T(1,128)S(1)}, f32[1,1024]{1,0:T(1,128)S(1)}, u32[]{:S(2)}, u32[]{:S(2)}) collective-permute-start(f32[1,1024]{1,0:T(1,128)S(1)} %add.358), channel_id=1, source_target_pairs={{0,8},{4,12},{8,0},{12,4},{16,24},{20,28},{24,16},{28,20},{1,9},{5... | collective-permute-start | bytes 12296 | tf_op jit(solution)/shard_map/ppermute | solution.py:214
  434.1 6.6 %collective-permute-start.26 = (f32[1,1024]{1,0:T(1,128)S(1)}, f32[1,1024]{1,0:T(1,128)S(1)}, u32[]{:S(2)}, u32[]{:S(2)}) collective-permute-start(f32[1,1024]{1,0:T(1,128)S(1)} %collective-permute-done.24), channel_id=1, source_target_pairs={{0,8},{4,12},{8,0},{12,4},{16,24},{20,28},{24,16},{28,20},{1,9},{5... | collective-permute-start | bytes 12296 | tf_op jit(solution)/shard_map/ppermute | solution.py:214
  443.6 30.7 %collective-permute-start.28 = (bf16[4,128,768]{2,1,0:T(8,128)(2,1)}, bf16[4,128,768]{2,1,0:T(8,128)(2,1)}, u32[]{:S(2)}, u32[]{:S(2)}) collective-permute-start(bf16[4,128,768]{2,1,0:T(8,128)(2,1)} %fusion.38), channel_id=1, source_target_pairs={{0,4},{4,0},{8,12},{12,8},{16,20},{20,16},{24,28},{28,24},{1,5},{5... | collective-permute-start | bytes 2359304 | tf_op jit(solution)/shard_map/ppermute | solution.py:214
  444.7 65.5 %collective-permute-start.9 = (bf16[512,1024]{1,0:T(8,128)(2,1)}, bf16[512,1024]{1,0:T(8,128)(2,1)}, u32[]{:S(2)}, u32[]{:S(2)}) collective-permute-start(bf16[512,1024]{1,0:T(8,128)(2,1)} %convolution_convert_fusion.2), channel_id=1, source_target_pairs={{0,1},{1,0},{2,3},{3,2},{4,5},{5,4},{6,7},{7,6},{8,9},{9,8},{10,11... | collective-permute-start | bytes 3145736 | tf_op jit(solution)/shard_map/ppermute | solution.py:214
  444.8 59.4 %collective-permute-start.10 = (bf16[512,1024]{1,0:T(8,128)(2,1)}, bf16[512,1024]{1,0:T(8,128)(2,1)}, u32[]{:S(2)}, u32[]{:S(2)}) collective-permute-start(bf16[512,1024]{1,0:T(8,128)(2,1)} %convolution_convert_fusion.1), channel_id=1, source_target_pairs={{0,1},{1,0},{2,3},{3,2},{4,5},{5,4},{6,7},{7,6},{8,9},{9,8},{10,11... | collective-permute-start | bytes 3145736 | tf_op jit(solution)/shard_map/ppermute | solution.py:214
  451.9 25.6 %collective-permute-start.38 = (f32[1,384]{1,0:T(1,128)S(1)}, f32[1,384]{1,0:T(1,128)S(1)}, u32[]{:S(2)}, u32[]{:S(2)}) collective-permute-start(f32[1,384]{1,0:T(1,128)S(1)} %constant_dynamic-slice_fusion.7), channel_id=1, source_target_pairs={{0,2},{1,3},{2,0},{3,1},{4,6},{5,7},{6,4},{7,5},{8,10},{9,11},{10,... | collective-permute-start | bytes 4616 | tf_op jit(solution)/shard_map/ppermute | solution.py:214
  476.2 9.9 %collective-permute-start.29 = (bf16[2,128,768]{2,1,0:T(8,128)(2,1)S(1)}, bf16[2,128,768]{2,1,0:T(8,128)(2,1)S(1)}, u32[]{:S(2)}, u32[]{:S(2)}) collective-permute-start(bf16[2,128,768]{2,1,0:T(8,128)(2,1)S(1)} %fusion.44), channel_id=1, source_target_pairs={{0,8},{4,12},{8,0},{12,4},{16,24},{20,28},{24,16},{28,20},{1,9},{5... | collective-permute-start | bytes 1179656 | tf_op jit(solution)/shard_map/ppermute | solution.py:214
  486.2 15.9 %collective-permute-start.30 = (bf16[1,128,768]{2,1,0:T(8,128)(2,1)S(1)}, bf16[1,128,768]{2,1,0:T(8,128)(2,1)S(1)}, u32[]{:S(2)}, u32[]{:S(2)}) collective-permute-start(bf16[1,128,768]{2,1,0:T(8,128)(2,1)S(1)} %dynamic-slice_convert_fusion.2), channel_id=1, source_target_pairs={{0,16},{4,20},{8,24},{12,28},{16,0},{20,4},{24,8},{28,12},{1,17},{... | collective-permute-start | bytes 589832 | tf_op jit(solution)/shard_map/ppermute | solution.py:214
  506.6 25.1 %collective-permute-start.11 = (bf16[512,1024]{1,0:T(8,128)(2,1)S(1)}, bf16[512,1024]{1,0:T(8,128)(2,1)S(1)}, u32[]{:S(2)}, u32[]{:S(2)}) collective-permute-start(bf16[512,1024]{1,0:T(8,128)(2,1)S(1)} %add_convert_fusion.3), channel_id=1, source_target_pairs={{0,2},{1,3},{2,0},{3,1},{4,6},{5,7},{6,4},{7,5},{8,10},{9,11},{10,... | collective-permute-start | bytes 3145736 | tf_op jit(solution)/shard_map/ppermute | solution.py:214
  (54 other events, 598.4 us)
Sparse Core Ops, SparseCore 0:
  13.9 82.2 all-gather.3
  99.6 96.0 all-gather.5
  198.6 74.2 all-gather.7
  334.0 219.9 reduce-scatter.1

commit v2 on v1

--- a/solution.py
+++ b/solution.py
@@ -225,6 +225,17 @@
     return [held[k] for k in range(len(held))]
 
 
+def gather_stacked(value, axis):
+    for bit in reversed(bits(lax.axis_size(axis))):
+        value = jnp.concatenate([value, swap(value, axis, bit)])
+    return value
+
+
+def flipped(index, size):
+    flags = bits(size)
+    return sum(lax.bitwise_and(index // bit, 1) * mirror for bit, mirror in zip(flags, reversed(flags)))
+
+
 def trade(pieces, axis):
     return [pieces[0]] + [swap(pieces[k], axis, k) for k in range(1, len(pieces))]
 
@@ -278,32 +289,39 @@
     per_chunk = piece // BLOCK
     tokens, cotangent, ids = tokens[0], cotangent[0], segment_ids[0]
 
+    second = lax.all_gather(jnp.concatenate([up_weight, output_weight], axis=1), BOTH, axis=0, tiled=True)
+    down_full = lax.all_gather(down_weight, BOTH, axis=0, tiled=True)
+    up_full, output_full = second[:, :hidden], second[:, hidden:]
+
+    token_chunks = gather_relative(tokens, "ctx")
     vectors = [
         time_bias, query_bias, value_bias, output_bias, mixing_gain, mixing_bias, down_bias, final_gain, final_bias
     ]
     small = jnp.concatenate([jnp.stack(vectors), up_bias.reshape(ratio, own)]).T
     small = jnp.pad(small, ((0, 0), (0, 128 - small.shape[1])))
-    first = lax.all_gather(
-        jnp.concatenate([query_weight, key_weight, value_weight, time_weight, small], axis=1), BOTH, axis=0, tiled=True
-    )
-    second = lax.all_gather(jnp.concatenate([up_weight, output_weight], axis=1), BOTH, axis=0, tiled=True)
-    down_full = lax.all_gather(down_weight, BOTH, axis=0, tiled=True)
-    up_full, output_full = second[:, :hidden], second[:, hidden:]
-
-    token_chunks = gather_relative(tokens, "ctx")
-    time_feats = jnp.concatenate(gather_relative(time_feat, "dp"))
-
-    table = first[:, 4 * width :].astype(f32).T
+    pieces = []
+    for k in range(ctx):
+        at = lax.bitwise_xor(me, k) * cols
+        parts = [
+            lax.dynamic_slice_in_dim(w, at, cols, 1) for w in (query_weight, key_weight, value_weight, time_weight)
+        ]
+        pieces.append(jnp.concatenate(parts + [small], axis=1))
+    first = jnp.concatenate(to_absolute(trade(pieces, "ctx"), me))
+    first = gather_stacked(first[None], "dp")
+    first = jnp.concatenate(
+        [
+            lax.dynamic_index_in_dim(first, flipped(lax.bitwise_xor(me_dp, c), dp), 0, False)
+            for c in range(dp)
+        ]
+    )
+    qkv_weight = first[:, : 3 * cols]
+    table = first[:, 4 * cols :].astype(f32).T
     time_shift_bias, query_shift, value_shift, output_shift, gain_one, bias_one, down_shift, gain_two, bias_two = [
         table[n] for n in range(len(vectors))
     ]
     up_shift = table[len(vectors) : len(vectors) + ratio].reshape(ratio, devices, own).transpose(1, 0, 2).reshape(hidden)
-    time_shift = nn(time_feat, first[:, 3 * width : 4 * width]) + time_shift_bias
-
-    def my_cols(n):
-        return lax.dynamic_slice_in_dim(first, n * width + me * cols, cols, 1)
-
-    qkv_weight = jnp.concatenate([my_cols(n) for n in range(3)], axis=1)
+    shift_cols = trade([nn(time_feat, first[:, 3 * cols : 4 * cols])] * ctx, "ctx")
+    time_shift = jnp.concatenate(to_absolute(shift_cols, me), axis=1) + time_shift_bias
     qkv_shift = jnp.concatenate(
         [
             lax.dynamic_slice_in_dim(query_shift, me * cols, cols),
@@ -347,15 +365,27 @@
     output_grad = tn(attended, grad_branch).astype(bf16)
     output_shift_grad = jnp.sum(grad_branch.astype(f32), axis=0)
     down_blocks = down_grad.reshape(devices, ratio, own, width)
+    vector_grads = jnp.stack(
+        [output_shift_grad, gain_one_grad, bias_one_grad, down_shift_grad, gain_two_grad, bias_two_grad]
+    )
+    up_shift_grad = up_shift_grad.reshape(devices, ratio, own).transpose(1, 0, 2).reshape(ratio, width)
+    vector_grads = jnp.concatenate([vector_grads, up_shift_grad])
+    vector_grads = jnp.pad(vector_grads, ((0, 128 - vector_grads.shape[0]), (0, 0))).T.astype(bf16)
     packed = jnp.concatenate(
-        [up_grad] + [down_blocks[:, n].reshape(width, width) for n in range(ratio)] + [output_grad], axis=1
+        [up_grad] + [down_blocks[:, n].reshape(width, width) for n in range(ratio)] + [output_grad, vector_grads],
+        axis=1,
     )
     packed = lax.psum_scatter(packed, BOTH, scatter_dimension=0, tiled=True).astype(f32)
     up_weight_grad = packed[:, :hidden]
     down_weight_grad = jnp.concatenate(
         [packed[:, hidden + n * width : hidden + (n + 1) * width] for n in range(ratio)], axis=0
     )
-    output_weight_grad = packed[:, 2 * hidden :]
+    output_weight_grad = packed[:, 2 * hidden : 2 * hidden + width]
+    vector_grads = packed[:, 2 * hidden + width :].T
+    output_bias_grad, mixing_gain_grad, mixing_bias_grad, down_bias_grad, final_gain_grad, final_bias_grad = [
+        vector_grads[n] for n in range(6)
+    ]
+    up_bias_grad = vector_grads[6 : 6 + ratio].reshape(ratio * own)
 
     grad_attended = nt(grad_branch, output_full).astype(bf16)
     pieces = [lax.dynamic_slice_in_dim(grad_attended, lax.bitwise_xor(me, k) * cols, cols, 1) for k in range(ctx)]
@@ -379,18 +409,24 @@
         precision=lax.Precision.HIGHEST,
         preferred_element_type=f32,
     )
-    for bit in bits(ctx):
-        row_sum = row_sum + swap(row_sum, "ctx", bit)
-    row_sums = jnp.concatenate(gather_relative(row_sum, "dp"))
+    message = jnp.concatenate(
+        [row_sum, qkv_sum[None, :cols], qkv_sum[None, 2 * cols :], time_feat.astype(f32)], axis=1
+    )
+    message = gather_stacked(gather_stacked(message, "dp"), "ctx").reshape(ctx, dp, -1)
     mine = (me_dp * ctx + me) * own
+    row_sums = jnp.sum(message[:, :, :width], axis=0)
     time_weight_grad = lax.dot_general(
-        lax.dynamic_slice_in_dim(time_feats, mine, own, 1).astype(f32),
+        lax.dynamic_slice_in_dim(message[0, :, width + 2 * cols :], mine, own, 1),
         row_sums,
         (((0,), (0,)), ((), ())),
         precision=lax.Precision.HIGHEST,
         preferred_element_type=f32,
     )
     time_bias_grad = lax.dynamic_slice_in_dim(jnp.sum(row_sums, axis=0), mine, own)
+    sums = jnp.sum(message[:, :, width : width + 2 * cols], axis=1)
+    sums = lax.dynamic_index_in_dim(sums, flipped(lax.bitwise_xor(mine // cols, me), ctx), 0, False)
+    query_bias_grad = lax.dynamic_slice_in_dim(sums[:cols], lax.rem(mine, cols), own)
+    value_bias_grad = lax.dynamic_slice_in_dim(sums[cols:], lax.rem(mine, cols), own)
 
     summed = halve(qkv_grad.reshape(dp, ctx * own, 3 * cols), "dp", bf16).reshape(ctx, own, 3 * cols)
     blocks_out = to_absolute(
@@ -400,36 +436,6 @@
         jnp.concatenate([block[:, n * cols : (n + 1) * cols] for block in blocks_out], axis=1) for n in range(3)
     ]
 
-    def spread(part):
-        return lax.dynamic_update_slice_in_dim(jnp.zeros((width,), f32), part, me * cols, 0)
-
-    vector_grads = jnp.stack(
-        [
-            spread(qkv_sum[:cols]),
-            spread(qkv_sum[2 * cols :]),
-            output_shift_grad,
-            gain_one_grad,
-            bias_one_grad,
-            down_shift_grad,
-            gain_two_grad,
-            bias_two_grad,
-        ]
-    ).reshape(8, devices, own)
-    vector_grads = jnp.concatenate(
-        [vector_grads.transpose(1, 0, 2).reshape(devices, 8 * own), up_shift_grad.reshape(devices, ratio * own)], axis=1
-    )
-    vector_grads = halve(halve(vector_grads.reshape(dp, ctx, -1), "dp", f32), "ctx", f32)
-    (
-        query_bias_grad,
-        value_bias_grad,
-        output_bias_grad,
-        mixing_gain_grad,
-        mixing_bias_grad,
-        down_bias_grad,
-        final_gain_grad,
-        final_bias_grad,
-    ) = [vector_grads[n * own : (n + 1) * own] for n in range(8)]
-    up_bias_grad = vector_grads[8 * own :]
     return (
         layer_out[None],
         tokens_grad[None],

time: 570 us -> 560 us (0.982)
  starting transfers between devices: 40.3 us -> 23.3 us
  matrix products: 90.1 us -> 83.4 us
  local copies, waits for them, and re-layouts: 32.1 us -> 38.4 us
    ppermute x39 -> x32, waiting for transfers between devices: 115 us -> 252 us  [swap(): return lax.ppermute(value, axis, [(i, i ^ mask) for i in range(size)])]
    all_gather x1, waiting for transfers between devices: 61.6 us -> 0.01 us  [shards(): down_full = lax.all_gather(down_weight, BOTH, axis=0, tiled=True)]
    all_gather x1 -> x0, waiting for transfers between devices: 51.7 us -> none  [shards(): lax.all_gather(jnp.concatenate([query_weight, key_weight, value_weight, t...]
    ppermute x39 -> x32, starting transfers between devices: 40.2 us -> 23.2 us  [swap(): return lax.ppermute(value, axis, [(i, i ^ mask) for i in range(size)])]
    all_gather x1, waiting for transfers between devices: 14.4 us -> 0.01 us  [shards(): lax.all_gather(jnp.concatenate([up_weight, output_weight], axis=1), BOTH,...]
    reduce_scatter x1, waiting for transfers between devices: 19.3 us -> 11.6 us  [shards(): lax.psum_scatter(packed, BOTH, scatter_dimension=0, tiled=True).astype(f32)]
    unnamed x84 -> x59, local copies, waits for them, and re-layouts: 16.1 us -> 18.8 us
  transfers between devices with their start and end apart: 43 -> 35, of which waited for: 20 -> 23; matrix products, arithmetic and copies ran while one was open for 12% -> 12% of each run, Pallas kernels for 18% -> 20%
where the time goes in v2:
time: 560 us; the launch traced here: 553 us
  waiting for transfers between devices  264 us (47%)
  Pallas kernels  108 us (19%)
  matrix products  83.4 us (15%)
  local copies, waits for them, and re-layouts  38.4 us (7%)
  starting transfers between devices  23.3 us (4%)
  other arithmetic  21.3 us (4%)
  between operations  14.8 us (3%)
    ppermute x32, waiting for transfers between devices, swap(): return lax.ppermute(value, axis, [(i, i ^ mask) for i in range(size)])  252 us
    pallas_call x1, Pallas kernels, attention_backward(): pl.pallas_call(functools.partial(backward_kernel, per_chunk, heads // 2),...  57.3 us
    pallas_call x1, Pallas kernels, attention_forward(): pl.pallas_call(functools.partial(forward_kernel, per_chunk, heads // 2),...  50.6 us
    dot_general x5, matrix products, nn(): return jnp.dot(left, right, preferred_element_type=f32)  29.5 us
    dot_general x7, matrix products, nt(): lax.dot_general(left, right, (((1,), (1,)), ((), ())), preferred_element_...  27.6 us
    dot_general x4, matrix products, tn(): lax.dot_general(left, right, (((0,), (0,)), ((), ())), preferred_element_...  23.9 us
    ppermute x32, starting transfers between devices, swap(): return lax.ppermute(value, axis, [(i, i ^ mask) for i in range(size)])  23.2 us
    unnamed x59, local copies, waits for them, and re-layouts  18.8 us
  transfers between devices with their start and end apart: 35, of which 23 were waited for; matrix products, arithmetic and copies ran while one was open for 12% of the time, Pallas kernels for 20%

profile of v2, /device:TPU:0, one launch (start us, length us, event | category | flops | bytes accessed | tf_op | source)
XLA Modules:
  0.0 552.9 jit_solution(4025292667384124366)
XLA Ops:
  25.7 20.5 %collective-permute-done.3 = bf16[1,128,1152]{2,1,0:T(8,128)(2,1)S(1)} collective-permute-done((bf16[1,128,1152]{2,1,0:T(8,128)(2,1)S(1)}, bf16[1,128,1152]{2,1,0:T(8,128)(2,1)S(1)}, u32[]{:S(2)}, u32[]{:S(2)}) %collective-permute-start.3) | collective-permute-done | bytes 294944 | tf_op jit(solution)/shard_map/ppermute | solution.py:214
  46.4 29.3 %collective-permute-done.4 = bf16[2,128,1152]{2,1,0:T(8,128)(2,1)S(1)} collective-permute-done((bf16[2,128,1152]{2,1,0:T(8,128)(2,1)S(1)}, bf16[2,128,1152]{2,1,0:T(8,128)(2,1)S(1)}, u32[]{:S(2)}, u32[]{:S(2)}) %collective-permute-start.4) | collective-permute-done | bytes 589856 | tf_op jit(solution)/shard_map/ppermute | solution.py:214
  86.9 33.3 %collective-permute-done.10 = bf16[512,1024]{1,0:T(8,128)(2,1)} collective-permute-done((bf16[512,1024]{1,0:T(8,128)(2,1)}, bf16[512,1024]{1,0:T(8,128)(2,1)}, u32[]{:S(2)}, u32[]{:S(2)}) %collective-permute-start.10) | collective-permute-done | bytes 1048608 | tf_op jit(solution)/shard_map/ppermute | solution.py:214
  129.2 7.5 %add_convert_fusion.1.q_ref.k_ref.v_ref = bf16[2048,768]{1,0:T(8,128)(2,1)} fusion(f32[768]{0:T(1024)S(1)} %pad_maximum_fusion.21, bf16[1024,1152]{1,0:T(8,128)(2,1)S(1)} %copy-done.11, bf16[512,1024]{1,0:T(8,128)(2,1)} %collective-permute-done.11, bf16[512,1024]{1,0:T(8,128)(2,1)} %collective-permute-done.10, ...), kind=kOutput, calls=%fused_computation.17 | convolution fusion | flops 3245342720 | bytes 8921088 | tf_op jit(solution)/shard_map/dot_general | solution.py:21
  136.7 50.6 %attention_forward.1 = (bf16[2048,256]{1,0:T(8,128)(2,1)}, f32[8,4,256]{2,1,0:T(4,128)}) custom-call(s32[3,8]{1,0:T(4,128)} %add_add_fusion.2.info, bf16[2048,768]{1,0:T(8,128)(2,1)} %add_convert_fusion.1.q_ref.k_ref.v_ref, bf16[2048,768]{1,0:T(8,128)(2,1)} %add_convert_fusion.1.q_ref.k_ref.v_ref, bf16[2048,768]{1,0:T(8,128)(2,1)} %add_convert_fusion.1.q_ref.k_ref.v_ref, ...), custom_call_target="tpu_custom_call" | custom-call | tf_op jit(solution)/shard_map/attention_forward/pallas_call | solution.py:84
  192.0 11.7 %collective-permute-done.14 = bf16[512,256]{1,0:T(8,128)(2,1)S(1)} collective-permute-done((bf16[512,256]{1,0:T(8,128)(2,1)}, bf16[512,256]{1,0:T(8,128)(2,1)S(1)}, u32[]{:S(2)}, u32[]{:S(2)}) %collective-permute-start.14) | collective-permute-done | bytes 262176 | tf_op jit(solution)/shard_map/ppermute | solution.py:214
  203.8 7.1 %collective-permute-done.13 = bf16[512,256]{1,0:T(8,128)(2,1)S(1)} collective-permute-done((bf16[512,256]{1,0:T(8,128)(2,1)S(1)}, bf16[512,256]{1,0:T(8,128)(2,1)S(1)}, u32[]{:S(2)}, u32[]{:S(2)}) %collective-permute-start.13) | collective-permute-done | bytes 262176 | tf_op jit(solution)/shard_map/ppermute | solution.py:214
  218.8 9.8 %fusion.4 = (bf16[512,4096]{1,0:T(8,128)(2,1)}, bf16[512,4096]{1,0:T(8,128)(2,1)}) fusion(f32[4096]{0:T(1024)S(1)} %add.427, bf16[1024,5120]{1,0:T(8,128)(2,1)S(1)} %copy-done.18, f32[512,1024]{1,0:T(8,128)S(1)} %get-tuple-element.138, f32[1024]{0:T(1024)S(1)} %get-tuple-element.37, f32[1024]{0:T(1024)S(1)} %get-tuple-element.38, ...), kind=kOutput, calls=%fused_computation.5 | convolution fusion | flops 4322754560 | bytes 18903040 | tf_op jit(solution)/shard_map/dot_general | solution.py:21
  228.6 8.4 %fusion.78 = (f32[512]{0:T(512)S(1)}, f32[512,1024]{1,0:T(8,128)S(1)}) fusion(f32[1024]{0:T(1024)S(1)} %get-tuple-element.36, bf16[512,4096]{1,0:T(8,128)(2,1)} %get-tuple-element.24, bf16[4096,1024]{1,0:T(8,128)(2,1)} %all-gather.5.cloned.1.call-done, f32[1024]{0:T(1024)S(1)} %get-tuple-element.37, f32[1024]{0:T(1024)S(1)} %get-tuple-element.38, ...), kind=kOutput, calls=%fused_computation.227 | convolution fusion | flops 4298636800 | bytes 16795648 | tf_op jit(solution)/shard_map/dot_general | solution.py:21
  242.1 5.1 convolution_convert_fusion
  247.3 11.7 %fusion.79 = (bf16[4096]{0:T(1024)(128)(2,1)S(1)}, bf16[512,4096]{1,0:T(8,128)(2,1)}) fusion(bf16[512,4096]{1,0:T(8,128)(2,1)} %get-tuple-element.25, bf16[4096,1024]{1,0:T(8,128)(2,1)} %all-gather.5.cloned.1.call-done, f32[512,1024]{1,0:T(8,128)} %copy-done.8), kind=kOutput, calls=%fused_computation.228 | convolution fusion | flops 4303876096 | bytes 18882560 | tf_op jit(solution)/shard_map/dot_general | solution.py:29
  258.9 9.3 %convert_dynamic-update-slice_fusion = bf16[1024,9344]{1,0:T(8,128)(2,1)} fusion(bf16[512,4096]{1,0:T(8,128)(2,1)} %get-tuple-element.143, f32[512,1024]{1,0:T(8,128)S(1)} %get-tuple-element.138, f32[1024]{0:T(1024)S(1)} %get-tuple-element.37, f32[1024]{0:T(1024)S(1)} %get-tuple-element.38, f32[512]{0:T(512)S(1)} %add_rsqrt_fusion.1, ...), kind=kOutput, calls=%fused_computation.6 | convolution fusion | flops 4301783040 | bytes 14692352 | tf_op jit(solution)/shard_map/dot_general | solution.py:25
  268.3 9.0 %multiply_reduce_fusion = (bf16[1024]{0:T(1024)(128)(2,1)S(1)}, f32[512]{0:T(512)S(1)}, f32[512]{0:T(512)S(1)}, bf16[1024]{0:T(1024)(128)(2,1)S(1)}, f32[512,1024]{1,0:T(8,128)S(1)}) fusion(f32[512,1024]{1,0:T(8,128)S(1)} %get-tuple-element.138, f32[512]{0:T(512)S(1)} %add_rsqrt_fusion.1, f32[512]{0:T(512)S(1)} %broadcast_multiply_fusion.5, ...), kind=kOutput, calls=%fused_computation.28 | convolution fusion | flops 4300207104 | bytes 18890752 | tf_op jit(solution)/shard_map/dot_general | solution.py:29
  299.9 14.9 %collective-permute-done.17 = bf16[512,256]{1,0:T(8,128)(2,1)S(1)} collective-permute-done((bf16[512,256]{1,0:T(8,128)(2,1)S(1)}, bf16[512,256]{1,0:T(8,128)(2,1)S(1)}, u32[]{:S(2)}, u32[]{:S(2)}) %collective-permute-start.17) | collective-permute-done | bytes 262176 | tf_op jit(solution)/shard_map/ppermute | solution.py:214
  314.9 12.8 %collective-permute-done.16 = bf16[512,256]{1,0:T(8,128)(2,1)} collective-permute-done((bf16[512,256]{1,0:T(8,128)(2,1)S(1)}, bf16[512,256]{1,0:T(8,128)(2,1)}, u32[]{:S(2)}, u32[]{:S(2)}) %collective-permute-start.16) | collective-permute-done | bytes 262176 | tf_op jit(solution)/shard_map/ppermute | solution.py:214
  329.8 57.3 %attention_backward.1 = bf16[2048,768]{1,0:T(8,128)(2,1)} custom-call(s32[3,8]{1,0:T(4,128)} %add_add_fusion.2.info, bf16[2048,768]{1,0:T(8,128)(2,1)} %add_convert_fusion.1.q_ref.k_ref.v_ref, bf16[2048,768]{1,0:T(8,128)(2,1)} %add_convert_fusion.1.q_ref.k_ref.v_ref, bf16[2048,768]{1,0:T(8,128)(2,1)} %add_convert_fusion.1.q_ref.k_ref.v_ref, ...), custom_call_target="tpu_custom_call" | custom-call | tf_op jit(solution)/shard_map/attention_backward/pallas_call | solution.py:176
  387.1 6.7 %fusion.48 = f32[1024,768]{1,0:T(8,128)S(1)} fusion(bf16[2048,768]{1,0:T(8,128)(2,1)} %attention_backward.1, bf16[512,1024]{1,0:T(8,128)(2,1)} %collective-permute-done.11, bf16[512,1024]{1,0:T(8,128)(2,1)} %collective-permute-done.10, bf16[512,1024]{1,0:T(8,128)(2,1)} %collective-permute-done.9, bf16[512,1024]{1,0:T(8,128)(2,1)} %bitcast, ...), kind=kOutput, calls=%fused_computation.109 | convolution fusion | flops 3242196992 | bytes 10489856 | tf_op jit(solution)/shard_map/dot_general | solution.py:25
  397.1 31.5 %collective-permute-done.26 = bf16[4,128,768]{2,1,0:T(8,128)(2,1)S(1)} collective-permute-done((bf16[4,128,768]{2,1,0:T(8,128)(2,1)S(1)}, bf16[4,128,768]{2,1,0:T(8,128)(2,1)S(1)}, u32[]{:S(2)}, u32[]{:S(2)}) %collective-permute-start.26) | collective-permute-done | bytes 786464 | tf_op jit(solution)/shard_map/ppermute | solution.py:214
  431.3 11.9 %collective-permute-done.27 = bf16[2,128,768]{2,1,0:T(8,128)(2,1)S(1)} collective-permute-done((bf16[2,128,768]{2,1,0:T(8,128)(2,1)S(1)}, bf16[2,128,768]{2,1,0:T(8,128)(2,1)S(1)}, u32[]{:S(2)}, u32[]{:S(2)}) %collective-permute-start.27) | collective-permute-done | bytes 393248 | tf_op jit(solution)/shard_map/ppermute | solution.py:214
  445.2 10.3 %collective-permute-done.28 = bf16[1,128,768]{2,1,0:T(8,128)(2,1)S(1)} collective-permute-done((bf16[1,128,768]{2,1,0:T(8,128)(2,1)S(1)}, bf16[1,128,768]{2,1,0:T(8,128)(2,1)S(1)}, u32[]{:S(2)}, u32[]{:S(2)}) %collective-permute-start.28) | collective-permute-done | bytes 196640 | tf_op jit(solution)/shard_map/ppermute | solution.py:214
  457.5 42.2 %collective-permute-done.31 = f32[32,768]{1,0:T(8,128)S(1)} collective-permute-done((f32[32,768]{1,0:T(8,128)S(1)}, f32[32,768]{1,0:T(8,128)S(1)}, u32[]{:S(2)}, u32[]{:S(2)}) %collective-permute-start.31) | collective-permute-done | bytes 98336 | tf_op jit(solution)/shard_map/ppermute | solution.py:214
  505.1 4.4 collective-permute-done.21
  520.8 4.8 collective-permute-done.24
  529.5 11.6 %reduce-scatter.2.cloned.1.call-done = bf16[32,9344]{1,0:T(8,128)(2,1)} async-done(((bf16[1024,9344]{1,0:T(8,128)(2,1)}), bf16[32,9344]{1,0:T(8,128)(2,1)}) %reduce-scatter.2.cloned.1.call-update) | async-done | bytes 598032 | tf_op jit(solution)/shard_map/reduce_scatter | solution.py:378
  (233 shorter events, 116.6 us)
Async XLA Ops:
  7.2 205.7 %all-gather.3.cloned.1.call-start = ((), (), s32[]{:S(2)}) async-start(), calls=%async_computation.1 | async-start | bytes 10813440 | tf_op jit(solution)/shard_map/all_gather | solution.py:292
  9.0 219.6 %all-gather.5.cloned.1.call-start = ((), (), s32[]{:S(2)}) async-start(), calls=%async_computation.2 | async-start | bytes 8650752 | tf_op jit(solution)/shard_map/all_gather | solution.py:293
  9.7 531.3 %reduce-scatter.2.cloned.1.call-start = ((), (), s32[]{:S(2)}) async-start(), calls=%async_computation.3 | async-start | bytes 19734528 | tf_op jit(solution)/shard_map/reduce_scatter | solution.py:378
  22.7 23.5 %collective-permute-start.3 = (bf16[1,128,1152]{2,1,0:T(8,128)(2,1)S(1)}, bf16[1,128,1152]{2,1,0:T(8,128)(2,1)S(1)}, u32[]{:S(2)}, u32[]{:S(2)}) collective-permute-start(bf16[1,128,1152]{2,1,0:T(8,128)(2,1)S(1)} %maximum_bitcast_fusion), channel_id=1, source_target_pairs={{0,16},{4,20},{8,24},{12,28},{16,0},{20,4},{24,8},{28,12},{1,17},{... | collective-permute-start | bytes 884744 | tf_op jit(solution)/shard_map/ppermute | solution.py:214
  46.3 29.3 %collective-permute-start.4 = (bf16[2,128,1152]{2,1,0:T(8,128)(2,1)S(1)}, bf16[2,128,1152]{2,1,0:T(8,128)(2,1)S(1)}, u32[]{:S(2)}, u32[]{:S(2)}) collective-permute-start(bf16[2,128,1152]{2,1,0:T(8,128)(2,1)S(1)} %pad_maximum_fusion.5), channel_id=1, source_target_pairs={{0,8},{4,12},{8,0},{12,4},{16,24},{20,28},{24,16},{28,20},{1,9},{5... | collective-permute-start | bytes 1769480 | tf_op jit(solution)/shard_map/ppermute | solution.py:214
  75.8 45.6 %collective-permute-start.5 = (bf16[4,128,1152]{2,1,0:T(8,128)(2,1)S(1)}, bf16[4,128,1152]{2,1,0:T(8,128)(2,1)S(1)}, u32[]{:S(2)}, u32[]{:S(2)}) collective-permute-start(bf16[4,128,1152]{2,1,0:T(8,128)(2,1)S(1)} %pad_maximum_fusion.1), channel_id=1, source_target_pairs={{0,4},{4,0},{8,12},{12,8},{16,20},{20,16},{24,28},{28,24},{1,5},{5... | collective-permute-start | bytes 3538952 | tf_op jit(solution)/shard_map/ppermute | solution.py:214
  77.3 42.9 %collective-permute-start.10 = (bf16[512,1024]{1,0:T(8,128)(2,1)}, bf16[512,1024]{1,0:T(8,128)(2,1)}, u32[]{:S(2)}, u32[]{:S(2)}) collective-permute-start(bf16[512,1024]{1,0:T(8,128)(2,1)} %bitcast), channel_id=1, source_target_pairs={{0,2},{1,3},{2,0},{3,1},{4,6},{5,7},{6,4},{7,5},{8,10},{9,11},{10,... | collective-permute-start | bytes 3145736 | tf_op jit(solution)/shard_map/ppermute | solution.py:214
  78.7 50.4 %collective-permute-start.9 = (bf16[512,1024]{1,0:T(8,128)(2,1)}, bf16[512,1024]{1,0:T(8,128)(2,1)}, u32[]{:S(2)}, u32[]{:S(2)}) collective-permute-start(bf16[512,1024]{1,0:T(8,128)(2,1)} %bitcast), channel_id=1, source_target_pairs={{0,1},{1,0},{2,3},{3,2},{4,5},{5,4},{6,7},{7,6},{8,9},{9,8},{10,11... | collective-permute-start | bytes 3145736 | tf_op jit(solution)/shard_map/ppermute | solution.py:214
  120.2 9.0 %collective-permute-start.11 = (bf16[512,1024]{1,0:T(8,128)(2,1)}, bf16[512,1024]{1,0:T(8,128)(2,1)}, u32[]{:S(2)}, u32[]{:S(2)}) collective-permute-start(bf16[512,1024]{1,0:T(8,128)(2,1)} %collective-permute-done.10), channel_id=1, source_target_pairs={{0,1},{1,0},{2,3},{3,2},{4,5},{5,4},{6,7},{7,6},{8,9},{9,8},{10,11... | collective-permute-start | bytes 3145736 | tf_op jit(solution)/shard_map/ppermute | solution.py:214
  189.3 14.4 %collective-permute-start.14 = (bf16[512,256]{1,0:T(8,128)(2,1)}, bf16[512,256]{1,0:T(8,128)(2,1)S(1)}, u32[]{:S(2)}, u32[]{:S(2)}) collective-permute-start(bf16[512,256]{1,0:T(8,128)(2,1)} %get-tuple-element.73), channel_id=1, source_target_pairs={{0,3},{1,2},{2,1},{3,0},{4,7},{5,6},{6,5},{7,4},{8,11},{9,10},{10,... | collective-permute-start | bytes 786440 | tf_op jit(solution)/shard_map/ppermute | solution.py:214
  189.9 20.9 %collective-permute-start.13 = (bf16[512,256]{1,0:T(8,128)(2,1)S(1)}, bf16[512,256]{1,0:T(8,128)(2,1)S(1)}, u32[]{:S(2)}, u32[]{:S(2)}) collective-permute-start(bf16[512,256]{1,0:T(8,128)(2,1)S(1)} %get-tuple-element.74), channel_id=1, source_target_pairs={{0,2},{1,3},{2,0},{3,1},{4,6},{5,7},{6,4},{7,5},{8,10},{9,11},{10,... | collective-permute-start | bytes 786440 | tf_op jit(solution)/shard_map/ppermute | solution.py:214
  191.3 19.6 %collective-permute-start.12 = (bf16[512,256]{1,0:T(8,128)(2,1)S(1)}, bf16[512,256]{1,0:T(8,128)(2,1)}, u32[]{:S(2)}, u32[]{:S(2)}) collective-permute-start(bf16[512,256]{1,0:T(8,128)(2,1)S(1)} %get-tuple-element.75), channel_id=1, source_target_pairs={{0,1},{1,0},{2,3},{3,2},{4,5},{5,4},{6,7},{7,6},{8,9},{9,8},{10,11... | collective-permute-start | bytes 786440 | tf_op jit(solution)/shard_map/ppermute | solution.py:214
  297.9 17.0 %collective-permute-start.17 = (bf16[512,256]{1,0:T(8,128)(2,1)S(1)}, bf16[512,256]{1,0:T(8,128)(2,1)S(1)}, u32[]{:S(2)}, u32[]{:S(2)}) collective-permute-start(bf16[512,256]{1,0:T(8,128)(2,1)S(1)} %get-tuple-element.65), channel_id=1, source_target_pairs={{0,3},{1,2},{2,1},{3,0},{4,7},{5,6},{6,5},{7,4},{8,11},{9,10},{10,... | collective-permute-start | bytes 786440 | tf_op jit(solution)/shard_map/ppermute | solution.py:214
  298.4 29.3 %collective-permute-start.16 = (bf16[512,256]{1,0:T(8,128)(2,1)S(1)}, bf16[512,256]{1,0:T(8,128)(2,1)}, u32[]{:S(2)}, u32[]{:S(2)}) collective-permute-start(bf16[512,256]{1,0:T(8,128)(2,1)S(1)} %get-tuple-element.66), channel_id=1, source_target_pairs={{0,2},{1,3},{2,0},{3,1},{4,6},{5,7},{6,4},{7,5},{8,10},{9,11},{10,... | collective-permute-start | bytes 786440 | tf_op jit(solution)/shard_map/ppermute | solution.py:214
  299.8 27.9 %collective-permute-start.15 = (bf16[512,256]{1,0:T(8,128)(2,1)S(1)}, bf16[512,256]{1,0:T(8,128)(2,1)}, u32[]{:S(2)}, u32[]{:S(2)}) collective-permute-start(bf16[512,256]{1,0:T(8,128)(2,1)S(1)} %get-tuple-element.67), channel_id=1, source_target_pairs={{0,1},{1,0},{2,3},{3,2},{4,5},{5,4},{6,7},{7,6},{8,9},{9,8},{10,11... | collective-permute-start | bytes 786440 | tf_op jit(solution)/shard_map/ppermute | solution.py:214
  393.8 34.8 %collective-permute-start.26 = (bf16[4,128,768]{2,1,0:T(8,128)(2,1)S(1)}, bf16[4,128,768]{2,1,0:T(8,128)(2,1)S(1)}, u32[]{:S(2)}, u32[]{:S(2)}) collective-permute-start(bf16[4,128,768]{2,1,0:T(8,128)(2,1)S(1)} %fusion.31), channel_id=1, source_target_pairs={{0,4},{4,0},{8,12},{12,8},{16,20},{20,16},{24,28},{28,24},{1,5},{5... | collective-permute-start | bytes 2359304 | tf_op jit(solution)/shard_map/ppermute | solution.py:214
  395.0 49.1 %collective-permute-start.19 = (bf16[512,1024]{1,0:T(8,128)(2,1)S(1)}, bf16[512,1024]{1,0:T(8,128)(2,1)S(1)}, u32[]{:S(2)}, u32[]{:S(2)}) collective-permute-start(bf16[512,1024]{1,0:T(8,128)(2,1)S(1)} %convolution_convert_fusion.1), channel_id=1, source_target_pairs={{0,1},{1,0},{2,3},{3,2},{4,5},{5,4},{6,7},{7,6},{8,9},{9,8},{10,11... | collective-permute-start | bytes 3145736 | tf_op jit(solution)/shard_map/ppermute | solution.py:214
  396.1 106.9 %collective-permute-start.18 = (bf16[512,1024]{1,0:T(8,128)(2,1)S(1)}, bf16[512,1024]{1,0:T(8,128)(2,1)S(1)}, u32[]{:S(2)}, u32[]{:S(2)}) collective-permute-start(bf16[512,1024]{1,0:T(8,128)(2,1)S(1)} %convolution_convert_fusion.2), channel_id=1, source_target_pairs={{0,1},{1,0},{2,3},{3,2},{4,5},{5,4},{6,7},{7,6},{8,9},{9,8},{10,11... | collective-permute-start | bytes 3145736 | tf_op jit(solution)/shard_map/ppermute | solution.py:214
  428.9 14.3 %collective-permute-start.27 = (bf16[2,128,768]{2,1,0:T(8,128)(2,1)S(1)}, bf16[2,128,768]{2,1,0:T(8,128)(2,1)S(1)}, u32[]{:S(2)}, u32[]{:S(2)}) collective-permute-start(bf16[2,128,768]{2,1,0:T(8,128)(2,1)S(1)} %fusion.47), channel_id=1, source_target_pairs={{0,8},{4,12},{8,0},{12,4},{16,24},{20,28},{24,16},{28,20},{1,9},{5... | collective-permute-start | bytes 1179656 | tf_op jit(solution)/shard_map/ppermute | solution.py:214
  443.3 12.2 %collective-permute-start.28 = (bf16[1,128,768]{2,1,0:T(8,128)(2,1)S(1)}, bf16[1,128,768]{2,1,0:T(8,128)(2,1)S(1)}, u32[]{:S(2)}, u32[]{:S(2)}) collective-permute-start(bf16[1,128,768]{2,1,0:T(8,128)(2,1)S(1)} %dynamic-slice_convert_fusion.2), channel_id=1, source_target_pairs={{0,16},{4,20},{8,24},{12,28},{16,0},{20,4},{24,8},{28,12},{1,17},{... | collective-permute-start | bytes 589832 | tf_op jit(solution)/shard_map/ppermute | solution.py:214
  445.1 57.9 %collective-permute-start.20 = (bf16[512,1024]{1,0:T(8,128)(2,1)S(1)}, bf16[512,1024]{1,0:T(8,128)(2,1)S(1)}, u32[]{:S(2)}, u32[]{:S(2)}) collective-permute-start(bf16[512,1024]{1,0:T(8,128)(2,1)S(1)} %add_convert_fusion.3), channel_id=1, source_target_pairs={{0,2},{1,3},{2,0},{3,1},{4,6},{5,7},{6,4},{7,5},{8,10},{9,11},{10,... | collective-permute-start | bytes 3145736 | tf_op jit(solution)/shard_map/ppermute | solution.py:214
  455.6 44.2 %collective-permute-start.31 = (f32[32,768]{1,0:T(8,128)S(1)}, f32[32,768]{1,0:T(8,128)S(1)}, u32[]{:S(2)}, u32[]{:S(2)}) collective-permute-start(f32[32,768]{1,0:T(8,128)S(1)} %get-tuple-element.88), channel_id=1, source_target_pairs={{0,3},{1,2},{2,1},{3,0},{4,7},{5,6},{6,5},{7,4},{8,11},{9,10},{10,... | collective-permute-start | bytes 294920 | tf_op jit(solution)/shard_map/ppermute | solution.py:214
  455.7 47.2 %collective-permute-start.30 = (f32[32,768]{1,0:T(8,128)S(1)}, f32[32,768]{1,0:T(8,128)S(1)}, u32[]{:S(2)}, u32[]{:S(2)}) collective-permute-start(f32[32,768]{1,0:T(8,128)S(1)} %get-tuple-element.89), channel_id=1, source_target_pairs={{0,2},{1,3},{2,0},{3,1},{4,6},{5,7},{6,4},{7,5},{8,10},{9,11},{10,... | collective-permute-start | bytes 294920 | tf_op jit(solution)/shard_map/ppermute | solution.py:214
  455.7 47.2 %collective-permute-start.29 = (f32[32,768]{1,0:T(8,128)S(1)}, f32[32,768]{1,0:T(8,128)S(1)}, u32[]{:S(2)}, u32[]{:S(2)}) collective-permute-start(f32[32,768]{1,0:T(8,128)S(1)} %get-tuple-element.90), channel_id=1, source_target_pairs={{0,1},{1,0},{2,3},{3,2},{4,5},{5,4},{6,7},{7,6},{8,9},{9,8},{10,11... | collective-permute-start | bytes 294920 | tf_op jit(solution)/shard_map/ppermute | solution.py:214
  (31 other events, 217.6 us)
Sparse Core Ops, SparseCore 0:
  11.4 121.1 all-gather.2
  135.5 88.3 all-gather.4
  294.9 246.0 reduce-scatter.1

commit v3 on v2

--- a/solution.py
+++ b/solution.py
@@ -39,22 +39,22 @@
     return lax.bitwise_xor(block // per_chunk, me) * per_chunk + lax.rem(block, per_chunk)
 
 
-def forward_kernel(
-    per_chunk, pairs, info, q_ref, k_ref, v_ref, idc_ref, idr_ref, o_ref, lse_ref, o_acc, m_acc, l_acc
-):
+def forward_kernel(per_chunk, pairs, info, qkv_ref, idc_ref, idr_ref, o_ref, lse_ref, o_acc, m_acc, l_acc):
     i = pl.program_id(0)
     me = info[2, 0]
     m_acc[...] = jnp.full_like(m_acc, MASKED)
     l_acc[...] = jnp.zeros_like(l_acc)
     o_acc[...] = jnp.zeros_like(o_acc)
     ids_q = idr_ref[pl.ds(i, 1)][0]
+    here = pl.multiple_of(place(i, me, per_chunk) * BLOCK, BLOCK)
 
     def step(j, carry):
         at = pl.multiple_of(place(j, me, per_chunk) * BLOCK, BLOCK)
         same = idc_ref[pl.ds(pl.multiple_of(j * BLOCK, BLOCK), BLOCK), :] == ids_q
         for p in range(pairs):
-            cols = slice(p * 128, (p + 1) * 128)
-            k_pair, v_pair, q_pair = k_ref[pl.ds(at, BLOCK), cols], v_ref[pl.ds(at, BLOCK), cols], q_ref[:, cols]
+            q_pair = qkv_ref[pl.ds(here, BLOCK), (3 * p) * 128 : (3 * p + 1) * 128]
+            k_pair = qkv_ref[pl.ds(at, BLOCK), (3 * p + 1) * 128 : (3 * p + 2) * 128]
+            v_pair = qkv_ref[pl.ds(at, BLOCK), (3 * p + 2) * 128 : (3 * p + 3) * 128]
             for w in range(2):
                 h = 2 * p + w
                 t = jnp.where(same, nt(k_pair, head_only(q_pair, w)) * SCALE_LOG2, MASKED)
@@ -87,9 +87,7 @@
             num_scalar_prefetch=1,
             grid=(blocks,),
             in_specs=[
-                pl.BlockSpec((BLOCK, width), lambda i, info: (place(i, info[2, 0], per_chunk), 0)),
-                pl.BlockSpec((rows, width), lambda i, info: (0, 1)),
-                pl.BlockSpec((rows, width), lambda i, info: (0, 2)),
+                pl.BlockSpec((rows, 3 * width), lambda i, info: (0, 0)),
                 pl.BlockSpec((rows, 1), lambda i, info: (0, 0)),
                 pl.BlockSpec((blocks, 1, BLOCK), lambda i, info: (0, 0, 0)),
             ],
@@ -107,18 +105,18 @@
             jax.ShapeDtypeStruct((rows, width), bf16),
             jax.ShapeDtypeStruct((blocks, heads, BLOCK), f32),
         ],
+        cost_estimate=pl.CostEstimate(flops=30 * 10**9, bytes_accessed=6 * rows * width, transcendentals=10**7),
         name="attention_forward",
-    )(info, qkv, qkv, qkv, ids_col, ids_row)
+    )(info, qkv, ids_col, ids_row)
 
 
 def backward_kernel(
-    per_chunk, pairs, info, q_ref, k_ref, v_ref, do_ref, o_ref, lse_ref, idc_ref, idr_ref,
+    per_chunk, first, info, q_ref, k_ref, v_ref, do_ref, o_ref, lse_ref, idc_ref, idr_ref,
     out_ref, delta_ref, dq_acc, dk_acc, dv_acc,
 ):
     j = pl.program_id(0)
     blocks = pl.num_programs(0)
     me = info[2, 0]
-    width = 128 * pairs
 
     @pl.when(j == 0)
     def _():
@@ -126,14 +124,9 @@
 
         def fill(i, carry):
             at = pl.multiple_of(place(i, me, per_chunk) * BLOCK, BLOCK)
-            for p in range(pairs):
-                cols = slice(p * 128, (p + 1) * 128)
-                prod = (do_ref[pl.ds(at, BLOCK), cols].astype(f32) * o_ref[pl.ds(at, BLOCK), cols].astype(f32)).T
-                for w in range(2):
-                    h = 2 * p + w
-                    delta_ref[i, h : h + 1, :] = jnp.sum(
-                        prod[w * HEAD_DIM : (w + 1) * HEAD_DIM], axis=0, keepdims=True
-                    )
+            prod = (do_ref[pl.ds(at, BLOCK), :].astype(f32) * o_ref[pl.ds(at, BLOCK), :].astype(f32)).T
+            for w in range(2):
+                delta_ref[i, w : w + 1, :] = jnp.sum(prod[w * HEAD_DIM : (w + 1) * HEAD_DIM], axis=0, keepdims=True)
             return carry
 
         lax.fori_loop(0, blocks, fill, 0)
@@ -145,58 +138,60 @@
     def step(i, carry):
         at = pl.multiple_of(place(i, me, per_chunk) * BLOCK, BLOCK)
         same = ids_k == idr_ref[pl.ds(i, 1)][0]
-        for p in range(pairs):
-            cols = slice(p * 128, (p + 1) * 128)
-            k_pair, v_pair = k_ref[:, cols], v_ref[:, cols]
-            q_pair, do_pair = q_ref[pl.ds(at, BLOCK), cols], do_ref[pl.ds(at, BLOCK), cols]
-            for w in range(2):
-                h = 2 * p + w
-                q_one, do_one = head_only(q_pair, w), head_only(do_pair, w)
-                t = nt(k_pair, q_one) * SCALE_LOG2 - lse_ref[i, h : h + 1, :]
-                e = jnp.exp2(jnp.where(same, t, MASKED))
-                ds = (e * (nt(v_pair, do_one) - delta_ref[i, h : h + 1, :])).astype(bf16)
-                dv_acc[:, cols] += nn(e.astype(bf16), do_one)
-                dk_acc[:, cols] += nn(ds, q_one)
-                dq_acc[pl.ds(at, BLOCK), cols] += tn(ds, head_only(k_pair, w))
+        k_pair, v_pair = k_ref[...], v_ref[...]
+        q_pair, do_pair = q_ref[pl.ds(at, BLOCK), :], do_ref[pl.ds(at, BLOCK), :]
+        dv, dk, dq = [], [], []
+        for w in range(2):
+            q_one, do_one = head_only(q_pair, w), head_only(do_pair, w)
+            t = nt(k_pair, q_one) * SCALE_LOG2 - lse_ref[i, first + w : first + w + 1, :]
+            e = jnp.exp2(jnp.where(same, t, MASKED))
+            ds = (e * (nt(v_pair, do_one) - delta_ref[i, w : w + 1, :])).astype(bf16)
+            dv.append(nn(e.astype(bf16), do_one))
+            dk.append(nn(ds, q_one))
+            dq.append(tn(ds, head_only(k_pair, w)))
+        dv_acc[...] += dv[0] + dv[1]
+        dk_acc[...] += dk[0] + dk[1]
+        dq_acc[pl.ds(at, BLOCK), :] += dq[0] + dq[1]
         return carry
 
     lax.fori_loop(info[0, j], info[1, j], step, 0)
     mine = pl.multiple_of(place(j, me, per_chunk) * BLOCK, BLOCK)
-    out_ref[pl.ds(mine, BLOCK), width : 2 * width] = (dk_acc[...] * SCALE).astype(bf16)
-    out_ref[pl.ds(mine, BLOCK), 2 * width : 3 * width] = dv_acc[...].astype(bf16)
+    out_ref[pl.ds(mine, BLOCK), 128:256] = (dk_acc[...] * SCALE).astype(bf16)
+    out_ref[pl.ds(mine, BLOCK), 256:384] = dv_acc[...].astype(bf16)
 
     @pl.when(j == blocks - 1)
     def _():
-        out_ref[:, 0:width] = (dq_acc[...] * SCALE).astype(bf16)
-
-
-def attention_backward(info, qkv, do, o, lse, ids_col, ids_row, per_chunk):
+        out_ref[:, 0:128] = (dq_acc[...] * SCALE).astype(bf16)
+
+
+def attention_backward(pair, info, qkv, do, o, lse, ids_col, ids_row, per_chunk):
     rows, width = o.shape
     blocks, heads = rows // BLOCK, width // HEAD_DIM
     return pl.pallas_call(
-        functools.partial(backward_kernel, per_chunk, heads // 2),
+        functools.partial(backward_kernel, per_chunk, 2 * pair),
         grid_spec=pltpu.PrefetchScalarGridSpec(
             num_scalar_prefetch=1,
             grid=(blocks,),
             in_specs=[
-                pl.BlockSpec((rows, width), lambda i, info: (0, 0)),
-                pl.BlockSpec((BLOCK, width), lambda i, info: (place(i, info[2, 0], per_chunk), 1)),
-                pl.BlockSpec((BLOCK, width), lambda i, info: (place(i, info[2, 0], per_chunk), 2)),
-                pl.BlockSpec((rows, width), lambda i, info: (0, 0)),
-                pl.BlockSpec((rows, width), lambda i, info: (0, 0)),
+                pl.BlockSpec((rows, 128), lambda i, info: (0, 3 * pair)),
+                pl.BlockSpec((BLOCK, 128), lambda i, info: (place(i, info[2, 0], per_chunk), 3 * pair + 1)),
+                pl.BlockSpec((BLOCK, 128), lambda i, info: (place(i, info[2, 0], per_chunk), 3 * pair + 2)),
+                pl.BlockSpec((rows, 128), lambda i, info: (0, pair)),
+                pl.BlockSpec((rows, 128), lambda i, info: (0, pair)),
                 pl.BlockSpec((blocks, heads, BLOCK), lambda i, info: (0, 0, 0)),
                 pl.BlockSpec((rows, 1), lambda i, info: (0, 0)),
                 pl.BlockSpec((blocks, 1, BLOCK), lambda i, info: (0, 0, 0)),
             ],
-            out_specs=pl.BlockSpec((rows, 3 * width), lambda i, info: (0, 0)),
+            out_specs=pl.BlockSpec((rows, 384), lambda i, info: (0, 0)),
             scratch_shapes=[
-                pltpu.VMEM((blocks, heads, BLOCK), f32),
-                pltpu.VMEM((rows, width), f32),
-                pltpu.VMEM((BLOCK, width), f32),
-                pltpu.VMEM((BLOCK, width), f32),
+                pltpu.VMEM((blocks, 2, BLOCK), f32),
+                pltpu.VMEM((rows, 128), f32),
+                pltpu.VMEM((BLOCK, 128), f32),
+                pltpu.VMEM((BLOCK, 128), f32),
             ],
         ),
-        out_shape=jax.ShapeDtypeStruct((rows, 3 * width), bf16),
+        out_shape=jax.ShapeDtypeStruct((rows, 384), bf16),
+        cost_estimate=pl.CostEstimate(flops=25 * 10**9, bytes_accessed=8 * rows * 128, transcendentals=10**7),
         name="attention_backward",
     )(info, qkv, qkv, qkv, do, o, lse, ids_col, ids_row)
 
@@ -206,7 +201,11 @@
     per_block = ids.reshape(blocks, BLOCK)
     low = jnp.sum(ids[None, :] < per_block[:, :1], axis=1) // BLOCK
     high = (jnp.sum(ids[None, :] <= per_block[:, -1:], axis=1) + BLOCK - 1) // BLOCK
-    return jnp.stack([low, high, jnp.full((blocks,), me)]).astype(jnp.int32)
+    return jnp.stack([low, high, jnp.full((blocks,), me.astype(low.dtype))]).astype(jnp.int32)
+
+
+def own_index(axis):
+    return lax.axis_index(axis).astype(jnp.uint32)
 
 
 def swap(value, axis, mask):
@@ -233,7 +232,7 @@
 
 def flipped(index, size):
     flags = bits(size)
-    return sum(lax.bitwise_and(index // bit, 1) * mirror for bit, mirror in zip(flags, reversed(flags)))
+    return sum(((index >> n) & 1) << (len(flags) - 1 - n) for n in range(len(flags)))
 
 
 def trade(pieces, axis):
@@ -242,20 +241,46 @@
 
 def to_absolute(pieces, me):
     stacked = jnp.stack(pieces)
-    return [lax.dynamic_index_in_dim(stacked, lax.bitwise_xor(me, c), 0, False) for c in range(len(pieces))]
-
-
-def halve(value, axis, dtype):
-    me, size = lax.axis_index(axis), lax.axis_size(axis)
-    count = size
-    for bit in bits(size):
-        value = value.reshape((count // 2, 2) + value.shape[1:])
-        mine = lax.rem(me // bit, 2)
-        give = lax.dynamic_index_in_dim(value, 1 - mine, 1, False).astype(dtype)
-        keep = lax.dynamic_index_in_dim(value, mine, 1, False)
-        value = keep + swap(give, axis, bit).astype(f32)
-        count //= 2
-    return value[0]
+    return [lax.dynamic_index_in_dim(stacked, (me ^ c), 0, False) for c in range(len(pieces))]
+
+
+class Halving:
+    def __init__(self, names, shape):
+        self.me = {n: (own_index(n[0]) >> (n[1].bit_length() - 1)) & 1 for n in names}
+        self.names, self.terms, self.fixed, self.shape = list(names), [], {}, shape
+
+    def cut(self, term, chosen):
+        array, names, part = term
+        starts, sizes = [], []
+        for n in names:
+            starts.append(chosen.get(n, jnp.uint32(0)))
+            sizes.append(1 if n in chosen else 2)
+        for low, high in part:
+            starts.append(jnp.uint32(low))
+            sizes.append(high - low)
+        left = [2 for n in names if n not in chosen]
+        return lax.dynamic_slice(array, starts, sizes).reshape(left + [h - l for l, h in part])
+
+    def total(self, chosen):
+        groups = []
+        for group in self.terms:
+            pieces = [self.cut(t, chosen).astype(f32) for t in group]
+            groups.append(pieces[0] if len(pieces) == 1 else jnp.concatenate(pieces, axis=-1))
+        return sum(groups[1:], groups[0])
+
+    def outgoing(self, name):
+        return self.total({**self.fixed, name: 1 - self.me[name]}).astype(bf16)
+
+    def arrived(self, name, value):
+        self.fixed[name] = self.me[name]
+        names = [n for n in self.names if n not in self.fixed]
+        self.terms.append([(value, names, [(0, d) for d in self.shape])])
+
+    def exchange(self, name):
+        self.arrived(name, swap(self.outgoing(name), *name))
+
+    def result(self):
+        return self.total(self.fixed)
 
 
 def normalize(values, gain, shift):
@@ -279,7 +304,7 @@
     value_weight, value_bias, output_weight, output_bias, mixing_gain, mixing_bias, up_weight, up_bias,
     down_weight, down_bias, final_gain, final_bias,
 ):
-    me_dp, me = lax.axis_index("dp"), lax.axis_index("ctx")
+    me_dp, me = own_index("dp"), own_index("ctx")
     dp, ctx = lax.axis_size("dp"), lax.axis_size("ctx")
     devices = dp * ctx
     piece, width = tokens.shape[1], tokens.shape[2]
@@ -301,16 +326,18 @@
     small = jnp.pad(small, ((0, 0), (0, 128 - small.shape[1])))
     pieces = []
     for k in range(ctx):
-        at = lax.bitwise_xor(me, k) * cols
+        at = (me ^ k) * cols
         parts = [
-            lax.dynamic_slice_in_dim(w, at, cols, 1) for w in (query_weight, key_weight, value_weight, time_weight)
-        ]
+            lax.dynamic_slice_in_dim(w, at + p * 128, 128, 1)
+            for p in range(cols // 128)
+            for w in (query_weight, key_weight, value_weight)
+        ] + [lax.dynamic_slice_in_dim(time_weight, at, cols, 1)]
         pieces.append(jnp.concatenate(parts + [small], axis=1))
     first = jnp.concatenate(to_absolute(trade(pieces, "ctx"), me))
     first = gather_stacked(first[None], "dp")
     first = jnp.concatenate(
         [
-            lax.dynamic_index_in_dim(first, flipped(lax.bitwise_xor(me_dp, c), dp), 0, False)
+            lax.dynamic_index_in_dim(first, flipped((me_dp ^ c), dp), 0, False)
             for c in range(dp)
         ]
     )
@@ -322,13 +349,13 @@
     up_shift = table[len(vectors) : len(vectors) + ratio].reshape(ratio, devices, own).transpose(1, 0, 2).reshape(hidden)
     shift_cols = trade([nn(time_feat, first[:, 3 * cols : 4 * cols])] * ctx, "ctx")
     time_shift = jnp.concatenate(to_absolute(shift_cols, me), axis=1) + time_shift_bias
-    qkv_shift = jnp.concatenate(
-        [
-            lax.dynamic_slice_in_dim(query_shift, me * cols, cols),
-            jnp.zeros((cols,), f32),
-            lax.dynamic_slice_in_dim(value_shift, me * cols, cols),
-        ]
-    )
+    qkv_shift = []
+    for p in range(cols // 128):
+        at = me * cols + p * 128
+        qkv_shift.append(lax.dynamic_slice_in_dim(query_shift, at, 128))
+        qkv_shift.append(jnp.zeros((128,), f32))
+        qkv_shift.append(lax.dynamic_slice_in_dim(value_shift, at, 128))
+    qkv_shift = jnp.concatenate(qkv_shift)
     start_row = (jnp.concatenate(token_chunks).astype(f32) + time_shift).astype(bf16)
     residual_in = tokens.astype(f32) + time_shift
     qkv = (nn(start_row, qkv_weight) + qkv_shift).astype(bf16)
@@ -364,33 +391,61 @@
     grad_branch = grad_one.astype(bf16)
     output_grad = tn(attended, grad_branch).astype(bf16)
     output_shift_grad = jnp.sum(grad_branch.astype(f32), axis=0)
-    down_blocks = down_grad.reshape(devices, ratio, own, width)
     vector_grads = jnp.stack(
         [output_shift_grad, gain_one_grad, bias_one_grad, down_shift_grad, gain_two_grad, bias_two_grad]
     )
     up_shift_grad = up_shift_grad.reshape(devices, ratio, own).transpose(1, 0, 2).reshape(ratio, width)
     vector_grads = jnp.concatenate([vector_grads, up_shift_grad])
     vector_grads = jnp.pad(vector_grads, ((0, 128 - vector_grads.shape[0]), (0, 0))).T.astype(bf16)
-    packed = jnp.concatenate(
-        [up_grad] + [down_blocks[:, n].reshape(width, width) for n in range(ratio)] + [output_grad, vector_grads],
-        axis=1,
-    )
-    packed = lax.psum_scatter(packed, BOTH, scatter_dimension=0, tiled=True).astype(f32)
-    up_weight_grad = packed[:, :hidden]
-    down_weight_grad = jnp.concatenate(
-        [packed[:, hidden + n * width : hidden + (n + 1) * width] for n in range(ratio)], axis=0
-    )
-    output_weight_grad = packed[:, 2 * hidden : 2 * hidden + width]
-    vector_grads = packed[:, 2 * hidden + width :].T
-    output_bias_grad, mixing_gain_grad, mixing_bias_grad, down_bias_grad, final_gain_grad, final_bias_grad = [
-        vector_grads[n] for n in range(6)
+    rest_grad = jnp.concatenate([output_grad, vector_grads], axis=1)
+
+    dp_names, ctx_names = [("dp", b) for b in bits(dp)], [("ctx", b) for b in bits(ctx)]
+    names = dp_names[::-1] + ctx_names[::-1]
+    core, turn, rest = ctx_names[0], dp_names[:2] + ctx_names[1:], dp_names[2:]
+    whole = {}
+    for label, array, height in (("down", down_grad, ratio * own), ("up", up_grad, own), ("rest", rest_grad, own)):
+        size = (height, array.shape[1])
+        sums = Halving(names, size)
+        sums.terms = [[(array.reshape([2] * len(names) + list(size)), names, [(0, d) for d in size])]]
+        sums.exchange(core)
+        whole[label] = [term[0] for term in sums.terms]
+
+    def stream(parts, shape):
+        sums = Halving(names, shape)
+        sums.fixed = {core: sums.me[core]}
+        sums.terms = [[(whole[l][n][0], whole[l][n][1], part) for l, part in parts] for n in range(2)]
+        return sums
+
+    most = 3 * hidden // 4
+    streams = [
+        stream([("up", [(0, own), (0, most)])], (own, most)),
+        stream([("down", [(0, (ratio - 1) * own), (0, width)])], ((ratio - 1) * own, width)),
+        stream(
+            [
+                ("up", [(0, own), (most, hidden)]),
+                ("down", [((ratio - 1) * own, ratio * own), (0, width)]),
+                ("rest", [(0, own), (0, width + 128)]),
+            ],
+            (own, hidden - most + 2 * width + 128),
+        ),
     ]
-    up_bias_grad = vector_grads[6 : 6 + ratio].reshape(ratio * own)
+    order = [turn[2:] + turn[:2], turn, turn[1:] + turn[:1]]
 
     grad_attended = nt(grad_branch, output_full).astype(bf16)
-    pieces = [lax.dynamic_slice_in_dim(grad_attended, lax.bitwise_xor(me, k) * cols, cols, 1) for k in range(ctx)]
+    pieces = [lax.dynamic_slice_in_dim(grad_attended, (me ^ k) * cols, cols, 1) for k in range(ctx)]
     grad_mixed = jnp.concatenate(trade(pieces, "ctx"))
-    grad_qkv = attention_backward(info, qkv, grad_mixed, mixed, logsum, ids_col, ids_row, per_chunk)
+    grads = []
+    for stage in range(len(turn)):
+        going = [s.outgoing(o[stage]) for s, o in zip(streams, order)]
+        grad_mixed, grads, going = lax.optimization_barrier((grad_mixed, grads, going))
+        for s, o, value in zip(streams, order, going):
+            s.arrived(o[stage], swap(value, *o[stage]))
+        if stage < cols // 128:
+            grads.append(
+                attention_backward(stage, info, qkv, grad_mixed, mixed, logsum, ids_col, ids_row, per_chunk)
+            )
+            grad_mixed, grads[-1] = lax.optimization_barrier((grad_mixed, grads[-1]))
+    grad_qkv = jnp.concatenate(grads, axis=1)
 
     partial = {}
     for k in reversed(range(ctx)):
@@ -400,8 +455,22 @@
             partial[k ^ bit] = partial[k ^ bit] + swap(partial.pop(k).astype(bf16), "ctx", bit).astype(f32)
     tokens_grad = (grad_one + partial[0]).astype(bf16)
 
+    for s, o in zip(streams, order):
+        for name in rest:
+            s.exchange(name)
+    up_left, down_left, mixed_left = [s.result() for s in streams]
+    up_weight_grad = jnp.concatenate([up_left, mixed_left[:, : hidden - most]], axis=1)
+    mixed_left = mixed_left[:, hidden - most :]
+    down_weight_grad = jnp.concatenate([down_left, mixed_left[:, :width]])
+    output_weight_grad = mixed_left[:, width : 2 * width]
+    vector_grads = mixed_left[:, 2 * width :].T
+    output_bias_grad, mixing_gain_grad, mixing_bias_grad, down_bias_grad, final_gain_grad, final_bias_grad = [
+        vector_grads[n] for n in range(6)
+    ]
+    up_bias_grad = vector_grads[6 : 6 + ratio].reshape(ratio * own)
+
+    qkv_sum = jnp.sum(grad_qkv.astype(f32), axis=0)
     qkv_grad = tn(start_row, grad_qkv)
-    qkv_sum = jnp.sum(grad_qkv.astype(f32), axis=0)
     row_sum = jnp.sum(grad_one, axis=0, keepdims=True) + lax.dot_general(
         qkv_sum[None],
         qkv_weight.astype(f32),
@@ -410,7 +479,10 @@
         preferred_element_type=f32,
     )
     message = jnp.concatenate(
-        [row_sum, qkv_sum[None, :cols], qkv_sum[None, 2 * cols :], time_feat.astype(f32)], axis=1
+        [row_sum]
+        + [qkv_sum[None, (3 * p + n) * 128 : (3 * p + n + 1) * 128] for n in (0, 2) for p in range(cols // 128)]
+        + [time_feat.astype(f32)],
+        axis=1,
     )
     message = gather_stacked(gather_stacked(message, "dp"), "ctx").reshape(ctx, dp, -1)
     mine = (me_dp * ctx + me) * own
@@ -424,18 +496,32 @@
     )
     time_bias_grad = lax.dynamic_slice_in_dim(jnp.sum(row_sums, axis=0), mine, own)
     sums = jnp.sum(message[:, :, width : width + 2 * cols], axis=1)
-    sums = lax.dynamic_index_in_dim(sums, flipped(lax.bitwise_xor(mine // cols, me), ctx), 0, False)
-    query_bias_grad = lax.dynamic_slice_in_dim(sums[:cols], lax.rem(mine, cols), own)
-    value_bias_grad = lax.dynamic_slice_in_dim(sums[cols:], lax.rem(mine, cols), own)
-
-    summed = halve(qkv_grad.reshape(dp, ctx * own, 3 * cols), "dp", bf16).reshape(ctx, own, 3 * cols)
+    sums = lax.dynamic_index_in_dim(sums, flipped((mine // cols ^ me), ctx), 0, False)
+    query_bias_grad = lax.dynamic_slice_in_dim(sums[:cols], mine % cols, own)
+    value_bias_grad = lax.dynamic_slice_in_dim(sums[cols:], mine % cols, own)
+
+    size = (ctx * own, 3 * cols)
+    summed = Halving(dp_names[::-1], size)
+    summed.terms = [
+        [(qkv_grad.reshape([2] * len(dp_names) + list(size)), dp_names[::-1], [(0, d) for d in size])]
+    ]
+    for name in dp_names:
+        summed.exchange(name)
+    summed = summed.result().reshape(ctx, own, 3 * cols)
     blocks_out = to_absolute(
-        trade([lax.dynamic_index_in_dim(summed, lax.bitwise_xor(me, k), 0, False) for k in range(ctx)], "ctx"), me
+        trade([lax.dynamic_index_in_dim(summed, (me ^ k), 0, False) for k in range(ctx)], "ctx"), me
     )
     query_weight_grad, key_weight_grad, value_weight_grad = [
-        jnp.concatenate([block[:, n * cols : (n + 1) * cols] for block in blocks_out], axis=1) for n in range(3)
+        jnp.concatenate(
+            [
+                block[:, (3 * p + n) * 128 : (3 * p + n + 1) * 128]
+                for block in blocks_out
+                for p in range(cols // 128)
+            ],
+            axis=1,
+        )
+        for n in range(3)
     ]
-
     return (
         layer_out[None],
         tokens_grad[None],

time: 560 us -> 554 us (0.989)
  waiting for transfers between devices: 264 us -> 183 us
  other arithmetic: 21.3 us -> 56.5 us
  local copies, waits for them, and re-layouts: 38.4 us -> 63 us
  starting transfers between devices: 23.3 us -> 40.3 us
    ppermute x32 -> x47, waiting for transfers between devices: 252 us -> 183 us  [swap(): return lax.ppermute(value, axis, [(i, i ^ mask) for i in range(size)])]
    convert_element_type x2 -> x14, other arithmetic: 1.22 us -> 30.9 us  [outgoing(): return self.total({**self.fixed, name: 1 - self.me[name]}).astype(bf16)]
    convert_element_type x3 -> x22, local copies, waits for them, and re-layouts: 0.17 us -> 18.6 us  [the longest x20 17.6 us: total(): pieces = [self.cut(t, chosen).astype(f32) for t in group]]
    ppermute x32 -> x47, starting transfers between devices: 23.2 us -> 40.2 us  [swap(): return lax.ppermute(value, axis, [(i, i ^ mask) for i in range(size)])]
    reduce_scatter x1 -> x0, waiting for transfers between devices: 11.6 us -> none  [shards(): lax.psum_scatter(packed, BOTH, scatter_dimension=0, tiled=True).astype(f32)]
    reshape x0 -> x3, local copies, waits for them, and re-layouts: none -> 6.25 us  [cut(): lax.dynamic_slice(array, starts, sizes)]
    pallas_call x1 -> x2, Pallas kernels: 57.3 us -> 54.6 us  [attention_backward(): pl.pallas_call(functools.partial(backward_kernel, per_chunk, 2 * pair), g...]
    unnamed x59 -> x142, local copies, waits for them, and re-layouts: 18.8 us -> 16.7 us
  transfers between devices with their start and end apart: 35 -> 49, of which waited for: 23 -> 18; matrix products, arithmetic and copies ran while one was open for 12% -> 22% of each run, Pallas kernels for 20% -> 19%
where the time goes in v3:
time: 554 us; the launch traced here: 547 us
  waiting for transfers between devices  183 us (33%)
  Pallas kernels  103 us (19%)
  matrix products  85.3 us (15%)
  local copies, waits for them, and re-layouts  63 us (11%)
  other arithmetic  56.5 us (10%)
  starting transfers between devices  40.3 us (7%)
  between operations  15.9 us (3%)
    ppermute x47, waiting for transfers between devices, swap(): return lax.ppermute(value, axis, [(i, i ^ mask) for i in range(size)])  183 us
    pallas_call x2, Pallas kernels, attention_backward(): pl.pallas_call(functools.partial(backward_kernel, per_chunk, 2 * pair), g...  54.6 us
    pallas_call x1, Pallas kernels, attention_forward(): pl.pallas_call(functools.partial(forward_kernel, per_chunk, heads // 2),...  48.4 us
    ppermute x47, starting transfers between devices, swap(): return lax.ppermute(value, axis, [(i, i ^ mask) for i in range(size)])  40.2 us
    dot_general x7, matrix products, nt(): lax.dot_general(left, right, (((1,), (1,)), ((), ())), preferred_element_...  31 us
    convert_element_type x14, other arithmetic, outgoing(): return self.total({**self.fixed, name: 1 - self.me[name]}).astype(bf16)  30.9 us
    dot_general x5, matrix products, nn(): return jnp.dot(left, right, preferred_element_type=f32)  29.5 us
    dot_general x4, matrix products, tn(): lax.dot_general(left, right, (((0,), (0,)), ((), ())), preferred_element_...  23.1 us
  transfers between devices with their start and end apart: 49, of which 18 were waited for; matrix products, arithmetic and copies ran while one was open for 22% of the time, Pallas kernels for 19%

profile of v3, /device:TPU:0, one launch (start us, length us, event | category | flops | bytes accessed | tf_op | source)
XLA Modules:
  0.0 546.7 jit_solution(16818402997389312813)
XLA Ops:
  27.2 19.2 %collective-permute-done.3 = bf16[1,128,1152]{2,1,0:T(8,128)(2,1)S(1)} collective-permute-done((bf16[1,128,1152]{2,1,0:T(8,128)(2,1)S(1)}, bf16[1,128,1152]{2,1,0:T(8,128)(2,1)S(1)}, u32[]{:S(2)}, u32[]{:S(2)}) %collective-permute-start.3) | collective-permute-done | bytes 294944 | tf_op jit(solution)/shard_map/ppermute | solution.py:213
  46.5 29.1 %collective-permute-done.4 = bf16[2,128,1152]{2,1,0:T(8,128)(2,1)S(1)} collective-permute-done((bf16[2,128,1152]{2,1,0:T(8,128)(2,1)S(1)}, bf16[2,128,1152]{2,1,0:T(8,128)(2,1)S(1)}, u32[]{:S(2)}, u32[]{:S(2)}) %collective-permute-start.4) | collective-permute-done | bytes 589856 | tf_op jit(solution)/shard_map/ppermute | solution.py:213
  87.3 33.2 %collective-permute-done.10 = bf16[512,1024]{1,0:T(8,128)(2,1)} collective-permute-done((bf16[512,1024]{1,0:T(8,128)(2,1)}, bf16[512,1024]{1,0:T(8,128)(2,1)}, u32[]{:S(2)}, u32[]{:S(2)}) %collective-permute-start.10) | collective-permute-done | bytes 1048608 | tf_op jit(solution)/shard_map/ppermute | solution.py:213
  129.5 7.1 %add_convert_fusion.1.qkv_ref.q_ref.k_ref.v_ref = bf16[2048,768]{1,0:T(8,128)(2,1)} fusion(f32[768]{0:T(1024)S(1)} %constant_dynamic-update-slice_fusion.66, bf16[1024,1152]{0,1:T(8,128)(2,1)S(1)} %bitcast_dynamic-update-slice_fusion, bf16[512,1024]{1,0:T(8,128)(2,1)} %collective-permute-done.11, bf16[512,1024]{1,0:T(8,128)(2,1)} %collective-permute-done.10, ...), kind=kOutput, calls=%fused_computation.17 | convolution fusion | flops 3245342720 | bytes 8921088 | tf_op jit(solution)/shard_map/dot_general | solution.py:21
  136.6 48.4 %attention_forward.1 = (bf16[2048,256]{1,0:T(8,128)(2,1)}, f32[8,4,256]{2,1,0:T(4,128)}) custom-call(s32[3,8]{1,0:T(4,128)} %add_add_fusion.2.info, bf16[2048,768]{1,0:T(8,128)(2,1)} %add_convert_fusion.1.qkv_ref.q_ref.k_ref.v_ref, s32[2048,1]{1,0:T(8,128)} %copy.157.idc_ref, s32[8,1,256]{2,1,0:T(1,128)} %bitcast.489), custom_call_target="tpu_custom_call" | custom-call | flops 30000001024 | bytes 3145728 | tf_op jit(solution)/shard_map/attention_forward/pallas_call | solution.py:84
  188.9 11.7 %collective-permute-done.14 = bf16[512,256]{1,0:T(8,128)(2,1)S(1)} collective-permute-done((bf16[512,256]{1,0:T(8,128)(2,1)S(1)}, bf16[512,256]{1,0:T(8,128)(2,1)S(1)}, u32[]{:S(2)}, u32[]{:S(2)}) %collective-permute-start.14) | collective-permute-done | bytes 262176 | tf_op jit(solution)/shard_map/ppermute | solution.py:213
  200.6 11.2 %collective-permute-done.13 = bf16[512,256]{1,0:T(8,128)(2,1)S(1)} collective-permute-done((bf16[512,256]{1,0:T(8,128)(2,1)S(1)}, bf16[512,256]{1,0:T(8,128)(2,1)S(1)}, u32[]{:S(2)}, u32[]{:S(2)}) %collective-permute-start.13) | collective-permute-done | bytes 262176 | tf_op jit(solution)/shard_map/ppermute | solution.py:213
  218.9 10.1 %fusion.4 = (bf16[512,4096]{1,0:T(8,128)(2,1)}, bf16[512,4096]{1,0:T(8,128)(2,1)}) fusion(f32[4096]{0:T(1024)S(1)} %add.431, bf16[1024,5120]{1,0:T(8,128)(2,1)S(1)} %copy-done.42, f32[512,1024]{1,0:T(8,128)S(1)} %get-tuple-element.206, f32[1024]{0:T(1024)S(1)} %bitcast.511, f32[1024]{0:T(1024)S(1)} %bitcast.499, f32[512]{0:T(512)S(1)} %add_rsqrt_fusion.1, ...), kind=kOutput, calls=%fused_computation.5 | convolution fusion | flops 4322754560 | bytes 18903040 | tf_op jit(solution)/shard_map/dot_general | solution.py:21
  229.0 8.4 %fusion.95 = (f32[512]{0:T(512)S(1)}, f32[512,1024]{1,0:T(8,128)S(1)}) fusion(f32[1024]{0:T(1024)S(1)} %bitcast.514, bf16[512,4096]{1,0:T(8,128)(2,1)} %get-tuple-element.41, bf16[4096,1024]{1,0:T(8,128)(2,1)} %all-gather.5.cloned.1.call-done, f32[1024]{0:T(1024)S(1)} %bitcast.512, f32[1024]{0:T(1024)S(1)} %bitcast.500, f32[512]{0:T(512)S(1)} %add_rsqrt_fusion.1, ...), kind=kOutput, calls=%fused_computation.387 | convolution fusion | flops 4298636800 | bytes 16795648 | tf_op jit(solution)/shard_map/dot_general | solution.py:21
  242.5 7.1 %convolution_convert_fusion = bf16[4096,1024]{1,0:T(8,128)(2,1)} fusion(bf16[512,4096]{1,0:T(8,128)(2,1)S(1)} %copy-done.48, f32[512,1024]{1,0:T(8,128)S(1)} %get-tuple-element.81), kind=kOutput, calls=%fused_computation.10 | convolution fusion | flops 4299685888 | bytes 14680064 | tf_op jit(solution)/shard_map/dot_general | solution.py:25
  249.7 9.6 %fusion.96 = (bf16[4096]{0:T(1024)(128)(2,1)S(1)}, bf16[512,4096]{1,0:T(8,128)(2,1)}) fusion(bf16[512,4096]{1,0:T(8,128)(2,1)S(1)} %copy-done.46, bf16[4096,1024]{1,0:T(8,128)(2,1)} %all-gather.5.cloned.1.call-done, f32[512,1024]{1,0:T(8,128)S(1)} %get-tuple-element.81), kind=kOutput, calls=%fused_computation.388 | convolution fusion | flops 4303876096 | bytes 18882560 | tf_op jit(solution)/shard_map/dot_general | solution.py:29
  259.6 9.4 %convolution_convert_fusion.1 = bf16[1024,4096]{1,0:T(8,128)(2,1)} fusion(bf16[512,4096]{1,0:T(8,128)(2,1)} %get-tuple-element.211, f32[512,1024]{1,0:T(8,128)S(1)} %get-tuple-element.206, f32[1024]{0:T(1024)S(1)} %bitcast.513, f32[1024]{0:T(1024)S(1)} %bitcast.501, f32[512]{0:T(512)S(1)} %add_rsqrt_fusion.1, f32[512]{0:T(512)S(1)} %broadcast_multiply_fusion.5), kind=kOutput, calls=%fused_computation.11 | convolution fusion | flops 4301783040 | bytes 14692352 | tf_op jit(solution)/shard_map/dot_general | solution.py:25
  269.0 8.1 %multiply_reduce_fusion = (bf16[1024]{0:T(1024)(128)(2,1)S(1)}, f32[512]{0:T(512)S(1)}, f32[512]{0:T(512)S(1)}, bf16[1024]{0:T(1024)(128)(2,1)S(1)}, f32[512,1024]{1,0:T(8,128)S(1)}) fusion(f32[512,1024]{1,0:T(8,128)S(1)} %get-tuple-element.206, f32[512]{0:T(512)S(1)} %add_rsqrt_fusion.1, f32[512]{0:T(512)S(1)} %broadcast_multiply_fusion.5, ...), kind=kOutput, calls=%fused_computation.38 | convolution fusion | flops 4300207104 | bytes 18890752 | tf_op jit(solution)/shard_map/dot_general | solution.py:29
  294.6 4.3 copy.162
  318.1 3.8 fusion.9
  324.6 27.2 %attention_backward.2 = bf16[2048,384]{1,0:T(8,128)(2,1)} custom-call(s32[3,8]{1,0:T(4,128)} %add_add_fusion.2.info, bf16[2048,768]{1,0:T(8,128)(2,1)} %add_convert_fusion.1.qkv_ref.q_ref.k_ref.v_ref, bf16[2048,768]{1,0:T(8,128)(2,1)} %add_convert_fusion.1.qkv_ref.q_ref.k_ref.v_ref, bf16[2048,768]{1,0:T(8,128)(2,1)} %add_convert_fusion.1.qkv_ref.q_ref.k_ref.v_ref, ...), custom_call_target="tpu_custom_call" | custom-call | flops 24999999488 | bytes 2097152 | tf_op jit(solution)/shard_map/attention_backward/pallas_call | solution.py:170
  372.3 27.4 %attention_backward.3 = bf16[2048,384]{1,0:T(8,128)(2,1)} custom-call(s32[3,8]{1,0:T(4,128)} %add_add_fusion.2.info, bf16[2048,768]{1,0:T(8,128)(2,1)} %add_convert_fusion.1.qkv_ref.q_ref.k_ref.v_ref, bf16[2048,768]{1,0:T(8,128)(2,1)} %add_convert_fusion.1.qkv_ref.q_ref.k_ref.v_ref, bf16[2048,768]{1,0:T(8,128)(2,1)} %add_convert_fusion.1.qkv_ref.q_ref.k_ref.v_ref, ...), custom_call_target="tpu_custom_call" | custom-call | flops 24999999488 | bytes 2097152 | tf_op jit(solution)/shard_map/attention_backward/pallas_call | solution.py:170
  413.4 5.2 fusion.66
  432.6 5.2 collective-permute-done.33
  454.1 10.9 %collective-permute-done.44 = bf16[32,3072]{1,0:T(8,128)(2,1)S(1)} collective-permute-done((bf16[32,3072]{1,0:T(8,128)(2,1)S(1)}, bf16[32,3072]{1,0:T(8,128)(2,1)S(1)}, u32[]{:S(2)}, u32[]{:S(2)}) %collective-permute-start.44) | collective-permute-done | bytes 196640 | tf_op jit(solution)/shard_map/ppermute | solution.py:213
  466.4 7.2 %collective-permute-done.46 = bf16[96,1024]{1,0:T(8,128)(2,1)S(1)} collective-permute-done((bf16[96,1024]{1,0:T(8,128)(2,1)S(1)}, bf16[96,1024]{1,0:T(8,128)(2,1)S(1)}, u32[]{:S(2)}, u32[]{:S(2)}) %collective-permute-start.46) | collective-permute-done | bytes 196640 | tf_op jit(solution)/shard_map/ppermute | solution.py:213
  483.0 10.2 %collective-permute-done.36 = bf16[2,128,768]{2,1,0:T(8,128)(2,1)S(1)} collective-permute-done((bf16[2,128,768]{2,1,0:T(8,128)(2,1)S(1)}, bf16[2,128,768]{2,1,0:T(8,128)(2,1)S(1)}, u32[]{:S(2)}, u32[]{:S(2)}) %collective-permute-start.36) | collective-permute-done | bytes 393248 | tf_op jit(solution)/shard_map/ppermute | solution.py:213
  496.0 9.5 %collective-permute-done.37 = bf16[128,768]{1,0:T(8,128)(2,1)S(1)} collective-permute-done((bf16[128,768]{1,0:T(8,128)(2,1)S(1)}, bf16[128,768]{1,0:T(8,128)(2,1)S(1)}, u32[]{:S(2)}, u32[]{:S(2)}) %collective-permute-start.37) | collective-permute-done | bytes 196640 | tf_op jit(solution)/shard_map/ppermute | solution.py:213
  514.2 22.3 %collective-permute-done.29 = bf16[512,1024]{1,0:T(8,128)(2,1)S(1)} collective-permute-done((bf16[512,1024]{1,0:T(8,128)(2,1)S(1)}, bf16[512,1024]{1,0:T(8,128)(2,1)S(1)}, u32[]{:S(2)}, u32[]{:S(2)}) %collective-permute-start.29) | collective-permute-done | bytes 1048608 | tf_op jit(solution)/shard_map/ppermute | solution.py:213
  (382 shorter events, 184.8 us)
Async XLA Ops:
  7.2 205.7 %all-gather.3.cloned.1.call-start = ((), (), s32[]{:S(2)}) async-start(), calls=%async_computation | async-start | bytes 10813440 | tf_op jit(solution)/shard_map/all_gather | solution.py:317
  9.0 220.0 %all-gather.5.cloned.1.call-start = ((), (), s32[]{:S(2)}) async-start(), calls=%async_computation.1 | async-start | bytes 8650752 | tf_op jit(solution)/shard_map/all_gather | solution.py:318
  24.4 21.9 %collective-permute-start.3 = (bf16[1,128,1152]{2,1,0:T(8,128)(2,1)S(1)}, bf16[1,128,1152]{2,1,0:T(8,128)(2,1)S(1)}, u32[]{:S(2)}, u32[]{:S(2)}) collective-permute-start(bf16[1,128,1152]{2,1,0:T(8,128)(2,1)S(1)} %maximum_bitcast_fusion), channel_id=1, source_target_pairs={{0,16},{4,20},{8,24},{12,28},{16,0},{20,4},{24,8},{28,12},{1,17},{... | collective-permute-start | bytes 884744 | tf_op jit(solution)/shard_map/ppermute | solution.py:213
  46.4 29.2 %collective-permute-start.4 = (bf16[2,128,1152]{2,1,0:T(8,128)(2,1)S(1)}, bf16[2,128,1152]{2,1,0:T(8,128)(2,1)S(1)}, u32[]{:S(2)}, u32[]{:S(2)}) collective-permute-start(bf16[2,128,1152]{2,1,0:T(8,128)(2,1)S(1)} %pad_maximum_fusion.6), channel_id=1, source_target_pairs={{0,8},{4,12},{8,0},{12,4},{16,24},{20,28},{24,16},{28,20},{1,9},{5... | collective-permute-start | bytes 1769480 | tf_op jit(solution)/shard_map/ppermute | solution.py:213
  75.8 45.5 %collective-permute-start.5 = (bf16[4,128,1152]{2,1,0:T(8,128)(2,1)S(1)}, bf16[4,128,1152]{2,1,0:T(8,128)(2,1)S(1)}, u32[]{:S(2)}, u32[]{:S(2)}) collective-permute-start(bf16[4,128,1152]{2,1,0:T(8,128)(2,1)S(1)} %pad_maximum_fusion.2), channel_id=1, source_target_pairs={{0,4},{4,0},{8,12},{12,8},{16,20},{20,16},{24,28},{28,24},{1,5},{5... | collective-permute-start | bytes 3538952 | tf_op jit(solution)/shard_map/ppermute | solution.py:213
  77.1 43.4 %collective-permute-start.10 = (bf16[512,1024]{1,0:T(8,128)(2,1)}, bf16[512,1024]{1,0:T(8,128)(2,1)}, u32[]{:S(2)}, u32[]{:S(2)}) collective-permute-start(bf16[512,1024]{1,0:T(8,128)(2,1)} %bitcast.531), channel_id=1, source_target_pairs={{0,2},{1,3},{2,0},{3,1},{4,6},{5,7},{6,4},{7,5},{8,10},{9,11},{10,... | collective-permute-start | bytes 3145736 | tf_op jit(solution)/shard_map/ppermute | solution.py:213
  79.1 50.4 %collective-permute-start.9 = (bf16[512,1024]{1,0:T(8,128)(2,1)}, bf16[512,1024]{1,0:T(8,128)(2,1)}, u32[]{:S(2)}, u32[]{:S(2)}) collective-permute-start(bf16[512,1024]{1,0:T(8,128)(2,1)} %bitcast.532), channel_id=1, source_target_pairs={{0,1},{1,0},{2,3},{3,2},{4,5},{5,4},{6,7},{7,6},{8,9},{9,8},{10,11... | collective-permute-start | bytes 3145736 | tf_op jit(solution)/shard_map/ppermute | solution.py:213
  187.0 24.9 %collective-permute-start.13 = (bf16[512,256]{1,0:T(8,128)(2,1)S(1)}, bf16[512,256]{1,0:T(8,128)(2,1)S(1)}, u32[]{:S(2)}, u32[]{:S(2)}) collective-permute-start(bf16[512,256]{1,0:T(8,128)(2,1)S(1)} %get-tuple-element.115), channel_id=1, source_target_pairs={{0,2},{1,3},{2,0},{3,1},{4,6},{5,7},{6,4},{7,5},{8,10},{9,11},{10,... | collective-permute-start | bytes 786440 | tf_op jit(solution)/shard_map/ppermute | solution.py:213
  188.5 23.4 %collective-permute-start.12 = (bf16[512,256]{1,0:T(8,128)(2,1)S(1)}, bf16[512,256]{1,0:T(8,128)(2,1)S(1)}, u32[]{:S(2)}, u32[]{:S(2)}) collective-permute-start(bf16[512,256]{1,0:T(8,128)(2,1)S(1)} %get-tuple-element.116), channel_id=1, source_target_pairs={{0,1},{1,0},{2,3},{3,2},{4,5},{5,4},{6,7},{7,6},{8,9},{9,8},{10,11... | collective-permute-start | bytes 786440 | tf_op jit(solution)/shard_map/ppermute | solution.py:213
  285.4 25.2 %collective-permute-start.18 = (bf16[2,2,2,2,32,4096]{5,4,3,2,1,0:T(8,128)(2,1)}, bf16[2,2,2,2,32,4096]{5,4,3,2,1,0:T(8,128)(2,1)}, u32[]{:S(2)}, u32[]{:S(2)}) collective-permute-start(bf16[2,2,2,2,32,4096]{5,4,3,2,1,0:T(8,128)(2,1)} %dynamic-slice_bitcast_fusion.1), channel_id=1, source_target_pairs={{0,1},{1,0},{2,3},{3,2},{4,5},{5,4},{6,7},{7,6},{8,9},{9,8},{10,11... | collective-permute-start | bytes 12582920 | tf_op jit(solution)/shard_map/ppermute | solution.py:213
  285.4 26.2 %collective-permute-start.19 = (bf16[2,2,2,2,128,1024]{5,4,3,2,1,0:T(8,128)(2,1)}, bf16[2,2,2,2,128,1024]{5,4,3,2,1,0:T(8,128)(2,1)}, u32[]{:S(2)}, u32[]{:S(2)}) collective-permute-start(bf16[2,2,2,2,128,1024]{5,4,3,2,1,0:T(8,128)(2,1)} %dynamic-slice_bitcast_fusion), channel_id=1, source_target_pairs={{0,1},{1,0},{2,3},{3,2},{4,5},{5,4},{6,7},{7,6},{8,9},{9,8},{10,11... | collective-permute-start | bytes 12582920 | tf_op jit(solution)/shard_map/ppermute | solution.py:213
  321.9 40.9 %collective-permute-start.21 = (bf16[2,2,2,32,3072]{4,3,2,1,0:T(8,128)(2,1)}, bf16[2,2,2,32,3072]{4,3,2,1,0:T(8,128)(2,1)}, u32[]{:S(2)}, u32[]{:S(2)}) collective-permute-start(bf16[2,2,2,32,3072]{4,3,2,1,0:T(8,128)(2,1)} %fusion.10), channel_id=1, source_target_pairs={{0,2},{1,3},{2,0},{3,1},{4,6},{5,7},{6,4},{7,5},{8,10},{9,11},{10,... | collective-permute-start | bytes 4718600 | tf_op jit(solution)/shard_map/ppermute | solution.py:213
  322.3 37.7 %collective-permute-start.22 = (bf16[2,2,2,96,1024]{4,3,2,1,0:T(8,128)(2,1)}, bf16[2,2,2,96,1024]{4,3,2,1,0:T(8,128)(2,1)}, u32[]{:S(2)}, u32[]{:S(2)}) collective-permute-start(bf16[2,2,2,96,1024]{4,3,2,1,0:T(8,128)(2,1)} %fusion.9), channel_id=1, source_target_pairs={{0,4},{4,0},{8,12},{12,8},{16,20},{20,16},{24,28},{28,24},{1,5},{5... | collective-permute-start | bytes 4718600 | tf_op jit(solution)/shard_map/ppermute | solution.py:213
  324.0 41.7 %collective-permute-start.23 = (bf16[2,2,2,32,3200]{4,3,2,1,0:T(8,128)(2,1)}, bf16[2,2,2,32,3200]{4,3,2,1,0:T(8,128)(2,1)}, u32[]{:S(2)}, u32[]{:S(2)}) collective-permute-start(bf16[2,2,2,32,3200]{4,3,2,1,0:T(8,128)(2,1)} %add_convert_fusion.2), channel_id=1, source_target_pairs={{0,8},{4,12},{8,0},{12,4},{16,24},{20,28},{24,16},{28,20},{1,9},{5... | collective-permute-start | bytes 4915208 | tf_op jit(solution)/shard_map/ppermute | solution.py:213
  368.2 34.1 %collective-permute-start.24 = (bf16[2,2,32,3072]{3,2,1,0:T(8,128)(2,1)}, bf16[2,2,32,3072]{3,2,1,0:T(8,128)(2,1)}, u32[]{:S(2)}, u32[]{:S(2)}) collective-permute-start(bf16[2,2,32,3072]{3,2,1,0:T(8,128)(2,1)} %fusion.25), channel_id=1, source_target_pairs={{0,4},{4,0},{8,12},{12,8},{16,20},{20,16},{24,28},{28,24},{1,5},{5... | collective-permute-start | bytes 2359304 | tf_op jit(solution)/shard_map/ppermute | solution.py:213
  369.9 29.8 %collective-permute-start.25 = (bf16[2,2,96,1024]{3,2,1,0:T(8,128)(2,1)}, bf16[2,2,96,1024]{3,2,1,0:T(8,128)(2,1)}, u32[]{:S(2)}, u32[]{:S(2)}) collective-permute-start(bf16[2,2,96,1024]{3,2,1,0:T(8,128)(2,1)} %fusion.24), channel_id=1, source_target_pairs={{0,8},{4,12},{8,0},{12,4},{16,24},{20,28},{24,16},{28,20},{1,9},{5... | collective-permute-start | bytes 2359304 | tf_op jit(solution)/shard_map/ppermute | solution.py:213
  370.9 33.8 %collective-permute-start.26 = (bf16[2,2,32,3200]{3,2,1,0:T(8,128)(2,1)}, bf16[2,2,32,3200]{3,2,1,0:T(8,128)(2,1)S(1)}, u32[]{:S(2)}, u32[]{:S(2)}) collective-permute-start(bf16[2,2,32,3200]{3,2,1,0:T(8,128)(2,1)} %fusion.23), channel_id=1, source_target_pairs={{0,2},{1,3},{2,0},{3,1},{4,6},{5,7},{6,4},{7,5},{8,10},{9,11},{10,... | collective-permute-start | bytes 2457608 | tf_op jit(solution)/shard_map/ppermute | solution.py:213
  427.5 20.8 %collective-permute-start.45 = (bf16[2,96,1024]{2,1,0:T(8,128)(2,1)}, bf16[2,96,1024]{2,1,0:T(8,128)(2,1)}, u32[]{:S(2)}, u32[]{:S(2)}) collective-permute-start(bf16[2,96,1024]{2,1,0:T(8,128)(2,1)} %fusion.47), channel_id=1, source_target_pairs={{0,2},{1,3},{2,0},{3,1},{4,6},{5,7},{6,4},{7,5},{8,10},{9,11},{10,... | collective-permute-start | bytes 1179656 | tf_op jit(solution)/shard_map/ppermute | solution.py:213
  428.0 22.4 %collective-permute-start.41 = (bf16[2,32,3200]{2,1,0:T(8,128)(2,1)}, bf16[2,32,3200]{2,1,0:T(8,128)(2,1)}, u32[]{:S(2)}, u32[]{:S(2)}) collective-permute-start(bf16[2,32,3200]{2,1,0:T(8,128)(2,1)} %fusion.36), channel_id=1, source_target_pairs={{0,4},{4,0},{8,12},{12,8},{16,20},{20,16},{24,28},{28,24},{1,5},{5... | collective-permute-start | bytes 1228808 | tf_op jit(solution)/shard_map/ppermute | solution.py:213
  431.7 49.0 %collective-permute-start.35 = (bf16[2,2,128,768]{3,2,1,0:T(8,128)(2,1)}, bf16[2,2,128,768]{3,2,1,0:T(8,128)(2,1)}, u32[]{:S(2)}, u32[]{:S(2)}) collective-permute-start(bf16[2,2,128,768]{3,2,1,0:T(8,128)(2,1)} %fusion.37), channel_id=1, source_target_pairs={{0,4},{4,0},{8,12},{12,8},{16,20},{20,16},{24,28},{28,24},{1,5},{5... | collective-permute-start | bytes 2359304 | tf_op jit(solution)/shard_map/ppermute | solution.py:213
  442.3 71.8 %collective-permute-start.27 = (bf16[512,1024]{1,0:T(8,128)(2,1)}, bf16[512,1024]{1,0:T(8,128)(2,1)}, u32[]{:S(2)}, u32[]{:S(2)}) collective-permute-start(bf16[512,1024]{1,0:T(8,128)(2,1)} %convolution_convert_fusion.4), channel_id=1, source_target_pairs={{0,1},{1,0},{2,3},{3,2},{4,5},{5,4},{6,7},{7,6},{8,9},{9,8},{10,11... | collective-permute-start | bytes 3145736 | tf_op jit(solution)/shard_map/ppermute | solution.py:213
  446.9 61.7 %collective-permute-start.28 = (bf16[512,1024]{1,0:T(8,128)(2,1)}, bf16[512,1024]{1,0:T(8,128)(2,1)}, u32[]{:S(2)}, u32[]{:S(2)}) collective-permute-start(bf16[512,1024]{1,0:T(8,128)(2,1)} %convolution_convert_fusion.3), channel_id=1, source_target_pairs={{0,1},{1,0},{2,3},{3,2},{4,5},{5,4},{6,7},{7,6},{8,9},{9,8},{10,11... | collective-permute-start | bytes 3145736 | tf_op jit(solution)/shard_map/ppermute | solution.py:213
  450.4 23.2 %collective-permute-start.46 = (bf16[96,1024]{1,0:T(8,128)(2,1)S(1)}, bf16[96,1024]{1,0:T(8,128)(2,1)S(1)}, u32[]{:S(2)}, u32[]{:S(2)}) collective-permute-start(bf16[96,1024]{1,0:T(8,128)(2,1)S(1)} %fusion.60), channel_id=1, source_target_pairs={{0,16},{4,20},{8,24},{12,28},{16,0},{20,4},{24,8},{28,12},{1,17},{... | collective-permute-start | bytes 589832 | tf_op jit(solution)/shard_map/ppermute | solution.py:213
  511.1 25.4 %collective-permute-start.29 = (bf16[512,1024]{1,0:T(8,128)(2,1)S(1)}, bf16[512,1024]{1,0:T(8,128)(2,1)S(1)}, u32[]{:S(2)}, u32[]{:S(2)}) collective-permute-start(bf16[512,1024]{1,0:T(8,128)(2,1)S(1)} %add_convert_fusion.4), channel_id=1, source_target_pairs={{0,2},{1,3},{2,0},{3,1},{4,6},{5,7},{6,4},{7,5},{8,10},{9,11},{10,... | collective-permute-start | bytes 3145736 | tf_op jit(solution)/shard_map/ppermute | solution.py:213
  (78 other events, 933.9 us)
Sparse Core Ops, SparseCore 0:
  11.4 122.1 all-gather.2
  136.4 88.1 all-gather.4

commit v4 on v3

--- a/solution.py
+++ b/solution.py
@@ -262,11 +262,8 @@
         return lax.dynamic_slice(array, starts, sizes).reshape(left + [h - l for l, h in part])
 
     def total(self, chosen):
-        groups = []
-        for group in self.terms:
-            pieces = [self.cut(t, chosen).astype(f32) for t in group]
-            groups.append(pieces[0] if len(pieces) == 1 else jnp.concatenate(pieces, axis=-1))
-        return sum(groups[1:], groups[0])
+        pieces = [self.cut(t, chosen).astype(f32) for t in self.terms]
+        return sum(pieces[1:], pieces[0])
 
     def outgoing(self, name):
         return self.total({**self.fixed, name: 1 - self.me[name]}).astype(bf16)
@@ -274,7 +271,7 @@
     def arrived(self, name, value):
         self.fixed[name] = self.me[name]
         names = [n for n in self.names if n not in self.fixed]
-        self.terms.append([(value, names, [(0, d) for d in self.shape])])
+        self.terms.append((value, names, [(0, d) for d in self.shape]))
 
     def exchange(self, name):
         self.arrived(name, swap(self.outgoing(name), *name))
@@ -397,7 +394,7 @@
     up_shift_grad = up_shift_grad.reshape(devices, ratio, own).transpose(1, 0, 2).reshape(ratio, width)
     vector_grads = jnp.concatenate([vector_grads, up_shift_grad])
     vector_grads = jnp.pad(vector_grads, ((0, 128 - vector_grads.shape[0]), (0, 0))).T.astype(bf16)
-    rest_grad = jnp.concatenate([output_grad, vector_grads], axis=1)
+    rest_grad = jnp.concatenate([output_grad, lax.optimization_barrier(vector_grads)], axis=1)
 
     dp_names, ctx_names = [("dp", b) for b in bits(dp)], [("ctx", b) for b in bits(ctx)]
     names = dp_names[::-1] + ctx_names[::-1]
@@ -405,72 +402,62 @@
     whole = {}
     for label, array, height in (("down", down_grad, ratio * own), ("up", up_grad, own), ("rest", rest_grad, own)):
         size = (height, array.shape[1])
-        sums = Halving(names, size)
-        sums.terms = [[(array.reshape([2] * len(names) + list(size)), names, [(0, d) for d in size])]]
-        sums.exchange(core)
-        whole[label] = [term[0] for term in sums.terms]
-
-    def stream(parts, shape):
-        sums = Halving(names, shape)
+        whole[label] = Halving(names, size)
+        whole[label].terms = [(array.reshape([2] * len(names) + list(size)), names, [(0, d) for d in size])]
+        whole[label].exchange(core)
+
+    def stream(label, part, turned):
+        sums = Halving(names, [high - low for low, high in part])
         sums.fixed = {core: sums.me[core]}
-        sums.terms = [[(whole[l][n][0], whole[l][n][1], part) for l, part in parts] for n in range(2)]
-        return sums
-
-    most = 3 * hidden // 4
+        sums.terms = [(array, left, part) for array, left, _ in whole[label].terms]
+        return sums, turn[turned:] + turn[:turned] + rest
+
+    most, tall = 3 * hidden // 4, (ratio - 1) * own
     streams = [
-        stream([("up", [(0, own), (0, most)])], (own, most)),
-        stream([("down", [(0, (ratio - 1) * own), (0, width)])], ((ratio - 1) * own, width)),
-        stream(
-            [
-                ("up", [(0, own), (most, hidden)]),
-                ("down", [((ratio - 1) * own, ratio * own), (0, width)]),
-                ("rest", [(0, own), (0, width + 128)]),
-            ],
-            (own, hidden - most + 2 * width + 128),
-        ),
+        stream("up", [(0, own), (0, most)], 2),
+        stream("down", [(0, tall), (0, width)], 0),
+        stream("up", [(0, own), (most, hidden)], 1),
+        stream("down", [(tall, ratio * own), (0, width)], 1),
+        stream("rest", [(0, own), (0, width + 128)], 1),
     ]
-    order = [turn[2:] + turn[:2], turn, turn[1:] + turn[:1]]
 
     grad_attended = nt(grad_branch, output_full).astype(bf16)
     pieces = [lax.dynamic_slice_in_dim(grad_attended, (me ^ k) * cols, cols, 1) for k in range(ctx)]
     grad_mixed = jnp.concatenate(trade(pieces, "ctx"))
-    grads = []
-    for stage in range(len(turn)):
-        going = [s.outgoing(o[stage]) for s, o in zip(streams, order)]
-        grad_mixed, grads, going = lax.optimization_barrier((grad_mixed, grads, going))
-        for s, o, value in zip(streams, order, going):
-            s.arrived(o[stage], swap(value, *o[stage]))
-        if stage < cols // 128:
-            grads.append(
-                attention_backward(stage, info, qkv, grad_mixed, mixed, logsum, ids_col, ids_row, per_chunk)
-            )
-            grad_mixed, grads[-1] = lax.optimization_barrier((grad_mixed, grads[-1]))
-    grad_qkv = jnp.concatenate(grads, axis=1)
-
-    partial = {}
-    for k in reversed(range(ctx)):
-        partial[k] = nt(grad_qkv[k * piece : (k + 1) * piece], qkv_weight)
-    for bit in bits(ctx):
-        for k in [k for k in partial if k & bit]:
-            partial[k ^ bit] = partial[k ^ bit] + swap(partial.pop(k).astype(bf16), "ctx", bit).astype(f32)
-    tokens_grad = (grad_one + partial[0]).astype(bf16)
-
-    for s, o in zip(streams, order):
-        for name in rest:
-            s.exchange(name)
-    up_left, down_left, mixed_left = [s.result() for s in streams]
-    up_weight_grad = jnp.concatenate([up_left, mixed_left[:, : hidden - most]], axis=1)
-    mixed_left = mixed_left[:, hidden - most :]
-    down_weight_grad = jnp.concatenate([down_left, mixed_left[:, :width]])
-    output_weight_grad = mixed_left[:, width : 2 * width]
-    vector_grads = mixed_left[:, 2 * width :].T
-    output_bias_grad, mixing_gain_grad, mixing_bias_grad, down_bias_grad, final_gain_grad, final_bias_grad = [
-        vector_grads[n] for n in range(6)
-    ]
-    up_bias_grad = vector_grads[6 : 6 + ratio].reshape(ratio * own)
-
-    qkv_sum = jnp.sum(grad_qkv.astype(f32), axis=0)
-    qkv_grad = tn(start_row, grad_qkv)
+    def weight_stream(grad):
+        size = (ctx * own, grad.shape[1])
+        sums = Halving(dp_names[::-1], size)
+        array = tn(start_row, grad).reshape([2] * len(dp_names) + list(size))
+        sums.terms = [(array, dp_names[::-1], [(0, d) for d in size])]
+        return sums, list(dp_names)
+
+    def start_part(k):
+        rows = slice(k * piece, (k + 1) * piece)
+        return nt(jnp.concatenate([g[rows] for g in grads], axis=1), qkv_weight)
+
+    def depart(moving, beside):
+        going = [s.outgoing(name) for s, name in moving]
+        going, beside = lax.optimization_barrier((going, beside))
+        return [(s, name, swap(value, *name)) for (s, name), value in zip(moving, going)], beside
+
+    def land(flights, beside):
+        values, beside = lax.optimization_barrier(([value for _, _, value in flights], beside))
+        for (s, name, _), value in zip(flights, values):
+            s.arrived(name, value)
+        return beside
+
+    def following(pairs):
+        return [(s, o.pop(0)) for s, o in pairs if o]
+
+    grads, pair_streams = [], []
+    for pair in range(cols // 128):
+        flights, grad_mixed = depart(following(streams + pair_streams), grad_mixed)
+        grad = attention_backward(pair, info, qkv, grad_mixed, mixed, logsum, ids_col, ids_row, per_chunk)
+        grad_mixed, grad = land(flights, (grad_mixed, grad))
+        grads.append(grad)
+        pair_streams.append(weight_stream(grad))
+
+    qkv_sum = jnp.concatenate([jnp.sum(g.astype(f32), axis=0) for g in grads])
     row_sum = jnp.sum(grad_one, axis=0, keepdims=True) + lax.dot_general(
         qkv_sum[None],
         qkv_weight.astype(f32),
@@ -484,7 +471,48 @@
         + [time_feat.astype(f32)],
         axis=1,
     )
-    message = gather_stacked(gather_stacked(message, "dp"), "ctx").reshape(ctx, dp, -1)
+    message_names = dp_names[::-1]
+
+    odd = [start_part(k).astype(bf16) for k in range(1, ctx, 2)]
+    flights, (grads, odd, message) = depart(following(streams + pair_streams), (grads, odd, message))
+    odd = [swap(value, *core) for value in odd]
+    reply = swap(message, *message_names.pop(0))
+    even = [start_part(k) for k in range(0, ctx, 2)]
+    even, odd, message, reply = land(flights, (even, odd, message, reply))
+    message = jnp.concatenate([message, reply])
+    even = [e + o.astype(f32) for e, o in zip(even, odd)]
+    away = [value.astype(bf16) for value in even[1:]]
+    kept, came = [], None
+    while any(o for _, o in streams + pair_streams) or message_names:
+        fast, slow = following(pair_streams), following(streams)
+        flights, (away, message) = depart(fast + slow, (away, message))
+        if came is None:
+            came = [swap(value, "ctx", 2 * n + 2) for n, value in enumerate(away)]
+        if message_names:
+            message = jnp.concatenate([message, swap(message, *message_names.pop(0))])
+        kept += flights[len(fast) :]
+        flights = flights[: len(fast)]
+        if any(o for _, o in streams):
+            flights, kept = flights + kept, []
+        if not any(o for _, o in pair_streams):
+            flights, kept = flights + kept, []
+        message, came = land(flights, (message, came)) if not kept else (land(flights, message), came)
+    summed = jnp.concatenate([s.result() for s, _ in pair_streams], axis=1).reshape(ctx, own, 3 * cols)
+    summed = [lax.dynamic_index_in_dim(summed, (me ^ k), 0, False) for k in range(ctx)]
+    summed, message = lax.optimization_barrier((summed, message))
+    blocks_out = to_absolute(trade(summed, "ctx"), me)
+    message = jnp.stack(trade([message] * ctx, "ctx"))
+    tokens_grad = (grad_one + sum([c.astype(f32) for c in came], even[0])).astype(bf16)
+    up_left, down_left, up_right, down_right, rest_left = [s.result() for s, _ in streams]
+    up_weight_grad = jnp.concatenate([up_left, up_right], axis=1)
+    down_weight_grad = jnp.concatenate([down_left, down_right])
+    output_weight_grad = rest_left[:, :width]
+    vector_grads = rest_left[:, width:].T
+    output_bias_grad, mixing_gain_grad, mixing_bias_grad, down_bias_grad, final_gain_grad, final_bias_grad = [
+        vector_grads[n] for n in range(6)
+    ]
+    up_bias_grad = vector_grads[6 : 6 + ratio].reshape(ratio * own)
+
     mine = (me_dp * ctx + me) * own
     row_sums = jnp.sum(message[:, :, :width], axis=0)
     time_weight_grad = lax.dot_general(
@@ -496,21 +524,10 @@
     )
     time_bias_grad = lax.dynamic_slice_in_dim(jnp.sum(row_sums, axis=0), mine, own)
     sums = jnp.sum(message[:, :, width : width + 2 * cols], axis=1)
-    sums = lax.dynamic_index_in_dim(sums, flipped((mine // cols ^ me), ctx), 0, False)
+    sums = lax.dynamic_index_in_dim(sums, mine // cols ^ me, 0, False)
     query_bias_grad = lax.dynamic_slice_in_dim(sums[:cols], mine % cols, own)
     value_bias_grad = lax.dynamic_slice_in_dim(sums[cols:], mine % cols, own)
 
-    size = (ctx * own, 3 * cols)
-    summed = Halving(dp_names[::-1], size)
-    summed.terms = [
-        [(qkv_grad.reshape([2] * len(dp_names) + list(size)), dp_names[::-1], [(0, d) for d in size])]
-    ]
-    for name in dp_names:
-        summed.exchange(name)
-    summed = summed.result().reshape(ctx, own, 3 * cols)
-    blocks_out = to_absolute(
-        trade([lax.dynamic_index_in_dim(summed, (me ^ k), 0, False) for k in range(ctx)], "ctx"), me
-    )
     query_weight_grad, key_weight_grad, value_weight_grad = [
         jnp.concatenate(
             [

time: 554 us -> 555 us (level)
  other arithmetic: 56.5 us -> 72.4 us
  starting transfers between devices: 40.3 us -> 56 us
  local copies, waits for them, and re-layouts: 63 us -> 48.7 us
  waiting for transfers between devices: 183 us -> 173 us
  matrix products: 85.3 us -> 78.9 us
    convert_element_type x20 -> x0, local copies, waits for them, and re-layouts: 17.6 us -> none  [total(): pieces = [self.cut(t, chosen).astype(f32) for t in group]]
    ppermute x47 -> x59, starting transfers between devices: 40.2 us -> 56 us  [swap(): return lax.ppermute(value, axis, [(i, i ^ mask) for i in range(size)])]
    ppermute x47 -> x59, waiting for transfers between devices: 183 us -> 173 us  [swap(): return lax.ppermute(value, axis, [(i, i ^ mask) for i in range(size)])]
    convert_element_type x14 -> x24, other arithmetic: 30.9 us -> 40.6 us  [outgoing(): return self.total({**self.fixed, name: 1 - self.me[name]}).astype(bf16)]
    unnamed x142 -> x125, local copies, waits for them, and re-layouts: 16.7 us -> 19.9 us
    dot_general x4 -> x5, matrix products: 23.1 us -> 22.4 us  [tn(): lax.dot_general(left, right, (((0,), (0,)), ((), ())), preferred_element_...]
  transfers between devices with their start and end apart: 49 -> 61, of which waited for: 18 -> 27; matrix products, arithmetic and copies ran while one was open for 22% -> 21% of each run, Pallas kernels for 19% -> 19%
where the time goes in v4:
time: 555 us; the launch traced here: 548 us
  waiting for transfers between devices  173 us (31%)
  Pallas kernels  103 us (19%)
  matrix products  78.9 us (14%)
  other arithmetic  72.4 us (13%)
  starting transfers between devices  56 us (10%)
  local copies, waits for them, and re-layouts  48.7 us (9%)
  between operations  15.7 us (3%)
    ppermute x59, waiting for transfers between devices, swap(): return lax.ppermute(value, axis, [(i, i ^ mask) for i in range(size)])  173 us
    ppermute x59, starting transfers between devices, swap(): return lax.ppermute(value, axis, [(i, i ^ mask) for i in range(size)])  56 us
    pallas_call x2, Pallas kernels, attention_backward(): pl.pallas_call(functools.partial(backward_kernel, per_chunk, 2 * pair), g...  54.6 us
    pallas_call x1, Pallas kernels, attention_forward(): pl.pallas_call(functools.partial(forward_kernel, per_chunk, heads // 2),...  48.4 us
    convert_element_type x24, other arithmetic, outgoing(): return self.total({**self.fixed, name: 1 - self.me[name]}).astype(bf16)  40.6 us
    dot_general x5, matrix products, nn(): return jnp.dot(left, right, preferred_element_type=f32)  29.2 us
    dot_general x7, matrix products, nt(): lax.dot_general(left, right, (((1,), (1,)), ((), ())), preferred_element_...  25.5 us
    dot_general x5, matrix products, tn(): lax.dot_general(left, right, (((0,), (0,)), ((), ())), preferred_element_...  22.4 us
  transfers between devices with their start and end apart: 61, of which 27 were waited for; matrix products, arithmetic and copies ran while one was open for 21% of the time, Pallas kernels for 19%

profile of v4, /device:TPU:0, one launch (start us, length us, event | category | flops | bytes accessed | tf_op | source)
XLA Modules:
  0.0 547.8 jit_solution(4710663590310362070)
XLA Ops:
  27.2 19.2 %collective-permute-done.3 = bf16[1,128,1152]{2,1,0:T(8,128)(2,1)S(1)} collective-permute-done((bf16[1,128,1152]{2,1,0:T(8,128)(2,1)S(1)}, bf16[1,128,1152]{2,1,0:T(8,128)(2,1)S(1)}, u32[]{:S(2)}, u32[]{:S(2)}) %collective-permute-start.3) | collective-permute-done | bytes 294944 | tf_op jit(solution)/shard_map/ppermute | solution.py:213
  46.5 29.1 %collective-permute-done.4 = bf16[2,128,1152]{2,1,0:T(8,128)(2,1)S(1)} collective-permute-done((bf16[2,128,1152]{2,1,0:T(8,128)(2,1)S(1)}, bf16[2,128,1152]{2,1,0:T(8,128)(2,1)S(1)}, u32[]{:S(2)}, u32[]{:S(2)}) %collective-permute-start.4) | collective-permute-done | bytes 589856 | tf_op jit(solution)/shard_map/ppermute | solution.py:213
  87.3 33.2 %collective-permute-done.10 = bf16[512,1024]{1,0:T(8,128)(2,1)} collective-permute-done((bf16[512,1024]{1,0:T(8,128)(2,1)}, bf16[512,1024]{1,0:T(8,128)(2,1)}, u32[]{:S(2)}, u32[]{:S(2)}) %collective-permute-start.10) | collective-permute-done | bytes 1048608 | tf_op jit(solution)/shard_map/ppermute | solution.py:213
  129.9 7.2 %add_convert_fusion.1.qkv_ref.q_ref.k_ref.v_ref = bf16[2048,768]{1,0:T(8,128)(2,1)} fusion(f32[768]{0:T(1024)S(1)} %constant_dynamic-update-slice_fusion.63, bf16[1024,1152]{0,1:T(8,128)(2,1)S(1)} %bitcast_dynamic-update-slice_fusion, bf16[512,1024]{1,0:T(8,128)(2,1)} %collective-permute-done.11, bf16[512,1024]{1,0:T(8,128)(2,1)} %collective-permute-done.10, ...), kind=kOutput, calls=%fused_computation.16 | convolution fusion | flops 3245342720 | bytes 8921088 | tf_op jit(solution)/shard_map/dot_general | solution.py:21
  137.1 48.4 %attention_forward.1 = (bf16[2048,256]{1,0:T(8,128)(2,1)}, f32[8,4,256]{2,1,0:T(4,128)}) custom-call(s32[3,8]{1,0:T(4,128)} %add_add_fusion.2.info, bf16[2048,768]{1,0:T(8,128)(2,1)} %add_convert_fusion.1.qkv_ref.q_ref.k_ref.v_ref, s32[2048,1]{1,0:T(8,128)} %copy.215.idc_ref, s32[8,1,256]{2,1,0:T(1,128)} %bitcast.630), custom_call_target="tpu_custom_call" | custom-call | flops 30000001024 | bytes 3145728 | tf_op jit(solution)/shard_map/attention_forward/pallas_call | solution.py:84
  189.3 12.9 %collective-permute-done.13 = bf16[512,256]{1,0:T(8,128)(2,1)S(1)} collective-permute-done((bf16[512,256]{1,0:T(8,128)(2,1)S(1)}, bf16[512,256]{1,0:T(8,128)(2,1)S(1)}, u32[]{:S(2)}, u32[]{:S(2)}) %collective-permute-start.13) | collective-permute-done | bytes 262176 | tf_op jit(solution)/shard_map/ppermute | solution.py:213
  202.2 9.4 %collective-permute-done.14 = bf16[512,256]{1,0:T(8,128)(2,1)S(1)} collective-permute-done((bf16[512,256]{1,0:T(8,128)(2,1)S(1)}, bf16[512,256]{1,0:T(8,128)(2,1)S(1)}, u32[]{:S(2)}, u32[]{:S(2)}) %collective-permute-start.14) | collective-permute-done | bytes 262176 | tf_op jit(solution)/shard_map/ppermute | solution.py:213
  218.7 9.8 %fusion.4 = (bf16[512,4096]{1,0:T(8,128)(2,1)}, bf16[512,4096]{1,0:T(8,128)(2,1)}) fusion(f32[4096]{0:T(1024)S(1)} %add.536, bf16[1024,5120]{1,0:T(8,128)(2,1)S(1)} %copy-done.38, f32[512,1024]{1,0:T(8,128)S(1)} %get-tuple-element.323, f32[1024]{0:T(1024)S(1)} %bitcast.653, f32[1024]{0:T(1024)S(1)} %bitcast.640, f32[512]{0:T(512)S(1)} %add_rsqrt_fusion.1, ...), kind=kOutput, calls=%fused_computation.5 | convolution fusion | flops 4322754560 | bytes 18903040 | tf_op jit(solution)/shard_map/dot_general | solution.py:21
  228.5 8.4 %fusion.125 = (f32[512]{0:T(512)S(1)}, f32[512,1024]{1,0:T(8,128)S(1)}) fusion(f32[1024]{0:T(1024)S(1)} %bitcast.656, bf16[512,4096]{1,0:T(8,128)(2,1)} %get-tuple-element.103, bf16[4096,1024]{1,0:T(8,128)(2,1)} %all-gather.5.cloned.1.call-done, f32[1024]{0:T(1024)S(1)} %bitcast.654, f32[1024]{0:T(1024)S(1)} %bitcast.641, f32[512]{0:T(512)S(1)} %add_rsqrt_fusion.1, ...), kind=kOutput, calls=%fused_computation.434 | convolution fusion | flops 4298636800 | bytes 16795648 | tf_op jit(solution)/shard_map/dot_general | solution.py:21
  241.2 5.1 convolution_convert_fusion
  252.1 9.6 %fusion.126 = (bf16[4096]{0:T(1024)(128)(2,1)S(1)}, bf16[512,4096]{1,0:T(8,128)(2,1)}) fusion(bf16[512,4096]{1,0:T(8,128)(2,1)S(1)} %copy-done.42, bf16[4096,1024]{1,0:T(8,128)(2,1)} %all-gather.5.cloned.1.call-done, f32[512,1024]{1,0:T(8,128)S(1)} %get-tuple-element.205), kind=kOutput, calls=%fused_computation.435 | convolution fusion | flops 4303876096 | bytes 18882560 | tf_op jit(solution)/shard_map/dot_general | solution.py:29
  261.7 7.2 %convolution_convert_fusion.1 = bf16[1024,4096]{1,0:T(8,128)(2,1)S(1)} fusion(bf16[512,4096]{1,0:T(8,128)(2,1)} %get-tuple-element.328, f32[512,1024]{1,0:T(8,128)S(1)} %get-tuple-element.323, f32[1024]{0:T(1024)S(1)} %bitcast.655, f32[1024]{0:T(1024)S(1)} %bitcast.642, f32[512]{0:T(512)S(1)} %add_rsqrt_fusion.1, f32[512]{0:T(512)S(1)} %broadcast_multiply_fusion.5), kind=kOutput, calls=%fused_computation.11 | convolution fusion | flops 4301783040 | bytes 14692352 | tf_op jit(solution)/shard_map/dot_general | solution.py:25
  274.8 7.7 %multiply_reduce_fusion = (bf16[1024]{0:T(1024)(128)(2,1)S(1)}, f32[512]{0:T(512)S(1)}, f32[512]{0:T(512)S(1)}, bf16[1024]{0:T(1024)(128)(2,1)S(1)}, f32[512,1024]{1,0:T(8,128)S(1)}) fusion(f32[512,1024]{1,0:T(8,128)S(1)} %get-tuple-element.323, f32[512]{0:T(512)S(1)} %add_rsqrt_fusion.1, f32[512]{0:T(512)S(1)} %broadcast_multiply_fusion.5, ...), kind=kOutput, calls=%fused_computation.38 | convolution fusion | flops 4300207104 | bytes 18890752 | tf_op jit(solution)/shard_map/dot_general | solution.py:29
  288.8 4.4 copy.226
  301.3 7.2 %collective-permute-done.19 = bf16[512,256]{1,0:T(8,128)(2,1)} collective-permute-done((bf16[512,256]{1,0:T(8,128)(2,1)}, bf16[512,256]{1,0:T(8,128)(2,1)}, u32[]{:S(2)}, u32[]{:S(2)}) %collective-permute-start.19) | collective-permute-done | bytes 262176 | tf_op jit(solution)/shard_map/ppermute | solution.py:213
  308.5 4.1 collective-permute-done.20
  333.8 27.2 %attention_backward.2 = bf16[2048,384]{1,0:T(8,128)(2,1)} custom-call(s32[3,8]{1,0:T(4,128)} %add_add_fusion.2.info, bf16[2048,768]{1,0:T(8,128)(2,1)} %add_convert_fusion.1.qkv_ref.q_ref.k_ref.v_ref, bf16[2048,768]{1,0:T(8,128)(2,1)} %add_convert_fusion.1.qkv_ref.q_ref.k_ref.v_ref, bf16[2048,768]{1,0:T(8,128)(2,1)} %add_convert_fusion.1.qkv_ref.q_ref.k_ref.v_ref, ...), custom_call_target="tpu_custom_call" | custom-call | flops 24999999488 | bytes 2097152 | tf_op jit(solution)/shard_map/attention_backward/pallas_call | solution.py:170
  361.0 6.9 %collective-permute-done.24 = bf16[2,2,2,32,1024]{4,3,2,1,0:T(8,128)(2,1)} collective-permute-done((bf16[2,2,2,32,1024]{4,3,2,1,0:T(8,128)(2,1)}, bf16[2,2,2,32,1024]{4,3,2,1,0:T(8,128)(2,1)}, u32[]{:S(2)}, u32[]{:S(2)}) %collective-permute-start.24) | collective-permute-done | bytes 524320 | tf_op jit(solution)/shard_map/ppermute | solution.py:213
  367.9 4.8 fusion.115
  388.0 27.4 %attention_backward.3 = bf16[2048,384]{1,0:T(8,128)(2,1)} custom-call(s32[3,8]{1,0:T(4,128)} %add_add_fusion.2.info, bf16[2048,768]{1,0:T(8,128)(2,1)} %add_convert_fusion.1.qkv_ref.q_ref.k_ref.v_ref, bf16[2048,768]{1,0:T(8,128)(2,1)} %add_convert_fusion.1.qkv_ref.q_ref.k_ref.v_ref, bf16[2048,768]{1,0:T(8,128)(2,1)} %add_convert_fusion.1.qkv_ref.q_ref.k_ref.v_ref, ...), custom_call_target="tpu_custom_call" | custom-call | flops 24999999488 | bytes 2097152 | tf_op jit(solution)/shard_map/attention_backward/pallas_call | solution.py:170
  422.3 8.7 %collective-permute-done.29 = bf16[2,2,32,1024]{3,2,1,0:T(8,128)(2,1)S(1)} collective-permute-done((bf16[2,2,32,1024]{3,2,1,0:T(8,128)(2,1)}, bf16[2,2,32,1024]{3,2,1,0:T(8,128)(2,1)S(1)}, u32[]{:S(2)}, u32[]{:S(2)}) %collective-permute-start.29) | collective-permute-done | bytes 262176 | tf_op jit(solution)/shard_map/ppermute | solution.py:213
  453.5 5.2 collective-permute-done.35
  494.0 5.2 collective-permute-done.48
  504.3 12.0 %collective-permute-done.50 = bf16[32,1152]{1,0:T(8,128)(2,1)S(1)} collective-permute-done((bf16[32,1152]{1,0:T(8,128)(2,1)S(1)}, bf16[32,1152]{1,0:T(8,128)(2,1)S(1)}, u32[]{:S(2)}, u32[]{:S(2)}) %collective-permute-start.50) | collective-permute-done | bytes 73760 | tf_op jit(solution)/shard_map/ppermute | solution.py:213
  (389 shorter events, 211.7 us)
Async XLA Ops:
  7.2 205.5 %all-gather.3.cloned.1.call-start = ((), (), s32[]{:S(2)}) async-start(), calls=%async_computation | async-start | bytes 10813440 | tf_op jit(solution)/shard_map/all_gather | solution.py:314
  9.0 219.5 %all-gather.5.cloned.1.call-start = ((), (), s32[]{:S(2)}) async-start(), calls=%async_computation.1 | async-start | bytes 8650752 | tf_op jit(solution)/shard_map/all_gather | solution.py:315
  24.5 21.9 %collective-permute-start.3 = (bf16[1,128,1152]{2,1,0:T(8,128)(2,1)S(1)}, bf16[1,128,1152]{2,1,0:T(8,128)(2,1)S(1)}, u32[]{:S(2)}, u32[]{:S(2)}) collective-permute-start(bf16[1,128,1152]{2,1,0:T(8,128)(2,1)S(1)} %maximum_bitcast_fusion), channel_id=1, source_target_pairs={{0,16},{4,20},{8,24},{12,28},{16,0},{20,4},{24,8},{28,12},{1,17},{... | collective-permute-start | bytes 884744 | tf_op jit(solution)/shard_map/ppermute | solution.py:213
  46.4 29.2 %collective-permute-start.4 = (bf16[2,128,1152]{2,1,0:T(8,128)(2,1)S(1)}, bf16[2,128,1152]{2,1,0:T(8,128)(2,1)S(1)}, u32[]{:S(2)}, u32[]{:S(2)}) collective-permute-start(bf16[2,128,1152]{2,1,0:T(8,128)(2,1)S(1)} %pad_maximum_fusion.6), channel_id=1, source_target_pairs={{0,8},{4,12},{8,0},{12,4},{16,24},{20,28},{24,16},{28,20},{1,9},{5... | collective-permute-start | bytes 1769480 | tf_op jit(solution)/shard_map/ppermute | solution.py:213
  75.8 45.5 %collective-permute-start.5 = (bf16[4,128,1152]{2,1,0:T(8,128)(2,1)S(1)}, bf16[4,128,1152]{2,1,0:T(8,128)(2,1)S(1)}, u32[]{:S(2)}, u32[]{:S(2)}) collective-permute-start(bf16[4,128,1152]{2,1,0:T(8,128)(2,1)S(1)} %pad_maximum_fusion.2), channel_id=1, source_target_pairs={{0,4},{4,0},{8,12},{12,8},{16,20},{20,16},{24,28},{28,24},{1,5},{5... | collective-permute-start | bytes 3538952 | tf_op jit(solution)/shard_map/ppermute | solution.py:213
  77.1 43.4 %collective-permute-start.10 = (bf16[512,1024]{1,0:T(8,128)(2,1)}, bf16[512,1024]{1,0:T(8,128)(2,1)}, u32[]{:S(2)}, u32[]{:S(2)}) collective-permute-start(bf16[512,1024]{1,0:T(8,128)(2,1)} %bitcast.673), channel_id=1, source_target_pairs={{0,2},{1,3},{2,0},{3,1},{4,6},{5,7},{6,4},{7,5},{8,10},{9,11},{10,... | collective-permute-start | bytes 3145736 | tf_op jit(solution)/shard_map/ppermute | solution.py:213
  79.1 50.8 %collective-permute-start.9 = (bf16[512,1024]{1,0:T(8,128)(2,1)}, bf16[512,1024]{1,0:T(8,128)(2,1)}, u32[]{:S(2)}, u32[]{:S(2)}) collective-permute-start(bf16[512,1024]{1,0:T(8,128)(2,1)} %bitcast.674), channel_id=1, source_target_pairs={{0,1},{1,0},{2,3},{3,2},{4,5},{5,4},{6,7},{7,6},{8,9},{9,8},{10,11... | collective-permute-start | bytes 3145736 | tf_op jit(solution)/shard_map/ppermute | solution.py:213
  187.6 24.1 %collective-permute-start.14 = (bf16[512,256]{1,0:T(8,128)(2,1)S(1)}, bf16[512,256]{1,0:T(8,128)(2,1)S(1)}, u32[]{:S(2)}, u32[]{:S(2)}) collective-permute-start(bf16[512,256]{1,0:T(8,128)(2,1)S(1)} %get-tuple-element.234), channel_id=1, source_target_pairs={{0,3},{1,2},{2,1},{3,0},{4,7},{5,6},{6,5},{7,4},{8,11},{9,10},{10,... | collective-permute-start | bytes 786440 | tf_op jit(solution)/shard_map/ppermute | solution.py:213
  251.9 64.2 %collective-permute-start.16 = (bf16[2,2,2,2,128,1024]{5,4,3,2,1,0:T(8,128)(2,1)}, bf16[2,2,2,2,128,1024]{5,4,3,2,1,0:T(8,128)(2,1)}, u32[]{:S(2)}, u32[]{:S(2)}) collective-permute-start(bf16[2,2,2,2,128,1024]{5,4,3,2,1,0:T(8,128)(2,1)} %dynamic-slice_bitcast_fusion), channel_id=1, source_target_pairs={{0,1},{1,0},{2,3},{3,2},{4,5},{5,4},{6,7},{7,6},{8,9},{9,8},{10,11... | collective-permute-start | bytes 12582920 | tf_op jit(solution)/shard_map/ppermute | solution.py:213
  274.5 43.8 %collective-permute-start.15 = (bf16[2,2,2,2,32,4096]{5,4,3,2,1,0:T(8,128)(2,1)}, bf16[2,2,2,2,32,4096]{5,4,3,2,1,0:T(8,128)(2,1)}, u32[]{:S(2)}, u32[]{:S(2)}) collective-permute-start(bf16[2,2,2,2,32,4096]{5,4,3,2,1,0:T(8,128)(2,1)} %dynamic-slice_bitcast_fusion.1), channel_id=1, source_target_pairs={{0,1},{1,0},{2,3},{3,2},{4,5},{5,4},{6,7},{7,6},{8,9},{9,8},{10,11... | collective-permute-start | bytes 12582920 | tf_op jit(solution)/shard_map/ppermute | solution.py:213
  294.6 20.1 %collective-permute-start.17 = (bf16[2,2,2,2,32,1152]{5,4,0,3,2,1:T(8,128)(2,1)S(1)}, bf16[2,2,2,2,32,1152]{5,4,0,3,2,1:T(8,128)(2,1)}, u32[]{:S(2)}, u32[]{:S(2)}) collective-permute-start(bf16[2,2,2,2,32,1152]{5,4,0,3,2,1:T(8,128)(2,1)S(1)} %copy_bitcast_fusion), channel_id=1, source_target_pairs={{0,1},{1,0},{2,3},{3,2},{4,5},{5,4},{6,7},{7,6},{8,9},{9,8},{10,11... | collective-permute-start | bytes 3538952 | tf_op jit(solution)/shard_map/ppermute | solution.py:213
  327.9 40.0 %collective-permute-start.21 = (bf16[2,2,2,32,3072]{4,3,2,1,0:T(8,128)(2,1)}, bf16[2,2,2,32,3072]{4,3,2,1,0:T(8,128)(2,1)}, u32[]{:S(2)}, u32[]{:S(2)}) collective-permute-start(bf16[2,2,2,32,3072]{4,3,2,1,0:T(8,128)(2,1)} %fusion.10), channel_id=1, source_target_pairs={{0,2},{1,3},{2,0},{3,1},{4,6},{5,7},{6,4},{7,5},{8,10},{9,11},{10,... | collective-permute-start | bytes 4718600 | tf_op jit(solution)/shard_map/ppermute | solution.py:213
  328.4 39.5 %collective-permute-start.22 = (bf16[2,2,2,96,1024]{4,3,2,1,0:T(8,128)(2,1)}, bf16[2,2,2,96,1024]{4,3,2,1,0:T(8,128)(2,1)}, u32[]{:S(2)}, u32[]{:S(2)}) collective-permute-start(bf16[2,2,2,96,1024]{4,3,2,1,0:T(8,128)(2,1)} %fusion.9), channel_id=1, source_target_pairs={{0,4},{4,0},{8,12},{12,8},{16,20},{20,16},{24,28},{28,24},{1,5},{5... | collective-permute-start | bytes 4718600 | tf_op jit(solution)/shard_map/ppermute | solution.py:213
  329.8 38.1 %collective-permute-start.25 = (bf16[2,2,2,32,1152]{4,3,2,1,0:T(8,128)(2,1)S(1)}, bf16[2,2,2,32,1152]{4,3,2,1,0:T(8,128)(2,1)S(1)}, u32[]{:S(2)}, u32[]{:S(2)}) collective-permute-start(bf16[2,2,2,32,1152]{4,3,2,1,0:T(8,128)(2,1)S(1)} %copy.229), channel_id=1, source_target_pairs={{0,8},{4,12},{8,0},{12,4},{16,24},{20,28},{24,16},{28,20},{1,9},{5... | collective-permute-start | bytes 1769480 | tf_op jit(solution)/shard_map/ppermute | solution.py:213
  331.7 29.3 %collective-permute-start.23 = (bf16[2,2,2,32,1024]{4,3,2,1,0:T(8,128)(2,1)}, bf16[2,2,2,32,1024]{4,3,2,1,0:T(8,128)(2,1)}, u32[]{:S(2)}, u32[]{:S(2)}) collective-permute-start(bf16[2,2,2,32,1024]{4,3,2,1,0:T(8,128)(2,1)} %fusion.37), channel_id=1, source_target_pairs={{0,8},{4,12},{8,0},{12,4},{16,24},{20,28},{24,16},{28,20},{1,9},{5... | collective-permute-start | bytes 1572872 | tf_op jit(solution)/shard_map/ppermute | solution.py:213
  331.9 36.0 %collective-permute-start.24 = (bf16[2,2,2,32,1024]{4,3,2,1,0:T(8,128)(2,1)}, bf16[2,2,2,32,1024]{4,3,2,1,0:T(8,128)(2,1)}, u32[]{:S(2)}, u32[]{:S(2)}) collective-permute-start(bf16[2,2,2,32,1024]{4,3,2,1,0:T(8,128)(2,1)} %fusion.36), channel_id=1, source_target_pairs={{0,8},{4,12},{8,0},{12,4},{16,24},{20,28},{24,16},{28,20},{1,9},{5... | collective-permute-start | bytes 1572872 | tf_op jit(solution)/shard_map/ppermute | solution.py:213
  383.5 47.5 %collective-permute-start.26 = (bf16[2,2,32,3072]{3,2,0,1:T(8,128)(2,1)S(1)}, bf16[2,2,32,3072]{3,2,0,1:T(8,128)(2,1)}, u32[]{:S(2)}, u32[]{:S(2)}) collective-permute-start(bf16[2,2,32,3072]{3,2,0,1:T(8,128)(2,1)S(1)} %copy.241), channel_id=1, source_target_pairs={{0,4},{4,0},{8,12},{12,8},{16,20},{20,16},{24,28},{28,24},{1,5},{5... | collective-permute-start | bytes 2359304 | tf_op jit(solution)/shard_map/ppermute | solution.py:213
  385.0 46.0 %collective-permute-start.27 = (bf16[2,2,96,1024]{3,2,0,1:T(8,128)(2,1)}, bf16[2,2,96,1024]{3,2,0,1:T(8,128)(2,1)}, u32[]{:S(2)}, u32[]{:S(2)}) collective-permute-start(bf16[2,2,96,1024]{3,2,0,1:T(8,128)(2,1)} %copy.242), channel_id=1, source_target_pairs={{0,8},{4,12},{8,0},{12,4},{16,24},{20,28},{24,16},{28,20},{1,9},{5... | collective-permute-start | bytes 2359304 | tf_op jit(solution)/shard_map/ppermute | solution.py:213
  386.2 32.5 %collective-permute-start.28 = (bf16[2,2,32,1024]{3,2,1,0:T(8,128)(2,1)}, bf16[2,2,32,1024]{3,2,1,0:T(8,128)(2,1)}, u32[]{:S(2)}, u32[]{:S(2)}) collective-permute-start(bf16[2,2,32,1024]{3,2,1,0:T(8,128)(2,1)} %fusion.65), channel_id=1, source_target_pairs={{0,2},{1,3},{2,0},{3,1},{4,6},{5,7},{6,4},{7,5},{8,10},{9,11},{10,... | collective-permute-start | bytes 786440 | tf_op jit(solution)/shard_map/ppermute | solution.py:213
  445.9 23.4 %collective-permute-start.39 = (bf16[512,1024]{1,0:T(8,128)(2,1)S(1)}, bf16[512,1024]{1,0:T(8,128)(2,1)S(1)}, u32[]{:S(2)}, u32[]{:S(2)}) collective-permute-start(bf16[512,1024]{1,0:T(8,128)(2,1)S(1)} %convolution_convert_fusion.4), channel_id=1, source_target_pairs={{0,1},{1,0},{2,3},{3,2},{4,5},{5,4},{6,7},{7,6},{8,9},{9,8},{10,11... | collective-permute-start | bytes 3145736 | tf_op jit(solution)/shard_map/ppermute | solution.py:213
  446.0 23.3 %collective-permute-start.40 = (bf16[512,1024]{1,0:T(8,128)(2,1)S(1)}, bf16[512,1024]{1,0:T(8,128)(2,1)S(1)}, u32[]{:S(2)}, u32[]{:S(2)}) collective-permute-start(bf16[512,1024]{1,0:T(8,128)(2,1)S(1)} %convolution_convert_fusion.3), channel_id=1, source_target_pairs={{0,1},{1,0},{2,3},{3,2},{4,5},{5,4},{6,7},{7,6},{8,9},{9,8},{10,11... | collective-permute-start | bytes 3145736 | tf_op jit(solution)/shard_map/ppermute | solution.py:213
  480.1 37.3 %collective-permute-start.52 = (bf16[512,1024]{1,0:T(8,128)(2,1)}, bf16[512,1024]{1,0:T(8,128)(2,1)}, u32[]{:S(2)}, u32[]{:S(2)}) collective-permute-start(bf16[512,1024]{1,0:T(8,128)(2,1)} %add_convert_fusion.3), channel_id=1, source_target_pairs={{0,2},{1,3},{2,0},{3,1},{4,6},{5,7},{6,4},{7,5},{8,10},{9,11},{10,... | collective-permute-start | bytes 3145736 | tf_op jit(solution)/shard_map/ppermute | solution.py:213
  492.8 23.5 %collective-permute-start.46 = (bf16[32,3072]{1,0:T(8,128)(2,1)}, bf16[32,3072]{1,0:T(8,128)(2,1)S(1)}, u32[]{:S(2)}, u32[]{:S(2)}) collective-permute-start(bf16[32,3072]{1,0:T(8,128)(2,1)} %fusion.71), channel_id=1, source_target_pairs={{0,16},{4,20},{8,24},{12,28},{16,0},{20,4},{24,8},{28,12},{1,17},{... | collective-permute-start | bytes 589832 | tf_op jit(solution)/shard_map/ppermute | solution.py:213
  499.2 17.2 %collective-permute-start.47 = (bf16[96,1024]{1,0:T(8,128)(2,1)}, bf16[96,1024]{1,0:T(8,128)(2,1)S(1)}, u32[]{:S(2)}, u32[]{:S(2)}) collective-permute-start(bf16[96,1024]{1,0:T(8,128)(2,1)} %fusion.70), channel_id=1, source_target_pairs={{0,16},{4,20},{8,24},{12,28},{16,0},{20,4},{24,8},{28,12},{1,17},{... | collective-permute-start | bytes 589832 | tf_op jit(solution)/shard_map/ppermute | solution.py:213
  (82 other events, 937.8 us)
Sparse Core Ops, SparseCore 0:
  11.4 122.1 all-gather.2
  136.4 85.8 all-gather.4

commit v5 on v4

--- a/solution.py
+++ b/solution.py
@@ -48,24 +48,35 @@
     ids_q = idr_ref[pl.ds(i, 1)][0]
     here = pl.multiple_of(place(i, me, per_chunk) * BLOCK, BLOCK)
 
+    queries = []
+    for p in range(pairs):
+        pair = qkv_ref[pl.ds(here, BLOCK), (3 * p) * 128 : (3 * p + 1) * 128]
+        queries += [head_only(pair, 0), head_only(pair, 1)]
+
     def step(j, carry):
         at = pl.multiple_of(place(j, me, per_chunk) * BLOCK, BLOCK)
         same = idc_ref[pl.ds(pl.multiple_of(j * BLOCK, BLOCK), BLOCK), :] == ids_q
+        heads = range(2 * pairs)
+        peak = [m_acc[h] for h in heads]
+        count = [l_acc[h] for h in heads]
+        mixed = [o_acc[h * HEAD_DIM : (h + 1) * HEAD_DIM] for h in heads]
+        values, scores = [], []
         for p in range(pairs):
-            q_pair = qkv_ref[pl.ds(here, BLOCK), (3 * p) * 128 : (3 * p + 1) * 128]
             k_pair = qkv_ref[pl.ds(at, BLOCK), (3 * p + 1) * 128 : (3 * p + 2) * 128]
-            v_pair = qkv_ref[pl.ds(at, BLOCK), (3 * p + 2) * 128 : (3 * p + 3) * 128]
-            for w in range(2):
-                h = 2 * p + w
-                t = jnp.where(same, nt(k_pair, head_only(q_pair, w)) * SCALE_LOG2, MASKED)
-                m_old = m_acc[h]
-                m_new = jnp.maximum(m_old, jnp.max(t, axis=0, keepdims=True))
-                alpha = jnp.exp2(m_old - m_new)
-                e = jnp.exp2(t - m_new)
-                l_acc[h] = l_acc[h] * alpha + jnp.sum(e, axis=0, keepdims=True)
-                m_acc[h] = m_new
-                rows = slice(h * HEAD_DIM, (h + 1) * HEAD_DIM)
-                o_acc[rows] = o_acc[rows] * alpha + tn(v_pair, e.astype(bf16))[w * HEAD_DIM : (w + 1) * HEAD_DIM]
+            values.append(qkv_ref[pl.ds(at, BLOCK), (3 * p + 2) * 128 : (3 * p + 3) * 128])
+            scores += [nt(k_pair, queries[2 * p + w]) for w in range(2)]
+        for h in heads:
+            t = jnp.where(same, scores[h] * SCALE_LOG2, MASKED)
+            new = jnp.maximum(peak[h], jnp.max(t, axis=0, keepdims=True))
+            alpha = jnp.exp2(peak[h] - new)
+            e = jnp.exp2(t - new)
+            count[h] = count[h] * alpha + jnp.sum(e, axis=0, keepdims=True)
+            peak[h] = new
+            w = h % 2
+            mixed[h] = mixed[h] * alpha + tn(values[h // 2], e.astype(bf16))[w * HEAD_DIM : (w + 1) * HEAD_DIM]
+        for h in heads:
+            m_acc[h], l_acc[h] = peak[h], count[h]
+            o_acc[h * HEAD_DIM : (h + 1) * HEAD_DIM] = mixed[h]
         return carry
 
     lax.fori_loop(info[0, i], info[1, i], step, 0)
@@ -311,9 +322,17 @@
     per_chunk = piece // BLOCK
     tokens, cotangent, ids = tokens[0], cotangent[0], segment_ids[0]
 
-    second = lax.all_gather(jnp.concatenate([up_weight, output_weight], axis=1), BOTH, axis=0, tiled=True)
-    down_full = lax.all_gather(down_weight, BOTH, axis=0, tiled=True)
-    up_full, output_full = second[:, :hidden], second[:, hidden:]
+    second = lax.all_gather(
+        jnp.concatenate([up_weight, output_weight] + [down_weight[n * own : (n + 1) * own] for n in range(ratio)], axis=1),
+        BOTH,
+        axis=0,
+        tiled=True,
+    )
+    up_full, output_full = second[:, :hidden], second[:, hidden : hidden + width]
+    down_full = jnp.stack(
+        [second[:, hidden + n * width : hidden + (n + 1) * width].reshape(devices, own, width) for n in range(1, 1 + ratio)],
+        axis=1,
+    ).reshape(hidden, width)
 
     token_chunks = gather_relative(tokens, "ctx")
     vectors = [
@@ -391,17 +410,21 @@
     vector_grads = jnp.stack(
         [output_shift_grad, gain_one_grad, bias_one_grad, down_shift_grad, gain_two_grad, bias_two_grad]
     )
-    up_shift_grad = up_shift_grad.reshape(devices, ratio, own).transpose(1, 0, 2).reshape(ratio, width)
-    vector_grads = jnp.concatenate([vector_grads, up_shift_grad])
-    vector_grads = jnp.pad(vector_grads, ((0, 128 - vector_grads.shape[0]), (0, 0))).T.astype(bf16)
-    rest_grad = jnp.concatenate([output_grad, lax.optimization_barrier(vector_grads)], axis=1)
+    vector_grads = lax.optimization_barrier(vector_grads).reshape(6, devices, own).transpose(1, 0, 2).reshape(devices, 6 * own)
+    vector_grads = jnp.concatenate([vector_grads, up_shift_grad.reshape(devices, ratio * own)], axis=1)
+    vector_grads = jnp.pad(vector_grads, ((0, 0), (0, width - vector_grads.shape[1]))).astype(bf16)
+    extra = 8
+    rest_grad = jnp.concatenate(
+        [output_grad.reshape(devices, own, width), jnp.broadcast_to(vector_grads[:, None], (devices, extra, width))],
+        axis=1,
+    )
 
     dp_names, ctx_names = [("dp", b) for b in bits(dp)], [("ctx", b) for b in bits(ctx)]
     names = dp_names[::-1] + ctx_names[::-1]
     core, turn, rest = ctx_names[0], dp_names[:2] + ctx_names[1:], dp_names[2:]
     whole = {}
-    for label, array, height in (("down", down_grad, ratio * own), ("up", up_grad, own), ("rest", rest_grad, own)):
-        size = (height, array.shape[1])
+    for label, array, height in (("down", down_grad, ratio * own), ("up", up_grad, own), ("rest", rest_grad, own + extra)):
+        size = (height, array.shape[-1])
         whole[label] = Halving(names, size)
         whole[label].terms = [(array.reshape([2] * len(names) + list(size)), names, [(0, d) for d in size])]
         whole[label].exchange(core)
@@ -418,7 +441,7 @@
         stream("down", [(0, tall), (0, width)], 0),
         stream("up", [(0, own), (most, hidden)], 1),
         stream("down", [(tall, ratio * own), (0, width)], 1),
-        stream("rest", [(0, own), (0, width + 128)], 1),
+        stream("rest", [(0, own + extra), (0, width)], 1),
     ]
 
     grad_attended = nt(grad_branch, output_full).astype(bf16)
@@ -506,12 +529,11 @@
     up_left, down_left, up_right, down_right, rest_left = [s.result() for s, _ in streams]
     up_weight_grad = jnp.concatenate([up_left, up_right], axis=1)
     down_weight_grad = jnp.concatenate([down_left, down_right])
-    output_weight_grad = rest_left[:, :width]
-    vector_grads = rest_left[:, width:].T
+    output_weight_grad, vector_grads = rest_left[:own], rest_left[own]
     output_bias_grad, mixing_gain_grad, mixing_bias_grad, down_bias_grad, final_gain_grad, final_bias_grad = [
-        vector_grads[n] for n in range(6)
+        vector_grads[n * own : (n + 1) * own] for n in range(6)
     ]
-    up_bias_grad = vector_grads[6 : 6 + ratio].reshape(ratio * own)
+    up_bias_grad = vector_grads[6 * own : (6 + ratio) * own]
 
     mine = (me_dp * ctx + me) * own
     row_sums = jnp.sum(message[:, :, :width], axis=0)

time: 555 us -> 545 us (0.982)
  Pallas kernels: 103 us -> 82.4 us
  waiting for transfers between devices: 173 us -> 188 us
  starting transfers between devices: 56 us -> 47.9 us
  matrix products: 78.9 us -> 84.7 us
    pallas_call x1, Pallas kernels: 48.4 us -> 27.9 us  [attention_forward(): pl.pallas_call(functools.partial(forward_kernel, per_chunk, heads // 2),...]
    ppermute x59, waiting for transfers between devices: 173 us -> 188 us  [swap(): return lax.ppermute(value, axis, [(i, i ^ mask) for i in range(size)])]
    ppermute x59, starting transfers between devices: 56 us -> 47.9 us  [swap(): return lax.ppermute(value, axis, [(i, i ^ mask) for i in range(size)])]
    dot_general x7, matrix products: 25.5 us -> 31.3 us  [nt(): lax.dot_general(left, right, (((1,), (1,)), ((), ())), preferred_element_...]
    unnamed x125 -> x134, local copies, waits for them, and re-layouts: 19.9 us -> 20.1 us
  transfers between devices with their start and end apart: 61 -> 60, of which waited for: 27 -> 26; matrix products, arithmetic and copies ran while one was open for 21% -> 15% of each run, Pallas kernels for 19% -> 15%
where the time goes in v5:
time: 545 us; the launch traced here: 535 us
  waiting for transfers between devices  188 us (34%)
  matrix products  84.7 us (16%)
  Pallas kernels  82.4 us (15%)
  other arithmetic  70.9 us (13%)
  starting transfers between devices  47.9 us (9%)
  local copies, waits for them, and re-layouts  45.7 us (8%)
  between operations  15.7 us (3%)
    ppermute x59, waiting for transfers between devices, swap(): return lax.ppermute(value, axis, [(i, i ^ mask) for i in range(size)])  188 us
    pallas_call x2, Pallas kernels, attention_backward(): pl.pallas_call(functools.partial(backward_kernel, per_chunk, 2 * pair), g...  54.6 us
    ppermute x59, starting transfers between devices, swap(): return lax.ppermute(value, axis, [(i, i ^ mask) for i in range(size)])  47.9 us
    convert_element_type x24, other arithmetic, outgoing(): return self.total({**self.fixed, name: 1 - self.me[name]}).astype(bf16)  41.8 us
    dot_general x7, matrix products, nt(): lax.dot_general(left, right, (((1,), (1,)), ((), ())), preferred_element_...  31.3 us
    pallas_call x1, Pallas kernels, attention_forward(): pl.pallas_call(functools.partial(forward_kernel, per_chunk, heads // 2),...  27.9 us
    dot_general x5, matrix products, nn(): return jnp.dot(left, right, preferred_element_type=f32)  27.1 us
    dot_general x5, matrix products, tn(): lax.dot_general(left, right, (((0,), (0,)), ((), ())), preferred_element_...  24.4 us
  transfers between devices with their start and end apart: 60, of which 26 were waited for; matrix products, arithmetic and copies ran while one was open for 15% of the time, Pallas kernels for 15%

profile of v5, /device:TPU:0, one launch (start us, length us, event | category | flops | bytes accessed | tf_op | source)
XLA Modules:
  0.0 535.4 jit_solution(607395729787416280)
XLA Ops:
  29.3 25.0 %collective-permute-done.3 = bf16[1,128,1152]{2,1,0:T(8,128)(2,1)S(1)} collective-permute-done((bf16[1,128,1152]{2,1,0:T(8,128)(2,1)S(1)}, bf16[1,128,1152]{2,1,0:T(8,128)(2,1)S(1)}, u32[]{:S(2)}, u32[]{:S(2)}) %collective-permute-start.3) | collective-permute-done | bytes 294944 | tf_op jit(solution)/shard_map/ppermute | solution.py:224
  54.4 39.1 %collective-permute-done.4 = bf16[2,128,1152]{2,1,0:T(8,128)(2,1)S(1)} collective-permute-done((bf16[2,128,1152]{2,1,0:T(8,128)(2,1)S(1)}, bf16[2,128,1152]{2,1,0:T(8,128)(2,1)S(1)}, u32[]{:S(2)}, u32[]{:S(2)}) %collective-permute-start.4) | collective-permute-done | bytes 589856 | tf_op jit(solution)/shard_map/ppermute | solution.py:224
  104.9 32.8 %collective-permute-done.10 = bf16[512,1024]{1,0:T(8,128)(2,1)} collective-permute-done((bf16[512,1024]{1,0:T(8,128)(2,1)}, bf16[512,1024]{1,0:T(8,128)(2,1)}, u32[]{:S(2)}, u32[]{:S(2)}) %collective-permute-start.10) | collective-permute-done | bytes 1048608 | tf_op jit(solution)/shard_map/ppermute | solution.py:224
  148.2 7.4 %add_convert_fusion.1.qkv_ref.q_ref.k_ref.v_ref = bf16[2048,768]{1,0:T(8,128)(2,1)} fusion(f32[768]{0:T(1024)S(1)} %constant_dynamic-update-slice_fusion.69, bf16[1024,1152]{0,1:T(8,128)(2,1)S(1)} %bitcast_dynamic-update-slice_fusion, bf16[512,1024]{1,0:T(8,128)(2,1)} %collective-permute-done.11, bf16[512,1024]{1,0:T(8,128)(2,1)} %collective-permute-done.10, ...), kind=kOutput, calls=%fused_computation.23 | convolution fusion | flops 3245342720 | bytes 8921088 | tf_op jit(solution)/shard_map/dot_general | solution.py:21
  155.6 27.9 %attention_forward.1 = (bf16[2048,256]{1,0:T(8,128)(2,1)}, f32[8,4,256]{2,1,0:T(4,128)}) custom-call(s32[3,8]{1,0:T(4,128)} %add_add_fusion.2.info, bf16[2048,768]{1,0:T(8,128)(2,1)} %add_convert_fusion.1.qkv_ref.q_ref.k_ref.v_ref, s32[2048,1]{1,0:T(8,128)} %copy.207.idc_ref, s32[8,1,256]{2,1,0:T(1,128)} %bitcast.676), custom_call_target="tpu_custom_call" | custom-call | flops 30000001024 | bytes 3145728 | tf_op jit(solution)/shard_map/attention_forward/pallas_call | solution.py:95
  187.3 7.3 %collective-permute-done.13 = bf16[512,256]{1,0:T(8,128)(2,1)S(1)} collective-permute-done((bf16[512,256]{1,0:T(8,128)(2,1)S(1)}, bf16[512,256]{1,0:T(8,128)(2,1)S(1)}, u32[]{:S(2)}, u32[]{:S(2)}) %collective-permute-start.13) | collective-permute-done | bytes 262176 | tf_op jit(solution)/shard_map/ppermute | solution.py:224
  203.3 11.3 %fusion.4 = (bf16[512,4096]{1,0:T(8,128)(2,1)}, bf16[512,4096]{1,0:T(8,128)(2,1)S(1)}) fusion(f32[4096]{0:T(1024)S(1)} %add.536, bf16[1024,9216]{1,0:T(8,128)(2,1)} %all-gather.2.cloned.1.call-done, f32[512,1024]{1,0:T(8,128)S(1)} %get-tuple-element.328, f32[1024]{0:T(1024)S(1)} %bitcast.704, f32[1024]{0:T(1024)S(1)} %bitcast.691, ...), kind=kOutput, calls=%fused_computation.5 | convolution fusion | flops 4322754560 | bytes 18903040 | tf_op jit(solution)/shard_map/dot_general | solution.py:21
  214.6 3.9 fusion.131
  220.2 4.8 fusion.139
  229.5 5.1 convolution_convert_fusion
  234.6 14.7 %fusion.140 = (bf16[4096]{0:T(1024)(128)(2,1)S(1)}, bf16[512,4096]{1,0:T(8,128)(2,1)}) fusion(bf16[512,4096]{1,0:T(8,128)(2,1)} %get-tuple-element.104, bf16[4096,1024]{1,0:T(8,128)(2,1)} %bitcast.643, f32[512,1024]{1,0:T(8,128)} %copy-done.9), kind=kOutput, calls=%fused_computation.460 | convolution fusion | flops 4303876096 | bytes 18882560 | tf_op jit(solution)/shard_map/dot_general | solution.py:29
  252.5 7.2 %convolution_convert_fusion.1 = bf16[1024,4096]{1,0:T(8,128)(2,1)S(1)} fusion(bf16[512,4096]{1,0:T(8,128)(2,1)} %get-tuple-element.333, f32[512,1024]{1,0:T(8,128)S(1)} %get-tuple-element.328, f32[1024]{0:T(1024)S(1)} %bitcast.706, f32[1024]{0:T(1024)S(1)} %bitcast.693, f32[512]{0:T(512)S(1)} %add_rsqrt_fusion.1, f32[512]{0:T(512)S(1)} %broadcast_multiply_fusion.5), kind=kOutput, calls=%fused_computation.18 | convolution fusion | flops 4301783040 | bytes 14692352 | tf_op jit(solution)/shard_map/dot_general | solution.py:25
  267.0 8.3 %multiply_reduce_fusion = (f32[1024]{0:T(1024)S(1)}, f32[512]{0:T(512)S(1)}, f32[512]{0:T(512)S(1)}, f32[1024]{0:T(1024)S(1)}, f32[512,1024]{1,0:T(8,128)S(1)}) fusion(f32[512,1024]{1,0:T(8,128)S(1)} %get-tuple-element.328, f32[512]{0:T(512)S(1)} %add_rsqrt_fusion.1, f32[512]{0:T(512)S(1)} %broadcast_multiply_fusion.5, f32[1024]{0:T(1024)S(1)} %bitcast.694, ...), kind=kOutput, calls=%fused_computation.53 | convolution fusion | flops 4300207104 | bytes 18894848 | tf_op jit(solution)/shard_map/dot_general | solution.py:29
  288.7 6.8 %collective-permute-done.19 = bf16[512,256]{1,0:T(8,128)(2,1)} collective-permute-done((bf16[512,256]{1,0:T(8,128)(2,1)S(1)}, bf16[512,256]{1,0:T(8,128)(2,1)}, u32[]{:S(2)}, u32[]{:S(2)}) %collective-permute-start.19) | collective-permute-done | bytes 262176 | tf_op jit(solution)/shard_map/ppermute | solution.py:224
  295.5 4.5 collective-permute-done.20
  318.7 27.2 %attention_backward.2 = bf16[2048,384]{1,0:T(8,128)(2,1)} custom-call(s32[3,8]{1,0:T(4,128)} %add_add_fusion.2.info, bf16[2048,768]{1,0:T(8,128)(2,1)} %add_convert_fusion.1.qkv_ref.q_ref.k_ref.v_ref, bf16[2048,768]{1,0:T(8,128)(2,1)} %add_convert_fusion.1.qkv_ref.q_ref.k_ref.v_ref, bf16[2048,768]{1,0:T(8,128)(2,1)} %add_convert_fusion.1.qkv_ref.q_ref.k_ref.v_ref, ...), custom_call_target="tpu_custom_call" | custom-call | flops 24999999488 | bytes 2097152 | tf_op jit(solution)/shard_map/attention_backward/pallas_call | solution.py:181
  345.9 10.3 %collective-permute-done.24 = bf16[2,2,2,32,1024]{4,3,2,1,0:T(8,128)(2,1)} collective-permute-done((bf16[2,2,2,32,1024]{4,3,2,1,0:T(8,128)(2,1)}, bf16[2,2,2,32,1024]{4,3,2,1,0:T(8,128)(2,1)}, u32[]{:S(2)}, u32[]{:S(2)}) %collective-permute-start.24) | collective-permute-done | bytes 524320 | tf_op jit(solution)/shard_map/ppermute | solution.py:224
  356.2 4.9 fusion.128
  376.4 27.4 %attention_backward.3 = bf16[2048,384]{1,0:T(8,128)(2,1)} custom-call(s32[3,8]{1,0:T(4,128)} %add_add_fusion.2.info, bf16[2048,768]{1,0:T(8,128)(2,1)} %add_convert_fusion.1.qkv_ref.q_ref.k_ref.v_ref, bf16[2048,768]{1,0:T(8,128)(2,1)} %add_convert_fusion.1.qkv_ref.q_ref.k_ref.v_ref, bf16[2048,768]{1,0:T(8,128)(2,1)} %add_convert_fusion.1.qkv_ref.q_ref.k_ref.v_ref, ...), custom_call_target="tpu_custom_call" | custom-call | flops 24999999488 | bytes 2097152 | tf_op jit(solution)/shard_map/attention_backward/pallas_call | solution.py:181
  407.8 10.0 %collective-permute-done.29 = bf16[2,2,32,1024]{3,2,1,0:T(8,128)(2,1)S(1)} collective-permute-done((bf16[2,2,32,1024]{3,2,1,0:T(8,128)(2,1)}, bf16[2,2,32,1024]{3,2,1,0:T(8,128)(2,1)S(1)}, u32[]{:S(2)}, u32[]{:S(2)}) %collective-permute-start.29) | collective-permute-done | bytes 262176 | tf_op jit(solution)/shard_map/ppermute | solution.py:224
  420.1 4.1 fusion.127
  441.9 5.5 %collective-permute-done.35 = bf16[2,32,1024]{2,1,0:T(8,128)(2,1)S(1)} collective-permute-done((bf16[2,32,1024]{2,1,0:T(8,128)(2,1)S(1)}, bf16[2,32,1024]{2,1,0:T(8,128)(2,1)S(1)}, u32[]{:S(2)}, u32[]{:S(2)}) %collective-permute-start.35) | collective-permute-done | bytes 131104 | tf_op jit(solution)/shard_map/ppermute | solution.py:224
  475.9 13.0 %collective-permute-done.42 = bf16[128,384]{1,0:T(8,128)(2,1)S(1)} collective-permute-done((bf16[128,384]{1,0:T(8,128)(2,1)S(1)}, bf16[128,384]{1,0:T(8,128)(2,1)S(1)}, u32[]{:S(2)}, u32[]{:S(2)}) %collective-permute-start.42) | collective-permute-done | bytes 98336 | tf_op jit(solution)/shard_map/ppermute | solution.py:224
  496.9 8.2 %collective-permute-done.50 = bf16[40,1024]{1,0:T(8,128)(2,1)S(1)} collective-permute-done((bf16[40,1024]{1,0:T(8,128)(2,1)}, bf16[40,1024]{1,0:T(8,128)(2,1)S(1)}, u32[]{:S(2)}, u32[]{:S(2)}) %collective-permute-start.50) | collective-permute-done | bytes 81952 | tf_op jit(solution)/shard_map/ppermute | solution.py:224
  (386 shorter events, 203.0 us)
Async XLA Ops:
  7.2 192.3 %all-gather.2.cloned.1.call-start = ((), (), s32[]{:S(2)}) async-start(), calls=%async_computation | async-start | bytes 19464192 | tf_op jit(solution)/shard_map/all_gather | solution.py:325
  26.5 27.8 %collective-permute-start.3 = (bf16[1,128,1152]{2,1,0:T(8,128)(2,1)S(1)}, bf16[1,128,1152]{2,1,0:T(8,128)(2,1)S(1)}, u32[]{:S(2)}, u32[]{:S(2)}) collective-permute-start(bf16[1,128,1152]{2,1,0:T(8,128)(2,1)S(1)} %maximum_bitcast_fusion), channel_id=1, source_target_pairs={{0,16},{4,20},{8,24},{12,28},{16,0},{20,4},{24,8},{28,12},{1,17},{... | collective-permute-start | bytes 884744 | tf_op jit(solution)/shard_map/ppermute | solution.py:224
  54.3 39.2 %collective-permute-start.4 = (bf16[2,128,1152]{2,1,0:T(8,128)(2,1)S(1)}, bf16[2,128,1152]{2,1,0:T(8,128)(2,1)S(1)}, u32[]{:S(2)}, u32[]{:S(2)}) collective-permute-start(bf16[2,128,1152]{2,1,0:T(8,128)(2,1)S(1)} %pad_maximum_fusion.6), channel_id=1, source_target_pairs={{0,8},{4,12},{8,0},{12,4},{16,24},{20,28},{24,16},{28,20},{1,9},{5... | collective-permute-start | bytes 1769480 | tf_op jit(solution)/shard_map/ppermute | solution.py:224
  93.7 45.9 %collective-permute-start.5 = (bf16[4,128,1152]{2,1,0:T(8,128)(2,1)S(1)}, bf16[4,128,1152]{2,1,0:T(8,128)(2,1)S(1)}, u32[]{:S(2)}, u32[]{:S(2)}) collective-permute-start(bf16[4,128,1152]{2,1,0:T(8,128)(2,1)S(1)} %pad_maximum_fusion.2), channel_id=1, source_target_pairs={{0,4},{4,0},{8,12},{12,8},{16,20},{20,16},{24,28},{28,24},{1,5},{5... | collective-permute-start | bytes 3538952 | tf_op jit(solution)/shard_map/ppermute | solution.py:224
  95.2 42.6 %collective-permute-start.10 = (bf16[512,1024]{1,0:T(8,128)(2,1)}, bf16[512,1024]{1,0:T(8,128)(2,1)}, u32[]{:S(2)}, u32[]{:S(2)}) collective-permute-start(bf16[512,1024]{1,0:T(8,128)(2,1)} %bitcast), channel_id=1, source_target_pairs={{0,2},{1,3},{2,0},{3,1},{4,6},{5,7},{6,4},{7,5},{8,10},{9,11},{10,... | collective-permute-start | bytes 3145736 | tf_op jit(solution)/shard_map/ppermute | solution.py:224
  96.7 51.4 %collective-permute-start.9 = (bf16[512,1024]{1,0:T(8,128)(2,1)}, bf16[512,1024]{1,0:T(8,128)(2,1)}, u32[]{:S(2)}, u32[]{:S(2)}) collective-permute-start(bf16[512,1024]{1,0:T(8,128)(2,1)} %bitcast), channel_id=1, source_target_pairs={{0,1},{1,0},{2,3},{3,2},{4,5},{5,4},{6,7},{7,6},{8,9},{9,8},{10,11... | collective-permute-start | bytes 3145736 | tf_op jit(solution)/shard_map/ppermute | solution.py:224
  251.8 52.6 %collective-permute-start.16 = (bf16[2,2,2,2,128,1024]{5,4,3,2,1,0:T(8,128)(2,1)}, bf16[2,2,2,2,128,1024]{5,4,3,2,1,0:T(8,128)(2,1)}, u32[]{:S(2)}, u32[]{:S(2)}) collective-permute-start(bf16[2,2,2,2,128,1024]{5,4,3,2,1,0:T(8,128)(2,1)} %dynamic-slice_bitcast_fusion), channel_id=1, source_target_pairs={{0,1},{1,0},{2,3},{3,2},{4,5},{5,4},{6,7},{7,6},{8,9},{9,8},{10,11... | collective-permute-start | bytes 12582920 | tf_op jit(solution)/shard_map/ppermute | solution.py:224
  266.0 40.7 %collective-permute-start.15 = (bf16[2,2,2,2,32,4096]{5,4,3,2,1,0:T(8,128)(2,1)}, bf16[2,2,2,2,32,4096]{5,4,3,2,1,0:T(8,128)(2,1)}, u32[]{:S(2)}, u32[]{:S(2)}) collective-permute-start(bf16[2,2,2,2,32,4096]{5,4,3,2,1,0:T(8,128)(2,1)} %dynamic-slice_bitcast_fusion.1), channel_id=1, source_target_pairs={{0,1},{1,0},{2,3},{3,2},{4,5},{5,4},{6,7},{7,6},{8,9},{9,8},{10,11... | collective-permute-start | bytes 12582920 | tf_op jit(solution)/shard_map/ppermute | solution.py:224
  282.1 20.0 %collective-permute-start.17 = (bf16[2,2,2,2,40,1024]{5,4,3,2,1,0:T(8,128)(2,1)}, bf16[2,2,2,2,40,1024]{5,4,3,2,1,0:T(8,128)(2,1)}, u32[]{:S(2)}, u32[]{:S(2)}) collective-permute-start(bf16[2,2,2,2,40,1024]{5,4,3,2,1,0:T(8,128)(2,1)} %fusion.34), channel_id=1, source_target_pairs={{0,1},{1,0},{2,3},{3,2},{4,5},{5,4},{6,7},{7,6},{8,9},{9,8},{10,11... | collective-permute-start | bytes 3932168 | tf_op jit(solution)/shard_map/ppermute | solution.py:224
  316.2 40.0 %collective-permute-start.21 = (bf16[2,2,2,32,3072]{4,3,2,1,0:T(8,128)(2,1)}, bf16[2,2,2,32,3072]{4,3,2,1,0:T(8,128)(2,1)}, u32[]{:S(2)}, u32[]{:S(2)}) collective-permute-start(bf16[2,2,2,32,3072]{4,3,2,1,0:T(8,128)(2,1)} %fusion.10), channel_id=1, source_target_pairs={{0,2},{1,3},{2,0},{3,1},{4,6},{5,7},{6,4},{7,5},{8,10},{9,11},{10,... | collective-permute-start | bytes 4718600 | tf_op jit(solution)/shard_map/ppermute | solution.py:224
  316.7 39.5 %collective-permute-start.22 = (bf16[2,2,2,96,1024]{4,3,2,1,0:T(8,128)(2,1)}, bf16[2,2,2,96,1024]{4,3,2,1,0:T(8,128)(2,1)}, u32[]{:S(2)}, u32[]{:S(2)}) collective-permute-start(bf16[2,2,2,96,1024]{4,3,2,1,0:T(8,128)(2,1)} %fusion.9), channel_id=1, source_target_pairs={{0,4},{4,0},{8,12},{12,8},{16,20},{20,16},{24,28},{28,24},{1,5},{5... | collective-permute-start | bytes 4718600 | tf_op jit(solution)/shard_map/ppermute | solution.py:224
  316.7 39.5 %collective-permute-start.25 = (bf16[2,2,2,40,1024]{4,3,2,1,0:T(8,128)(2,1)}, bf16[2,2,2,40,1024]{4,3,2,1,0:T(8,128)(2,1)S(1)}, u32[]{:S(2)}, u32[]{:S(2)}) collective-permute-start(bf16[2,2,2,40,1024]{4,3,2,1,0:T(8,128)(2,1)} %fusion.35), channel_id=1, source_target_pairs={{0,8},{4,12},{8,0},{12,4},{16,24},{20,28},{24,16},{28,20},{1,9},{5... | collective-permute-start | bytes 1966088 | tf_op jit(solution)/shard_map/ppermute | solution.py:224
  316.7 29.2 %collective-permute-start.23 = (bf16[2,2,2,32,1024]{4,3,2,1,0:T(8,128)(2,1)}, bf16[2,2,2,32,1024]{4,3,2,1,0:T(8,128)(2,1)}, u32[]{:S(2)}, u32[]{:S(2)}) collective-permute-start(bf16[2,2,2,32,1024]{4,3,2,1,0:T(8,128)(2,1)} %fusion.41), channel_id=1, source_target_pairs={{0,8},{4,12},{8,0},{12,4},{16,24},{20,28},{24,16},{28,20},{1,9},{5... | collective-permute-start | bytes 1572872 | tf_op jit(solution)/shard_map/ppermute | solution.py:224
  318.7 37.5 %collective-permute-start.24 = (bf16[2,2,2,32,1024]{4,3,2,1,0:T(8,128)(2,1)}, bf16[2,2,2,32,1024]{4,3,2,1,0:T(8,128)(2,1)}, u32[]{:S(2)}, u32[]{:S(2)}) collective-permute-start(bf16[2,2,2,32,1024]{4,3,2,1,0:T(8,128)(2,1)} %fusion.40), channel_id=1, source_target_pairs={{0,8},{4,12},{8,0},{12,4},{16,24},{20,28},{24,16},{28,20},{1,9},{5... | collective-permute-start | bytes 1572872 | tf_op jit(solution)/shard_map/ppermute | solution.py:224
  371.8 46.0 %collective-permute-start.26 = (bf16[2,2,32,3072]{3,2,0,1:T(8,128)(2,1)S(1)}, bf16[2,2,32,3072]{3,2,0,1:T(8,128)(2,1)}, u32[]{:S(2)}, u32[]{:S(2)}) collective-permute-start(bf16[2,2,32,3072]{3,2,0,1:T(8,128)(2,1)S(1)} %copy.230), channel_id=1, source_target_pairs={{0,4},{4,0},{8,12},{12,8},{16,20},{20,16},{24,28},{28,24},{1,5},{5... | collective-permute-start | bytes 2359304 | tf_op jit(solution)/shard_map/ppermute | solution.py:224
  374.5 43.3 %collective-permute-start.27 = (bf16[2,2,96,1024]{3,2,0,1:T(8,128)(2,1)}, bf16[2,2,96,1024]{3,2,0,1:T(8,128)(2,1)}, u32[]{:S(2)}, u32[]{:S(2)}) collective-permute-start(bf16[2,2,96,1024]{3,2,0,1:T(8,128)(2,1)} %copy.231), channel_id=1, source_target_pairs={{0,8},{4,12},{8,0},{12,4},{16,24},{20,28},{24,16},{28,20},{1,9},{5... | collective-permute-start | bytes 2359304 | tf_op jit(solution)/shard_map/ppermute | solution.py:224
  374.8 29.6 %collective-permute-start.28 = (bf16[2,2,32,1024]{3,2,1,0:T(8,128)(2,1)}, bf16[2,2,32,1024]{3,2,1,0:T(8,128)(2,1)}, u32[]{:S(2)}, u32[]{:S(2)}) collective-permute-start(bf16[2,2,32,1024]{3,2,1,0:T(8,128)(2,1)} %fusion.71), channel_id=1, source_target_pairs={{0,2},{1,3},{2,0},{3,1},{4,6},{5,7},{6,4},{7,5},{8,10},{9,11},{10,... | collective-permute-start | bytes 786440 | tf_op jit(solution)/shard_map/ppermute | solution.py:224
  432.9 24.5 %collective-permute-start.39 = (bf16[512,1024]{1,0:T(8,128)(2,1)S(1)}, bf16[512,1024]{1,0:T(8,128)(2,1)}, u32[]{:S(2)}, u32[]{:S(2)}) collective-permute-start(bf16[512,1024]{1,0:T(8,128)(2,1)S(1)} %convolution_convert_fusion.4), channel_id=1, source_target_pairs={{0,1},{1,0},{2,3},{3,2},{4,5},{5,4},{6,7},{7,6},{8,9},{9,8},{10,11... | collective-permute-start | bytes 3145736 | tf_op jit(solution)/shard_map/ppermute | solution.py:224
  432.9 24.4 %collective-permute-start.40 = (bf16[512,1024]{1,0:T(8,128)(2,1)S(1)}, bf16[512,1024]{1,0:T(8,128)(2,1)S(1)}, u32[]{:S(2)}, u32[]{:S(2)}) collective-permute-start(bf16[512,1024]{1,0:T(8,128)(2,1)S(1)} %convolution_convert_fusion.3), channel_id=1, source_target_pairs={{0,1},{1,0},{2,3},{3,2},{4,5},{5,4},{6,7},{7,6},{8,9},{9,8},{10,11... | collective-permute-start | bytes 3145736 | tf_op jit(solution)/shard_map/ppermute | solution.py:224
  468.6 37.5 %collective-permute-start.52 = (bf16[512,1024]{1,0:T(8,128)(2,1)}, bf16[512,1024]{1,0:T(8,128)(2,1)}, u32[]{:S(2)}, u32[]{:S(2)}) collective-permute-start(bf16[512,1024]{1,0:T(8,128)(2,1)} %add_convert_fusion.3), channel_id=1, source_target_pairs={{0,2},{1,3},{2,0},{3,1},{4,6},{5,7},{6,4},{7,5},{8,10},{9,11},{10,... | collective-permute-start | bytes 3145736 | tf_op jit(solution)/shard_map/ppermute | solution.py:224
  470.9 18.0 %collective-permute-start.43 = (bf16[2,128,384]{2,1,0:T(8,128)(2,1)S(1)}, bf16[2,128,384]{2,1,0:T(8,128)(2,1)S(1)}, u32[]{:S(2)}, u32[]{:S(2)}) collective-permute-start(bf16[2,128,384]{2,1,0:T(8,128)(2,1)S(1)} %fusion.78), channel_id=1, source_target_pairs={{0,8},{4,12},{8,0},{12,4},{16,24},{20,28},{24,16},{28,20},{1,9},{5... | collective-permute-start | bytes 589832 | tf_op jit(solution)/shard_map/ppermute | solution.py:224
  472.2 16.8 %collective-permute-start.42 = (bf16[128,384]{1,0:T(8,128)(2,1)S(1)}, bf16[128,384]{1,0:T(8,128)(2,1)S(1)}, u32[]{:S(2)}, u32[]{:S(2)}) collective-permute-start(bf16[128,384]{1,0:T(8,128)(2,1)S(1)} %fusion.87), channel_id=1, source_target_pairs={{0,16},{4,20},{8,24},{12,28},{16,0},{20,4},{24,8},{28,12},{1,17},{... | collective-permute-start | bytes 294920 | tf_op jit(solution)/shard_map/ppermute | solution.py:224
  473.0 17.5 %collective-permute-start.48 = (bf16[32,1024]{1,0:T(8,128)(2,1)}, bf16[32,1024]{1,0:T(8,128)(2,1)}, u32[]{:S(2)}, u32[]{:S(2)}) collective-permute-start(bf16[32,1024]{1,0:T(8,128)(2,1)} %fusion.96), channel_id=1, source_target_pairs={{0,16},{4,20},{8,24},{12,28},{16,0},{20,4},{24,8},{28,12},{1,17},{... | collective-permute-start | bytes 196616 | tf_op jit(solution)/shard_map/ppermute | solution.py:224
  475.1 18.8 %collective-permute-start.49 = (bf16[32,1024]{1,0:T(8,128)(2,1)}, bf16[32,1024]{1,0:T(8,128)(2,1)}, u32[]{:S(2)}, u32[]{:S(2)}) collective-permute-start(bf16[32,1024]{1,0:T(8,128)(2,1)} %fusion.95), channel_id=1, source_target_pairs={{0,16},{4,20},{8,24},{12,28},{16,0},{20,4},{24,8},{28,12},{1,17},{... | collective-permute-start | bytes 196616 | tf_op jit(solution)/shard_map/ppermute | solution.py:224
  (83 other events, 902.6 us)
Sparse Core Ops, SparseCore 0:
  13.5 157.0 all-gather.1

commit v6 on v5

--- a/solution.py
+++ b/solution.py
@@ -228,19 +228,6 @@
     return [1 << b for b in range(size.bit_length() - 1)]
 
 
-def gather_relative(value, axis):
-    held = {0: value}
-    for bit in reversed(bits(lax.axis_size(axis))):
-        held.update({k | bit: swap(v, axis, bit) for k, v in list(held.items())})
-    return [held[k] for k in range(len(held))]
-
-
-def gather_stacked(value, axis):
-    for bit in reversed(bits(lax.axis_size(axis))):
-        value = jnp.concatenate([value, swap(value, axis, bit)])
-    return value
-
-
 def flipped(index, size):
     flags = bits(size)
     return sum(((index >> n) & 1) << (len(flags) - 1 - n) for n in range(len(flags)))
@@ -334,7 +321,7 @@
         axis=1,
     ).reshape(hidden, width)
 
-    token_chunks = gather_relative(tokens, "ctx")
+    held = {0: tokens, ctx // 2: swap(tokens, "ctx", ctx // 2)}
     vectors = [
         time_bias, query_bias, value_bias, output_bias, mixing_gain, mixing_bias, down_bias, final_gain, final_bias
     ]
@@ -350,7 +337,14 @@
         ] + [lax.dynamic_slice_in_dim(time_weight, at, cols, 1)]
         pieces.append(jnp.concatenate(parts + [small], axis=1))
     first = jnp.concatenate(to_absolute(trade(pieces, "ctx"), me))
-    first = gather_stacked(first[None], "dp")
+    first = first[None]
+    for n, bit in enumerate(reversed(bits(dp))):
+        if n == 1:
+            first, held[ctx // 2] = lax.optimization_barrier((first, held[ctx // 2]))
+        first = jnp.concatenate([first, swap(first, "dp", bit)])
+    for bit in reversed(bits(ctx)[:-1]):
+        held.update({k | bit: swap(v, "ctx", bit) for k, v in list(held.items())})
+    token_chunks = [held[k] for k in range(ctx)]
     first = jnp.concatenate(
         [
             lax.dynamic_index_in_dim(first, flipped((me_dp ^ c), dp), 0, False)
@@ -405,6 +399,41 @@
     grad_hidden = grad_two + nt(grad_inner, up_full)
     grad_one, gain_one_grad, bias_one_grad = normalize_back(grad_hidden, normed_one, inverse_one, gain_one)
     grad_branch = grad_one.astype(bf16)
+    dp_names, ctx_names = [("dp", b) for b in bits(dp)], [("ctx", b) for b in bits(ctx)]
+    names = dp_names[::-1] + ctx_names[::-1]
+    core, turn, rest = ctx_names[0], dp_names[:2] + ctx_names[1:], dp_names[2:]
+    whole = {}
+
+    def share(label, array, height):
+        size = (height, array.shape[-1])
+        whole[label] = Halving(names, size)
+        whole[label].terms = [(array.reshape([2] * len(names) + list(size)), names, [(0, d) for d in size])]
+        whole[label].exchange(core)
+
+    def stream(label, part, turned):
+        sums = Halving(names, [high - low for low, high in part])
+        sums.fixed = {core: sums.me[core]}
+        sums.terms = [(array, left, part) for array, left, _ in whole[label].terms]
+        return sums, turn[turned:] + turn[:turned] + rest
+
+    def depart(moving, beside):
+        going = [s.outgoing(name) for s, name in moving]
+        going, beside = lax.optimization_barrier((going, beside))
+        return [(s, name, swap(value, *name)) for (s, name), value in zip(moving, going)], beside
+
+    def land(flights, beside):
+        values, beside = lax.optimization_barrier(([value for _, _, value in flights], beside))
+        for (s, name, _), value in zip(flights, values):
+            s.arrived(name, value)
+        return beside
+
+    def following(pairs):
+        return [(s, o.pop(0)) for s, o in pairs if o]
+
+    share("down", down_grad, ratio * own)
+    streams = [stream("down", [(0, ratio * own), (0, width)], 0)]
+    ahead, grad_branch = depart(following(streams), grad_branch)
+
     output_grad = tn(attended, grad_branch).astype(bf16)
     output_shift_grad = jnp.sum(grad_branch.astype(f32), axis=0)
     vector_grads = jnp.stack(
@@ -419,58 +448,25 @@
         axis=1,
     )
 
-    dp_names, ctx_names = [("dp", b) for b in bits(dp)], [("ctx", b) for b in bits(ctx)]
-    names = dp_names[::-1] + ctx_names[::-1]
-    core, turn, rest = ctx_names[0], dp_names[:2] + ctx_names[1:], dp_names[2:]
-    whole = {}
-    for label, array, height in (("down", down_grad, ratio * own), ("up", up_grad, own), ("rest", rest_grad, own + extra)):
-        size = (height, array.shape[-1])
-        whole[label] = Halving(names, size)
-        whole[label].terms = [(array.reshape([2] * len(names) + list(size)), names, [(0, d) for d in size])]
-        whole[label].exchange(core)
-
-    def stream(label, part, turned):
-        sums = Halving(names, [high - low for low, high in part])
-        sums.fixed = {core: sums.me[core]}
-        sums.terms = [(array, left, part) for array, left, _ in whole[label].terms]
-        return sums, turn[turned:] + turn[:turned] + rest
-
-    most, tall = 3 * hidden // 4, (ratio - 1) * own
-    streams = [
-        stream("up", [(0, own), (0, most)], 2),
-        stream("down", [(0, tall), (0, width)], 0),
-        stream("up", [(0, own), (most, hidden)], 1),
-        stream("down", [(tall, ratio * own), (0, width)], 1),
-        stream("rest", [(0, own + extra), (0, width)], 1),
+    share("up", up_grad, own)
+    share("rest", rest_grad, own + extra)
+    streams += [
+        stream("up", [(0, own), (0, hidden // 2)], 2),
+        stream("up", [(0, own), (hidden // 2, hidden)], 0),
+        stream("rest", [(0, own + extra), (0, width)], 0),
     ]
 
     grad_attended = nt(grad_branch, output_full).astype(bf16)
     pieces = [lax.dynamic_slice_in_dim(grad_attended, (me ^ k) * cols, cols, 1) for k in range(ctx)]
     grad_mixed = jnp.concatenate(trade(pieces, "ctx"))
+    grad_mixed = land(ahead, grad_mixed)
+
     def weight_stream(grad):
         size = (ctx * own, grad.shape[1])
         sums = Halving(dp_names[::-1], size)
         array = tn(start_row, grad).reshape([2] * len(dp_names) + list(size))
         sums.terms = [(array, dp_names[::-1], [(0, d) for d in size])]
         return sums, list(dp_names)
-
-    def start_part(k):
-        rows = slice(k * piece, (k + 1) * piece)
-        return nt(jnp.concatenate([g[rows] for g in grads], axis=1), qkv_weight)
-
-    def depart(moving, beside):
-        going = [s.outgoing(name) for s, name in moving]
-        going, beside = lax.optimization_barrier((going, beside))
-        return [(s, name, swap(value, *name)) for (s, name), value in zip(moving, going)], beside
-
-    def land(flights, beside):
-        values, beside = lax.optimization_barrier(([value for _, _, value in flights], beside))
-        for (s, name, _), value in zip(flights, values):
-            s.arrived(name, value)
-        return beside
-
-    def following(pairs):
-        return [(s, o.pop(0)) for s, o in pairs if o]
 
     grads, pair_streams = [], []
     for pair in range(cols // 128):
@@ -496,15 +492,16 @@
     )
     message_names = dp_names[::-1]
 
-    odd = [start_part(k).astype(bf16) for k in range(1, ctx, 2)]
-    flights, (grads, odd, message) = depart(following(streams + pair_streams), (grads, odd, message))
-    odd = [swap(value, *core) for value in odd]
+    rows = jnp.concatenate(grads, axis=1).reshape(ctx // 2, 2, piece, 3 * cols)
+    odd = nt(rows[:, 1].reshape(-1, 3 * cols), qkv_weight).astype(bf16)
+    flights, (rows, odd, message) = depart(following(streams + pair_streams), (rows, odd, message))
+    odd = swap(odd, *core)
     reply = swap(message, *message_names.pop(0))
-    even = [start_part(k) for k in range(0, ctx, 2)]
+    even = nt(rows[:, 0].reshape(-1, 3 * cols), qkv_weight)
     even, odd, message, reply = land(flights, (even, odd, message, reply))
     message = jnp.concatenate([message, reply])
-    even = [e + o.astype(f32) for e, o in zip(even, odd)]
-    away = [value.astype(bf16) for value in even[1:]]
+    even = (even + odd.astype(f32)).reshape(ctx // 2, piece, width)
+    away = [even[n].astype(bf16) for n in range(1, ctx // 2)]
     kept, came = [], None
     while any(o for _, o in streams + pair_streams) or message_names:
         fast, slow = following(pair_streams), following(streams)
@@ -526,9 +523,8 @@
     blocks_out = to_absolute(trade(summed, "ctx"), me)
     message = jnp.stack(trade([message] * ctx, "ctx"))
     tokens_grad = (grad_one + sum([c.astype(f32) for c in came], even[0])).astype(bf16)
-    up_left, down_left, up_right, down_right, rest_left = [s.result() for s, _ in streams]
+    down_weight_grad, up_left, up_right, rest_left = [s.result() for s, _ in streams]
     up_weight_grad = jnp.concatenate([up_left, up_right], axis=1)
-    down_weight_grad = jnp.concatenate([down_left, down_right])
     output_weight_grad, vector_grads = rest_left[:own], rest_left[own]
     output_bias_grad, mixing_gain_grad, mixing_bias_grad, down_bias_grad, final_gain_grad, final_bias_grad = [
         vector_grads[n * own : (n + 1) * own] for n in range(6)

time: 545 us -> 529 us (0.971)
  waiting for transfers between devices: 188 us -> 172 us
  starting transfers between devices: 47.9 us -> 59.2 us
  other arithmetic: 70.9 us -> 63.6 us
    ppermute x59 -> x54, waiting for transfers between devices: 188 us -> 172 us  [swap(): return lax.ppermute(value, axis, [(i, i ^ mask) for i in range(size)])]
    ppermute x59 -> x54, starting transfers between devices: 47.9 us -> 59.1 us  [swap(): return lax.ppermute(value, axis, [(i, i ^ mask) for i in range(size)])]
    convert_element_type x24 -> x16, other arithmetic: 41.8 us -> 33.7 us  [outgoing(): return self.total({**self.fixed, name: 1 - self.me[name]}).astype(bf16)]
    unnamed x134 -> x114, local copies, waits for them, and re-layouts: 20.1 us -> 18.1 us
    dot_general x7 -> x5, matrix products: 31.3 us -> 30.7 us  [nt(): lax.dot_general(left, right, (((1,), (1,)), ((), ())), preferred_element_...]
  transfers between devices with their start and end apart: 60 -> 55, of which waited for: 26 -> 22; matrix products, arithmetic and copies ran while one was open for 15% -> 16% of each run, Pallas kernels for 15% -> 16%
where the time goes in v6:
time: 529 us; the launch traced here: 520 us
  waiting for transfers between devices  172 us (33%)
  matrix products  83.2 us (16%)
  Pallas kernels  82.8 us (16%)
  other arithmetic  63.6 us (12%)
  starting transfers between devices  59.2 us (11%)
  local copies, waits for them, and re-layouts  43.8 us (8%)
  between operations  15.6 us (3%)
    ppermute x54, waiting for transfers between devices, swap(): return lax.ppermute(value, axis, [(i, i ^ mask) for i in range(size)])  172 us
    ppermute x54, starting transfers between devices, swap(): return lax.ppermute(value, axis, [(i, i ^ mask) for i in range(size)])  59.1 us
    pallas_call x2, Pallas kernels, attention_backward(): pl.pallas_call(functools.partial(backward_kernel, per_chunk, 2 * pair), g...  54.7 us
    convert_element_type x16, other arithmetic, outgoing(): return self.total({**self.fixed, name: 1 - self.me[name]}).astype(bf16)  33.7 us
    dot_general x5, matrix products, nt(): lax.dot_general(left, right, (((1,), (1,)), ((), ())), preferred_element_...  30.7 us
    pallas_call x1, Pallas kernels, attention_forward(): pl.pallas_call(functools.partial(forward_kernel, per_chunk, heads // 2),...  28.1 us
    dot_general x5, matrix products, nn(): return jnp.dot(left, right, preferred_element_type=f32)  27.1 us
    dot_general x5, matrix products, tn(): lax.dot_general(left, right, (((0,), (0,)), ((), ())), preferred_element_...  23.7 us
  transfers between devices with their start and end apart: 55, of which 22 were waited for; matrix products, arithmetic and copies ran while one was open for 16% of the time, Pallas kernels for 16%

profile of v6, /device:TPU:0, one launch (start us, length us, event | category | flops | bytes accessed | tf_op | source)
XLA Modules:
  0.0 519.9 jit_solution(6562724416861933513)
XLA Ops:
  29.4 24.8 %collective-permute-done.3 = bf16[1,128,1152]{2,1,0:T(8,128)(2,1)S(1)} collective-permute-done((bf16[1,128,1152]{2,1,0:T(8,128)(2,1)S(1)}, bf16[1,128,1152]{2,1,0:T(8,128)(2,1)S(1)}, u32[]{:S(2)}, u32[]{:S(2)}) %collective-permute-start.3) | collective-permute-done | bytes 294944 | tf_op jit(solution)/shard_map/ppermute | solution.py:224
  56.4 37.0 %collective-permute-done.5 = bf16[2,128,1152]{2,1,0:T(8,128)(2,1)S(1)} collective-permute-done((bf16[2,128,1152]{2,1,0:T(8,128)(2,1)S(1)}, bf16[2,128,1152]{2,1,0:T(8,128)(2,1)S(1)}, u32[]{:S(2)}, u32[]{:S(2)}) %collective-permute-start.5) | collective-permute-done | bytes 589856 | tf_op jit(solution)/shard_map/ppermute | solution.py:224
  99.3 37.0 %collective-permute-done.6 = bf16[4,128,1152]{2,1,0:T(8,128)(2,1)S(1)} collective-permute-done((bf16[4,128,1152]{2,1,0:T(8,128)(2,1)S(1)}, bf16[4,128,1152]{2,1,0:T(8,128)(2,1)S(1)}, u32[]{:S(2)}, u32[]{:S(2)}) %collective-permute-start.6) | collective-permute-done | bytes 1179680 | tf_op jit(solution)/shard_map/ppermute | solution.py:224
  143.3 7.4 %add_convert_fusion.1.qkv_ref.q_ref.k_ref.v_ref = bf16[2048,768]{1,0:T(8,128)(2,1)} fusion(f32[768]{0:T(1024)S(1)} %constant_dynamic-update-slice_fusion.72, bf16[1024,1152]{0,1:T(8,128)(2,1)S(1)} %bitcast_dynamic-update-slice_fusion, bf16[512,1024]{1,0:T(8,128)(2,1)} %collective-permute-done.11, bf16[512,1024]{1,0:T(8,128)(2,1)} %collective-permute-done.4, ...), kind=kOutput, calls=%fused_computation.23 | convolution fusion | flops 3245342720 | bytes 8921088 | tf_op jit(solution)/shard_map/dot_general | solution.py:21
  150.7 28.1 %attention_forward.1 = (bf16[2048,256]{1,0:T(8,128)(2,1)}, f32[8,4,256]{2,1,0:T(4,128)}) custom-call(s32[3,8]{1,0:T(4,128)} %add_add_fusion.2.info, bf16[2048,768]{1,0:T(8,128)(2,1)} %add_convert_fusion.1.qkv_ref.q_ref.k_ref.v_ref, s32[2048,1]{1,0:T(8,128)} %copy.186.idc_ref, s32[8,1,256]{2,1,0:T(1,128)} %bitcast.608), custom_call_target="tpu_custom_call" | custom-call | flops 30000001024 | bytes 3145728 | tf_op jit(solution)/shard_map/attention_forward/pallas_call | solution.py:95
  182.8 5.3 %collective-permute-done.14 = bf16[512,256]{1,0:T(8,128)(2,1)S(1)} collective-permute-done((bf16[512,256]{1,0:T(8,128)(2,1)S(1)}, bf16[512,256]{1,0:T(8,128)(2,1)S(1)}, u32[]{:S(2)}, u32[]{:S(2)}) %collective-permute-start.14) | collective-permute-done | bytes 262176 | tf_op jit(solution)/shard_map/ppermute | solution.py:224
  188.1 6.3 %collective-permute-done.13 = bf16[512,256]{1,0:T(8,128)(2,1)S(1)} collective-permute-done((bf16[512,256]{1,0:T(8,128)(2,1)S(1)}, bf16[512,256]{1,0:T(8,128)(2,1)S(1)}, u32[]{:S(2)}, u32[]{:S(2)}) %collective-permute-start.13) | collective-permute-done | bytes 262176 | tf_op jit(solution)/shard_map/ppermute | solution.py:224
  198.4 11.4 %fusion.4 = (bf16[512,4096]{1,0:T(8,128)(2,1)}, bf16[512,4096]{1,0:T(8,128)(2,1)S(1)}) fusion(f32[4096]{0:T(1024)S(1)} %add.488, bf16[1024,9216]{1,0:T(8,128)(2,1)} %all-gather.2.cloned.1.call-done, f32[512,1024]{1,0:T(8,128)S(1)} %get-tuple-element.313, f32[1024]{0:T(1024)S(1)} %bitcast.636, f32[1024]{0:T(1024)S(1)} %bitcast.618, ...), kind=kOutput, calls=%fused_computation.5 | convolution fusion | flops 4322754560 | bytes 18903040 | tf_op jit(solution)/shard_map/dot_general | solution.py:21
  215.4 4.8 fusion.111
  224.7 5.1 convolution_convert_fusion.1
  229.8 14.7 %fusion.112 = (bf16[4096]{0:T(1024)(128)(2,1)S(1)}, bf16[512,4096]{1,0:T(8,128)(2,1)}) fusion(bf16[512,4096]{1,0:T(8,128)(2,1)} %get-tuple-element.98, bf16[4096,1024]{1,0:T(8,128)(2,1)} %bitcast.573, f32[512,1024]{1,0:T(8,128)} %copy-done.10), kind=kOutput, calls=%fused_computation.420 | convolution fusion | flops 4303876096 | bytes 18882560 | tf_op jit(solution)/shard_map/dot_general | solution.py:29
  247.0 7.3 %convolution_convert_fusion = bf16[1024,4096]{1,0:T(8,128)(2,1)S(1)} fusion(bf16[512,4096]{1,0:T(8,128)(2,1)} %get-tuple-element.318, f32[512,1024]{1,0:T(8,128)S(1)} %get-tuple-element.313, f32[1024]{0:T(1024)S(1)} %bitcast.638, f32[1024]{0:T(1024)S(1)} %bitcast.620, f32[512]{0:T(512)S(1)} %add_rsqrt_fusion.1, f32[512]{0:T(512)S(1)} %broadcast_multiply_fusion.5), kind=kOutput, calls=%fused_computation.17 | convolution fusion | flops 4301783040 | bytes 14692352 | tf_op jit(solution)/shard_map/dot_general | solution.py:25
  259.5 9.2 %multiply_reduce_fusion = (f32[1024]{0:T(1024)S(1)}, f32[512]{0:T(512)S(1)}, f32[512]{0:T(512)S(1)}, f32[1024]{0:T(1024)S(1)}, f32[512,1024]{1,0:T(8,128)S(1)}) fusion(f32[512,1024]{1,0:T(8,128)S(1)} %get-tuple-element.313, f32[512]{0:T(512)S(1)} %add_rsqrt_fusion.1, f32[512]{0:T(512)S(1)} %broadcast_multiply_fusion.5, f32[1024]{0:T(1024)S(1)} %bitcast.621, ...), kind=kOutput, calls=%fused_computation.61 | convolution fusion | flops 4300207104 | bytes 18894848 | tf_op jit(solution)/shard_map/dot_general | solution.py:29
  287.8 4.4 fusion.21
  293.8 6.1 %collective-permute-done.18 = bf16[512,256]{1,0:T(8,128)(2,1)S(1)} collective-permute-done((bf16[512,256]{1,0:T(8,128)(2,1)S(1)}, bf16[512,256]{1,0:T(8,128)(2,1)S(1)}, u32[]{:S(2)}, u32[]{:S(2)}) %collective-permute-start.18) | collective-permute-done | bytes 262176 | tf_op jit(solution)/shard_map/ppermute | solution.py:224
  303.2 20.7 %collective-permute-done.16 = bf16[2,2,2,128,1024]{4,3,0,2,1:T(8,128)(2,1)} collective-permute-done((bf16[2,2,2,128,1024]{4,3,0,2,1:T(8,128)(2,1)}, bf16[2,2,2,128,1024]{4,3,0,2,1:T(8,128)(2,1)}, u32[]{:S(2)}, u32[]{:S(2)}) %collective-permute-start.16) | collective-permute-done | bytes 2097184 | tf_op jit(solution)/shard_map/ppermute | solution.py:224
  330.8 27.2 %attention_backward.2 = bf16[2048,384]{1,0:T(8,128)(2,1)} custom-call(s32[3,8]{1,0:T(4,128)} %add_add_fusion.2.info, bf16[2048,768]{1,0:T(8,128)(2,1)} %add_convert_fusion.1.qkv_ref.q_ref.k_ref.v_ref, bf16[2048,768]{1,0:T(8,128)(2,1)} %add_convert_fusion.1.qkv_ref.q_ref.k_ref.v_ref, bf16[2048,768]{1,0:T(8,128)(2,1)} %add_convert_fusion.1.qkv_ref.q_ref.k_ref.v_ref, ...), custom_call_target="tpu_custom_call" | custom-call | flops 24999999488 | bytes 2097152 | tf_op jit(solution)/shard_map/attention_backward/pallas_call | solution.py:181
  358.0 9.2 %collective-permute-done.25 = bf16[2,2,2,40,1024]{4,3,2,1,0:T(8,128)(2,1)S(1)} collective-permute-done((bf16[2,2,2,40,1024]{4,3,2,1,0:T(8,128)(2,1)}, bf16[2,2,2,40,1024]{4,3,2,1,0:T(8,128)(2,1)S(1)}, u32[]{:S(2)}, u32[]{:S(2)}) %collective-permute-start.25) | collective-permute-done | bytes 655392 | tf_op jit(solution)/shard_map/ppermute | solution.py:224
  367.3 4.7 fusion.104
  386.1 27.5 %attention_backward.3 = bf16[2048,384]{1,0:T(8,128)(2,1)} custom-call(s32[3,8]{1,0:T(4,128)} %add_add_fusion.2.info, bf16[2048,768]{1,0:T(8,128)(2,1)} %add_convert_fusion.1.qkv_ref.q_ref.k_ref.v_ref, bf16[2048,768]{1,0:T(8,128)(2,1)} %add_convert_fusion.1.qkv_ref.q_ref.k_ref.v_ref, bf16[2048,768]{1,0:T(8,128)(2,1)} %add_convert_fusion.1.qkv_ref.q_ref.k_ref.v_ref, ...), custom_call_target="tpu_custom_call" | custom-call | flops 24999999488 | bytes 2097152 | tf_op jit(solution)/shard_map/attention_backward/pallas_call | solution.py:181
  418.7 4.1 fusion.103
  435.4 5.7 %collective-permute-start.38 = (f32[1,2560]{1,0:T(1,128)S(1)}, f32[1,2560]{1,0:T(1,128)S(1)}, u32[]{:S(2)}, u32[]{:S(2)}) collective-permute-start(f32[1,2560]{1,0:T(1,128)S(1)} %constant_dynamic-update-slice_fusion.42), channel_id=1, source_target_pairs={{0,16},{4,20},{8,24},{12,28},{16,0},{20,4},{24,8},{28,12},{1,17},{... | collective-permute-start | bytes 30728 | tf_op jit(solution)/shard_map/ppermute | solution.py:224
  450.1 5.6 %collective-permute-done.31 = bf16[128,1024]{1,0:T(8,128)(2,1)S(1)} collective-permute-done((bf16[128,1024]{1,0:T(8,128)(2,1)S(1)}, bf16[128,1024]{1,0:T(8,128)(2,1)S(1)}, u32[]{:S(2)}, u32[]{:S(2)}) %collective-permute-start.31) | collective-permute-done | bytes 262176 | tf_op jit(solution)/shard_map/ppermute | solution.py:224
  467.3 4.0 collective-permute-start.39
  (346 shorter events, 186.7 us)
Async XLA Ops:
  7.2 187.5 %all-gather.2.cloned.1.call-start = ((), (), s32[]{:S(2)}) async-start(), calls=%async_computation | async-start | bytes 19464192 | tf_op jit(solution)/shard_map/all_gather | solution.py:312
  22.0 32.3 %collective-permute-start.4 = (bf16[512,1024]{1,0:T(8,128)(2,1)}, bf16[512,1024]{1,0:T(8,128)(2,1)}, u32[]{:S(2)}, u32[]{:S(2)}) collective-permute-start(bf16[512,1024]{1,0:T(8,128)(2,1)} %bitcast), channel_id=1, source_target_pairs={{0,2},{1,3},{2,0},{3,1},{4,6},{5,7},{6,4},{7,5},{8,10},{9,11},{10,... | collective-permute-start | bytes 3145736 | tf_op jit(solution)/shard_map/ppermute | solution.py:224
  26.6 27.6 %collective-permute-start.3 = (bf16[1,128,1152]{2,1,0:T(8,128)(2,1)S(1)}, bf16[1,128,1152]{2,1,0:T(8,128)(2,1)S(1)}, u32[]{:S(2)}, u32[]{:S(2)}) collective-permute-start(bf16[1,128,1152]{2,1,0:T(8,128)(2,1)S(1)} %maximum_bitcast_fusion), channel_id=1, source_target_pairs={{0,16},{4,20},{8,24},{12,28},{16,0},{20,4},{24,8},{28,12},{1,17},{... | collective-permute-start | bytes 884744 | tf_op jit(solution)/shard_map/ppermute | solution.py:224
  54.3 39.0 %collective-permute-start.5 = (bf16[2,128,1152]{2,1,0:T(8,128)(2,1)S(1)}, bf16[2,128,1152]{2,1,0:T(8,128)(2,1)S(1)}, u32[]{:S(2)}, u32[]{:S(2)}) collective-permute-start(bf16[2,128,1152]{2,1,0:T(8,128)(2,1)S(1)} %pad_maximum_fusion.6), channel_id=1, source_target_pairs={{0,8},{4,12},{8,0},{12,4},{16,24},{20,28},{24,16},{28,20},{1,9},{5... | collective-permute-start | bytes 1769480 | tf_op jit(solution)/shard_map/ppermute | solution.py:224
  54.9 88.4 %collective-permute-start.10 = (bf16[512,1024]{1,0:T(8,128)(2,1)}, bf16[512,1024]{1,0:T(8,128)(2,1)}, u32[]{:S(2)}, u32[]{:S(2)}) collective-permute-start(bf16[512,1024]{1,0:T(8,128)(2,1)} %bitcast), channel_id=1, source_target_pairs={{0,1},{1,0},{2,3},{3,2},{4,5},{5,4},{6,7},{7,6},{8,9},{9,8},{10,11... | collective-permute-start | bytes 3145736 | tf_op jit(solution)/shard_map/ppermute | solution.py:224
  93.5 42.8 %collective-permute-start.6 = (bf16[4,128,1152]{2,1,0:T(8,128)(2,1)S(1)}, bf16[4,128,1152]{2,1,0:T(8,128)(2,1)S(1)}, u32[]{:S(2)}, u32[]{:S(2)}) collective-permute-start(bf16[4,128,1152]{2,1,0:T(8,128)(2,1)S(1)} %pad_maximum_fusion.2), channel_id=1, source_target_pairs={{0,4},{4,0},{8,12},{12,8},{16,20},{20,16},{24,28},{28,24},{1,5},{5... | collective-permute-start | bytes 3538952 | tf_op jit(solution)/shard_map/ppermute | solution.py:224
  99.2 44.2 %collective-permute-start.11 = (bf16[512,1024]{1,0:T(8,128)(2,1)}, bf16[512,1024]{1,0:T(8,128)(2,1)}, u32[]{:S(2)}, u32[]{:S(2)}) collective-permute-start(bf16[512,1024]{1,0:T(8,128)(2,1)} %collective-permute-done.4), channel_id=1, source_target_pairs={{0,1},{1,0},{2,3},{3,2},{4,5},{5,4},{6,7},{7,6},{8,9},{9,8},{10,11... | collective-permute-start | bytes 3145736 | tf_op jit(solution)/shard_map/ppermute | solution.py:224
  247.0 24.0 %collective-permute-start.15 = (bf16[2,2,2,2,128,1024]{5,4,3,2,1,0:T(8,128)(2,1)}, bf16[2,2,2,2,128,1024]{5,4,3,2,1,0:T(8,128)(2,1)}, u32[]{:S(2)}, u32[]{:S(2)}) collective-permute-start(bf16[2,2,2,2,128,1024]{5,4,3,2,1,0:T(8,128)(2,1)} %dynamic-slice_bitcast_fusion.1), channel_id=1, source_target_pairs={{0,1},{1,0},{2,3},{3,2},{4,5},{5,4},{6,7},{7,6},{8,9},{9,8},{10,11... | collective-permute-start | bytes 12582920 | tf_op jit(solution)/shard_map/ppermute | solution.py:224
  259.0 28.8 %collective-permute-start.20 = (bf16[2,2,2,2,32,4096]{5,4,3,2,1,0:T(8,128)(2,1)}, bf16[2,2,2,2,32,4096]{5,4,3,2,1,0:T(8,128)(2,1)}, u32[]{:S(2)}, u32[]{:S(2)}) collective-permute-start(bf16[2,2,2,2,32,4096]{5,4,3,2,1,0:T(8,128)(2,1)} %dynamic-slice_bitcast_fusion), channel_id=1, source_target_pairs={{0,1},{1,0},{2,3},{3,2},{4,5},{5,4},{6,7},{7,6},{8,9},{9,8},{10,11... | collective-permute-start | bytes 12582920 | tf_op jit(solution)/shard_map/ppermute | solution.py:224
  275.6 48.3 %collective-permute-start.16 = (bf16[2,2,2,128,1024]{4,3,0,2,1:T(8,128)(2,1)}, bf16[2,2,2,128,1024]{4,3,0,2,1:T(8,128)(2,1)}, u32[]{:S(2)}, u32[]{:S(2)}) collective-permute-start(bf16[2,2,2,128,1024]{4,3,0,2,1:T(8,128)(2,1)} %copy.189), channel_id=1, source_target_pairs={{0,4},{4,0},{8,12},{12,8},{16,20},{20,16},{24,28},{28,24},{1,5},{5... | collective-permute-start | bytes 6291464 | tf_op jit(solution)/shard_map/ppermute | solution.py:224
  282.2 18.7 %collective-permute-start.21 = (bf16[2,2,2,2,40,1024]{5,4,3,2,1,0:T(8,128)(2,1)}, bf16[2,2,2,2,40,1024]{5,4,3,2,1,0:T(8,128)(2,1)}, u32[]{:S(2)}, u32[]{:S(2)}) collective-permute-start(bf16[2,2,2,2,40,1024]{5,4,3,2,1,0:T(8,128)(2,1)} %fusion.36), channel_id=1, source_target_pairs={{0,1},{1,0},{2,3},{3,2},{4,5},{5,4},{6,7},{7,6},{8,9},{9,8},{10,11... | collective-permute-start | bytes 3932168 | tf_op jit(solution)/shard_map/ppermute | solution.py:224
  327.4 39.8 %collective-permute-start.22 = (bf16[2,2,128,1024]{3,2,1,0:T(8,128)(2,1)}, bf16[2,2,128,1024]{3,2,1,0:T(8,128)(2,1)}, u32[]{:S(2)}, u32[]{:S(2)}) collective-permute-start(bf16[2,2,128,1024]{3,2,1,0:T(8,128)(2,1)} %fusion.23), channel_id=1, source_target_pairs={{0,8},{4,12},{8,0},{12,4},{16,24},{20,28},{24,16},{28,20},{1,9},{5... | collective-permute-start | bytes 3145736 | tf_op jit(solution)/shard_map/ppermute | solution.py:224
  327.4 39.8 %collective-permute-start.23 = (bf16[2,2,2,32,2048]{4,3,2,1,0:T(8,128)(2,1)}, bf16[2,2,2,32,2048]{4,3,2,1,0:T(8,128)(2,1)}, u32[]{:S(2)}, u32[]{:S(2)}) collective-permute-start(bf16[2,2,2,32,2048]{4,3,2,1,0:T(8,128)(2,1)} %get-tuple-element.104), channel_id=1, source_target_pairs={{0,2},{1,3},{2,0},{3,1},{4,6},{5,7},{6,4},{7,5},{8,10},{9,11},{10,... | collective-permute-start | bytes 3145736 | tf_op jit(solution)/shard_map/ppermute | solution.py:224
  328.8 38.5 %collective-permute-start.24 = (bf16[2,2,2,32,2048]{4,3,2,1,0:T(8,128)(2,1)}, bf16[2,2,2,32,2048]{4,3,2,1,0:T(8,128)(2,1)}, u32[]{:S(2)}, u32[]{:S(2)}) collective-permute-start(bf16[2,2,2,32,2048]{4,3,2,1,0:T(8,128)(2,1)} %get-tuple-element.105), channel_id=1, source_target_pairs={{0,4},{4,0},{8,12},{12,8},{16,20},{20,16},{24,28},{28,24},{1,5},{5... | collective-permute-start | bytes 3145736 | tf_op jit(solution)/shard_map/ppermute | solution.py:224
  330.5 36.7 %collective-permute-start.25 = (bf16[2,2,2,40,1024]{4,3,2,1,0:T(8,128)(2,1)}, bf16[2,2,2,40,1024]{4,3,2,1,0:T(8,128)(2,1)S(1)}, u32[]{:S(2)}, u32[]{:S(2)}) collective-permute-start(bf16[2,2,2,40,1024]{4,3,2,1,0:T(8,128)(2,1)} %fusion.37), channel_id=1, source_target_pairs={{0,4},{4,0},{8,12},{12,8},{16,20},{20,16},{24,28},{28,24},{1,5},{5... | collective-permute-start | bytes 1966088 | tf_op jit(solution)/shard_map/ppermute | solution.py:224
  380.6 34.9 %collective-permute-start.26 = (bf16[2,128,1024]{2,1,0:T(8,128)(2,1)}, bf16[2,128,1024]{2,1,0:T(8,128)(2,1)}, u32[]{:S(2)}, u32[]{:S(2)}) collective-permute-start(bf16[2,128,1024]{2,1,0:T(8,128)(2,1)} %fusion.44), channel_id=1, source_target_pairs={{0,2},{1,3},{2,0},{3,1},{4,6},{5,7},{6,4},{7,5},{8,10},{9,11},{10,... | collective-permute-start | bytes 1572872 | tf_op jit(solution)/shard_map/ppermute | solution.py:224
  382.1 33.4 %collective-permute-start.27 = (bf16[2,2,32,2048]{3,2,0,1:T(8,128)(2,1)}, bf16[2,2,32,2048]{3,2,0,1:T(8,128)(2,1)}, u32[]{:S(2)}, u32[]{:S(2)}) collective-permute-start(bf16[2,2,32,2048]{3,2,0,1:T(8,128)(2,1)} %copy.206), channel_id=1, source_target_pairs={{0,4},{4,0},{8,12},{12,8},{16,20},{20,16},{24,28},{28,24},{1,5},{5... | collective-permute-start | bytes 1572872 | tf_op jit(solution)/shard_map/ppermute | solution.py:224
  383.5 31.9 %collective-permute-start.28 = (bf16[2,2,32,2048]{3,2,1,0:T(8,128)(2,1)}, bf16[2,2,32,2048]{3,2,1,0:T(8,128)(2,1)}, u32[]{:S(2)}, u32[]{:S(2)}) collective-permute-start(bf16[2,2,32,2048]{3,2,1,0:T(8,128)(2,1)} %get-tuple-element.117), channel_id=1, source_target_pairs={{0,8},{4,12},{8,0},{12,4},{16,24},{20,28},{24,16},{28,20},{1,9},{5... | collective-permute-start | bytes 1572872 | tf_op jit(solution)/shard_map/ppermute | solution.py:224
  385.3 30.1 %collective-permute-start.29 = (bf16[2,2,40,1024]{3,2,1,0:T(8,128)(2,1)}, bf16[2,2,40,1024]{3,2,1,0:T(8,128)(2,1)}, u32[]{:S(2)}, u32[]{:S(2)}) collective-permute-start(bf16[2,2,40,1024]{3,2,1,0:T(8,128)(2,1)} %fusion.53), channel_id=1, source_target_pairs={{0,8},{4,12},{8,0},{12,4},{16,24},{20,28},{24,16},{28,20},{1,9},{5... | collective-permute-start | bytes 983048 | tf_op jit(solution)/shard_map/ppermute | solution.py:224
  385.6 29.9 %collective-permute-start.30 = (bf16[2,2,128,384]{3,2,1,0:T(8,128)(2,1)}, bf16[2,2,128,384]{3,2,1,0:T(8,128)(2,1)}, u32[]{:S(2)}, u32[]{:S(2)}) collective-permute-start(bf16[2,2,128,384]{3,2,1,0:T(8,128)(2,1)} %fusion.60), channel_id=1, source_target_pairs={{0,4},{4,0},{8,12},{12,8},{16,20},{20,16},{24,28},{28,24},{1,5},{5... | collective-permute-start | bytes 1179656 | tf_op jit(solution)/shard_map/ppermute | solution.py:224
  432.2 24.6 %collective-permute-start.37 = (bf16[1024,1024]{1,0:T(8,128)(2,1)S(1)}, bf16[1024,1024]{1,0:T(8,128)(2,1)S(1)}, u32[]{:S(2)}, u32[]{:S(2)}) collective-permute-start(bf16[1024,1024]{1,0:T(8,128)(2,1)S(1)} %convolution_convert_fusion.3), channel_id=1, source_target_pairs={{0,1},{1,0},{2,3},{3,2},{4,5},{5,4},{6,7},{7,6},{8,9},{9,8},{10,11... | collective-permute-start | bytes 6291464 | tf_op jit(solution)/shard_map/ppermute | solution.py:224
  466.9 25.6 %collective-permute-start.47 = (bf16[512,1024]{1,0:T(8,128)(2,1)}, bf16[512,1024]{1,0:T(8,128)(2,1)}, u32[]{:S(2)}, u32[]{:S(2)}) collective-permute-start(bf16[512,1024]{1,0:T(8,128)(2,1)} %slice.468), channel_id=1, source_target_pairs={{0,2},{1,3},{2,0},{3,1},{4,6},{5,7},{6,4},{7,5},{8,10},{9,11},{10,... | collective-permute-start | bytes 3145736 | tf_op jit(solution)/shard_map/ppermute | solution.py:224
  472.9 17.7 %collective-permute-start.43 = (bf16[32,2048]{1,0:T(8,128)(2,1)}, bf16[32,2048]{1,0:T(8,128)(2,1)S(1)}, u32[]{:S(2)}, u32[]{:S(2)}) collective-permute-start(bf16[32,2048]{1,0:T(8,128)(2,1)} %get-tuple-element.152), channel_id=1, source_target_pairs={{0,16},{4,20},{8,24},{12,28},{16,0},{20,4},{24,8},{28,12},{1,17},{... | collective-permute-start | bytes 393224 | tf_op jit(solution)/shard_map/ppermute | solution.py:224
  473.0 17.7 %collective-permute-start.44 = (bf16[32,2048]{1,0:T(8,128)(2,1)}, bf16[32,2048]{1,0:T(8,128)(2,1)S(1)}, u32[]{:S(2)}, u32[]{:S(2)}) collective-permute-start(bf16[32,2048]{1,0:T(8,128)(2,1)} %get-tuple-element.153), channel_id=1, source_target_pairs={{0,16},{4,20},{8,24},{12,28},{16,0},{20,4},{24,8},{28,12},{1,17},{... | collective-permute-start | bytes 393224 | tf_op jit(solution)/shard_map/ppermute | solution.py:224
  (67 other events, 584.4 us)
Sparse Core Ops, SparseCore 0:
  13.5 157.8 all-gather.1

commit v7 on v6

--- a/solution.py
+++ b/solution.py
@@ -144,6 +144,12 @@
 
     dk_acc[...] = jnp.zeros_like(dk_acc)
     dv_acc[...] = jnp.zeros_like(dv_acc)
+    k_turned = k_ref[...].T
+    feature = lax.broadcasted_iota(jnp.int32, k_turned.shape, 0)
+    turned = [
+        jnp.where(feature < HEAD_DIM, k_turned, jnp.zeros_like(k_turned)),
+        jnp.where(feature >= HEAD_DIM, k_turned, jnp.zeros_like(k_turned)),
+    ]
     ids_k = idc_ref[pl.ds(pl.multiple_of(j * BLOCK, BLOCK), BLOCK), :]
 
     def step(i, carry):
@@ -151,18 +157,19 @@
         same = ids_k == idr_ref[pl.ds(i, 1)][0]
         k_pair, v_pair = k_ref[...], v_ref[...]
         q_pair, do_pair = q_ref[pl.ds(at, BLOCK), :], do_ref[pl.ds(at, BLOCK), :]
-        dv, dk, dq = [], [], []
+        es, dss, qs, dos = [], [], [], []
         for w in range(2):
             q_one, do_one = head_only(q_pair, w), head_only(do_pair, w)
             t = nt(k_pair, q_one) * SCALE_LOG2 - lse_ref[i, first + w : first + w + 1, :]
             e = jnp.exp2(jnp.where(same, t, MASKED))
             ds = (e * (nt(v_pair, do_one) - delta_ref[i, w : w + 1, :])).astype(bf16)
-            dv.append(nn(e.astype(bf16), do_one))
-            dk.append(nn(ds, q_one))
-            dq.append(tn(ds, head_only(k_pair, w)))
-        dv_acc[...] += dv[0] + dv[1]
-        dk_acc[...] += dk[0] + dk[1]
-        dq_acc[pl.ds(at, BLOCK), :] += dq[0] + dq[1]
+            es.append(e.astype(bf16))
+            dss.append(ds)
+            qs.append(q_one)
+            dos.append(do_one)
+        dv_acc[...] += nn(jnp.concatenate(es, axis=1), jnp.concatenate(dos, axis=0))
+        dk_acc[...] += nn(jnp.concatenate(dss, axis=1), jnp.concatenate(qs, axis=0))
+        dq_acc[i] += nn(jnp.concatenate(turned, axis=1), jnp.concatenate(dss, axis=0))
         return carry
 
     lax.fori_loop(info[0, j], info[1, j], step, 0)
@@ -172,7 +179,12 @@
 
     @pl.when(j == blocks - 1)
     def _():
-        out_ref[:, 0:128] = (dq_acc[...] * SCALE).astype(bf16)
+        def turn_back(i, carry):
+            at = pl.multiple_of(place(i, me, per_chunk) * BLOCK, BLOCK)
+            out_ref[pl.ds(at, BLOCK), 0:128] = (dq_acc[i] * SCALE).T.astype(bf16)
+            return carry
+
+        lax.fori_loop(0, blocks, turn_back, 0)
 
 
 def attention_backward(pair, info, qkv, do, o, lse, ids_col, ids_row, per_chunk):
@@ -196,7 +208,7 @@
             out_specs=pl.BlockSpec((rows, 384), lambda i, info: (0, 0)),
             scratch_shapes=[
                 pltpu.VMEM((blocks, 2, BLOCK), f32),
-                pltpu.VMEM((rows, 128), f32),
+                pltpu.VMEM((blocks, 128, BLOCK), f32),
                 pltpu.VMEM((BLOCK, 128), f32),
                 pltpu.VMEM((BLOCK, 128), f32),
             ],
@@ -374,6 +386,7 @@
     ids_col, ids_row = ids.reshape(-1, 1), ids.reshape(-1, 1, BLOCK)
     mixed, logsum = attention_forward(info, qkv, ids_col, ids_row, per_chunk)
     returned = trade([mixed[k * piece : (k + 1) * piece] for k in range(ctx)], "ctx")
+    returned, down_full = lax.optimization_barrier((returned, down_full))
     attended = jnp.concatenate(to_absolute(returned, me), axis=1)
 
     branch = nn(attended, output_full) + output_shift
@@ -394,46 +407,45 @@
     down_grad = tn(activated, grad_feed).astype(bf16)
     down_shift_grad = jnp.sum(grad_feed.astype(f32), axis=0)
     grad_inner = (nt(grad_feed, down_full) * slope.astype(f32)).astype(bf16)
+    dp_names, ctx_names = [("dp", b) for b in bits(dp)], [("ctx", b) for b in bits(ctx)]
+    names = dp_names[::-1] + ctx_names[::-1]
+    core, turn, rest = ctx_names[0], dp_names[:2] + ctx_names[1:], dp_names[2:]
+    whole = {}
+
+    def share(label, array, height):
+        size = (height, array.shape[-1])
+        whole[label] = Halving(names, size)
+        whole[label].terms = [(array.reshape([2] * len(names) + list(size)), names, [(0, d) for d in size])]
+        whole[label].exchange(core)
+
+    def stream(label, part, turned):
+        sums = Halving(names, [high - low for low, high in part])
+        sums.fixed = {core: sums.me[core]}
+        sums.terms = [(array, left, part) for array, left, _ in whole[label].terms]
+        return sums, turn[turned:] + turn[:turned] + rest
+
+    def depart(moving, beside):
+        going = [s.outgoing(name) for s, name in moving]
+        going, beside = lax.optimization_barrier((going, beside))
+        return [(s, name, swap(value, *name)) for (s, name), value in zip(moving, going)], beside
+
+    def land(flights, beside):
+        values, beside = lax.optimization_barrier(([value for _, _, value in flights], beside))
+        for (s, name, _), value in zip(flights, values):
+            s.arrived(name, value)
+        return beside
+
+    def following(pairs):
+        return [(s, o.pop(0)) for s, o in pairs if o]
+
+    share("down", down_grad, ratio * own)
+    streams = [stream("down", [(0, ratio * own), (0, width)], 0)]
+    ahead, grad_inner = depart(following(streams), grad_inner)
     up_grad = tn(hidden_low, grad_inner).astype(bf16)
     up_shift_grad = jnp.sum(grad_inner.astype(f32), axis=0)
     grad_hidden = grad_two + nt(grad_inner, up_full)
     grad_one, gain_one_grad, bias_one_grad = normalize_back(grad_hidden, normed_one, inverse_one, gain_one)
     grad_branch = grad_one.astype(bf16)
-    dp_names, ctx_names = [("dp", b) for b in bits(dp)], [("ctx", b) for b in bits(ctx)]
-    names = dp_names[::-1] + ctx_names[::-1]
-    core, turn, rest = ctx_names[0], dp_names[:2] + ctx_names[1:], dp_names[2:]
-    whole = {}
-
-    def share(label, array, height):
-        size = (height, array.shape[-1])
-        whole[label] = Halving(names, size)
-        whole[label].terms = [(array.reshape([2] * len(names) + list(size)), names, [(0, d) for d in size])]
-        whole[label].exchange(core)
-
-    def stream(label, part, turned):
-        sums = Halving(names, [high - low for low, high in part])
-        sums.fixed = {core: sums.me[core]}
-        sums.terms = [(array, left, part) for array, left, _ in whole[label].terms]
-        return sums, turn[turned:] + turn[:turned] + rest
-
-    def depart(moving, beside):
-        going = [s.outgoing(name) for s, name in moving]
-        going, beside = lax.optimization_barrier((going, beside))
-        return [(s, name, swap(value, *name)) for (s, name), value in zip(moving, going)], beside
-
-    def land(flights, beside):
-        values, beside = lax.optimization_barrier(([value for _, _, value in flights], beside))
-        for (s, name, _), value in zip(flights, values):
-            s.arrived(name, value)
-        return beside
-
-    def following(pairs):
-        return [(s, o.pop(0)) for s, o in pairs if o]
-
-    share("down", down_grad, ratio * own)
-    streams = [stream("down", [(0, ratio * own), (0, width)], 0)]
-    ahead, grad_branch = depart(following(streams), grad_branch)
-
     output_grad = tn(attended, grad_branch).astype(bf16)
     output_shift_grad = jnp.sum(grad_branch.astype(f32), axis=0)
     vector_grads = jnp.stack(

time: 529 us -> 509 us (0.962)
  Pallas kernels: 82.8 us -> 62.8 us
  waiting for transfers between devices: 172 us -> 163 us
  matrix products: 83.2 us -> 76.3 us
  other arithmetic: 63.6 us -> 70 us
    pallas_call x2, Pallas kernels: 54.7 us -> 40.4 us  [attention_backward(): pl.pallas_call(functools.partial(backward_kernel, per_chunk, 2 * pair), g...]
    ppermute x54, waiting for transfers between devices: 172 us -> 163 us  [swap(): return lax.ppermute(value, axis, [(i, i ^ mask) for i in range(size)])]
    dot_general x5, matrix products: 30.7 us -> 24.6 us  [nt(): lax.dot_general(left, right, (((1,), (1,)), ((), ())), preferred_element_...]
    pallas_call x1, Pallas kernels: 28.1 us -> 22.5 us  [attention_forward(): pl.pallas_call(functools.partial(forward_kernel, per_chunk, heads // 2),...]
    unnamed x114 -> x124, local copies, waits for them, and re-layouts: 18.1 us -> 20 us
  transfers between devices with their start and end apart: 55 -> 55, of which waited for: 22 -> 24; matrix products, arithmetic and copies ran while one was open for 16% -> 19% of each run, Pallas kernels for 16% -> 13%
where the time goes in v7:
time: 509 us; the launch traced here: 499 us
  waiting for transfers between devices  163 us (32%)
  matrix products  76.3 us (15%)
  other arithmetic  70 us (14%)
  Pallas kernels  62.8 us (12%)
  starting transfers between devices  62.3 us (12%)
  local copies, waits for them, and re-layouts  48.8 us (10%)
  between operations  15.5 us (3%)
    ppermute x54, waiting for transfers between devices, swap(): return lax.ppermute(value, axis, [(i, i ^ mask) for i in range(size)])  163 us
    ppermute x54, starting transfers between devices, swap(): return lax.ppermute(value, axis, [(i, i ^ mask) for i in range(size)])  62.2 us
    pallas_call x2, Pallas kernels, attention_backward(): pl.pallas_call(functools.partial(backward_kernel, per_chunk, 2 * pair), g...  40.4 us
    convert_element_type x16, other arithmetic, outgoing(): return self.total({**self.fixed, name: 1 - self.me[name]}).astype(bf16)  35.5 us
    dot_general x5, matrix products, nn(): return jnp.dot(left, right, preferred_element_type=f32)  27.6 us
    dot_general x5, matrix products, nt(): lax.dot_general(left, right, (((1,), (1,)), ((), ())), preferred_element_...  24.6 us
    pallas_call x1, Pallas kernels, attention_forward(): pl.pallas_call(functools.partial(forward_kernel, per_chunk, heads // 2),...  22.5 us
    dot_general x5, matrix products, tn(): lax.dot_general(left, right, (((0,), (0,)), ((), ())), preferred_element_...  22.2 us
  transfers between devices with their start and end apart: 55, of which 24 were waited for; matrix products, arithmetic and copies ran while one was open for 19% of the time, Pallas kernels for 13%

profile of v7, /device:TPU:0, one launch (start us, length us, event | category | flops | bytes accessed | tf_op | source)
XLA Modules:
  0.0 499.1 jit_solution(11384771386788527032)
XLA Ops:
  29.8 24.5 %collective-permute-done.3 = bf16[1,128,1152]{2,1,0:T(8,128)(2,1)S(1)} collective-permute-done((bf16[1,128,1152]{2,1,0:T(8,128)(2,1)S(1)}, bf16[1,128,1152]{2,1,0:T(8,128)(2,1)S(1)}, u32[]{:S(2)}, u32[]{:S(2)}) %collective-permute-start.3) | collective-permute-done | bytes 294944 | tf_op jit(solution)/shard_map/ppermute | solution.py:236
  56.5 37.1 %collective-permute-done.5 = bf16[2,128,1152]{2,1,0:T(8,128)(2,1)S(1)} collective-permute-done((bf16[2,128,1152]{2,1,0:T(8,128)(2,1)S(1)}, bf16[2,128,1152]{2,1,0:T(8,128)(2,1)S(1)}, u32[]{:S(2)}, u32[]{:S(2)}) %collective-permute-start.5) | collective-permute-done | bytes 589856 | tf_op jit(solution)/shard_map/ppermute | solution.py:236
  99.5 38.6 %collective-permute-done.6 = bf16[4,128,1152]{2,1,0:T(8,128)(2,1)S(1)} collective-permute-done((bf16[4,128,1152]{2,1,0:T(8,128)(2,1)S(1)}, bf16[4,128,1152]{2,1,0:T(8,128)(2,1)S(1)}, u32[]{:S(2)}, u32[]{:S(2)}) %collective-permute-start.6) | collective-permute-done | bytes 1179680 | tf_op jit(solution)/shard_map/ppermute | solution.py:236
  151.7 7.7 %add_convert_fusion.1.qkv_ref.q_ref.k_ref.v_ref = bf16[2048,768]{1,0:T(8,128)(2,1)} fusion(f32[768]{0:T(1024)S(1)} %constant_dynamic-update-slice_fusion.72, bf16[1024,1152]{0,1:T(8,128)(2,1)S(1)} %bitcast_dynamic-update-slice_fusion, bf16[512,1024]{1,0:T(8,128)(2,1)} %collective-permute-done.11, bf16[512,1024]{1,0:T(8,128)(2,1)} %collective-permute-done.4, ...), kind=kOutput, calls=%fused_computation.23 | convolution fusion | flops 3245342720 | bytes 8921088 | tf_op jit(solution)/shard_map/dot_general | solution.py:21
  159.5 22.5 %attention_forward.1 = (bf16[2048,256]{1,0:T(8,128)(2,1)}, f32[8,4,256]{2,1,0:T(4,128)}) custom-call(s32[3,8]{1,0:T(4,128)} %add_add_fusion.2.info, bf16[2048,768]{1,0:T(8,128)(2,1)} %add_convert_fusion.1.qkv_ref.q_ref.k_ref.v_ref, s32[2048,1]{1,0:T(8,128)} %copy.186.idc_ref, s32[8,1,256]{2,1,0:T(1,128)} %bitcast.606), custom_call_target="tpu_custom_call" | custom-call | flops 30000001024 | bytes 3145728 | tf_op jit(solution)/shard_map/attention_forward/pallas_call | solution.py:95
  190.8 6.6 %collective-permute-done.13 = bf16[512,256]{1,0:T(8,128)(2,1)S(1)} collective-permute-done((bf16[512,256]{1,0:T(8,128)(2,1)S(1)}, bf16[512,256]{1,0:T(8,128)(2,1)S(1)}, u32[]{:S(2)}, u32[]{:S(2)}) %collective-permute-start.13) | collective-permute-done | bytes 262176 | tf_op jit(solution)/shard_map/ppermute | solution.py:236
  201.6 11.4 %fusion.4 = (bf16[512,4096]{1,0:T(8,128)(2,1)}, bf16[512,4096]{1,0:T(8,128)(2,1)S(1)}) fusion(f32[4096]{0:T(1024)S(1)} %add.488, bf16[1024,9216]{1,0:T(8,128)(2,1)} %all-gather.2.cloned.1.call-done, f32[512,1024]{1,0:T(8,128)S(1)} %get-tuple-element.324, f32[1024]{0:T(1024)S(1)} %bitcast.634, f32[1024]{0:T(1024)S(1)} %bitcast.622, ...), kind=kOutput, calls=%fused_computation.5 | convolution fusion | flops 4322754560 | bytes 18903040 | tf_op jit(solution)/shard_map/dot_general | solution.py:21
  213.1 4.8 fusion.114
  221.8 5.3 %convolution_convert_fusion.1 = bf16[4096,1024]{1,0:T(8,128)(2,1)S(1)} fusion(bf16[512,4096]{1,0:T(8,128)(2,1)S(1)} %get-tuple-element.106, f32[512,1024]{1,0:T(8,128)S(1)} %get-tuple-element.193), kind=kOutput, calls=%fused_computation.18 | convolution fusion | flops 4299685888 | bytes 14680064 | tf_op jit(solution)/shard_map/dot_general | solution.py:25
  232.1 9.9 %multiply_convert_fusion = bf16[512,4096]{1,0:T(8,128)(2,1)S(1)} fusion(bf16[512,4096]{1,0:T(8,128)(2,1)} %get-tuple-element.108, bf16[4096,1024]{1,0:T(8,128)(2,1)} %bitcast.570, f32[512,1024]{1,0:T(8,128)} %copy-done.10), kind=kOutput, calls=%fused_computation.7 | convolution fusion | flops 4301783040 | bytes 18874368 | tf_op jit(solution)/shard_map/dot_general | solution.py:29
  242.0 4.8 fusion.9
  248.4 5.2 %convolution_convert_fusion = bf16[1024,4096]{1,0:T(8,128)(2,1)S(1)} fusion(bf16[512,4096]{1,0:T(8,128)(2,1)S(1)} %multiply_convert_fusion, f32[512,1024]{1,0:T(8,128)S(1)} %get-tuple-element.324, f32[1024]{0:T(1024)S(1)} %bitcast.636, f32[1024]{0:T(1024)S(1)} %bitcast.624, f32[512]{0:T(512)S(1)} %add_rsqrt_fusion.1, f32[512]{0:T(512)S(1)} %broadcast_multiply_fusion.5), kind=kOutput, calls=%fused_computation.17 | convolution fusion | flops 4301783040 | bytes 14692352 | tf_op jit(solution)/shard_map/dot_general | solution.py:25
  253.6 7.3 %collective-permute-start.16 = (bf16[2,2,2,128,1024]{4,3,0,2,1:T(8,128)(2,1)}, bf16[2,2,2,128,1024]{4,3,0,2,1:T(8,128)(2,1)}, u32[]{:S(2)}, u32[]{:S(2)}) collective-permute-start(bf16[2,2,2,128,1024]{4,3,0,2,1:T(8,128)(2,1)} %copy.189), channel_id=1, source_target_pairs={{0,4},{4,0},{8,12},{12,8},{16,20},{20,16},{24,28},{28,24},{1,5},{5... | collective-permute-start | bytes 6291464 | tf_op jit(solution)/shard_map/ppermute | solution.py:236
  263.5 8.3 %multiply_reduce_fusion = (f32[1024]{0:T(1024)S(1)}, f32[512]{0:T(512)S(1)}, f32[512]{0:T(512)S(1)}, f32[1024]{0:T(1024)S(1)}, f32[512,1024]{1,0:T(8,128)S(1)}) fusion(f32[512,1024]{1,0:T(8,128)S(1)} %get-tuple-element.324, f32[512]{0:T(512)S(1)} %add_rsqrt_fusion.1, f32[512]{0:T(512)S(1)} %broadcast_multiply_fusion.5, f32[1024]{0:T(1024)S(1)} %bitcast.625, ...), kind=kOutput, calls=%fused_computation.61 | convolution fusion | flops 4300207104 | bytes 18894848 | tf_op jit(solution)/shard_map/dot_general | solution.py:29
  287.7 6.6 %collective-permute-done.19 = bf16[512,256]{1,0:T(8,128)(2,1)S(1)} collective-permute-done((bf16[512,256]{1,0:T(8,128)(2,1)S(1)}, bf16[512,256]{1,0:T(8,128)(2,1)S(1)}, u32[]{:S(2)}, u32[]{:S(2)}) %collective-permute-start.19) | collective-permute-done | bytes 262176 | tf_op jit(solution)/shard_map/ppermute | solution.py:236
  295.8 4.5 collective-permute-done.18
  311.1 4.4 fusion.21
  319.5 20.1 %attention_backward.2 = bf16[2048,384]{1,0:T(8,128)(2,1)} custom-call(s32[3,8]{1,0:T(4,128)} %add_add_fusion.2.info, bf16[2048,768]{1,0:T(8,128)(2,1)} %add_convert_fusion.1.qkv_ref.q_ref.k_ref.v_ref, bf16[2048,768]{1,0:T(8,128)(2,1)} %add_convert_fusion.1.qkv_ref.q_ref.k_ref.v_ref, bf16[2048,768]{1,0:T(8,128)(2,1)} %add_convert_fusion.1.qkv_ref.q_ref.k_ref.v_ref, ...), custom_call_target="tpu_custom_call" | custom-call | flops 24999999488 | bytes 2097152 | tf_op jit(solution)/shard_map/attention_backward/pallas_call | solution.py:193
  342.1 12.7 %collective-permute-done.24 = bf16[2,2,2,32,2048]{4,3,2,1,0:T(8,128)(2,1)} collective-permute-done((bf16[2,2,2,32,2048]{4,3,2,1,0:T(8,128)(2,1)}, bf16[2,2,2,32,2048]{4,3,2,1,0:T(8,128)(2,1)}, u32[]{:S(2)}, u32[]{:S(2)}) %collective-permute-start.24) | collective-permute-done | bytes 1048608 | tf_op jit(solution)/shard_map/ppermute | solution.py:236
  354.9 4.6 fusion.106
  375.0 20.3 %attention_backward.3 = bf16[2048,384]{1,0:T(8,128)(2,1)} custom-call(s32[3,8]{1,0:T(4,128)} %add_add_fusion.2.info, bf16[2048,768]{1,0:T(8,128)(2,1)} %add_convert_fusion.1.qkv_ref.q_ref.k_ref.v_ref, bf16[2048,768]{1,0:T(8,128)(2,1)} %add_convert_fusion.1.qkv_ref.q_ref.k_ref.v_ref, bf16[2048,768]{1,0:T(8,128)(2,1)} %add_convert_fusion.1.qkv_ref.q_ref.k_ref.v_ref, ...), custom_call_target="tpu_custom_call" | custom-call | flops 24999999488 | bytes 2097152 | tf_op jit(solution)/shard_map/attention_backward/pallas_call | solution.py:193
  402.4 4.1 fusion.105
  413.1 4.2 collective-permute-start.35
  453.5 8.2 %collective-permute-done.39 = bf16[128,384]{1,0:T(8,128)(2,1)S(1)} collective-permute-done((bf16[128,384]{1,0:T(8,128)(2,1)}, bf16[128,384]{1,0:T(8,128)(2,1)S(1)}, u32[]{:S(2)}, u32[]{:S(2)}) %collective-permute-start.39) | collective-permute-done | bytes 98336 | tf_op jit(solution)/shard_map/ppermute | solution.py:236
  (355 shorter events, 199.9 us)
Async XLA Ops:
  7.2 178.6 %all-gather.2.cloned.1.call-start = ((), (), s32[]{:S(2)}) async-start(), calls=%async_computation | async-start | bytes 19464192 | tf_op jit(solution)/shard_map/all_gather | solution.py:324
  22.0 32.3 %collective-permute-start.4 = (bf16[512,1024]{1,0:T(8,128)(2,1)}, bf16[512,1024]{1,0:T(8,128)(2,1)}, u32[]{:S(2)}, u32[]{:S(2)}) collective-permute-start(bf16[512,1024]{1,0:T(8,128)(2,1)} %bitcast), channel_id=1, source_target_pairs={{0,2},{1,3},{2,0},{3,1},{4,6},{5,7},{6,4},{7,5},{8,10},{9,11},{10,... | collective-permute-start | bytes 3145736 | tf_op jit(solution)/shard_map/ppermute | solution.py:236
  27.2 27.0 %collective-permute-start.3 = (bf16[1,128,1152]{2,1,0:T(8,128)(2,1)S(1)}, bf16[1,128,1152]{2,1,0:T(8,128)(2,1)S(1)}, u32[]{:S(2)}, u32[]{:S(2)}) collective-permute-start(bf16[1,128,1152]{2,1,0:T(8,128)(2,1)S(1)} %maximum_bitcast_fusion), channel_id=1, source_target_pairs={{0,16},{4,20},{8,24},{12,28},{16,0},{20,4},{24,8},{28,12},{1,17},{... | collective-permute-start | bytes 884744 | tf_op jit(solution)/shard_map/ppermute | solution.py:236
  54.3 39.3 %collective-permute-start.5 = (bf16[2,128,1152]{2,1,0:T(8,128)(2,1)S(1)}, bf16[2,128,1152]{2,1,0:T(8,128)(2,1)S(1)}, u32[]{:S(2)}, u32[]{:S(2)}) collective-permute-start(bf16[2,128,1152]{2,1,0:T(8,128)(2,1)S(1)} %pad_maximum_fusion.6), channel_id=1, source_target_pairs={{0,8},{4,12},{8,0},{12,4},{16,24},{20,28},{24,16},{28,20},{1,9},{5... | collective-permute-start | bytes 1769480 | tf_op jit(solution)/shard_map/ppermute | solution.py:236
  55.0 96.7 %collective-permute-start.10 = (bf16[512,1024]{1,0:T(8,128)(2,1)}, bf16[512,1024]{1,0:T(8,128)(2,1)}, u32[]{:S(2)}, u32[]{:S(2)}) collective-permute-start(bf16[512,1024]{1,0:T(8,128)(2,1)} %bitcast), channel_id=1, source_target_pairs={{0,1},{1,0},{2,3},{3,2},{4,5},{5,4},{6,7},{7,6},{8,9},{9,8},{10,11... | collective-permute-start | bytes 3145736 | tf_op jit(solution)/shard_map/ppermute | solution.py:236
  93.7 44.4 %collective-permute-start.6 = (bf16[4,128,1152]{2,1,0:T(8,128)(2,1)S(1)}, bf16[4,128,1152]{2,1,0:T(8,128)(2,1)S(1)}, u32[]{:S(2)}, u32[]{:S(2)}) collective-permute-start(bf16[4,128,1152]{2,1,0:T(8,128)(2,1)S(1)} %pad_maximum_fusion.2), channel_id=1, source_target_pairs={{0,4},{4,0},{8,12},{12,8},{16,20},{20,16},{24,28},{28,24},{1,5},{5... | collective-permute-start | bytes 3538952 | tf_op jit(solution)/shard_map/ppermute | solution.py:236
  99.3 52.4 %collective-permute-start.11 = (bf16[512,1024]{1,0:T(8,128)(2,1)}, bf16[512,1024]{1,0:T(8,128)(2,1)}, u32[]{:S(2)}, u32[]{:S(2)}) collective-permute-start(bf16[512,1024]{1,0:T(8,128)(2,1)} %collective-permute-done.4), channel_id=1, source_target_pairs={{0,1},{1,0},{2,3},{3,2},{4,5},{5,4},{6,7},{7,6},{8,9},{9,8},{10,11... | collective-permute-start | bytes 3145736 | tf_op jit(solution)/shard_map/ppermute | solution.py:236
  253.6 53.9 %collective-permute-start.16 = (bf16[2,2,2,128,1024]{4,3,0,2,1:T(8,128)(2,1)}, bf16[2,2,2,128,1024]{4,3,0,2,1:T(8,128)(2,1)}, u32[]{:S(2)}, u32[]{:S(2)}) collective-permute-start(bf16[2,2,2,128,1024]{4,3,0,2,1:T(8,128)(2,1)} %copy.189), channel_id=1, source_target_pairs={{0,4},{4,0},{8,12},{12,8},{16,20},{20,16},{24,28},{28,24},{1,5},{5... | collective-permute-start | bytes 6291464 | tf_op jit(solution)/shard_map/ppermute | solution.py:236
  263.2 47.9 %collective-permute-start.20 = (bf16[2,2,2,2,32,4096]{5,4,3,2,1,0:T(8,128)(2,1)}, bf16[2,2,2,2,32,4096]{5,4,3,2,1,0:T(8,128)(2,1)}, u32[]{:S(2)}, u32[]{:S(2)}) collective-permute-start(bf16[2,2,2,2,32,4096]{5,4,3,2,1,0:T(8,128)(2,1)} %dynamic-slice_bitcast_fusion), channel_id=1, source_target_pairs={{0,1},{1,0},{2,3},{3,2},{4,5},{5,4},{6,7},{7,6},{8,9},{9,8},{10,11... | collective-permute-start | bytes 12582920 | tf_op jit(solution)/shard_map/ppermute | solution.py:236
  281.7 20.7 %collective-permute-start.21 = (bf16[2,2,2,2,40,1024]{5,4,3,2,1,0:T(8,128)(2,1)}, bf16[2,2,2,2,40,1024]{5,4,3,2,1,0:T(8,128)(2,1)}, u32[]{:S(2)}, u32[]{:S(2)}) collective-permute-start(bf16[2,2,2,2,40,1024]{5,4,3,2,1,0:T(8,128)(2,1)} %fusion.36), channel_id=1, source_target_pairs={{0,1},{1,0},{2,3},{3,2},{4,5},{5,4},{6,7},{7,6},{8,9},{9,8},{10,11... | collective-permute-start | bytes 3932168 | tf_op jit(solution)/shard_map/ppermute | solution.py:236
  315.5 24.2 %collective-permute-start.25 = (bf16[2,2,2,40,1024]{4,3,2,1,0:T(8,128)(2,1)}, bf16[2,2,2,40,1024]{4,3,2,1,0:T(8,128)(2,1)S(1)}, u32[]{:S(2)}, u32[]{:S(2)}) collective-permute-start(bf16[2,2,2,40,1024]{4,3,2,1,0:T(8,128)(2,1)} %fusion.37), channel_id=1, source_target_pairs={{0,4},{4,0},{8,12},{12,8},{16,20},{20,16},{24,28},{28,24},{1,5},{5... | collective-permute-start | bytes 1966088 | tf_op jit(solution)/shard_map/ppermute | solution.py:236
  317.3 24.7 %collective-permute-start.22 = (bf16[2,2,128,1024]{3,2,1,0:T(8,128)(2,1)}, bf16[2,2,128,1024]{3,2,1,0:T(8,128)(2,1)}, u32[]{:S(2)}, u32[]{:S(2)}) collective-permute-start(bf16[2,2,128,1024]{3,2,1,0:T(8,128)(2,1)} %fusion.23), channel_id=1, source_target_pairs={{0,8},{4,12},{8,0},{12,4},{16,24},{20,28},{24,16},{28,20},{1,9},{5... | collective-permute-start | bytes 3145736 | tf_op jit(solution)/shard_map/ppermute | solution.py:236
  317.3 24.9 %collective-permute-start.23 = (bf16[2,2,2,32,2048]{4,3,2,1,0:T(8,128)(2,1)}, bf16[2,2,2,32,2048]{4,3,2,1,0:T(8,128)(2,1)}, u32[]{:S(2)}, u32[]{:S(2)}) collective-permute-start(bf16[2,2,2,32,2048]{4,3,2,1,0:T(8,128)(2,1)} %get-tuple-element.114), channel_id=1, source_target_pairs={{0,2},{1,3},{2,0},{3,1},{4,6},{5,7},{6,4},{7,5},{8,10},{9,11},{10,... | collective-permute-start | bytes 3145736 | tf_op jit(solution)/shard_map/ppermute | solution.py:236
  319.3 35.6 %collective-permute-start.24 = (bf16[2,2,2,32,2048]{4,3,2,1,0:T(8,128)(2,1)}, bf16[2,2,2,32,2048]{4,3,2,1,0:T(8,128)(2,1)}, u32[]{:S(2)}, u32[]{:S(2)}) collective-permute-start(bf16[2,2,2,32,2048]{4,3,2,1,0:T(8,128)(2,1)} %get-tuple-element.115), channel_id=1, source_target_pairs={{0,4},{4,0},{8,12},{12,8},{16,20},{20,16},{24,28},{28,24},{1,5},{5... | collective-permute-start | bytes 3145736 | tf_op jit(solution)/shard_map/ppermute | solution.py:236
  368.2 29.0 %collective-permute-start.29 = (bf16[2,2,40,1024]{3,2,1,0:T(8,128)(2,1)}, bf16[2,2,40,1024]{3,2,1,0:T(8,128)(2,1)}, u32[]{:S(2)}, u32[]{:S(2)}) collective-permute-start(bf16[2,2,40,1024]{3,2,1,0:T(8,128)(2,1)} %fusion.53), channel_id=1, source_target_pairs={{0,8},{4,12},{8,0},{12,4},{16,24},{20,28},{24,16},{28,20},{1,9},{5... | collective-permute-start | bytes 983048 | tf_op jit(solution)/shard_map/ppermute | solution.py:236
  368.2 29.0 %collective-permute-start.30 = (bf16[2,2,128,384]{3,2,1,0:T(8,128)(2,1)}, bf16[2,2,128,384]{3,2,1,0:T(8,128)(2,1)}, u32[]{:S(2)}, u32[]{:S(2)}) collective-permute-start(bf16[2,2,128,384]{3,2,1,0:T(8,128)(2,1)} %fusion.60), channel_id=1, source_target_pairs={{0,4},{4,0},{8,12},{12,8},{16,20},{20,16},{24,28},{28,24},{1,5},{5... | collective-permute-start | bytes 1179656 | tf_op jit(solution)/shard_map/ppermute | solution.py:236
  370.4 26.7 %collective-permute-start.27 = (bf16[2,2,32,2048]{3,2,0,1:T(8,128)(2,1)}, bf16[2,2,32,2048]{3,2,0,1:T(8,128)(2,1)}, u32[]{:S(2)}, u32[]{:S(2)}) collective-permute-start(bf16[2,2,32,2048]{3,2,0,1:T(8,128)(2,1)} %copy.206), channel_id=1, source_target_pairs={{0,4},{4,0},{8,12},{12,8},{16,20},{20,16},{24,28},{28,24},{1,5},{5... | collective-permute-start | bytes 1572872 | tf_op jit(solution)/shard_map/ppermute | solution.py:236
  371.0 26.1 %collective-permute-start.26 = (bf16[2,128,1024]{2,1,0:T(8,128)(2,1)}, bf16[2,128,1024]{2,1,0:T(8,128)(2,1)}, u32[]{:S(2)}, u32[]{:S(2)}) collective-permute-start(bf16[2,128,1024]{2,1,0:T(8,128)(2,1)} %fusion.44), channel_id=1, source_target_pairs={{0,2},{1,3},{2,0},{3,1},{4,6},{5,7},{6,4},{7,5},{8,10},{9,11},{10,... | collective-permute-start | bytes 1572872 | tf_op jit(solution)/shard_map/ppermute | solution.py:236
  372.9 24.2 %collective-permute-start.28 = (bf16[2,2,32,2048]{3,2,1,0:T(8,128)(2,1)}, bf16[2,2,32,2048]{3,2,1,0:T(8,128)(2,1)}, u32[]{:S(2)}, u32[]{:S(2)}) collective-permute-start(bf16[2,2,32,2048]{3,2,1,0:T(8,128)(2,1)} %get-tuple-element.127), channel_id=1, source_target_pairs={{0,8},{4,12},{8,0},{12,4},{16,24},{20,28},{24,16},{28,20},{1,9},{5... | collective-permute-start | bytes 1572872 | tf_op jit(solution)/shard_map/ppermute | solution.py:236
  413.0 24.5 %collective-permute-start.37 = (bf16[1024,1024]{1,0:T(8,128)(2,1)S(1)}, bf16[1024,1024]{1,0:T(8,128)(2,1)S(1)}, u32[]{:S(2)}, u32[]{:S(2)}) collective-permute-start(bf16[1024,1024]{1,0:T(8,128)(2,1)S(1)} %convolution_convert_fusion.3), channel_id=1, source_target_pairs={{0,1},{1,0},{2,3},{3,2},{4,5},{5,4},{6,7},{7,6},{8,9},{9,8},{10,11... | collective-permute-start | bytes 6291464 | tf_op jit(solution)/shard_map/ppermute | solution.py:236
  419.0 14.6 %collective-permute-start.31 = (bf16[128,1024]{1,0:T(8,128)(2,1)S(1)}, bf16[128,1024]{1,0:T(8,128)(2,1)S(1)}, u32[]{:S(2)}, u32[]{:S(2)}) collective-permute-start(bf16[128,1024]{1,0:T(8,128)(2,1)S(1)} %fusion.59), channel_id=1, source_target_pairs={{0,16},{4,20},{8,24},{12,28},{16,0},{20,4},{24,8},{28,12},{1,17},{... | collective-permute-start | bytes 786440 | tf_op jit(solution)/shard_map/ppermute | solution.py:236
  447.3 25.1 %collective-permute-start.47 = (bf16[512,1024]{1,0:T(8,128)(2,1)}, bf16[512,1024]{1,0:T(8,128)(2,1)}, u32[]{:S(2)}, u32[]{:S(2)}) collective-permute-start(bf16[512,1024]{1,0:T(8,128)(2,1)} %slice.467), channel_id=1, source_target_pairs={{0,2},{1,3},{2,0},{3,1},{4,6},{5,7},{6,4},{7,5},{8,10},{9,11},{10,... | collective-permute-start | bytes 3145736 | tf_op jit(solution)/shard_map/ppermute | solution.py:236
  447.3 22.4 %collective-permute-start.45 = (bf16[40,1024]{1,0:T(8,128)(2,1)}, bf16[40,1024]{1,0:T(8,128)(2,1)S(1)}, u32[]{:S(2)}, u32[]{:S(2)}) collective-permute-start(bf16[40,1024]{1,0:T(8,128)(2,1)} %fusion.76), channel_id=1, source_target_pairs={{0,16},{4,20},{8,24},{12,28},{16,0},{20,4},{24,8},{28,12},{1,17},{... | collective-permute-start | bytes 245768 | tf_op jit(solution)/shard_map/ppermute | solution.py:236
  450.3 19.5 %collective-permute-start.43 = (bf16[32,2048]{1,0:T(8,128)(2,1)}, bf16[32,2048]{1,0:T(8,128)(2,1)S(1)}, u32[]{:S(2)}, u32[]{:S(2)}) collective-permute-start(bf16[32,2048]{1,0:T(8,128)(2,1)} %get-tuple-element.162), channel_id=1, source_target_pairs={{0,16},{4,20},{8,24},{12,28},{16,0},{20,4},{24,8},{28,12},{1,17},{... | collective-permute-start | bytes 393224 | tf_op jit(solution)/shard_map/ppermute | solution.py:236
  (72 other events, 580.1 us)
Sparse Core Ops, SparseCore 0:
  13.5 157.7 all-gather.1

commit v8 on v7

--- a/solution.py
+++ b/solution.py
@@ -321,18 +321,6 @@
     per_chunk = piece // BLOCK
     tokens, cotangent, ids = tokens[0], cotangent[0], segment_ids[0]
 
-    second = lax.all_gather(
-        jnp.concatenate([up_weight, output_weight] + [down_weight[n * own : (n + 1) * own] for n in range(ratio)], axis=1),
-        BOTH,
-        axis=0,
-        tiled=True,
-    )
-    up_full, output_full = second[:, :hidden], second[:, hidden : hidden + width]
-    down_full = jnp.stack(
-        [second[:, hidden + n * width : hidden + (n + 1) * width].reshape(devices, own, width) for n in range(1, 1 + ratio)],
-        axis=1,
-    ).reshape(hidden, width)
-
     held = {0: tokens, ctx // 2: swap(tokens, "ctx", ctx // 2)}
     vectors = [
         time_bias, query_bias, value_bias, output_bias, mixing_gain, mixing_bias, down_bias, final_gain, final_bias
@@ -349,6 +337,17 @@
         ] + [lax.dynamic_slice_in_dim(time_weight, at, cols, 1)]
         pieces.append(jnp.concatenate(parts + [small], axis=1))
     first = jnp.concatenate(to_absolute(trade(pieces, "ctx"), me))
+    second = jnp.concatenate(
+        [up_weight, output_weight] + [down_weight[n * own : (n + 1) * own] for n in range(ratio)], axis=1
+    )
+    second, first = lax.optimization_barrier((second, first))
+    second = lax.all_gather(second, BOTH, axis=0, tiled=True)
+    up_full, output_full = second[:, :hidden], second[:, hidden : hidden + width]
+    down_full = jnp.stack(
+        [second[:, hidden + n * width : hidden + (n + 1) * width].reshape(devices, own, width) for n in range(1, 1 + ratio)],
+        axis=1,
+    ).reshape(hidden, width)
+
     first = first[None]
     for n, bit in enumerate(reversed(bits(dp))):
         if n == 1:
@@ -473,22 +472,30 @@
     grad_mixed = jnp.concatenate(trade(pieces, "ctx"))
     grad_mixed = land(ahead, grad_mixed)
 
-    def weight_stream(grad):
-        size = (ctx * own, grad.shape[1])
+    def weight_stream(product):
+        size = (ctx * own, product.shape[1])
         sums = Halving(dp_names[::-1], size)
-        array = tn(start_row, grad).reshape([2] * len(dp_names) + list(size))
+        array = product.reshape([2] * len(dp_names) + list(size))
         sums.terms = [(array, dp_names[::-1], [(0, d) for d in size])]
         return sums, list(dp_names)
 
-    grads, pair_streams = [], []
+    def products(grad):
+        return tn(start_row, grad), jnp.sum(grad.astype(f32), axis=0)
+
+    grads, pair_streams, qkv_sum = [], [], []
     for pair in range(cols // 128):
         flights, grad_mixed = depart(following(streams + pair_streams), grad_mixed)
         grad = attention_backward(pair, info, qkv, grad_mixed, mixed, logsum, ids_col, ids_row, per_chunk)
-        grad_mixed, grad = land(flights, (grad_mixed, grad))
+        if pair == 0:
+            grad_mixed, grad, (product, total) = land(flights, (grad_mixed, grad, products(grad)))
+        else:
+            grad_mixed, grad = land(flights, (grad_mixed, grad))
+            product, total = products(grad)
         grads.append(grad)
-        pair_streams.append(weight_stream(grad))
-
-    qkv_sum = jnp.concatenate([jnp.sum(g.astype(f32), axis=0) for g in grads])
+        pair_streams.append(weight_stream(product))
+        qkv_sum.append(total)
+
+    qkv_sum = jnp.concatenate(qkv_sum)
     row_sum = jnp.sum(grad_one, axis=0, keepdims=True) + lax.dot_general(
         qkv_sum[None],
         qkv_weight.astype(f32),

time: 509 us -> 497 us (0.976)
  waiting for transfers between devices: 163 us -> 127 us
  starting transfers between devices: 62.3 us -> 85.3 us
    ppermute x54, waiting for transfers between devices: 163 us -> 125 us  [swap(): return lax.ppermute(value, axis, [(i, i ^ mask) for i in range(size)])]
    ppermute x54, starting transfers between devices: 62.2 us -> 85.3 us  [swap(): return lax.ppermute(value, axis, [(i, i ^ mask) for i in range(size)])]
    unnamed x124 -> x118, local copies, waits for them, and re-layouts: 20 us -> 21 us
  transfers between devices with their start and end apart: 55 -> 55, of which waited for: 24 -> 19; matrix products, arithmetic and copies ran while one was open for 19% -> 21% of each run, Pallas kernels for 13% -> 13%
where the time goes in v8:
time: 497 us; the launch traced here: 488 us
  waiting for transfers between devices  127 us (26%)
  starting transfers between devices  85.3 us (17%)
  matrix products  76 us (15%)
  other arithmetic  71.5 us (14%)
  Pallas kernels  62.9 us (13%)
  local copies, waits for them, and re-layouts  49.7 us (10%)
  between operations  15.5 us (3%)
    ppermute x54, waiting for transfers between devices, swap(): return lax.ppermute(value, axis, [(i, i ^ mask) for i in range(size)])  125 us
    ppermute x54, starting transfers between devices, swap(): return lax.ppermute(value, axis, [(i, i ^ mask) for i in range(size)])  85.3 us
    pallas_call x2, Pallas kernels, attention_backward(): pl.pallas_call(functools.partial(backward_kernel, per_chunk, 2 * pair), g...  40.4 us
    convert_element_type x16, other arithmetic, outgoing(): return self.total({**self.fixed, name: 1 - self.me[name]}).astype(bf16)  35.5 us
    dot_general x5, matrix products, nn(): return jnp.dot(left, right, preferred_element_type=f32)  27.3 us
    dot_general x5, matrix products, nt(): lax.dot_general(left, right, (((1,), (1,)), ((), ())), preferred_element_...  24.7 us
    pallas_call x1, Pallas kernels, attention_forward(): pl.pallas_call(functools.partial(forward_kernel, per_chunk, heads // 2),...  22.5 us
    dot_general x5, matrix products, tn(): lax.dot_general(left, right, (((0,), (0,)), ((), ())), preferred_element_...  22.2 us
  transfers between devices with their start and end apart: 55, of which 19 were waited for; matrix products, arithmetic and copies ran while one was open for 21% of the time, Pallas kernels for 13%

profile of v8, /device:TPU:0, one launch (start us, length us, event | category | flops | bytes accessed | tf_op | source)
XLA Modules:
  0.0 488.2 jit_solution(12780399328092152872)
XLA Ops:
  28.6 21.4 %collective-permute-done.3 = bf16[1,128,1152]{2,1,0:T(8,128)(2,1)S(1)} collective-permute-done((bf16[1,128,1152]{2,1,0:T(8,128)(2,1)S(1)}, bf16[1,128,1152]{2,1,0:T(8,128)(2,1)S(1)}, u32[]{:S(2)}, u32[]{:S(2)}) %collective-permute-start.3) | collective-permute-done | bytes 294944 | tf_op jit(solution)/shard_map/ppermute | solution.py:236
  57.5 27.8 %collective-permute-done.5 = bf16[2,128,1152]{2,1,0:T(8,128)(2,1)S(1)} collective-permute-done((bf16[2,128,1152]{2,1,0:T(8,128)(2,1)S(1)}, bf16[2,128,1152]{2,1,0:T(8,128)(2,1)S(1)}, u32[]{:S(2)}, u32[]{:S(2)}) %collective-permute-start.5) | collective-permute-done | bytes 589856 | tf_op jit(solution)/shard_map/ppermute | solution.py:236
  92.7 22.2 %collective-permute-done.6 = bf16[4,128,1152]{2,1,0:T(8,128)(2,1)S(1)} collective-permute-done((bf16[4,128,1152]{2,1,0:T(8,128)(2,1)S(1)}, bf16[4,128,1152]{2,1,0:T(8,128)(2,1)S(1)}, u32[]{:S(2)}, u32[]{:S(2)}) %collective-permute-start.6) | collective-permute-done | bytes 1179680 | tf_op jit(solution)/shard_map/ppermute | solution.py:236
  130.6 7.3 %add_convert_fusion.1.qkv_ref.q_ref.k_ref.v_ref = bf16[2048,768]{1,0:T(8,128)(2,1)} fusion(f32[768]{0:T(1024)S(1)} %constant_dynamic-update-slice_fusion.72, bf16[1024,1152]{0,1:T(8,128)(2,1)S(1)} %bitcast_dynamic-update-slice_fusion, bf16[512,1024]{1,0:T(8,128)(2,1)} %collective-permute-done.11, bf16[512,1024]{1,0:T(8,128)(2,1)} %collective-permute-done.4, ...), kind=kOutput, calls=%fused_computation.23 | convolution fusion | flops 3245342720 | bytes 8921088 | tf_op jit(solution)/shard_map/dot_general | solution.py:21
  137.9 22.5 %attention_forward.1 = (bf16[2048,256]{1,0:T(8,128)(2,1)}, f32[8,4,256]{2,1,0:T(4,128)}) custom-call(s32[3,8]{1,0:T(4,128)} %add_add_fusion.2.info, bf16[2048,768]{1,0:T(8,128)(2,1)} %add_convert_fusion.1.qkv_ref.q_ref.k_ref.v_ref, s32[2048,1]{1,0:T(8,128)} %copy.186.idc_ref, s32[8,1,256]{2,1,0:T(1,128)} %bitcast.607), custom_call_target="tpu_custom_call" | custom-call | flops 30000001024 | bytes 3145728 | tf_op jit(solution)/shard_map/attention_forward/pallas_call | solution.py:95
  180.1 11.5 %fusion.4 = (bf16[512,4096]{1,0:T(8,128)(2,1)}, bf16[512,4096]{1,0:T(8,128)(2,1)S(1)}) fusion(f32[4096]{0:T(1024)S(1)} %add.488, bf16[1024,9216]{1,0:T(8,128)(2,1)} %all-gather.2.cloned.1.call-done, f32[512,1024]{1,0:T(8,128)S(1)} %get-tuple-element.332, f32[1024]{0:T(1024)S(1)} %bitcast.635, f32[1024]{0:T(1024)S(1)} %bitcast.623, ...), kind=kOutput, calls=%fused_computation.5 | convolution fusion | flops 4322754560 | bytes 18903040 | tf_op jit(solution)/shard_map/dot_general | solution.py:21
  191.6 4.8 fusion.114
  200.4 5.3 %convolution_convert_fusion.1 = bf16[4096,1024]{1,0:T(8,128)(2,1)S(1)} fusion(bf16[512,4096]{1,0:T(8,128)(2,1)S(1)} %get-tuple-element.112, f32[512,1024]{1,0:T(8,128)S(1)} %get-tuple-element.201), kind=kOutput, calls=%fused_computation.18 | convolution fusion | flops 4299685888 | bytes 14680064 | tf_op jit(solution)/shard_map/dot_general | solution.py:25
  210.7 9.9 %multiply_convert_fusion = bf16[512,4096]{1,0:T(8,128)(2,1)S(1)} fusion(bf16[512,4096]{1,0:T(8,128)(2,1)} %get-tuple-element.114, bf16[4096,1024]{1,0:T(8,128)(2,1)} %bitcast.569, f32[512,1024]{1,0:T(8,128)} %copy-done.10), kind=kOutput, calls=%fused_computation.7 | convolution fusion | flops 4301783040 | bytes 18874368 | tf_op jit(solution)/shard_map/dot_general | solution.py:29
  220.6 4.8 fusion.9
  227.0 5.2 %convolution_convert_fusion = bf16[1024,4096]{1,0:T(8,128)(2,1)S(1)} fusion(bf16[512,4096]{1,0:T(8,128)(2,1)S(1)} %multiply_convert_fusion, f32[512,1024]{1,0:T(8,128)S(1)} %get-tuple-element.332, f32[1024]{0:T(1024)S(1)} %bitcast.637, f32[1024]{0:T(1024)S(1)} %bitcast.625, f32[512]{0:T(512)S(1)} %add_rsqrt_fusion.1, f32[512]{0:T(512)S(1)} %broadcast_multiply_fusion.5), kind=kOutput, calls=%fused_computation.17 | convolution fusion | flops 4301783040 | bytes 14692352 | tf_op jit(solution)/shard_map/dot_general | solution.py:25
  232.3 8.0 %collective-permute-start.16 = (bf16[2,2,2,128,1024]{4,3,0,2,1:T(8,128)(2,1)}, bf16[2,2,2,128,1024]{4,3,0,2,1:T(8,128)(2,1)}, u32[]{:S(2)}, u32[]{:S(2)}) collective-permute-start(bf16[2,2,2,128,1024]{4,3,0,2,1:T(8,128)(2,1)} %copy.189), channel_id=1, source_target_pairs={{0,4},{4,0},{8,12},{12,8},{16,20},{20,16},{24,28},{28,24},{1,5},{5... | collective-permute-start | bytes 6291464 | tf_op jit(solution)/shard_map/ppermute | solution.py:236
  242.7 8.3 %multiply_reduce_fusion = (f32[1024]{0:T(1024)S(1)}, f32[512]{0:T(512)S(1)}, f32[512]{0:T(512)S(1)}, f32[1024]{0:T(1024)S(1)}, f32[512,1024]{1,0:T(8,128)S(1)}) fusion(f32[512,1024]{1,0:T(8,128)S(1)} %get-tuple-element.332, f32[512]{0:T(512)S(1)} %add_rsqrt_fusion.1, f32[512]{0:T(512)S(1)} %broadcast_multiply_fusion.5, f32[1024]{0:T(1024)S(1)} %bitcast.626, ...), kind=kOutput, calls=%fused_computation.61 | convolution fusion | flops 4300207104 | bytes 18894848 | tf_op jit(solution)/shard_map/dot_general | solution.py:29
  266.8 6.4 %collective-permute-done.19 = bf16[512,256]{1,0:T(8,128)(2,1)S(1)} collective-permute-done((bf16[512,256]{1,0:T(8,128)(2,1)S(1)}, bf16[512,256]{1,0:T(8,128)(2,1)S(1)}, u32[]{:S(2)}, u32[]{:S(2)}) %collective-permute-start.19) | collective-permute-done | bytes 262176 | tf_op jit(solution)/shard_map/ppermute | solution.py:236
  290.3 4.4 fusion.21
  298.4 20.1 %attention_backward.2 = bf16[2048,384]{1,0:T(8,128)(2,1)} custom-call(s32[3,8]{1,0:T(4,128)} %add_add_fusion.2.info, bf16[2048,768]{1,0:T(8,128)(2,1)} %add_convert_fusion.1.qkv_ref.q_ref.k_ref.v_ref, bf16[2048,768]{1,0:T(8,128)(2,1)} %add_convert_fusion.1.qkv_ref.q_ref.k_ref.v_ref, bf16[2048,768]{1,0:T(8,128)(2,1)} %add_convert_fusion.1.qkv_ref.q_ref.k_ref.v_ref, ...), custom_call_target="tpu_custom_call" | custom-call | flops 24999999488 | bytes 2097152 | tf_op jit(solution)/shard_map/attention_backward/pallas_call | solution.py:193
  320.2 4.7 fusion.106
  324.9 9.2 %collective-permute-done.24 = bf16[2,2,2,32,2048]{4,3,2,1,0:T(8,128)(2,1)} collective-permute-done((bf16[2,2,2,32,2048]{4,3,2,1,0:T(8,128)(2,1)}, bf16[2,2,2,32,2048]{4,3,2,1,0:T(8,128)(2,1)}, u32[]{:S(2)}, u32[]{:S(2)}) %collective-permute-start.24) | collective-permute-done | bytes 1048608 | tf_op jit(solution)/shard_map/ppermute | solution.py:236
  349.0 20.3 %attention_backward.3 = bf16[2048,384]{1,0:T(8,128)(2,1)} custom-call(s32[3,8]{1,0:T(4,128)} %add_add_fusion.2.info, bf16[2048,768]{1,0:T(8,128)(2,1)} %add_convert_fusion.1.qkv_ref.q_ref.k_ref.v_ref, bf16[2048,768]{1,0:T(8,128)(2,1)} %add_convert_fusion.1.qkv_ref.q_ref.k_ref.v_ref, bf16[2048,768]{1,0:T(8,128)(2,1)} %add_convert_fusion.1.qkv_ref.q_ref.k_ref.v_ref, ...), custom_call_target="tpu_custom_call" | custom-call | flops 24999999488 | bytes 2097152 | tf_op jit(solution)/shard_map/attention_backward/pallas_call | solution.py:193
  385.9 5.2 %collective-permute-start.35 = (bf16[2,128,384]{2,1,0:T(8,128)(2,1)S(1)}, bf16[2,128,384]{2,1,0:T(8,128)(2,1)S(1)}, u32[]{:S(2)}, u32[]{:S(2)}) collective-permute-start(bf16[2,128,384]{2,1,0:T(8,128)(2,1)S(1)} %fusion.63), channel_id=1, source_target_pairs={{0,8},{4,12},{8,0},{12,4},{16,24},{20,28},{24,16},{28,20},{1,9},{5... | collective-permute-start | bytes 589832 | tf_op jit(solution)/shard_map/ppermute | solution.py:236
  391.6 16.2 %collective-permute-start.38 = (f32[1,2560]{1,0:T(1,128)S(1)}, f32[1,2560]{1,0:T(1,128)S(1)}, u32[]{:S(2)}, u32[]{:S(2)}) collective-permute-start(f32[1,2560]{1,0:T(1,128)S(1)} %constant_dynamic-update-slice_fusion.42), channel_id=1, source_target_pairs={{0,16},{4,20},{8,24},{12,28},{16,0},{20,4},{24,8},{28,12},{1,17},{... | collective-permute-start | bytes 30728 | tf_op jit(solution)/shard_map/ppermute | solution.py:236
  416.7 5.7 %collective-permute-done.31 = bf16[128,1024]{1,0:T(8,128)(2,1)S(1)} collective-permute-done((bf16[128,1024]{1,0:T(8,128)(2,1)S(1)}, bf16[128,1024]{1,0:T(8,128)(2,1)S(1)}, u32[]{:S(2)}, u32[]{:S(2)}) %collective-permute-start.31) | collective-permute-done | bytes 262176 | tf_op jit(solution)/shard_map/ppermute | solution.py:236
  443.3 5.6 %collective-permute-done.39 = bf16[128,384]{1,0:T(8,128)(2,1)S(1)} collective-permute-done((bf16[128,384]{1,0:T(8,128)(2,1)}, bf16[128,384]{1,0:T(8,128)(2,1)S(1)}, u32[]{:S(2)}, u32[]{:S(2)}) %collective-permute-start.39) | collective-permute-done | bytes 98336 | tf_op jit(solution)/shard_map/ppermute | solution.py:236
  457.0 4.5 collective-permute-done.42
  (349 shorter events, 211.4 us)
Async XLA Ops:
  7.2 160.5 %all-gather.2.cloned.1.call-start = ((), (), s32[]{:S(2)}) async-start(), calls=%async_computation | async-start | bytes 19464192 | tf_op jit(solution)/shard_map/all_gather | solution.py:344
  24.2 30.0 %collective-permute-start.4 = (bf16[512,1024]{1,0:T(8,128)(2,1)}, bf16[512,1024]{1,0:T(8,128)(2,1)}, u32[]{:S(2)}, u32[]{:S(2)}) collective-permute-start(bf16[512,1024]{1,0:T(8,128)(2,1)} %bitcast), channel_id=1, source_target_pairs={{0,2},{1,3},{2,0},{3,1},{4,6},{5,7},{6,4},{7,5},{8,10},{9,11},{10,... | collective-permute-start | bytes 3145736 | tf_op jit(solution)/shard_map/ppermute | solution.py:236
  26.0 24.0 %collective-permute-start.3 = (bf16[1,128,1152]{2,1,0:T(8,128)(2,1)S(1)}, bf16[1,128,1152]{2,1,0:T(8,128)(2,1)S(1)}, u32[]{:S(2)}, u32[]{:S(2)}) collective-permute-start(bf16[1,128,1152]{2,1,0:T(8,128)(2,1)S(1)} %bitcast.577), channel_id=1, source_target_pairs={{0,16},{4,20},{8,24},{12,28},{16,0},{20,4},{24,8},{28,12},{1,17},{... | collective-permute-start | bytes 884744 | tf_op jit(solution)/shard_map/ppermute | solution.py:236
  54.2 31.1 %collective-permute-start.5 = (bf16[2,128,1152]{2,1,0:T(8,128)(2,1)S(1)}, bf16[2,128,1152]{2,1,0:T(8,128)(2,1)S(1)}, u32[]{:S(2)}, u32[]{:S(2)}) collective-permute-start(bf16[2,128,1152]{2,1,0:T(8,128)(2,1)S(1)} %pad_maximum_fusion.6), channel_id=1, source_target_pairs={{0,8},{4,12},{8,0},{12,4},{16,24},{20,28},{24,16},{28,20},{1,9},{5... | collective-permute-start | bytes 1769480 | tf_op jit(solution)/shard_map/ppermute | solution.py:236
  56.0 74.6 %collective-permute-start.10 = (bf16[512,1024]{1,0:T(8,128)(2,1)}, bf16[512,1024]{1,0:T(8,128)(2,1)}, u32[]{:S(2)}, u32[]{:S(2)}) collective-permute-start(bf16[512,1024]{1,0:T(8,128)(2,1)} %bitcast), channel_id=1, source_target_pairs={{0,1},{1,0},{2,3},{3,2},{4,5},{5,4},{6,7},{7,6},{8,9},{9,8},{10,11... | collective-permute-start | bytes 3145736 | tf_op jit(solution)/shard_map/ppermute | solution.py:236
  85.4 29.6 %collective-permute-start.6 = (bf16[4,128,1152]{2,1,0:T(8,128)(2,1)S(1)}, bf16[4,128,1152]{2,1,0:T(8,128)(2,1)S(1)}, u32[]{:S(2)}, u32[]{:S(2)}) collective-permute-start(bf16[4,128,1152]{2,1,0:T(8,128)(2,1)S(1)} %pad_maximum_fusion.2), channel_id=1, source_target_pairs={{0,4},{4,0},{8,12},{12,8},{16,20},{20,16},{24,28},{28,24},{1,5},{5... | collective-permute-start | bytes 3538952 | tf_op jit(solution)/shard_map/ppermute | solution.py:236
  92.6 38.0 %collective-permute-start.11 = (bf16[512,1024]{1,0:T(8,128)(2,1)}, bf16[512,1024]{1,0:T(8,128)(2,1)}, u32[]{:S(2)}, u32[]{:S(2)}) collective-permute-start(bf16[512,1024]{1,0:T(8,128)(2,1)} %collective-permute-done.4), channel_id=1, source_target_pairs={{0,1},{1,0},{2,3},{3,2},{4,5},{5,4},{6,7},{7,6},{8,9},{9,8},{10,11... | collective-permute-start | bytes 3145736 | tf_op jit(solution)/shard_map/ppermute | solution.py:236
  232.3 54.6 %collective-permute-start.16 = (bf16[2,2,2,128,1024]{4,3,0,2,1:T(8,128)(2,1)}, bf16[2,2,2,128,1024]{4,3,0,2,1:T(8,128)(2,1)}, u32[]{:S(2)}, u32[]{:S(2)}) collective-permute-start(bf16[2,2,2,128,1024]{4,3,0,2,1:T(8,128)(2,1)} %copy.189), channel_id=1, source_target_pairs={{0,4},{4,0},{8,12},{12,8},{16,20},{20,16},{24,28},{28,24},{1,5},{5... | collective-permute-start | bytes 6291464 | tf_op jit(solution)/shard_map/ppermute | solution.py:236
  242.5 47.9 %collective-permute-start.20 = (bf16[2,2,2,2,32,4096]{5,4,3,2,1,0:T(8,128)(2,1)}, bf16[2,2,2,2,32,4096]{5,4,3,2,1,0:T(8,128)(2,1)}, u32[]{:S(2)}, u32[]{:S(2)}) collective-permute-start(bf16[2,2,2,2,32,4096]{5,4,3,2,1,0:T(8,128)(2,1)} %dynamic-slice_bitcast_fusion), channel_id=1, source_target_pairs={{0,1},{1,0},{2,3},{3,2},{4,5},{5,4},{6,7},{7,6},{8,9},{9,8},{10,11... | collective-permute-start | bytes 12582920 | tf_op jit(solution)/shard_map/ppermute | solution.py:236
  260.9 20.4 %collective-permute-start.21 = (bf16[2,2,2,2,40,1024]{5,4,3,2,1,0:T(8,128)(2,1)}, bf16[2,2,2,2,40,1024]{5,4,3,2,1,0:T(8,128)(2,1)}, u32[]{:S(2)}, u32[]{:S(2)}) collective-permute-start(bf16[2,2,2,2,40,1024]{5,4,3,2,1,0:T(8,128)(2,1)} %fusion.36), channel_id=1, source_target_pairs={{0,1},{1,0},{2,3},{3,2},{4,5},{5,4},{6,7},{7,6},{8,9},{9,8},{10,11... | collective-permute-start | bytes 3932168 | tf_op jit(solution)/shard_map/ppermute | solution.py:236
  294.7 30.1 %collective-permute-start.25 = (bf16[2,2,2,40,1024]{4,3,2,1,0:T(8,128)(2,1)}, bf16[2,2,2,40,1024]{4,3,2,1,0:T(8,128)(2,1)S(1)}, u32[]{:S(2)}, u32[]{:S(2)}) collective-permute-start(bf16[2,2,2,40,1024]{4,3,2,1,0:T(8,128)(2,1)} %fusion.37), channel_id=1, source_target_pairs={{0,4},{4,0},{8,12},{12,8},{16,20},{20,16},{24,28},{28,24},{1,5},{5... | collective-permute-start | bytes 1966088 | tf_op jit(solution)/shard_map/ppermute | solution.py:236
  296.5 28.4 %collective-permute-start.22 = (bf16[2,2,128,1024]{3,2,1,0:T(8,128)(2,1)}, bf16[2,2,128,1024]{3,2,1,0:T(8,128)(2,1)}, u32[]{:S(2)}, u32[]{:S(2)}) collective-permute-start(bf16[2,2,128,1024]{3,2,1,0:T(8,128)(2,1)} %fusion.23), channel_id=1, source_target_pairs={{0,8},{4,12},{8,0},{12,4},{16,24},{20,28},{24,16},{28,20},{1,9},{5... | collective-permute-start | bytes 3145736 | tf_op jit(solution)/shard_map/ppermute | solution.py:236
  296.5 28.4 %collective-permute-start.23 = (bf16[2,2,2,32,2048]{4,3,2,1,0:T(8,128)(2,1)}, bf16[2,2,2,32,2048]{4,3,2,1,0:T(8,128)(2,1)}, u32[]{:S(2)}, u32[]{:S(2)}) collective-permute-start(bf16[2,2,2,32,2048]{4,3,2,1,0:T(8,128)(2,1)} %get-tuple-element.120), channel_id=1, source_target_pairs={{0,2},{1,3},{2,0},{3,1},{4,6},{5,7},{6,4},{7,5},{8,10},{9,11},{10,... | collective-permute-start | bytes 3145736 | tf_op jit(solution)/shard_map/ppermute | solution.py:236
  298.1 36.0 %collective-permute-start.24 = (bf16[2,2,2,32,2048]{4,3,2,1,0:T(8,128)(2,1)}, bf16[2,2,2,32,2048]{4,3,2,1,0:T(8,128)(2,1)}, u32[]{:S(2)}, u32[]{:S(2)}) collective-permute-start(bf16[2,2,2,32,2048]{4,3,2,1,0:T(8,128)(2,1)} %get-tuple-element.121), channel_id=1, source_target_pairs={{0,4},{4,0},{8,12},{12,8},{16,20},{20,16},{24,28},{28,24},{1,5},{5... | collective-permute-start | bytes 3145736 | tf_op jit(solution)/shard_map/ppermute | solution.py:236
  342.6 26.7 %collective-permute-start.29 = (bf16[2,2,40,1024]{3,2,1,0:T(8,128)(2,1)}, bf16[2,2,40,1024]{3,2,1,0:T(8,128)(2,1)}, u32[]{:S(2)}, u32[]{:S(2)}) collective-permute-start(bf16[2,2,40,1024]{3,2,1,0:T(8,128)(2,1)} %fusion.53), channel_id=1, source_target_pairs={{0,8},{4,12},{8,0},{12,4},{16,24},{20,28},{24,16},{28,20},{1,9},{5... | collective-permute-start | bytes 983048 | tf_op jit(solution)/shard_map/ppermute | solution.py:236
  342.6 26.7 %collective-permute-start.30 = (bf16[2,2,128,384]{3,2,1,0:T(8,128)(2,1)}, bf16[2,2,128,384]{3,2,1,0:T(8,128)(2,1)}, u32[]{:S(2)}, u32[]{:S(2)}) collective-permute-start(bf16[2,2,128,384]{3,2,1,0:T(8,128)(2,1)} %fusion.60), channel_id=1, source_target_pairs={{0,4},{4,0},{8,12},{12,8},{16,20},{20,16},{24,28},{28,24},{1,5},{5... | collective-permute-start | bytes 1179656 | tf_op jit(solution)/shard_map/ppermute | solution.py:236
  344.9 24.4 %collective-permute-start.27 = (bf16[2,2,32,2048]{3,2,0,1:T(8,128)(2,1)}, bf16[2,2,32,2048]{3,2,0,1:T(8,128)(2,1)}, u32[]{:S(2)}, u32[]{:S(2)}) collective-permute-start(bf16[2,2,32,2048]{3,2,0,1:T(8,128)(2,1)} %copy.206), channel_id=1, source_target_pairs={{0,4},{4,0},{8,12},{12,8},{16,20},{20,16},{24,28},{28,24},{1,5},{5... | collective-permute-start | bytes 1572872 | tf_op jit(solution)/shard_map/ppermute | solution.py:236
  345.5 23.8 %collective-permute-start.26 = (bf16[2,128,1024]{2,1,0:T(8,128)(2,1)}, bf16[2,128,1024]{2,1,0:T(8,128)(2,1)}, u32[]{:S(2)}, u32[]{:S(2)}) collective-permute-start(bf16[2,128,1024]{2,1,0:T(8,128)(2,1)} %fusion.44), channel_id=1, source_target_pairs={{0,2},{1,3},{2,0},{3,1},{4,6},{5,7},{6,4},{7,5},{8,10},{9,11},{10,... | collective-permute-start | bytes 1572872 | tf_op jit(solution)/shard_map/ppermute | solution.py:236
  347.0 22.4 %collective-permute-start.28 = (bf16[2,2,32,2048]{3,2,1,0:T(8,128)(2,1)}, bf16[2,2,32,2048]{3,2,1,0:T(8,128)(2,1)}, u32[]{:S(2)}, u32[]{:S(2)}) collective-permute-start(bf16[2,2,32,2048]{3,2,1,0:T(8,128)(2,1)} %get-tuple-element.133), channel_id=1, source_target_pairs={{0,8},{4,12},{8,0},{12,4},{16,24},{20,28},{24,16},{28,20},{1,9},{5... | collective-permute-start | bytes 1572872 | tf_op jit(solution)/shard_map/ppermute | solution.py:236
  385.8 38.2 %collective-permute-start.37 = (bf16[1024,1024]{1,0:T(8,128)(2,1)S(1)}, bf16[1024,1024]{1,0:T(8,128)(2,1)S(1)}, u32[]{:S(2)}, u32[]{:S(2)}) collective-permute-start(bf16[1024,1024]{1,0:T(8,128)(2,1)S(1)} %convolution_convert_fusion.3), channel_id=1, source_target_pairs={{0,1},{1,0},{2,3},{3,2},{4,5},{5,4},{6,7},{7,6},{8,9},{9,8},{10,11... | collective-permute-start | bytes 6291464 | tf_op jit(solution)/shard_map/ppermute | solution.py:236
  385.9 29.1 %collective-permute-start.35 = (bf16[2,128,384]{2,1,0:T(8,128)(2,1)S(1)}, bf16[2,128,384]{2,1,0:T(8,128)(2,1)S(1)}, u32[]{:S(2)}, u32[]{:S(2)}) collective-permute-start(bf16[2,128,384]{2,1,0:T(8,128)(2,1)S(1)} %fusion.63), channel_id=1, source_target_pairs={{0,8},{4,12},{8,0},{12,4},{16,24},{20,28},{24,16},{28,20},{1,9},{5... | collective-permute-start | bytes 589832 | tf_op jit(solution)/shard_map/ppermute | solution.py:236
  391.1 22.4 %collective-permute-start.34 = (bf16[2,40,1024]{2,1,0:T(8,128)(2,1)S(1)}, bf16[2,40,1024]{2,1,0:T(8,128)(2,1)S(1)}, u32[]{:S(2)}, u32[]{:S(2)}) collective-permute-start(bf16[2,40,1024]{2,1,0:T(8,128)(2,1)S(1)} %fusion.65), channel_id=1, source_target_pairs={{0,2},{1,3},{2,0},{3,1},{4,6},{5,7},{6,4},{7,5},{8,10},{9,11},{10,... | collective-permute-start | bytes 491528 | tf_op jit(solution)/shard_map/ppermute | solution.py:236
  434.1 27.4 %collective-permute-start.47 = (bf16[512,1024]{1,0:T(8,128)(2,1)}, bf16[512,1024]{1,0:T(8,128)(2,1)}, u32[]{:S(2)}, u32[]{:S(2)}) collective-permute-start(bf16[512,1024]{1,0:T(8,128)(2,1)} %slice.467), channel_id=1, source_target_pairs={{0,2},{1,3},{2,0},{3,1},{4,6},{5,7},{6,4},{7,5},{8,10},{9,11},{10,... | collective-permute-start | bytes 3145736 | tf_op jit(solution)/shard_map/ppermute | solution.py:236
  434.7 22.3 %collective-permute-start.45 = (bf16[40,1024]{1,0:T(8,128)(2,1)}, bf16[40,1024]{1,0:T(8,128)(2,1)S(1)}, u32[]{:S(2)}, u32[]{:S(2)}) collective-permute-start(bf16[40,1024]{1,0:T(8,128)(2,1)} %fusion.76), channel_id=1, source_target_pairs={{0,16},{4,20},{8,24},{12,28},{16,0},{20,4},{24,8},{28,12},{1,17},{... | collective-permute-start | bytes 245768 | tf_op jit(solution)/shard_map/ppermute | solution.py:236
  (69 other events, 591.0 us)
Sparse Core Ops, SparseCore 0:
  24.3 143.3 all-gather.1

commit v9 on v8

--- a/solution.py
+++ b/solution.py
@@ -240,11 +240,6 @@
     return [1 << b for b in range(size.bit_length() - 1)]
 
 
-def flipped(index, size):
-    flags = bits(size)
-    return sum(((index >> n) & 1) << (len(flags) - 1 - n) for n in range(len(flags)))
-
-
 def trade(pieces, axis):
     return [pieces[0]] + [swap(pieces[k], axis, k) for k in range(1, len(pieces))]
 
@@ -352,16 +347,14 @@
     for n, bit in enumerate(reversed(bits(dp))):
         if n == 1:
             first, held[ctx // 2] = lax.optimization_barrier((first, held[ctx // 2]))
-        first = jnp.concatenate([first, swap(first, "dp", bit)])
+        other, side = swap(first, "dp", bit), jnp.minimum(me_dp & bit, 1)
+        own_side = lax.broadcasted_iota(jnp.uint32, (1, 2, 1, 1), 1) == side
+        first = jnp.where(own_side, first[:, None], other[:, None])
+        first = first.reshape((-1,) + first.shape[2:])
     for bit in reversed(bits(ctx)[:-1]):
         held.update({k | bit: swap(v, "ctx", bit) for k, v in list(held.items())})
     token_chunks = [held[k] for k in range(ctx)]
-    first = jnp.concatenate(
-        [
-            lax.dynamic_index_in_dim(first, flipped((me_dp ^ c), dp), 0, False)
-            for c in range(dp)
-        ]
-    )
+    first = first.reshape(width, -1)
     qkv_weight = first[:, : 3 * cols]
     table = first[:, 4 * cols :].astype(f32).T
     time_shift_bias, query_shift, value_shift, output_shift, gain_one, bias_one, down_shift, gain_two, bias_two = [

time: 497 us -> 513 us (1.032)
  Pallas kernels: 62.9 us -> 79.8 us
  starting transfers between devices: 85.3 us -> 77.4 us
  local copies, waits for them, and re-layouts: 49.7 us -> 55.9 us
    broadcast_in_dim x0 -> x11, local copies, waits for them, and re-layouts: none -> 12.8 us  [shards(): first = jnp.where(own_side, first[:, None], other[:, None])]
    pallas_call x2, Pallas kernels: 40.4 us -> 50.6 us  [attention_backward(): pl.pallas_call(functools.partial(backward_kernel, per_chunk, 2 * pair), g...]
    ppermute x54, starting transfers between devices: 85.3 us -> 77.4 us  [swap(): return lax.ppermute(value, axis, [(i, i ^ mask) for i in range(size)])]
    pallas_call x1, Pallas kernels: 22.5 us -> 29.1 us  [attention_forward(): pl.pallas_call(functools.partial(forward_kernel, per_chunk, heads // 2),...]
    unnamed x118 -> x101, local copies, waits for them, and re-layouts: 21 us -> 17.8 us
  transfers between devices with their start and end apart: 55 -> 55, of which waited for: 19 -> 20; matrix products, arithmetic and copies ran while one was open for 21% -> 21% of each run, Pallas kernels for 13% -> 16%
where the time goes in v9:
time: 513 us; the launch traced here: 503 us
  waiting for transfers between devices  126 us (25%)
  Pallas kernels  79.8 us (16%)
  starting transfers between devices  77.4 us (15%)
  matrix products  77.4 us (15%)
  other arithmetic  71.5 us (14%)
  local copies, waits for them, and re-layouts  55.9 us (11%)
  between operations  15.5 us (3%)
    ppermute x54, waiting for transfers between devices, swap(): return lax.ppermute(value, axis, [(i, i ^ mask) for i in range(size)])  126 us
    ppermute x54, starting transfers between devices, swap(): return lax.ppermute(value, axis, [(i, i ^ mask) for i in range(size)])  77.4 us
    pallas_call x2, Pallas kernels, attention_backward(): pl.pallas_call(functools.partial(backward_kernel, per_chunk, 2 * pair), g...  50.6 us
    convert_element_type x16, other arithmetic, outgoing(): return self.total({**self.fixed, name: 1 - self.me[name]}).astype(bf16)  34.4 us
    pallas_call x1, Pallas kernels, attention_forward(): pl.pallas_call(functools.partial(forward_kernel, per_chunk, heads // 2),...  29.1 us
    dot_general x5, matrix products, nn(): return jnp.dot(left, right, preferred_element_type=f32)  27.3 us
    dot_general x5, matrix products, nt(): lax.dot_general(left, right, (((1,), (1,)), ((), ())), preferred_element_...  26 us
    dot_general x5, matrix products, tn(): lax.dot_general(left, right, (((0,), (0,)), ((), ())), preferred_element_...  22.2 us
  transfers between devices with their start and end apart: 55, of which 20 were waited for; matrix products, arithmetic and copies ran while one was open for 21% of the time, Pallas kernels for 16%

profile of v9, /device:TPU:0, one launch (start us, length us, event | category | flops | bytes accessed | tf_op | source)
XLA Modules:
  0.0 503.3 jit_solution(10438877354136769761)
XLA Ops:
  28.8 21.2 %collective-permute-done.3 = bf16[1,128,1152]{2,1,0:T(8,128)(2,1)S(1)} collective-permute-done((bf16[1,128,1152]{2,1,0:T(8,128)(2,1)S(1)}, bf16[1,128,1152]{2,1,0:T(8,128)(2,1)S(1)}, u32[]{:S(2)}, u32[]{:S(2)}) %collective-permute-start.3) | collective-permute-done | bytes 294944 | tf_op jit(solution)/shard_map/ppermute | solution.py:236
  56.5 28.9 %collective-permute-done.5 = bf16[2,128,1152]{1,0,2:T(2,128)(2,1)S(1)} collective-permute-done((bf16[2,128,1152]{1,0,2:T(2,128)(2,1)S(1)}, bf16[2,128,1152]{1,0,2:T(2,128)(2,1)S(1)}, u32[]{:S(2)}, u32[]{:S(2)}) %collective-permute-start.5) | collective-permute-done | bytes 589856 | tf_op jit(solution)/shard_map/ppermute | solution.py:236
  98.8 22.2 %collective-permute-done.6 = bf16[4,128,1152]{1,0,2:T(4,128)(2,1)} collective-permute-done((bf16[4,128,1152]{1,0,2:T(4,128)(2,1)S(1)}, bf16[4,128,1152]{1,0,2:T(4,128)(2,1)}, u32[]{:S(2)}, u32[]{:S(2)}) %collective-permute-start.6) | collective-permute-done | bytes 1179680 | tf_op jit(solution)/shard_map/ppermute | solution.py:236
  135.8 7.3 %add_convert_fusion.1.qkv_ref.q_ref.k_ref.v_ref = bf16[2048,768]{1,0:T(8,128)(2,1)} fusion(f32[768]{0:T(1024)S(1)} %constant_dynamic-update-slice_fusion.69, bf16[1024,1152]{0,1:T(8,128)(2,1)S(1)} %broadcast_select_fusion, bf16[512,1024]{1,0:T(8,128)(2,1)} %collective-permute-done.11, bf16[512,1024]{1,0:T(8,128)(2,1)} %collective-permute-done.4, ...), kind=kOutput, calls=%fused_computation.23 | convolution fusion | flops 3245342720 | bytes 8921088 | tf_op jit(solution)/shard_map/dot_general | solution.py:21
  143.1 29.1 %attention_forward.1 = (bf16[2048,256]{1,0:T(8,128)(2,1)}, f32[8,4,256]{2,1,0:T(4,128)}) custom-call(s32[3,8]{1,0:T(4,128)} %add_add_fusion.2.info, bf16[2048,768]{1,0:T(8,128)(2,1)} %add_convert_fusion.1.qkv_ref.q_ref.k_ref.v_ref, s32[2048,1]{1,0:T(8,128)} %copy.161.idc_ref, s32[8,1,256]{2,1,0:T(1,128)} %bitcast.600), custom_call_target="tpu_custom_call" | custom-call | flops 30000001024 | bytes 3145728 | tf_op jit(solution)/shard_map/attention_forward/pallas_call | solution.py:95
  181.8 6.0 %collective-permute-done.13 = bf16[512,256]{1,0:T(8,128)(2,1)S(1)} collective-permute-done((bf16[512,256]{1,0:T(8,128)(2,1)S(1)}, bf16[512,256]{1,0:T(8,128)(2,1)S(1)}, u32[]{:S(2)}, u32[]{:S(2)}) %collective-permute-start.13) | collective-permute-done | bytes 262176 | tf_op jit(solution)/shard_map/ppermute | solution.py:236
  192.0 11.5 %fusion.4 = (bf16[512,4096]{1,0:T(8,128)(2,1)}, bf16[512,4096]{1,0:T(8,128)(2,1)S(1)}) fusion(f32[4096]{0:T(1024)S(1)} %add.424, bf16[1024,9216]{1,0:T(8,128)(2,1)} %all-gather.2.cloned.1.call-done, f32[512,1024]{1,0:T(8,128)S(1)} %get-tuple-element.324, f32[1024]{0:T(1024)S(1)} %bitcast.628, f32[1024]{0:T(1024)S(1)} %bitcast.616, ...), kind=kOutput, calls=%fused_computation.5 | convolution fusion | flops 4322754560 | bytes 18903040 | tf_op jit(solution)/shard_map/dot_general | solution.py:21
  203.5 4.8 fusion.114
  212.3 5.3 %convolution_convert_fusion.1 = bf16[4096,1024]{1,0:T(8,128)(2,1)S(1)} fusion(bf16[512,4096]{1,0:T(8,128)(2,1)S(1)} %get-tuple-element.112, f32[512,1024]{1,0:T(8,128)S(1)} %get-tuple-element.201), kind=kOutput, calls=%fused_computation.18 | convolution fusion | flops 4299685888 | bytes 14680064 | tf_op jit(solution)/shard_map/dot_general | solution.py:25
  222.6 9.9 %multiply_convert_fusion = bf16[512,4096]{1,0:T(8,128)(2,1)S(1)} fusion(bf16[512,4096]{1,0:T(8,128)(2,1)} %get-tuple-element.114, bf16[4096,1024]{1,0:T(8,128)(2,1)} %bitcast.560, f32[512,1024]{1,0:T(8,128)} %copy-done.13), kind=kOutput, calls=%fused_computation.7 | convolution fusion | flops 4301783040 | bytes 18874368 | tf_op jit(solution)/shard_map/dot_general | solution.py:29
  232.5 4.8 fusion.9
  238.9 5.2 %convolution_convert_fusion = bf16[1024,4096]{1,0:T(8,128)(2,1)S(1)} fusion(bf16[512,4096]{1,0:T(8,128)(2,1)S(1)} %multiply_convert_fusion, f32[512,1024]{1,0:T(8,128)S(1)} %get-tuple-element.324, f32[1024]{0:T(1024)S(1)} %bitcast.630, f32[1024]{0:T(1024)S(1)} %bitcast.618, f32[512]{0:T(512)S(1)} %add_rsqrt_fusion.1, f32[512]{0:T(512)S(1)} %broadcast_multiply_fusion.5), kind=kOutput, calls=%fused_computation.17 | convolution fusion | flops 4301783040 | bytes 14692352 | tf_op jit(solution)/shard_map/dot_general | solution.py:25
  249.5 8.3 %multiply_reduce_fusion = (f32[1024]{0:T(1024)S(1)}, f32[512]{0:T(512)S(1)}, f32[512]{0:T(512)S(1)}, f32[1024]{0:T(1024)S(1)}, f32[512,1024]{1,0:T(8,128)S(1)}) fusion(f32[512,1024]{1,0:T(8,128)S(1)} %get-tuple-element.324, f32[512]{0:T(512)S(1)} %add_rsqrt_fusion.1, f32[512]{0:T(512)S(1)} %broadcast_multiply_fusion.5, f32[1024]{0:T(1024)S(1)} %bitcast.619, ...), kind=kOutput, calls=%fused_computation.62 | convolution fusion | flops 4300207104 | bytes 18894848 | tf_op jit(solution)/shard_map/dot_general | solution.py:29
  273.8 6.3 %collective-permute-done.19 = bf16[512,256]{1,0:T(8,128)(2,1)S(1)} collective-permute-done((bf16[512,256]{1,0:T(8,128)(2,1)S(1)}, bf16[512,256]{1,0:T(8,128)(2,1)S(1)}, u32[]{:S(2)}, u32[]{:S(2)}) %collective-permute-start.19) | collective-permute-done | bytes 262176 | tf_op jit(solution)/shard_map/ppermute | solution.py:236
  281.8 4.2 collective-permute-done.18
  296.1 4.5 fusion.21
  304.6 25.2 %attention_backward.2 = bf16[2048,384]{1,0:T(8,128)(2,1)} custom-call(s32[3,8]{1,0:T(4,128)} %add_add_fusion.2.info, bf16[2048,768]{1,0:T(8,128)(2,1)} %add_convert_fusion.1.qkv_ref.q_ref.k_ref.v_ref, bf16[2048,768]{1,0:T(8,128)(2,1)} %add_convert_fusion.1.qkv_ref.q_ref.k_ref.v_ref, bf16[2048,768]{1,0:T(8,128)(2,1)} %add_convert_fusion.1.qkv_ref.q_ref.k_ref.v_ref, ...), custom_call_target="tpu_custom_call" | custom-call | flops 24999999488 | bytes 2097152 | tf_op jit(solution)/shard_map/attention_backward/pallas_call | solution.py:193
  331.6 4.7 fusion.106
  354.9 25.4 %attention_backward.3 = bf16[2048,384]{1,0:T(8,128)(2,1)} custom-call(s32[3,8]{1,0:T(4,128)} %add_add_fusion.2.info, bf16[2048,768]{1,0:T(8,128)(2,1)} %add_convert_fusion.1.qkv_ref.q_ref.k_ref.v_ref, bf16[2048,768]{1,0:T(8,128)(2,1)} %add_convert_fusion.1.qkv_ref.q_ref.k_ref.v_ref, bf16[2048,768]{1,0:T(8,128)(2,1)} %add_convert_fusion.1.qkv_ref.q_ref.k_ref.v_ref, ...), custom_call_target="tpu_custom_call" | custom-call | flops 24999999488 | bytes 2097152 | tf_op jit(solution)/shard_map/attention_backward/pallas_call | solution.py:193
  401.9 19.8 %collective-permute-start.38 = (f32[1,2560]{1,0:T(1,128)S(1)}, f32[1,2560]{1,0:T(1,128)}, u32[]{:S(2)}, u32[]{:S(2)}) collective-permute-start(f32[1,2560]{1,0:T(1,128)S(1)} %constant_dynamic-update-slice_fusion.39), channel_id=1, source_target_pairs={{0,16},{4,20},{8,24},{12,28},{16,0},{20,4},{24,8},{28,12},{1,17},{... | collective-permute-start | bytes 30728 | tf_op jit(solution)/shard_map/ppermute | solution.py:236
  423.5 4.6 collective-permute-start.32
  447.2 4.2 collective-permute-start.45
  462.7 5.9 %collective-permute-done.40 = bf16[2,128,384]{2,1,0:T(8,128)(2,1)S(1)} collective-permute-done((bf16[2,128,384]{2,1,0:T(8,128)(2,1)S(1)}, bf16[2,128,384]{2,1,0:T(8,128)(2,1)S(1)}, u32[]{:S(2)}, u32[]{:S(2)}) %collective-permute-start.40) | collective-permute-done | bytes 196640 | tf_op jit(solution)/shard_map/ppermute | solution.py:236
  472.7 5.5 %collective-permute-done.42 = bf16[128,384]{1,0:T(8,128)(2,1)S(1)} collective-permute-done((bf16[128,384]{1,0:T(8,128)(2,1)S(1)}, bf16[128,384]{1,0:T(8,128)(2,1)S(1)}, u32[]{:S(2)}, u32[]{:S(2)}) %collective-permute-start.42) | collective-permute-done | bytes 98336 | tf_op jit(solution)/shard_map/ppermute | solution.py:236
  (337 shorter events, 213.1 us)
Async XLA Ops:
  7.2 169.1 %all-gather.2.cloned.1.call-start = ((), (), s32[]{:S(2)}) async-start(), calls=%async_computation | async-start | bytes 19464192 | tf_op jit(solution)/shard_map/all_gather | solution.py:339
  24.2 30.0 %collective-permute-start.4 = (bf16[512,1024]{1,0:T(8,128)(2,1)}, bf16[512,1024]{1,0:T(8,128)(2,1)}, u32[]{:S(2)}, u32[]{:S(2)}) collective-permute-start(bf16[512,1024]{1,0:T(8,128)(2,1)} %bitcast), channel_id=1, source_target_pairs={{0,2},{1,3},{2,0},{3,1},{4,6},{5,7},{6,4},{7,5},{8,10},{9,11},{10,... | collective-permute-start | bytes 3145736 | tf_op jit(solution)/shard_map/ppermute | solution.py:236
  26.0 24.0 %collective-permute-start.3 = (bf16[1,128,1152]{2,1,0:T(8,128)(2,1)S(1)}, bf16[1,128,1152]{2,1,0:T(8,128)(2,1)S(1)}, u32[]{:S(2)}, u32[]{:S(2)}) collective-permute-start(bf16[1,128,1152]{2,1,0:T(8,128)(2,1)S(1)} %bitcast.570), channel_id=1, source_target_pairs={{0,16},{4,20},{8,24},{12,28},{16,0},{20,4},{24,8},{28,12},{1,17},{... | collective-permute-start | bytes 884744 | tf_op jit(solution)/shard_map/ppermute | solution.py:236
  54.2 31.2 %collective-permute-start.5 = (bf16[2,128,1152]{1,0,2:T(2,128)(2,1)S(1)}, bf16[2,128,1152]{1,0,2:T(2,128)(2,1)S(1)}, u32[]{:S(2)}, u32[]{:S(2)}) collective-permute-start(bf16[2,128,1152]{1,0,2:T(2,128)(2,1)S(1)} %broadcast_select_fusion.2), channel_id=1, source_target_pairs={{0,8},{4,12},{8,0},{12,4},{16,24},{20,28},{24,16},{28,20},{1,9},{5... | collective-permute-start | bytes 1769480 | tf_op jit(solution)/shard_map/ppermute | solution.py:236
  88.0 33.0 %collective-permute-start.6 = (bf16[4,128,1152]{1,0,2:T(4,128)(2,1)S(1)}, bf16[4,128,1152]{1,0,2:T(4,128)(2,1)}, u32[]{:S(2)}, u32[]{:S(2)}) collective-permute-start(bf16[4,128,1152]{1,0,2:T(4,128)(2,1)S(1)} %broadcast_select_fusion.1), channel_id=1, source_target_pairs={{0,4},{4,0},{8,12},{12,8},{16,20},{20,16},{24,28},{28,24},{1,5},{5... | collective-permute-start | bytes 3538952 | tf_op jit(solution)/shard_map/ppermute | solution.py:236
  89.8 45.9 %collective-permute-start.10 = (bf16[512,1024]{1,0:T(8,128)(2,1)}, bf16[512,1024]{1,0:T(8,128)(2,1)}, u32[]{:S(2)}, u32[]{:S(2)}) collective-permute-start(bf16[512,1024]{1,0:T(8,128)(2,1)} %bitcast), channel_id=1, source_target_pairs={{0,1},{1,0},{2,3},{3,2},{4,5},{5,4},{6,7},{7,6},{8,9},{9,8},{10,11... | collective-permute-start | bytes 3145736 | tf_op jit(solution)/shard_map/ppermute | solution.py:236
  93.7 42.1 %collective-permute-start.11 = (bf16[512,1024]{1,0:T(8,128)(2,1)}, bf16[512,1024]{1,0:T(8,128)(2,1)}, u32[]{:S(2)}, u32[]{:S(2)}) collective-permute-start(bf16[512,1024]{1,0:T(8,128)(2,1)} %collective-permute-done.4), channel_id=1, source_target_pairs={{0,1},{1,0},{2,3},{3,2},{4,5},{5,4},{6,7},{7,6},{8,9},{9,8},{10,11... | collective-permute-start | bytes 3145736 | tf_op jit(solution)/shard_map/ppermute | solution.py:236
  244.2 48.4 %collective-permute-start.16 = (bf16[2,2,2,128,1024]{4,3,0,2,1:T(8,128)(2,1)}, bf16[2,2,2,128,1024]{4,3,0,2,1:T(8,128)(2,1)}, u32[]{:S(2)}, u32[]{:S(2)}) collective-permute-start(bf16[2,2,2,128,1024]{4,3,0,2,1:T(8,128)(2,1)} %copy.164), channel_id=1, source_target_pairs={{0,4},{4,0},{8,12},{12,8},{16,20},{20,16},{24,28},{28,24},{1,5},{5... | collective-permute-start | bytes 6291464 | tf_op jit(solution)/shard_map/ppermute | solution.py:236
  249.0 47.1 %collective-permute-start.20 = (bf16[2,2,2,2,32,4096]{5,4,3,2,1,0:T(8,128)(2,1)}, bf16[2,2,2,2,32,4096]{5,4,3,2,1,0:T(8,128)(2,1)}, u32[]{:S(2)}, u32[]{:S(2)}) collective-permute-start(bf16[2,2,2,2,32,4096]{5,4,3,2,1,0:T(8,128)(2,1)} %dynamic-slice_bitcast_fusion), channel_id=1, source_target_pairs={{0,1},{1,0},{2,3},{3,2},{4,5},{5,4},{6,7},{7,6},{8,9},{9,8},{10,11... | collective-permute-start | bytes 12582920 | tf_op jit(solution)/shard_map/ppermute | solution.py:236
  300.5 35.7 %collective-permute-start.25 = (bf16[2,2,2,40,1024]{4,3,2,1,0:T(8,128)(2,1)}, bf16[2,2,2,40,1024]{4,3,2,1,0:T(8,128)(2,1)S(1)}, u32[]{:S(2)}, u32[]{:S(2)}) collective-permute-start(bf16[2,2,2,40,1024]{4,3,2,1,0:T(8,128)(2,1)} %fusion.37), channel_id=1, source_target_pairs={{0,4},{4,0},{8,12},{12,8},{16,20},{20,16},{24,28},{28,24},{1,5},{5... | collective-permute-start | bytes 1966088 | tf_op jit(solution)/shard_map/ppermute | solution.py:236
  301.8 34.5 %collective-permute-start.22 = (bf16[2,2,128,1024]{3,2,1,0:T(8,128)(2,1)}, bf16[2,2,128,1024]{3,2,1,0:T(8,128)(2,1)}, u32[]{:S(2)}, u32[]{:S(2)}) collective-permute-start(bf16[2,2,128,1024]{3,2,1,0:T(8,128)(2,1)} %fusion.23), channel_id=1, source_target_pairs={{0,8},{4,12},{8,0},{12,4},{16,24},{20,28},{24,16},{28,20},{1,9},{5... | collective-permute-start | bytes 3145736 | tf_op jit(solution)/shard_map/ppermute | solution.py:236
  301.8 34.5 %collective-permute-start.23 = (bf16[2,2,2,32,2048]{4,3,2,1,0:T(8,128)(2,1)}, bf16[2,2,2,32,2048]{4,3,2,1,0:T(8,128)(2,1)}, u32[]{:S(2)}, u32[]{:S(2)}) collective-permute-start(bf16[2,2,2,32,2048]{4,3,2,1,0:T(8,128)(2,1)} %get-tuple-element.120), channel_id=1, source_target_pairs={{0,2},{1,3},{2,0},{3,1},{4,6},{5,7},{6,4},{7,5},{8,10},{9,11},{10,... | collective-permute-start | bytes 3145736 | tf_op jit(solution)/shard_map/ppermute | solution.py:236
  303.5 36.1 %collective-permute-start.24 = (bf16[2,2,2,32,2048]{4,3,2,1,0:T(8,128)(2,1)}, bf16[2,2,2,32,2048]{4,3,2,1,0:T(8,128)(2,1)}, u32[]{:S(2)}, u32[]{:S(2)}) collective-permute-start(bf16[2,2,2,32,2048]{4,3,2,1,0:T(8,128)(2,1)} %get-tuple-element.121), channel_id=1, source_target_pairs={{0,4},{4,0},{8,12},{12,8},{16,20},{20,16},{24,28},{28,24},{1,5},{5... | collective-permute-start | bytes 3145736 | tf_op jit(solution)/shard_map/ppermute | solution.py:236
  348.1 32.3 %collective-permute-start.29 = (bf16[2,2,40,1024]{3,2,1,0:T(8,128)(2,1)}, bf16[2,2,40,1024]{3,2,1,0:T(8,128)(2,1)}, u32[]{:S(2)}, u32[]{:S(2)}) collective-permute-start(bf16[2,2,40,1024]{3,2,1,0:T(8,128)(2,1)} %fusion.53), channel_id=1, source_target_pairs={{0,8},{4,12},{8,0},{12,4},{16,24},{20,28},{24,16},{28,20},{1,9},{5... | collective-permute-start | bytes 983048 | tf_op jit(solution)/shard_map/ppermute | solution.py:236
  348.1 32.3 %collective-permute-start.30 = (bf16[2,2,128,384]{3,2,1,0:T(8,128)(2,1)}, bf16[2,2,128,384]{3,2,1,0:T(8,128)(2,1)}, u32[]{:S(2)}, u32[]{:S(2)}) collective-permute-start(bf16[2,2,128,384]{3,2,1,0:T(8,128)(2,1)} %fusion.60), channel_id=1, source_target_pairs={{0,4},{4,0},{8,12},{12,8},{16,20},{20,16},{24,28},{28,24},{1,5},{5... | collective-permute-start | bytes 1179656 | tf_op jit(solution)/shard_map/ppermute | solution.py:236
  350.2 30.2 %collective-permute-start.27 = (bf16[2,2,32,2048]{3,2,0,1:T(8,128)(2,1)}, bf16[2,2,32,2048]{3,2,0,1:T(8,128)(2,1)}, u32[]{:S(2)}, u32[]{:S(2)}) collective-permute-start(bf16[2,2,32,2048]{3,2,0,1:T(8,128)(2,1)} %copy.181), channel_id=1, source_target_pairs={{0,4},{4,0},{8,12},{12,8},{16,20},{20,16},{24,28},{28,24},{1,5},{5... | collective-permute-start | bytes 1572872 | tf_op jit(solution)/shard_map/ppermute | solution.py:236
  351.0 29.5 %collective-permute-start.26 = (bf16[2,128,1024]{2,1,0:T(8,128)(2,1)}, bf16[2,128,1024]{2,1,0:T(8,128)(2,1)}, u32[]{:S(2)}, u32[]{:S(2)}) collective-permute-start(bf16[2,128,1024]{2,1,0:T(8,128)(2,1)} %fusion.44), channel_id=1, source_target_pairs={{0,2},{1,3},{2,0},{3,1},{4,6},{5,7},{6,4},{7,5},{8,10},{9,11},{10,... | collective-permute-start | bytes 1572872 | tf_op jit(solution)/shard_map/ppermute | solution.py:236
  352.9 27.5 %collective-permute-start.28 = (bf16[2,2,32,2048]{3,2,1,0:T(8,128)(2,1)}, bf16[2,2,32,2048]{3,2,1,0:T(8,128)(2,1)}, u32[]{:S(2)}, u32[]{:S(2)}) collective-permute-start(bf16[2,2,32,2048]{3,2,1,0:T(8,128)(2,1)} %get-tuple-element.133), channel_id=1, source_target_pairs={{0,8},{4,12},{8,0},{12,4},{16,24},{20,28},{24,16},{28,20},{1,9},{5... | collective-permute-start | bytes 1572872 | tf_op jit(solution)/shard_map/ppermute | solution.py:236
  401.7 37.9 %collective-permute-start.37 = (bf16[1024,1024]{1,0:T(8,128)(2,1)}, bf16[1024,1024]{1,0:T(8,128)(2,1)}, u32[]{:S(2)}, u32[]{:S(2)}) collective-permute-start(bf16[1024,1024]{1,0:T(8,128)(2,1)} %convolution_convert_fusion.3), channel_id=1, source_target_pairs={{0,1},{1,0},{2,3},{3,2},{4,5},{5,4},{6,7},{7,6},{8,9},{9,8},{10,11... | collective-permute-start | bytes 6291464 | tf_op jit(solution)/shard_map/ppermute | solution.py:236
  401.7 28.4 %collective-permute-start.35 = (bf16[2,128,384]{2,1,0:T(8,128)(2,1)}, bf16[2,128,384]{2,1,0:T(8,128)(2,1)}, u32[]{:S(2)}, u32[]{:S(2)}) collective-permute-start(bf16[2,128,384]{2,1,0:T(8,128)(2,1)} %fusion.63), channel_id=1, source_target_pairs={{0,8},{4,12},{8,0},{12,4},{16,24},{20,28},{24,16},{28,20},{1,9},{5... | collective-permute-start | bytes 589832 | tf_op jit(solution)/shard_map/ppermute | solution.py:236
  401.7 26.3 %collective-permute-start.34 = (bf16[2,40,1024]{2,1,0:T(8,128)(2,1)}, bf16[2,40,1024]{2,1,0:T(8,128)(2,1)}, u32[]{:S(2)}, u32[]{:S(2)}) collective-permute-start(bf16[2,40,1024]{2,1,0:T(8,128)(2,1)} %fusion.65), channel_id=1, source_target_pairs={{0,2},{1,3},{2,0},{3,1},{4,6},{5,7},{6,4},{7,5},{8,10},{9,11},{10,... | collective-permute-start | bytes 491528 | tf_op jit(solution)/shard_map/ppermute | solution.py:236
  401.9 21.6 %collective-permute-start.38 = (f32[1,2560]{1,0:T(1,128)S(1)}, f32[1,2560]{1,0:T(1,128)}, u32[]{:S(2)}, u32[]{:S(2)}) collective-permute-start(f32[1,2560]{1,0:T(1,128)S(1)} %constant_dynamic-update-slice_fusion.39), channel_id=1, source_target_pairs={{0,16},{4,20},{8,24},{12,28},{16,0},{20,4},{24,8},{28,12},{1,17},{... | collective-permute-start | bytes 30728 | tf_op jit(solution)/shard_map/ppermute | solution.py:236
  447.2 25.5 %collective-permute-start.45 = (bf16[40,1024]{1,0:T(8,128)(2,1)S(1)}, bf16[40,1024]{1,0:T(8,128)(2,1)S(1)}, u32[]{:S(2)}, u32[]{:S(2)}) collective-permute-start(bf16[40,1024]{1,0:T(8,128)(2,1)S(1)} %fusion.76), channel_id=1, source_target_pairs={{0,16},{4,20},{8,24},{12,28},{16,0},{20,4},{24,8},{28,12},{1,17},{... | collective-permute-start | bytes 245768 | tf_op jit(solution)/shard_map/ppermute | solution.py:236
  454.3 23.9 %collective-permute-start.47 = (bf16[512,1024]{1,0:T(8,128)(2,1)S(1)}, bf16[512,1024]{1,0:T(8,128)(2,1)S(1)}, u32[]{:S(2)}, u32[]{:S(2)}) collective-permute-start(bf16[512,1024]{1,0:T(8,128)(2,1)S(1)} %slice.467), channel_id=1, source_target_pairs={{0,2},{1,3},{2,0},{3,1},{4,6},{5,7},{6,4},{7,5},{8,10},{9,11},{10,... | collective-permute-start | bytes 3145736 | tf_op jit(solution)/shard_map/ppermute | solution.py:236
  (65 other events, 483.3 us)
Sparse Core Ops, SparseCore 0:
  24.3 149.9 all-gather.1

commit v10 on v8

--- a/solution.py
+++ b/solution.py
@@ -462,8 +462,8 @@
     share("up", up_grad, own)
     share("rest", rest_grad, own + extra)
     streams += [
-        stream("up", [(0, own), (0, hidden // 2)], 2),
-        stream("up", [(0, own), (hidden // 2, hidden)], 0),
+        stream("up", [(0, own), (0, 5 * hidden // 8)], 2),
+        stream("up", [(0, own), (5 * hidden // 8, hidden)], 0),
         stream("rest", [(0, own + extra), (0, width)], 0),
     ]
 

time: 497 us -> 502 us (1.010)
  Pallas kernels: 62.9 us -> 76.4 us
  starting transfers between devices: 85.3 us -> 77.7 us
    pallas_call x2, Pallas kernels: 40.4 us -> 48.6 us  [attention_backward(): pl.pallas_call(functools.partial(backward_kernel, per_chunk, 2 * pair), g...]
    ppermute x54, starting transfers between devices: 85.3 us -> 77.6 us  [swap(): return lax.ppermute(value, axis, [(i, i ^ mask) for i in range(size)])]
    pallas_call x1, Pallas kernels: 22.5 us -> 27.8 us  [attention_forward(): pl.pallas_call(functools.partial(forward_kernel, per_chunk, heads // 2),...]
    convert_element_type x16 -> x20, other arithmetic: 35.5 us -> 39 us  [outgoing(): return self.total({**self.fixed, name: 1 - self.me[name]}).astype(bf16)]
    unnamed x118 -> x120, local copies, waits for them, and re-layouts: 21 us -> 21 us
  transfers between devices with their start and end apart: 55 -> 55, of which waited for: 19 -> 19; matrix products, arithmetic and copies ran while one was open for 21% -> 20% of each run, Pallas kernels for 13% -> 15%
where the time goes in v10:
time: 502 us; the launch traced here: 494 us
  waiting for transfers between devices  122 us (24%)
  starting transfers between devices  77.7 us (15%)
  Pallas kernels  76.4 us (15%)
  matrix products  76 us (15%)
  other arithmetic  75.9 us (15%)
  local copies, waits for them, and re-layouts  49.9 us (10%)
  between operations  15.5 us (3%)
    ppermute x54, waiting for transfers between devices, swap(): return lax.ppermute(value, axis, [(i, i ^ mask) for i in range(size)])  122 us
    ppermute x54, starting transfers between devices, swap(): return lax.ppermute(value, axis, [(i, i ^ mask) for i in range(size)])  77.6 us
    pallas_call x2, Pallas kernels, attention_backward(): pl.pallas_call(functools.partial(backward_kernel, per_chunk, 2 * pair), g...  48.6 us
    convert_element_type x20, other arithmetic, outgoing(): return self.total({**self.fixed, name: 1 - self.me[name]}).astype(bf16)  39 us
    pallas_call x1, Pallas kernels, attention_forward(): pl.pallas_call(functools.partial(forward_kernel, per_chunk, heads // 2),...  27.8 us
    dot_general x5, matrix products, nn(): return jnp.dot(left, right, preferred_element_type=f32)  27.4 us
    dot_general x5, matrix products, nt(): lax.dot_general(left, right, (((1,), (1,)), ((), ())), preferred_element_...  24.7 us
    dot_general x5, matrix products, tn(): lax.dot_general(left, right, (((0,), (0,)), ((), ())), preferred_element_...  22.2 us
  transfers between devices with their start and end apart: 55, of which 19 were waited for; matrix products, arithmetic and copies ran while one was open for 20% of the time, Pallas kernels for 15%

profile of v10, /device:TPU:0, one launch (start us, length us, event | category | flops | bytes accessed | tf_op | source)
XLA Modules:
  0.0 493.8 jit_solution(16484066209847872355)
XLA Ops:
  28.6 21.4 %collective-permute-done.3 = bf16[1,128,1152]{2,1,0:T(8,128)(2,1)S(1)} collective-permute-done((bf16[1,128,1152]{2,1,0:T(8,128)(2,1)S(1)}, bf16[1,128,1152]{2,1,0:T(8,128)(2,1)S(1)}, u32[]{:S(2)}, u32[]{:S(2)}) %collective-permute-start.3) | collective-permute-done | bytes 294944 | tf_op jit(solution)/shard_map/ppermute | solution.py:236
  50.0 4.2 collective-permute-done.4
  57.5 27.8 %collective-permute-done.5 = bf16[2,128,1152]{2,1,0:T(8,128)(2,1)S(1)} collective-permute-done((bf16[2,128,1152]{2,1,0:T(8,128)(2,1)S(1)}, bf16[2,128,1152]{2,1,0:T(8,128)(2,1)S(1)}, u32[]{:S(2)}, u32[]{:S(2)}) %collective-permute-start.5) | collective-permute-done | bytes 589856 | tf_op jit(solution)/shard_map/ppermute | solution.py:236
  92.7 22.2 %collective-permute-done.6 = bf16[4,128,1152]{2,1,0:T(8,128)(2,1)S(1)} collective-permute-done((bf16[4,128,1152]{2,1,0:T(8,128)(2,1)S(1)}, bf16[4,128,1152]{2,1,0:T(8,128)(2,1)S(1)}, u32[]{:S(2)}, u32[]{:S(2)}) %collective-permute-start.6) | collective-permute-done | bytes 1179680 | tf_op jit(solution)/shard_map/ppermute | solution.py:236
  124.8 3.9 collective-permute-start.8
  130.6 7.3 %add_convert_fusion.1.qkv_ref.q_ref.k_ref.v_ref = bf16[2048,768]{1,0:T(8,128)(2,1)} fusion(f32[768]{0:T(1024)S(1)} %constant_dynamic-update-slice_fusion.72, bf16[1024,1152]{0,1:T(8,128)(2,1)S(1)} %bitcast_dynamic-update-slice_fusion, bf16[512,1024]{1,0:T(8,128)(2,1)} %collective-permute-done.11, bf16[512,1024]{1,0:T(8,128)(2,1)} %collective-permute-done.4, ...), kind=kOutput, calls=%fused_computation.23 | convolution fusion | flops 3245342720 | bytes 8921088 | tf_op jit(solution)/shard_map/dot_general | solution.py:21
  137.9 27.8 %attention_forward.1 = (bf16[2048,256]{1,0:T(8,128)(2,1)}, f32[8,4,256]{2,1,0:T(4,128)}) custom-call(s32[3,8]{1,0:T(4,128)} %add_add_fusion.2.info, bf16[2048,768]{1,0:T(8,128)(2,1)} %add_convert_fusion.1.qkv_ref.q_ref.k_ref.v_ref, s32[2048,1]{1,0:T(8,128)} %copy.186.idc_ref, s32[8,1,256]{2,1,0:T(1,128)} %bitcast.612), custom_call_target="tpu_custom_call" | custom-call | flops 30000001024 | bytes 3145728 | tf_op jit(solution)/shard_map/attention_forward/pallas_call | solution.py:95
  175.6 5.7 %collective-permute-done.13 = bf16[512,256]{1,0:T(8,128)(2,1)S(1)} collective-permute-done((bf16[512,256]{1,0:T(8,128)(2,1)S(1)}, bf16[512,256]{1,0:T(8,128)(2,1)S(1)}, u32[]{:S(2)}, u32[]{:S(2)}) %collective-permute-start.13) | collective-permute-done | bytes 262176 | tf_op jit(solution)/shard_map/ppermute | solution.py:236
  185.4 11.5 %fusion.4 = (bf16[512,4096]{1,0:T(8,128)(2,1)}, bf16[512,4096]{1,0:T(8,128)(2,1)S(1)}) fusion(f32[4096]{0:T(1024)S(1)} %add.488, bf16[1024,9216]{1,0:T(8,128)(2,1)} %all-gather.2.cloned.1.call-done, f32[512,1024]{1,0:T(8,128)S(1)} %get-tuple-element.322, f32[1024]{0:T(1024)S(1)} %bitcast.640, f32[1024]{0:T(1024)S(1)} %bitcast.628, ...), kind=kOutput, calls=%fused_computation.5 | convolution fusion | flops 4322754560 | bytes 18903040 | tf_op jit(solution)/shard_map/dot_general | solution.py:21
  196.9 4.8 fusion.114
  205.7 5.3 %convolution_convert_fusion.1 = bf16[4096,1024]{1,0:T(8,128)(2,1)S(1)} fusion(bf16[512,4096]{1,0:T(8,128)(2,1)S(1)} %get-tuple-element.112, f32[512,1024]{1,0:T(8,128)S(1)} %get-tuple-element.201), kind=kOutput, calls=%fused_computation.18 | convolution fusion | flops 4299685888 | bytes 14680064 | tf_op jit(solution)/shard_map/dot_general | solution.py:25
  216.1 9.9 %multiply_convert_fusion = bf16[512,4096]{1,0:T(8,128)(2,1)S(1)} fusion(bf16[512,4096]{1,0:T(8,128)(2,1)} %get-tuple-element.114, bf16[4096,1024]{1,0:T(8,128)(2,1)} %bitcast.574, f32[512,1024]{1,0:T(8,128)} %copy-done.10), kind=kOutput, calls=%fused_computation.7 | convolution fusion | flops 4301783040 | bytes 18874368 | tf_op jit(solution)/shard_map/dot_general | solution.py:29
  226.0 4.8 fusion.9
  232.4 5.2 %convolution_convert_fusion = bf16[1024,4096]{1,0:T(8,128)(2,1)S(1)} fusion(bf16[512,4096]{1,0:T(8,128)(2,1)S(1)} %multiply_convert_fusion, f32[512,1024]{1,0:T(8,128)S(1)} %get-tuple-element.322, f32[1024]{0:T(1024)S(1)} %bitcast.642, f32[1024]{0:T(1024)S(1)} %bitcast.630, f32[512]{0:T(512)S(1)} %add_rsqrt_fusion.1, f32[512]{0:T(512)S(1)} %broadcast_multiply_fusion.5), kind=kOutput, calls=%fused_computation.17 | convolution fusion | flops 4301783040 | bytes 14692352 | tf_op jit(solution)/shard_map/dot_general | solution.py:25
  243.1 8.3 %multiply_reduce_fusion = (f32[1024]{0:T(1024)S(1)}, f32[512]{0:T(512)S(1)}, f32[512]{0:T(512)S(1)}, f32[1024]{0:T(1024)S(1)}, f32[512,1024]{1,0:T(8,128)S(1)}) fusion(f32[512,1024]{1,0:T(8,128)S(1)} %get-tuple-element.322, f32[512]{0:T(512)S(1)} %add_rsqrt_fusion.1, f32[512]{0:T(512)S(1)} %broadcast_multiply_fusion.5, f32[1024]{0:T(1024)S(1)} %bitcast.631, ...), kind=kOutput, calls=%fused_computation.59 | convolution fusion | flops 4300207104 | bytes 18894848 | tf_op jit(solution)/shard_map/dot_general | solution.py:29
  267.4 6.2 %collective-permute-done.19 = bf16[512,256]{1,0:T(8,128)(2,1)S(1)} collective-permute-done((bf16[512,256]{1,0:T(8,128)(2,1)S(1)}, bf16[512,256]{1,0:T(8,128)(2,1)S(1)}, u32[]{:S(2)}, u32[]{:S(2)}) %collective-permute-start.19) | collective-permute-done | bytes 262176 | tf_op jit(solution)/shard_map/ppermute | solution.py:236
  275.5 4.2 collective-permute-done.18
  298.7 24.2 %attention_backward.2 = bf16[2048,384]{1,0:T(8,128)(2,1)} custom-call(s32[3,8]{1,0:T(4,128)} %add_add_fusion.2.info, bf16[2048,768]{1,0:T(8,128)(2,1)} %add_convert_fusion.1.qkv_ref.q_ref.k_ref.v_ref, bf16[2048,768]{1,0:T(8,128)(2,1)} %add_convert_fusion.1.qkv_ref.q_ref.k_ref.v_ref, bf16[2048,768]{1,0:T(8,128)(2,1)} %add_convert_fusion.1.qkv_ref.q_ref.k_ref.v_ref, ...), custom_call_target="tpu_custom_call" | custom-call | flops 24999999488 | bytes 2097152 | tf_op jit(solution)/shard_map/attention_backward/pallas_call | solution.py:193
  324.7 4.7 fusion.106
  345.4 24.4 %attention_backward.3 = bf16[2048,384]{1,0:T(8,128)(2,1)} custom-call(s32[3,8]{1,0:T(4,128)} %add_add_fusion.2.info, bf16[2048,768]{1,0:T(8,128)(2,1)} %add_convert_fusion.1.qkv_ref.q_ref.k_ref.v_ref, bf16[2048,768]{1,0:T(8,128)(2,1)} %add_convert_fusion.1.qkv_ref.q_ref.k_ref.v_ref, bf16[2048,768]{1,0:T(8,128)(2,1)} %add_convert_fusion.1.qkv_ref.q_ref.k_ref.v_ref, ...), custom_call_target="tpu_custom_call" | custom-call | flops 24999999488 | bytes 2097152 | tf_op jit(solution)/shard_map/attention_backward/pallas_call | solution.py:193
  375.7 4.1 fusion.105
  389.3 17.8 %collective-permute-start.38 = (f32[1,2560]{1,0:T(1,128)S(1)}, f32[1,2560]{1,0:T(1,128)S(1)}, u32[]{:S(2)}, u32[]{:S(2)}) collective-permute-start(f32[1,2560]{1,0:T(1,128)S(1)} %constant_dynamic-update-slice_fusion.42), channel_id=1, source_target_pairs={{0,16},{4,20},{8,24},{12,28},{16,0},{20,4},{24,8},{28,12},{1,17},{... | collective-permute-start | bytes 30728 | tf_op jit(solution)/shard_map/ppermute | solution.py:236
  417.0 5.6 %collective-permute-done.31 = bf16[128,1024]{1,0:T(8,128)(2,1)S(1)} collective-permute-done((bf16[128,1024]{1,0:T(8,128)(2,1)S(1)}, bf16[128,1024]{1,0:T(8,128)(2,1)S(1)}, u32[]{:S(2)}, u32[]{:S(2)}) %collective-permute-start.31) | collective-permute-done | bytes 262176 | tf_op jit(solution)/shard_map/ppermute | solution.py:236
  446.0 6.7 %collective-permute-done.39 = bf16[128,384]{1,0:T(8,128)(2,1)S(1)} collective-permute-done((bf16[128,384]{1,0:T(8,128)(2,1)}, bf16[128,384]{1,0:T(8,128)(2,1)S(1)}, u32[]{:S(2)}, u32[]{:S(2)}) %collective-permute-start.39) | collective-permute-done | bytes 98336 | tf_op jit(solution)/shard_map/ppermute | solution.py:236
  (356 shorter events, 210.2 us)
Async XLA Ops:
  7.2 163.3 %all-gather.2.cloned.1.call-start = ((), (), s32[]{:S(2)}) async-start(), calls=%async_computation | async-start | bytes 19464192 | tf_op jit(solution)/shard_map/all_gather | solution.py:344
  24.2 30.0 %collective-permute-start.4 = (bf16[512,1024]{1,0:T(8,128)(2,1)}, bf16[512,1024]{1,0:T(8,128)(2,1)}, u32[]{:S(2)}, u32[]{:S(2)}) collective-permute-start(bf16[512,1024]{1,0:T(8,128)(2,1)} %bitcast), channel_id=1, source_target_pairs={{0,2},{1,3},{2,0},{3,1},{4,6},{5,7},{6,4},{7,5},{8,10},{9,11},{10,... | collective-permute-start | bytes 3145736 | tf_op jit(solution)/shard_map/ppermute | solution.py:236
  26.0 24.0 %collective-permute-start.3 = (bf16[1,128,1152]{2,1,0:T(8,128)(2,1)S(1)}, bf16[1,128,1152]{2,1,0:T(8,128)(2,1)S(1)}, u32[]{:S(2)}, u32[]{:S(2)}) collective-permute-start(bf16[1,128,1152]{2,1,0:T(8,128)(2,1)S(1)} %bitcast.582), channel_id=1, source_target_pairs={{0,16},{4,20},{8,24},{12,28},{16,0},{20,4},{24,8},{28,12},{1,17},{... | collective-permute-start | bytes 884744 | tf_op jit(solution)/shard_map/ppermute | solution.py:236
  54.2 31.1 %collective-permute-start.5 = (bf16[2,128,1152]{2,1,0:T(8,128)(2,1)S(1)}, bf16[2,128,1152]{2,1,0:T(8,128)(2,1)S(1)}, u32[]{:S(2)}, u32[]{:S(2)}) collective-permute-start(bf16[2,128,1152]{2,1,0:T(8,128)(2,1)S(1)} %pad_maximum_fusion.6), channel_id=1, source_target_pairs={{0,8},{4,12},{8,0},{12,4},{16,24},{20,28},{24,16},{28,20},{1,9},{5... | collective-permute-start | bytes 1769480 | tf_op jit(solution)/shard_map/ppermute | solution.py:236
  56.0 74.6 %collective-permute-start.10 = (bf16[512,1024]{1,0:T(8,128)(2,1)}, bf16[512,1024]{1,0:T(8,128)(2,1)}, u32[]{:S(2)}, u32[]{:S(2)}) collective-permute-start(bf16[512,1024]{1,0:T(8,128)(2,1)} %bitcast), channel_id=1, source_target_pairs={{0,1},{1,0},{2,3},{3,2},{4,5},{5,4},{6,7},{7,6},{8,9},{9,8},{10,11... | collective-permute-start | bytes 3145736 | tf_op jit(solution)/shard_map/ppermute | solution.py:236
  85.4 29.6 %collective-permute-start.6 = (bf16[4,128,1152]{2,1,0:T(8,128)(2,1)S(1)}, bf16[4,128,1152]{2,1,0:T(8,128)(2,1)S(1)}, u32[]{:S(2)}, u32[]{:S(2)}) collective-permute-start(bf16[4,128,1152]{2,1,0:T(8,128)(2,1)S(1)} %pad_maximum_fusion.2), channel_id=1, source_target_pairs={{0,4},{4,0},{8,12},{12,8},{16,20},{20,16},{24,28},{28,24},{1,5},{5... | collective-permute-start | bytes 3538952 | tf_op jit(solution)/shard_map/ppermute | solution.py:236
  92.6 38.0 %collective-permute-start.11 = (bf16[512,1024]{1,0:T(8,128)(2,1)}, bf16[512,1024]{1,0:T(8,128)(2,1)}, u32[]{:S(2)}, u32[]{:S(2)}) collective-permute-start(bf16[512,1024]{1,0:T(8,128)(2,1)} %collective-permute-done.4), channel_id=1, source_target_pairs={{0,1},{1,0},{2,3},{3,2},{4,5},{5,4},{6,7},{7,6},{8,9},{9,8},{10,11... | collective-permute-start | bytes 3145736 | tf_op jit(solution)/shard_map/ppermute | solution.py:236
  237.6 49.3 %collective-permute-start.16 = (bf16[2,2,2,128,1024]{4,3,0,2,1:T(8,128)(2,1)}, bf16[2,2,2,128,1024]{4,3,0,2,1:T(8,128)(2,1)}, u32[]{:S(2)}, u32[]{:S(2)}) collective-permute-start(bf16[2,2,2,128,1024]{4,3,0,2,1:T(8,128)(2,1)} %copy.189), channel_id=1, source_target_pairs={{0,4},{4,0},{8,12},{12,8},{16,20},{20,16},{24,28},{28,24},{1,5},{5... | collective-permute-start | bytes 6291464 | tf_op jit(solution)/shard_map/ppermute | solution.py:236
  242.6 47.8 %collective-permute-start.20 = (bf16[2,2,2,2,32,4096]{5,4,3,2,1,0:T(8,128)(2,1)}, bf16[2,2,2,2,32,4096]{5,4,3,2,1,0:T(8,128)(2,1)}, u32[]{:S(2)}, u32[]{:S(2)}) collective-permute-start(bf16[2,2,2,2,32,4096]{5,4,3,2,1,0:T(8,128)(2,1)} %dynamic-slice_bitcast_fusion), channel_id=1, source_target_pairs={{0,1},{1,0},{2,3},{3,2},{4,5},{5,4},{6,7},{7,6},{8,9},{9,8},{10,11... | collective-permute-start | bytes 12582920 | tf_op jit(solution)/shard_map/ppermute | solution.py:236
  261.4 20.5 %collective-permute-start.21 = (bf16[2,2,2,2,40,1024]{5,4,3,2,1,0:T(8,128)(2,1)}, bf16[2,2,2,2,40,1024]{5,4,3,2,1,0:T(8,128)(2,1)}, u32[]{:S(2)}, u32[]{:S(2)}) collective-permute-start(bf16[2,2,2,2,40,1024]{5,4,3,2,1,0:T(8,128)(2,1)} %fusion.36), channel_id=1, source_target_pairs={{0,1},{1,0},{2,3},{3,2},{4,5},{5,4},{6,7},{7,6},{8,9},{9,8},{10,11... | collective-permute-start | bytes 3932168 | tf_op jit(solution)/shard_map/ppermute | solution.py:236
  295.1 34.2 %collective-permute-start.25 = (bf16[2,2,2,40,1024]{4,3,2,1,0:T(8,128)(2,1)}, bf16[2,2,2,40,1024]{4,3,2,1,0:T(8,128)(2,1)}, u32[]{:S(2)}, u32[]{:S(2)}) collective-permute-start(bf16[2,2,2,40,1024]{4,3,2,1,0:T(8,128)(2,1)} %fusion.38), channel_id=1, source_target_pairs={{0,4},{4,0},{8,12},{12,8},{16,20},{20,16},{24,28},{28,24},{1,5},{5... | collective-permute-start | bytes 1966088 | tf_op jit(solution)/shard_map/ppermute | solution.py:236
  296.8 32.5 %collective-permute-start.24 = (bf16[2,2,2,32,1536]{4,3,2,1,0:T(8,128)(2,1)S(1)}, bf16[2,2,2,32,1536]{4,3,2,1,0:T(8,128)(2,1)}, u32[]{:S(2)}, u32[]{:S(2)}) collective-permute-start(bf16[2,2,2,32,1536]{4,3,2,1,0:T(8,128)(2,1)S(1)} %fusion.28), channel_id=1, source_target_pairs={{0,4},{4,0},{8,12},{12,8},{16,20},{20,16},{24,28},{28,24},{1,5},{5... | collective-permute-start | bytes 2359304 | tf_op jit(solution)/shard_map/ppermute | solution.py:236
  297.1 32.2 %collective-permute-start.22 = (bf16[2,2,128,1024]{3,2,1,0:T(8,128)(2,1)}, bf16[2,2,128,1024]{3,2,1,0:T(8,128)(2,1)}, u32[]{:S(2)}, u32[]{:S(2)}) collective-permute-start(bf16[2,2,128,1024]{3,2,1,0:T(8,128)(2,1)} %fusion.22), channel_id=1, source_target_pairs={{0,8},{4,12},{8,0},{12,4},{16,24},{20,28},{24,16},{28,20},{1,9},{5... | collective-permute-start | bytes 3145736 | tf_op jit(solution)/shard_map/ppermute | solution.py:236
  297.1 32.2 %collective-permute-start.23 = (bf16[2,2,2,32,2560]{4,3,2,1,0:T(8,128)(2,1)}, bf16[2,2,2,32,2560]{4,3,2,1,0:T(8,128)(2,1)}, u32[]{:S(2)}, u32[]{:S(2)}) collective-permute-start(bf16[2,2,2,32,2560]{4,3,2,1,0:T(8,128)(2,1)} %fusion.15), channel_id=1, source_target_pairs={{0,2},{1,3},{2,0},{3,1},{4,6},{5,7},{6,4},{7,5},{8,10},{9,11},{10,... | collective-permute-start | bytes 3932168 | tf_op jit(solution)/shard_map/ppermute | solution.py:236
  338.8 31.0 %collective-permute-start.29 = (bf16[2,2,40,1024]{3,2,1,0:T(8,128)(2,1)}, bf16[2,2,40,1024]{3,2,1,0:T(8,128)(2,1)}, u32[]{:S(2)}, u32[]{:S(2)}) collective-permute-start(bf16[2,2,40,1024]{3,2,1,0:T(8,128)(2,1)} %fusion.54), channel_id=1, source_target_pairs={{0,8},{4,12},{8,0},{12,4},{16,24},{20,28},{24,16},{28,20},{1,9},{5... | collective-permute-start | bytes 983048 | tf_op jit(solution)/shard_map/ppermute | solution.py:236
  341.9 27.9 %collective-permute-start.28 = (bf16[2,2,32,1536]{3,2,1,0:T(8,128)(2,1)}, bf16[2,2,32,1536]{3,2,1,0:T(8,128)(2,1)}, u32[]{:S(2)}, u32[]{:S(2)}) collective-permute-start(bf16[2,2,32,1536]{3,2,1,0:T(8,128)(2,1)} %fusion.50), channel_id=1, source_target_pairs={{0,8},{4,12},{8,0},{12,4},{16,24},{20,28},{24,16},{28,20},{1,9},{5... | collective-permute-start | bytes 1179656 | tf_op jit(solution)/shard_map/ppermute | solution.py:236
  342.0 27.8 %collective-permute-start.30 = (bf16[2,2,128,384]{3,2,1,0:T(8,128)(2,1)}, bf16[2,2,128,384]{3,2,1,0:T(8,128)(2,1)}, u32[]{:S(2)}, u32[]{:S(2)}) collective-permute-start(bf16[2,2,128,384]{3,2,1,0:T(8,128)(2,1)} %fusion.59), channel_id=1, source_target_pairs={{0,4},{4,0},{8,12},{12,8},{16,20},{20,16},{24,28},{28,24},{1,5},{5... | collective-permute-start | bytes 1179656 | tf_op jit(solution)/shard_map/ppermute | solution.py:236
  342.6 27.2 %collective-permute-start.26 = (bf16[2,128,1024]{2,1,0:T(8,128)(2,1)}, bf16[2,128,1024]{2,1,0:T(8,128)(2,1)}, u32[]{:S(2)}, u32[]{:S(2)}) collective-permute-start(bf16[2,128,1024]{2,1,0:T(8,128)(2,1)} %fusion.43), channel_id=1, source_target_pairs={{0,2},{1,3},{2,0},{3,1},{4,6},{5,7},{6,4},{7,5},{8,10},{9,11},{10,... | collective-permute-start | bytes 1572872 | tf_op jit(solution)/shard_map/ppermute | solution.py:236
  344.2 25.6 %collective-permute-start.27 = (bf16[2,2,32,2560]{3,2,0,1:T(8,128)(2,1)}, bf16[2,2,32,2560]{3,2,0,1:T(8,128)(2,1)S(1)}, u32[]{:S(2)}, u32[]{:S(2)}) collective-permute-start(bf16[2,2,32,2560]{3,2,0,1:T(8,128)(2,1)} %copy.206), channel_id=1, source_target_pairs={{0,4},{4,0},{8,12},{12,8},{16,20},{20,16},{24,28},{28,24},{1,5},{5... | collective-permute-start | bytes 1966088 | tf_op jit(solution)/shard_map/ppermute | solution.py:236
  387.2 39.0 %collective-permute-start.37 = (bf16[1024,1024]{1,0:T(8,128)(2,1)S(1)}, bf16[1024,1024]{1,0:T(8,128)(2,1)S(1)}, u32[]{:S(2)}, u32[]{:S(2)}) collective-permute-start(bf16[1024,1024]{1,0:T(8,128)(2,1)S(1)} %convolution_convert_fusion.3), channel_id=1, source_target_pairs={{0,1},{1,0},{2,3},{3,2},{4,5},{5,4},{6,7},{7,6},{8,9},{9,8},{10,11... | collective-permute-start | bytes 6291464 | tf_op jit(solution)/shard_map/ppermute | solution.py:236
  387.2 24.7 %collective-permute-start.33 = (bf16[2,32,1536]{2,1,0:T(8,128)(2,1)S(1)}, bf16[2,32,1536]{2,1,0:T(8,128)(2,1)S(1)}, u32[]{:S(2)}, u32[]{:S(2)}) collective-permute-start(bf16[2,32,1536]{2,1,0:T(8,128)(2,1)S(1)} %fusion.63), channel_id=1, source_target_pairs={{0,2},{1,3},{2,0},{3,1},{4,6},{5,7},{6,4},{7,5},{8,10},{9,11},{10,... | collective-permute-start | bytes 589832 | tf_op jit(solution)/shard_map/ppermute | solution.py:236
  388.9 22.9 %collective-permute-start.34 = (bf16[2,40,1024]{2,1,0:T(8,128)(2,1)S(1)}, bf16[2,40,1024]{2,1,0:T(8,128)(2,1)S(1)}, u32[]{:S(2)}, u32[]{:S(2)}) collective-permute-start(bf16[2,40,1024]{2,1,0:T(8,128)(2,1)S(1)} %fusion.67), channel_id=1, source_target_pairs={{0,2},{1,3},{2,0},{3,1},{4,6},{5,7},{6,4},{7,5},{8,10},{9,11},{10,... | collective-permute-start | bytes 491528 | tf_op jit(solution)/shard_map/ppermute | solution.py:236
  438.0 28.1 %collective-permute-start.47 = (bf16[512,1024]{1,0:T(8,128)(2,1)}, bf16[512,1024]{1,0:T(8,128)(2,1)}, u32[]{:S(2)}, u32[]{:S(2)}) collective-permute-start(bf16[512,1024]{1,0:T(8,128)(2,1)} %slice.467), channel_id=1, source_target_pairs={{0,2},{1,3},{2,0},{3,1},{4,6},{5,7},{6,4},{7,5},{8,10},{9,11},{10,... | collective-permute-start | bytes 3145736 | tf_op jit(solution)/shard_map/ppermute | solution.py:236
  439.3 22.2 %collective-permute-start.45 = (bf16[40,1024]{1,0:T(8,128)(2,1)}, bf16[40,1024]{1,0:T(8,128)(2,1)S(1)}, u32[]{:S(2)}, u32[]{:S(2)}) collective-permute-start(bf16[40,1024]{1,0:T(8,128)(2,1)} %fusion.76), channel_id=1, source_target_pairs={{0,16},{4,20},{8,24},{12,28},{16,0},{20,4},{24,8},{28,12},{1,17},{... | collective-permute-start | bytes 245768 | tf_op jit(solution)/shard_map/ppermute | solution.py:236
  (70 other events, 614.7 us)
Sparse Core Ops, SparseCore 0:
  24.3 142.9 all-gather.1
